TPU v7x, 32 devices: a whole 2x2x4 slice. The times are simulated.
32 devices in a mesh: seq: 4 (over z), fsdp: 8 (over y, x, core).
Axes of the slice: x: 2, y: 2, z: 4, core: 2. Of those that a mesh axis runs over, the one named last changes fastest.
Arguments:
- inputs: bfloat16 [2, 8, 1024, 1536], P(None, 'fsdp', 'seq'), may hold values from -6 to 6
- lengths: int32 [2, 8], P(None, 'fsdp'), may hold values from 256 to 1024, as said below
- expert_ids: int32 [2, 8, 1024, 8], P(None, 'fsdp', 'seq'), may hold values from 0 to 15, all different within a row; in each aligned block of 256 rows (0 to 255, 256 to 511, ..., all dimensions but the last counted through in order) at most 192 rows name the same one
- cotangent: bfloat16 [2, 8, 1024, 1536], P(None, 'fsdp', 'seq'), may hold values from -6 to 6
- gain_attn: bfloat16 [1536], P('fsdp'), may hold values from 0.5 to 1.5
- w_query: bfloat16 [1536, 1536], P('fsdp'), may hold values from -0.15625 to 0.15625
- key_projection: bfloat16 [1536, 512], P('fsdp'), may hold values from -0.15625 to 0.15625
- value_projection: bfloat16 [1536, 512], P('fsdp'), may hold values from -0.15625 to 0.15625
- w_out: bfloat16 [1536, 1536], P('fsdp'), may hold values from -1.75 to 1.75
- gain_moe: bfloat16 [1536], P('fsdp'), may hold values from 0.5 to 1.5
- router: bfloat16 [1536, 16], P('fsdp'), may hold values from -0.078125 to 0.078125
- w_gate: bfloat16 [16, 1536, 512], P('fsdp'), may hold values from -0.15625 to 0.15625
- w_up: bfloat16 [16, 1536, 512], P('fsdp'), may hold values from -0.15625 to 0.15625
- w_down: bfloat16 [16, 512, 1536], P('fsdp'), may hold values from -1.5 to 1.5
Outputs:
- out: bfloat16 [2, 8, 1024, 1536], P(None, 'fsdp', 'seq')
- d_input: bfloat16 [2, 8, 1024, 1536], P(None, 'fsdp', 'seq')
- d_gain_attn: float32 [1536], P('fsdp')
- d_query: float32 [1536, 1536], P('fsdp')
- d_key: float32 [1536, 512], P('fsdp')
- d_value: float32 [1536, 512], P('fsdp')
- d_out: float32 [1536, 1536], P('fsdp')
- d_gain_moe: float32 [1536], P('fsdp')
- d_router: float32 [1536, 16], P('fsdp')
- d_gate: float32 [16, 1536, 512], P('fsdp')
- d_up: float32 [16, 1536, 512], P('fsdp')
- d_down: float32 [16, 512, 1536], P('fsdp')
Inputs may be any that keep to these rules, and one draw needn't show every extreme that they name: `lengths`: rows at or after a sequence's length are padding. In every draw some sequence has exactly 1024 valid tokens. `expert_ids`: each token names 8 different experts. Among the rows of one device (aligned blocks of 1024 // 4 positions of one sequence) no expert is named by more than 192 rows, a bound that some block reaches.
All inputs are finite; a program needn't handle non-finite values.
Results may differ from a plain program's by a relative error of at most 0.024.
Values may be sent and summed in bfloat16 or wider, within the bound.
No kernel may reach another device: no remote copies, remote signals or barrier semaphores. Data moves between devices by JAX's collectives and lax.ppermute only.
A program may use at most 320 MiB of HBM per device.

v0:
```python
import jax
import jax.numpy as jnp
from jax import lax
from jax.sharding import PartitionSpec as P

MODEL_DIM = 1536
QUERY_HEAD_COUNT = 24
KEY_HEAD_COUNT = 8
HEAD_SIZE = 64
F = 512
TOPK = 8
E = 16


EPS = 1e-06
THETA = 10000.0
NEGATIVE = -1e30
HIGHEST = lax.Precision.HIGHEST


def rope_tables(positions):
    half_dim = HEAD_SIZE // 2
    frequency = THETA ** (-(jnp.arange(half_dim, dtype=jnp.float32) * 2.0) / HEAD_SIZE)
    angles = positions.astype(jnp.float32)[:, None] * frequency[None, :]
    return (jnp.cos(angles)[:, None, :], jnp.sin(angles)[:, None, :])


def apply_rotary(values, cosine_table, sine_table):
    half_dim = values.shape[-1] // 2
    first_half = values[..., :half_dim]
    second_half = values[..., half_dim:]
    return jnp.concatenate(
        [
            first_half * cosine_table - second_half * sine_table,
            second_half * cosine_table + first_half * sine_table,
        ],
        axis=-1,
    )


def reverse_rotary(gradient, cosine_table, sine_table):
    half_dim = gradient.shape[-1] // 2
    first_half = gradient[..., :half_dim]
    second_half = gradient[..., half_dim:]
    return jnp.concatenate(
        [
            first_half * cosine_table + second_half * sine_table,
            second_half * cosine_table - first_half * sine_table,
        ],
        axis=-1,
    )


def rows_product(left_side, right_side):
    return lax.dot_general(
        left_side, right_side, (((0,), (0,)), ((), ())), preferred_element_type=jnp.float32
    )


def against(left_side, right_side):
    return lax.dot_general(
        left_side, right_side, (((1,), (1,)), ((), ())), preferred_element_type=jnp.float32
    )


def normalize(rows_in, gain_full):
    inverse = lax.rsqrt(jnp.mean(rows_in * rows_in, axis=-1, keepdims=True) + EPS)
    unit_rows = rows_in * inverse
    return (unit_rows, inverse, (unit_rows * gain_full).astype(jnp.bfloat16))


def normalize_back(grad_normed, unit_rows, inverse, gain_full):
    grad_unit = grad_normed * gain_full
    grad_rows = inverse * (
        grad_unit - unit_rows * jnp.mean(grad_unit * unit_rows, axis=-1, keepdims=True)
    )
    return (grad_rows, jnp.sum(grad_normed * unit_rows, axis=0))


def block_mask(first_row, rows_per_block, full_len, seq_length):
    query_pos = first_row + jnp.arange(rows_per_block, dtype=jnp.int32)
    key_pos = jnp.arange(full_len, dtype=jnp.int32)
    return (key_pos[None, :] <= query_pos[:, None]) & (key_pos[None, :] < seq_length)


def attend_forward(query_seq, key_seq, value_seq, seq_length):
    full_len = query_seq.shape[0]
    kv_heads = key_seq.shape[1] // HEAD_SIZE
    query_group_width = query_seq.shape[1] // (HEAD_SIZE * kv_heads)
    rows_per_block = min(512, full_len)
    number_of_blocks = full_len // rows_per_block
    score_scale = HEAD_SIZE ** (-0.5)
    query_block_list = query_seq.reshape(
        number_of_blocks, rows_per_block, kv_heads, query_group_width, HEAD_SIZE
    )
    per_head_keys = key_seq.reshape(full_len, kv_heads, HEAD_SIZE)
    per_head_values = value_seq.reshape(full_len, kv_heads, HEAD_SIZE)

    def one_block(pieces):
        query_block, first_row = pieces
        scores = (
            jnp.einsum(
                "qkgd,skd->kgqs", query_block, per_head_keys, preferred_element_type=jnp.float32
            )
            * score_scale
        )
        allowed = block_mask(first_row, rows_per_block, full_len, seq_length)
        scores = jnp.where(allowed[None, None], scores, NEGATIVE)
        top_score = jnp.max(scores, axis=-1, keepdims=True)
        exponent = jnp.exp(scores - top_score)
        totals = jnp.sum(exponent, axis=-1, keepdims=True)
        attn_probs = (exponent / totals).astype(jnp.bfloat16)
        block_out = jnp.einsum(
            "kgqs,skd->qkgd", attn_probs, per_head_values, preferred_element_type=jnp.float32
        )
        return (
            block_out.astype(jnp.bfloat16).reshape(rows_per_block, -1),
            (top_score + jnp.log(totals))[..., 0],
        )

    starts = jnp.arange(number_of_blocks, dtype=jnp.int32) * rows_per_block
    outputs, log_total = lax.map(one_block, (query_block_list, starts))
    return (outputs.reshape(full_len, -1), log_total)


def attend_backward(query_seq, key_seq, value_seq, grad_seq, log_total, seq_length):
    full_len = query_seq.shape[0]
    kv_heads = key_seq.shape[1] // HEAD_SIZE
    query_group_width = query_seq.shape[1] // (HEAD_SIZE * kv_heads)
    rows_per_block = min(512, full_len)
    number_of_blocks = full_len // rows_per_block
    score_scale = HEAD_SIZE ** (-0.5)
    query_block_list = query_seq.reshape(
        number_of_blocks, rows_per_block, kv_heads, query_group_width, HEAD_SIZE
    )
    grad_blocks = grad_seq.reshape(
        number_of_blocks, rows_per_block, kv_heads, query_group_width, HEAD_SIZE
    )
    per_head_keys = key_seq.reshape(full_len, kv_heads, HEAD_SIZE)
    per_head_values = value_seq.reshape(full_len, kv_heads, HEAD_SIZE)

    def one_block(carry, pieces):
        grad_key, value_gradient = carry
        query_block, grad_block, total_block, first_row = pieces
        scores = (
            jnp.einsum(
                "qkgd,skd->kgqs", query_block, per_head_keys, preferred_element_type=jnp.float32
            )
            * score_scale
        )
        allowed = block_mask(first_row, rows_per_block, full_len, seq_length)
        scores = jnp.where(allowed[None, None], scores, NEGATIVE)
        attn_probs = jnp.exp(scores - total_block[..., None])
        probs_low = attn_probs.astype(jnp.bfloat16)
        value_gradient = value_gradient + jnp.einsum(
            "kgqs,qkgd->skd", probs_low, grad_block, preferred_element_type=jnp.float32
        )
        grad_probs = jnp.einsum(
            "qkgd,skd->kgqs", grad_block, per_head_values, preferred_element_type=jnp.float32
        )
        inner_sum = jnp.sum(attn_probs * grad_probs, axis=-1, keepdims=True)
        grad_scores = (attn_probs * (grad_probs - inner_sum)).astype(jnp.bfloat16)
        grad_query = (
            jnp.einsum(
                "kgqs,skd->qkgd", grad_scores, per_head_keys, preferred_element_type=jnp.float32
            )
            * score_scale
        )
        grad_key = (
            grad_key
            + jnp.einsum(
                "kgqs,qkgd->skd", grad_scores, query_block, preferred_element_type=jnp.float32
            )
            * score_scale
        )
        return (
            (grad_key, value_gradient),
            grad_query.astype(jnp.bfloat16).reshape(rows_per_block, -1),
        )

    starts = jnp.arange(number_of_blocks, dtype=jnp.int32) * rows_per_block
    empty_heads = jnp.zeros((full_len, kv_heads, HEAD_SIZE), jnp.float32)
    (grad_key, value_gradient), grad_query = lax.scan(
        one_block, (empty_heads, empty_heads), (query_block_list, grad_blocks, log_total, starts)
    )
    return (
        grad_query.reshape(full_len, -1),
        grad_key.astype(jnp.bfloat16).reshape(full_len, -1),
        value_gradient.astype(jnp.bfloat16).reshape(full_len, -1),
    )


def expert_forward(normed_rows, gate_piece, up_piece, down_piece):
    pre_gate = jnp.einsum(
        "rd,edf->erf", normed_rows, gate_piece, preferred_element_type=jnp.float32
    )
    pre_up = jnp.einsum("rd,edf->erf", normed_rows, up_piece, preferred_element_type=jnp.float32)
    hidden = (jax.nn.silu(pre_gate) * pre_up).astype(jnp.bfloat16)
    expert_out = jnp.einsum("erf,efd->erd", hidden, down_piece, preferred_element_type=jnp.float32)
    return (pre_gate, pre_up, hidden, expert_out)


def expert_backward(normed_rows, gate_sel, grad_out, gate_piece, up_piece, down_piece):
    pre_gate, pre_up, hidden, expert_out = expert_forward(
        normed_rows, gate_piece, up_piece, down_piece
    )
    grad_gates = jnp.transpose(jnp.sum(grad_out[None] * expert_out, axis=-1))
    grad_expert = (jnp.transpose(gate_sel)[:, :, None] * grad_out[None]).astype(jnp.bfloat16)
    grad_hidden = jnp.einsum(
        "erd,efd->erf", grad_expert, down_piece, preferred_element_type=jnp.float32
    )
    sigmoid_gate = jax.nn.sigmoid(pre_gate)
    grad_pre = jnp.concatenate(
        [
            grad_hidden * pre_up * sigmoid_gate * (1.0 + pre_gate * (1.0 - sigmoid_gate)),
            grad_hidden * pre_gate * sigmoid_gate,
        ],
        axis=-1,
    ).astype(jnp.bfloat16)
    hidden_width = gate_piece.shape[2]
    grad_normed = jnp.einsum(
        "erf,edf->rd", grad_pre[..., :hidden_width], gate_piece, preferred_element_type=jnp.float32
    )
    grad_normed = grad_normed + jnp.einsum(
        "erf,edf->rd", grad_pre[..., hidden_width:], up_piece, preferred_element_type=jnp.float32
    )
    return (grad_gates, grad_normed, grad_pre, hidden, grad_expert)


def expert_weight_grads(normed_rows, grad_pre, hidden, grad_expert):
    hidden_width = hidden.shape[2]
    grad_gate_w = jnp.einsum(
        "rd,erf->edf", normed_rows, grad_pre[..., :hidden_width], preferred_element_type=jnp.float32
    )
    grad_up_w = jnp.einsum(
        "rd,erf->edf", normed_rows, grad_pre[..., hidden_width:], preferred_element_type=jnp.float32
    )
    grad_down_w = jnp.einsum(
        "erf,erd->efd", hidden, grad_expert, preferred_element_type=jnp.float32
    )
    return (grad_gate_w, grad_up_w, grad_down_w)


def gated_sum(gate_sel, expert_out):
    return jnp.sum(jnp.transpose(gate_sel)[:, :, None] * expert_out, axis=0)


def on_device(
    inputs,
    lengths,
    expert_ids,
    cotangent,
    gain_attn,
    w_query,
    key_projection,
    value_projection,
    w_out,
    gain_moe,
    router,
    w_gate,
    w_up,
    w_down,
):
    micro_count, local_sequence, local_token_rows, model_width = inputs.shape
    total_row_count = local_sequence * local_token_rows
    local_experts = w_gate.shape[0]
    own_first = lax.axis_index("fsdp") * local_experts
    positions = lax.axis_index("seq") * local_token_rows + jnp.arange(
        local_token_rows, dtype=jnp.int32
    )
    cosine_table, sine_table = rope_tables(jnp.tile(positions, local_sequence))
    expert_range = jnp.arange(E, dtype=jnp.int32)
    acc_query = jnp.zeros((MODEL_DIM, QUERY_HEAD_COUNT * HEAD_SIZE), jnp.float32)
    summed_key_grad = jnp.zeros((MODEL_DIM, KEY_HEAD_COUNT * HEAD_SIZE), jnp.float32)
    summed_value_grad = jnp.zeros((MODEL_DIM, KEY_HEAD_COUNT * HEAD_SIZE), jnp.float32)
    acc_out = jnp.zeros((QUERY_HEAD_COUNT * HEAD_SIZE, MODEL_DIM), jnp.float32)
    acc_router = jnp.zeros((MODEL_DIM, E), jnp.float32)
    acc_gain_one = jnp.zeros((MODEL_DIM,), jnp.float32)
    acc_gain_two = jnp.zeros((MODEL_DIM,), jnp.float32)
    acc_gate = jnp.zeros((local_experts, MODEL_DIM, F), jnp.float32)
    acc_up = jnp.zeros((local_experts, MODEL_DIM, F), jnp.float32)
    acc_down = jnp.zeros((local_experts, F, MODEL_DIM), jnp.float32)
    outs_list, grads_list = ([], [])
    for micro_index in range(micro_count):
        gathered = (
            lax.all_gather(w_query, "fsdp", axis=0, tiled=True),
            lax.all_gather(key_projection, "fsdp", axis=0, tiled=True),
            lax.all_gather(value_projection, "fsdp", axis=0, tiled=True),
            lax.all_gather(w_out, "fsdp", axis=0, tiled=True),
            lax.all_gather(router, "fsdp", axis=0, tiled=True),
            lax.all_gather(gain_attn, "fsdp", axis=0, tiled=True),
            lax.all_gather(gain_moe, "fsdp", axis=0, tiled=True),
        )
        query_full, key_full, value_full, out_full, router_full, gain_one, gain_two = gathered
        gain_one = gain_one.astype(jnp.float32)
        gain_two = gain_two.astype(jnp.float32)
        seq_lengths = lengths[micro_index]
        rows_in = inputs[micro_index].reshape(total_row_count, model_width).astype(jnp.float32)
        valid_rows = (positions[None, :] < seq_lengths[:, None]).reshape(total_row_count)
        unit_one, inverse_one, first_normed_rows = normalize(rows_in, gain_one)
        query_row_data = jnp.dot(
            first_normed_rows, query_full, preferred_element_type=jnp.float32
        ).reshape(total_row_count, QUERY_HEAD_COUNT, HEAD_SIZE)
        query_row_data = apply_rotary(query_row_data, cosine_table, sine_table).astype(jnp.bfloat16)
        key_row_data = jnp.dot(
            first_normed_rows, key_full, preferred_element_type=jnp.float32
        ).reshape(total_row_count, KEY_HEAD_COUNT, HEAD_SIZE)
        key_row_data = apply_rotary(key_row_data, cosine_table, sine_table).astype(jnp.bfloat16)
        value_row_data = jnp.dot(
            first_normed_rows, value_full, preferred_element_type=jnp.float32
        ).astype(jnp.bfloat16)
        query_heads, per_head_keys, per_head_values = (
            lax.all_to_all(
                query_row_data.reshape(
                    local_sequence, local_token_rows, QUERY_HEAD_COUNT * HEAD_SIZE
                ),
                "seq",
                split_axis=2,
                concat_axis=1,
                tiled=True,
            ),
            lax.all_to_all(
                key_row_data.reshape(local_sequence, local_token_rows, KEY_HEAD_COUNT * HEAD_SIZE),
                "seq",
                split_axis=2,
                concat_axis=1,
                tiled=True,
            ),
            lax.all_to_all(
                value_row_data.reshape(
                    local_sequence, local_token_rows, KEY_HEAD_COUNT * HEAD_SIZE
                ),
                "seq",
                split_axis=2,
                concat_axis=1,
                tiled=True,
            ),
        )
        head_out, log_total = jax.vmap(attend_forward)(
            query_heads, per_head_keys, per_head_values, seq_lengths
        )
        head_rows = lax.all_to_all(
            head_out, "seq", split_axis=1, concat_axis=2, tiled=True
        ).reshape(total_row_count, QUERY_HEAD_COUNT * HEAD_SIZE)
        residual = rows_in + jnp.dot(head_rows, out_full, preferred_element_type=jnp.float32)
        unit_two, inverse_two, normed_two = normalize(residual, gain_two)
        logits = jnp.dot(normed_two, router_full, preferred_element_type=jnp.float32)
        chosen_ids = expert_ids[micro_index].reshape(total_row_count, TOPK)
        chosen = jnp.sum(
            (chosen_ids[:, :, None] == expert_range[None, None, :]).astype(jnp.float32), axis=1
        )
        top_logit = jnp.max(jnp.where(chosen > 0, logits, NEGATIVE), axis=-1, keepdims=True)
        exponent = jnp.exp(logits - top_logit) * chosen
        gates_exact = exponent / jnp.sum(exponent, axis=-1, keepdims=True)
        gates_low = gates_exact.astype(jnp.bfloat16)
        all_normed, all_gates = (
            lax.all_gather(normed_two, "fsdp", axis=0, tiled=True),
            lax.all_gather(gates_low, "fsdp", axis=0, tiled=True),
        )
        own_gates = lax.dynamic_slice_in_dim(all_gates, own_first, local_experts, 1).astype(
            jnp.float32
        )
        unused_gate, unused_up, unused_hidden, expert_out = expert_forward(
            all_normed, w_gate, w_up, w_down
        )
        moe_sum = lax.psum_scatter(
            gated_sum(own_gates, expert_out).astype(jnp.bfloat16),
            "fsdp",
            scatter_dimension=0,
            tiled=True,
        ).astype(jnp.float32)
        outs_list.append(
            jnp.where(valid_rows[:, None], residual + moe_sum, 0.0)
            .astype(jnp.bfloat16)
            .reshape(local_sequence, local_token_rows, model_width)
        )
        grad_out = jnp.where(
            valid_rows[:, None],
            cotangent[micro_index].reshape(total_row_count, model_width).astype(jnp.float32),
            0.0,
        )
        grad_low = grad_out.astype(jnp.bfloat16)
        all_grad = lax.all_gather(grad_low, "fsdp", axis=0, tiled=True)
        own_grad_gates, grad_normed_all, grad_pre, hidden, grad_expert = expert_backward(
            all_normed, own_gates, all_grad.astype(jnp.float32), w_gate, w_up, w_down
        )
        grad_gate_w, grad_up_w, grad_down_w = expert_weight_grads(
            all_normed, grad_pre, hidden, grad_expert
        )
        acc_gate = acc_gate + grad_gate_w
        acc_up = acc_up + grad_up_w
        acc_down = acc_down + grad_down_w
        gate_columns = lax.dynamic_update_slice_in_dim(
            jnp.zeros((all_normed.shape[0], E), jnp.float32), own_grad_gates, own_first, 1
        )
        back_term = jnp.concatenate([grad_normed_all, gate_columns], axis=1)
        returned = lax.psum_scatter(
            back_term.astype(jnp.bfloat16), "fsdp", scatter_dimension=0, tiled=True
        ).astype(jnp.float32)
        grad_normed_experts = returned[:, :MODEL_DIM]
        grad_gates = returned[:, MODEL_DIM:]
        grad_logits = gates_exact * (
            grad_gates - jnp.sum(gates_exact * grad_gates, axis=-1, keepdims=True)
        )
        acc_router = acc_router + jnp.dot(
            jnp.transpose(normed_two.astype(jnp.float32)),
            grad_logits,
            precision=HIGHEST,
            preferred_element_type=jnp.float32,
        )
        grad_normed_two = grad_normed_experts + jnp.dot(
            grad_logits,
            jnp.transpose(router_full.astype(jnp.float32)),
            precision=HIGHEST,
            preferred_element_type=jnp.float32,
        )
        grad_norm_two, gain_grad_two = normalize_back(
            grad_normed_two, unit_two, inverse_two, gain_two
        )
        acc_gain_two = acc_gain_two + gain_grad_two
        grad_residual = grad_out + grad_norm_two
        grad_attn = grad_residual.astype(jnp.bfloat16)
        acc_out = acc_out + rows_product(head_rows, grad_attn)
        grad_head_rows = against(grad_attn, out_full).astype(jnp.bfloat16)
        grad_heads = lax.all_to_all(
            grad_head_rows.reshape(local_sequence, local_token_rows, QUERY_HEAD_COUNT * HEAD_SIZE),
            "seq",
            split_axis=2,
            concat_axis=1,
            tiled=True,
        )
        grad_q_heads, grad_k_heads, grad_v_heads = jax.vmap(attend_backward)(
            query_heads, per_head_keys, per_head_values, grad_heads, log_total, seq_lengths
        )
        back_query, returned_key_grad, returned_value_grad = (
            lax.all_to_all(grad_q_heads, "seq", split_axis=1, concat_axis=2, tiled=True),
            lax.all_to_all(grad_k_heads, "seq", split_axis=1, concat_axis=2, tiled=True),
            lax.all_to_all(grad_v_heads, "seq", split_axis=1, concat_axis=2, tiled=True),
        )
        grad_query = (
            reverse_rotary(
                back_query.reshape(total_row_count, QUERY_HEAD_COUNT, HEAD_SIZE).astype(
                    jnp.float32
                ),
                cosine_table,
                sine_table,
            )
            .astype(jnp.bfloat16)
            .reshape(total_row_count, QUERY_HEAD_COUNT * HEAD_SIZE)
        )
        grad_key = (
            reverse_rotary(
                returned_key_grad.reshape(total_row_count, KEY_HEAD_COUNT, HEAD_SIZE).astype(
                    jnp.float32
                ),
                cosine_table,
                sine_table,
            )
            .astype(jnp.bfloat16)
            .reshape(total_row_count, KEY_HEAD_COUNT * HEAD_SIZE)
        )
        value_gradient = returned_value_grad.reshape(total_row_count, KEY_HEAD_COUNT * HEAD_SIZE)
        acc_query = acc_query + rows_product(first_normed_rows, grad_query)
        summed_key_grad = summed_key_grad + rows_product(first_normed_rows, grad_key)
        summed_value_grad = summed_value_grad + rows_product(first_normed_rows, value_gradient)
        grad_normed_one = (
            against(grad_query, query_full)
            + against(grad_key, key_full)
            + against(value_gradient, value_full)
        )
        grad_rows, gain_grad_one = normalize_back(grad_normed_one, unit_one, inverse_one, gain_one)
        acc_gain_one = acc_gain_one + gain_grad_one
        grads_list.append(
            (grad_rows + grad_residual)
            .astype(jnp.bfloat16)
            .reshape(local_sequence, local_token_rows, model_width)
        )
    gate_part, up_part, down_part = (acc_gate, acc_up, acc_down)
    shard_grads = (
        lax.psum_scatter(
            acc_query.astype(jnp.bfloat16), "fsdp", scatter_dimension=0, tiled=True
        ).astype(jnp.float32),
        lax.psum_scatter(
            summed_key_grad.astype(jnp.bfloat16), "fsdp", scatter_dimension=0, tiled=True
        ).astype(jnp.float32),
        lax.psum_scatter(
            summed_value_grad.astype(jnp.bfloat16), "fsdp", scatter_dimension=0, tiled=True
        ).astype(jnp.float32),
        lax.psum_scatter(
            acc_out.astype(jnp.bfloat16), "fsdp", scatter_dimension=0, tiled=True
        ).astype(jnp.float32),
        lax.psum_scatter(
            acc_router.astype(jnp.bfloat16), "fsdp", scatter_dimension=0, tiled=True
        ).astype(jnp.float32),
        lax.psum_scatter(
            acc_gain_one.astype(jnp.bfloat16), "fsdp", scatter_dimension=0, tiled=True
        ).astype(jnp.float32),
        lax.psum_scatter(
            acc_gain_two.astype(jnp.bfloat16), "fsdp", scatter_dimension=0, tiled=True
        ).astype(jnp.float32),
    )
    shared_pieces = (
        lax.psum_scatter(
            shard_grads[0].astype(jnp.bfloat16), "seq", scatter_dimension=1, tiled=True
        ).astype(jnp.float32),
        lax.psum_scatter(
            shard_grads[1].astype(jnp.bfloat16), "seq", scatter_dimension=1, tiled=True
        ).astype(jnp.float32),
        lax.psum_scatter(
            shard_grads[2].astype(jnp.bfloat16), "seq", scatter_dimension=1, tiled=True
        ).astype(jnp.float32),
        lax.psum_scatter(
            shard_grads[3].astype(jnp.bfloat16), "seq", scatter_dimension=1, tiled=True
        ).astype(jnp.float32),
        lax.psum_scatter(
            shard_grads[4].astype(jnp.bfloat16), "seq", scatter_dimension=1, tiled=True
        ).astype(jnp.float32),
        lax.psum_scatter(
            shard_grads[5].reshape(1, -1).astype(jnp.bfloat16),
            "seq",
            scatter_dimension=1,
            tiled=True,
        ).astype(jnp.float32),
        lax.psum_scatter(
            shard_grads[6].reshape(1, -1).astype(jnp.bfloat16),
            "seq",
            scatter_dimension=1,
            tiled=True,
        ).astype(jnp.float32),
        lax.psum_scatter(
            gate_part.astype(jnp.bfloat16), "seq", scatter_dimension=1, tiled=True
        ).astype(jnp.float32),
        lax.psum_scatter(
            up_part.astype(jnp.bfloat16), "seq", scatter_dimension=1, tiled=True
        ).astype(jnp.float32),
        lax.psum_scatter(
            down_part.astype(jnp.bfloat16), "seq", scatter_dimension=1, tiled=True
        ).astype(jnp.float32),
    )
    summed = (
        lax.all_gather(shared_pieces[0].astype(jnp.bfloat16), "seq", axis=1, tiled=True).astype(
            jnp.float32
        ),
        lax.all_gather(shared_pieces[1].astype(jnp.bfloat16), "seq", axis=1, tiled=True).astype(
            jnp.float32
        ),
        lax.all_gather(shared_pieces[2].astype(jnp.bfloat16), "seq", axis=1, tiled=True).astype(
            jnp.float32
        ),
        lax.all_gather(shared_pieces[3].astype(jnp.bfloat16), "seq", axis=1, tiled=True).astype(
            jnp.float32
        ),
        lax.all_gather(shared_pieces[4].astype(jnp.bfloat16), "seq", axis=1, tiled=True).astype(
            jnp.float32
        ),
        lax.all_gather(shared_pieces[5].astype(jnp.bfloat16), "seq", axis=1, tiled=True).astype(
            jnp.float32
        ),
        lax.all_gather(shared_pieces[6].astype(jnp.bfloat16), "seq", axis=1, tiled=True).astype(
            jnp.float32
        ),
        lax.all_gather(shared_pieces[7].astype(jnp.bfloat16), "seq", axis=1, tiled=True).astype(
            jnp.float32
        ),
        lax.all_gather(shared_pieces[8].astype(jnp.bfloat16), "seq", axis=1, tiled=True).astype(
            jnp.float32
        ),
        lax.all_gather(shared_pieces[9].astype(jnp.bfloat16), "seq", axis=1, tiled=True).astype(
            jnp.float32
        ),
    )
    return (
        jnp.stack(outs_list),
        jnp.stack(grads_list),
        summed[5].reshape(-1),
        summed[0],
        summed[1],
        summed[2],
        summed[3],
        summed[6].reshape(-1),
        summed[4],
        summed[7],
        summed[8],
        summed[9],
    )


def solution(mesh):
    placed = (
        P(None, "fsdp", "seq", None),
        P(None, "fsdp"),
        P(None, "fsdp", "seq", None),
        P(None, "fsdp", "seq", None),
        P("fsdp"),
        P("fsdp", None),
        P("fsdp", None),
        P("fsdp", None),
        P("fsdp", None),
        P("fsdp"),
        P("fsdp", None),
        P("fsdp", None, None),
        P("fsdp", None, None),
        P("fsdp", None, None),
    )
    return jax.shard_map(
        on_device,
        mesh=mesh,
        in_specs=placed,
        out_specs=(
            P(None, "fsdp", "seq", None),
            P(None, "fsdp", "seq", None),
            P("fsdp"),
            P("fsdp", None),
            P("fsdp", None),
            P("fsdp", None),
            P("fsdp", None),
            P("fsdp"),
            P("fsdp", None),
            P("fsdp", None, None),
            P("fsdp", None, None),
            P("fsdp", None, None),
        ),
        check_vma=False,
    )
```

profile of v0, /device:TPU:0, one launch (start us, length us, event | category | flops | bytes accessed | tf_op | source)
XLA Modules:
  0.0 1673.6 jit_solution(15752998764628560955)
XLA Ops:
  13.8 16.1 all-reduce.8
  77.1 29.8 %all-gather.14.cloned.1.call-done = bf16[1536,1536]{1,0:T(8,128)(2,1)} async-done(((bf16[192,1536]{1,0:T(8,128)(2,1)}), bf16[1536,1536]{1,0:T(8,128)(2,1)}) %all-gather.14.cloned.1.call-update) | async-done | bytes 4718608 | tf_op jit(solution)/shard_map/all_gather | solution.py:286
  189.7 35.9 %while.54 = (s32[]{:T(128)}, bf16[2,1,512,384]{3,2,0,1:T(8,128)(2,1)}, f32[2,1,2,3,512]{4,3,2,1,0:T(4,128)S(1)}, s32[2]{0:T(128)S(1)}, s32[1,1]{1,0:T(1,128)}, /...) while((s32[]{:T(128)}, ...), condition=%wide.region_4.5_spmd, body=%wide.region_1.4_spmd.sunk | while | flops 844298752 | bytes 43895952 | solution.py:122
  242.8 19.7 %all-to-all-done.3 = bf16[4,2,49152]{2,1,0:T(2,128)(2,1)} async-done(((bf16[4,2,49152]{2,1,0:T(2,128)(2,1)}), bf16[4,2,49152]{2,1,0:T(2,128)(2,1)}, u32[]{:S(2)}, u32[]{:S(2)}) %all-to-all-start.3) | async-done | bytes 786464 | tf_op jit(solution)/shard_map/all_to_all | solution.py:342
  307.3 15.9 all-gather.22.cloned.1.call-done
  344.5 17.3 %fusion.147 = (bf16[2,2048,512]{2,1,0:T(8,128)(2,1)}, bf16[2,2048,512]{2,1,0:T(8,128)(2,1)S(1)}, bf16[2,2048,512]{2,1,0:T(8,128)(2,1)}) fusion(f32[2048,2,512]{2,0,1:T(8,128)} %fusion.164, f32[2048,2,512]{2,0,1:T(8,128)} %fusion.162, bf16[2,512,1536]{2,1,0:T(8,128)(2,1)S(1)} %copy-done, f32[2048,1536]{0,1:T(8,128)} %convert_element_type.545, ...), kind=kOutput, calls=%fused_computation.191 | convolution fusion | flops 6488588288 | bytes 45105152 | tf_op jit(solution)/shard_map/erd,efd->erf/dot_general | solution.py:209
  370.9 16.7 multiply_reduce_fusion.1
  496.9 35.9 %while.55 = (s32[]{:T(128)}, bf16[2,1,512,384]{3,2,0,1:T(8,128)(2,1)}, f32[2,1,2,3,512]{4,3,2,1,0:T(4,128)S(1)}, s32[2]{0:T(128)S(1)}, s32[1,1]{1,0:T(1,128)}, /...) while((s32[]{:T(128)}, ...), condition=%wide.region_15.16_spmd, body=%wide.region_12.15_spmd.sunk | while | flops 844298752 | bytes 43895952 | solution.py:122
  545.8 23.9 %all_to_all.216 = bf16[4,2,49152]{2,1,0:T(2,128)(2,1)} all-to-all(bf16[4,2,49152]{2,1,0:T(2,128)(2,1)} %reshape.1102), channel_id=1, replica_groups=mesh['seq'=4,'fsdp'=8] {'seq'}, dimensions={0} | all-to-all | bytes 1572864 | tf_op jit(solution)/shard_map/all_to_all | solution.py:342
  616.1 25.5 %all-gather.24.cloned.1.call-done = bf16[2048,1536]{0,1:T(8,128)(2,1)} async-done(((bf16[256,1536]{0,1:T(8,128)(2,1)}), bf16[2048,1536]{0,1:T(8,128)(2,1)}) %all-gather.24.cloned.1.call-update) | async-done | bytes 6291472 | tf_op jit(solution)/shard_map/all_gather | solution.py:357
  662.7 17.3 %fusion.137 = (bf16[2,2048,512]{2,1,0:T(8,128)(2,1)}, bf16[2,2048,512]{2,1,0:T(8,128)(2,1)S(1)}, bf16[2,2048,512]{2,1,0:T(8,128)(2,1)}) fusion(f32[2048,2,512]{2,0,1:T(8,128)} %fusion.156, f32[2048,2,512]{2,0,1:T(8,128)} %fusion.154, bf16[2,512,1536]{2,1,0:T(8,128)(2,1)S(1)} %copy-done, f32[2048,1536]{0,1:T(8,128)} %convert_element_type.568, ...), kind=kOutput, calls=%fused_computation.175 | convolution fusion | flops 6488588288 | bytes 45105152 | tf_op jit(solution)/shard_map/erd,efd->erf/dot_general | solution.py:209
  689.1 16.6 multiply_reduce_fusion
  775.2 20.5 %all-to-all-done.8 = bf16[4,2,49152]{2,1,0:T(2,128)(2,1)S(1)} async-done(((bf16[4,2,49152]{2,1,0:T(2,128)(2,1)}), bf16[4,2,49152]{2,1,0:T(2,128)(2,1)S(1)}, u32[]{:S(2)}, u32[]{:S(2)}) %all-to-all-start.8) | async-done | bytes 786464 | tf_op jit(solution)/shard_map/all_to_all | solution.py:425
  833.9 66.7 %while.56 = (s32[]{:T(128)}, f32[1,1024,2,64]{1,3,2,0:T(8,128)S(1)}, f32[1,1024,2,64]{1,3,2,0:T(8,128)}, bf16[2,1,512,384]{3,2,0,1:T(8,128)(2,1)}, bf16[2,1,512,...) while((s32[]{:T(128)}, ...), condition=%wide.region_28.29_spmd.clone, body=%wide.region_26.28_spmd.clone.sunk | while | flops 2062547456 | bytes 184781616 | solution.py:183
  967.8 20.9 %all-to-all-done.12 = bf16[4,2,49152]{2,1,0:T(2,128)(2,1)} async-done(((bf16[4,2,49152]{2,1,0:T(2,128)(2,1)}), bf16[4,2,49152]{2,1,0:T(2,128)(2,1)}, u32[]{:S(2)}, u32[]{:S(2)}) %all-to-all-start.12) | async-done | bytes 786464 | tf_op jit(solution)/shard_map/all_to_all | solution.py:425
  999.8 66.8 %while.57 = (s32[]{:T(128)}, f32[1,1024,2,64]{1,3,2,0:T(8,128)S(1)}, f32[1,1024,2,64]{1,3,2,0:T(8,128)}, bf16[2,1,512,384]{3,2,0,1:T(8,128)(2,1)}, bf16[2,1,512,...) while((s32[]{:T(128)}, ...), condition=%wide.region_36.37_spmd.clone, body=%wide.region_34.36_spmd.clone.sunk | while | flops 2062547456 | bytes 184781616 | solution.py:183
  1249.0 15.1 reduce-scatter.67.cloned.1.call-done
  1264.9 64.1 %all-gather.34.cloned.1.call-done = bf16[2,512,1536]{2,1,0:T(8,128)(2,1)} async-done(((bf16[2,128,1536]{2,1,0:T(8,128)(2,1)}), bf16[2,512,1536]{2,1,0:T(8,128)(2,1)}) %all-gather.34.cloned.1.call-update) | async-done | bytes 3145744 | tf_op jit(solution)/shard_map/all_gather | solution.py:568
  1334.5 58.2 %all-gather.32.cloned.1.call-done = bf16[2,1536,512]{1,2,0:T(8,128)(2,1)} async-done(((bf16[2,384,512]{1,2,0:T(8,128)(2,1)}), bf16[2,1536,512]{1,2,0:T(8,128)(2,1)}) %all-gather.32.cloned.1.call-update) | async-done | bytes 3145744 | tf_op jit(solution)/shard_map/all_gather | solution.py:565
  1398.1 58.2 %all-gather.30.cloned.1.call-done = bf16[2,1536,512]{1,2,0:T(8,128)(2,1)} async-done(((bf16[2,384,512]{1,2,0:T(8,128)(2,1)}), bf16[2,1536,512]{1,2,0:T(8,128)(2,1)}) %all-gather.30.cloned.1.call-update) | async-done | bytes 3145744 | tf_op jit(solution)/shard_map/all_gather | solution.py:562
  1461.7 51.0 %reduce-scatter.45.cloned.1.call-done = bf16[192,1536]{1,0:T(8,128)(2,1)} async-done(((bf16[1536,1536]{1,0:T(8,128)(2,1)}), bf16[192,1536]{1,0:T(8,128)(2,1)}) %reduce-scatter.45.cloned.1.call-update) | async-done | bytes 589840 | tf_op jit(solution)/shard_map/reduce_scatter | solution.py:480
  1534.6 18.7 %reduce-scatter.55.cloned.1.call-done = bf16[48,1]{1,0:T(8,128)(2,1)} async-done(((bf16[192,1]{1,0:T(8,128)(2,1)}), bf16[48,1]{1,0:T(8,128)(2,1)}) %reduce-scatter.55.cloned.1.call-update) | async-done | bytes 112
  1620.4 20.0 %all_gather.93 = bf16[192,1536]{1,0:T(8,128)(2,1)S(1)} all-gather(bf16[192,384]{1,0:T(8,128)(2,1)S(1)} %copy.729), channel_id=1, replica_groups=mesh['seq'=4,'fsdp'=8] {'seq'}, dimensions={1}, use_global_device_ids=true | all-gather | bytes 737280 | tf_op jit(solution)/shard_map/all_gather | solution.py:550
  1649.1 16.6 all_gather.90
  (732 shorter events, 1111.5 us)
Async XLA Ops:
  9.4 261.5 %all-gather.20.cloned.1.call-start = ((), (), s32[]{:S(2)}) async-start(), calls=%async_computation.37 | async-start | bytes 5308416 | tf_op jit(solution)/shard_map/all_gather | solution.py:289
  156.8 141.6 %all-gather.26.cloned.1.call-start = ((), (), s32[]{:S(2)}) async-start(), calls=%async_computation.42 | async-start | bytes 7077888 | tf_op jit(solution)/shard_map/all_gather | solution.py:383
  278.0 306.0 %reduce-scatter.41.cloned.1.call-start = ((), (), s32[]{:S(2)}) async-start(), calls=%async_computation.43 | async-start | bytes 7151616 | tf_op jit(solution)/shard_map/reduce_scatter | solution.py:397
  407.2 183.7 %reduce-scatter.37.cloned.1.call-start = ((), (), s32[]{:S(2)}) async-start(), calls=%async_computation.39 | async-start | bytes 7077888 | tf_op jit(solution)/shard_map/reduce_scatter | solution.py:366
  464.5 131.7 %all-gather.28.cloned.1.call-start = ((), (), s32[]{:S(2)}) async-start(), calls=%async_computation.44 | async-start | bytes 7077888 | tf_op jit(solution)/shard_map/all_gather | solution.py:383
  470.2 171.4 %all-gather.24.cloned.1.call-start = ((), (), s32[]{:S(2)}) async-start(), calls=%async_computation.40 | async-start | bytes 7077888 | tf_op jit(solution)/shard_map/all_gather | solution.py:357
  596.2 321.5 %reduce-scatter.43.cloned.1.call-start = ((), (), s32[]{:S(2)}) async-start(), calls=%async_computation.45 | async-start | bytes 7151616 | tf_op jit(solution)/shard_map/reduce_scatter | solution.py:397
  725.5 197.5 %reduce-scatter.39.cloned.1.call-start = ((), (), s32[]{:S(2)}) async-start(), calls=%async_computation.41 | async-start | bytes 7077888 | tf_op jit(solution)/shard_map/reduce_scatter | solution.py:366
  726.1 408.2 %reduce-scatter.53.cloned.1.call-start = ((), (), s32[]{:S(2)}) async-start(), calls=%async_computation.52 | async-start | bytes 3932160 | tf_op jit(solution)/shard_map/reduce_scatter | solution.py:536
  775.2 359.7 %reduce-scatter.71.cloned.1.call-start = ((), (), s32[]{:S(2)}) async-start(), calls=%async_computation.62 | async-start | bytes 3932160
  945.9 194.0 %reduce-scatter.69.cloned.1.call-start = ((), (), s32[]{:S(2)}) async-start(), calls=%async_computation.61 | async-start | bytes 3932160
  1076.2 162.3 %reduce-scatter.49.cloned.1.call-start = ((), (), s32[]{:S(2)}) async-start(), calls=%async_computation.48 | async-start | bytes 1769472 | tf_op jit(solution)/shard_map/reduce_scatter | solution.py:486
  1108.0 132.4 %reduce-scatter.47.cloned.1.call-start = ((), (), s32[]{:S(2)}) async-start(), calls=%async_computation.47 | async-start | bytes 1769472 | tf_op jit(solution)/shard_map/reduce_scatter | solution.py:483
  1127.9 136.2 %reduce-scatter.67.cloned.1.call-start = ((), (), s32[]{:S(2)}) async-start(), calls=%async_computation.60 | async-start | bytes 442368
  1134.2 194.8 %all-gather.34.cloned.1.call-start = ((), (), s32[]{:S(2)}) async-start(), calls=%async_computation.53 | async-start | bytes 3932160 | tf_op jit(solution)/shard_map/all_gather | solution.py:568
  1134.8 257.9 %all-gather.32.cloned.1.call-start = ((), (), s32[]{:S(2)}) async-start(), calls=%async_computation.51 | async-start | bytes 3932160 | tf_op jit(solution)/shard_map/all_gather | solution.py:565
  1139.4 317.0 %all-gather.30.cloned.1.call-start = ((), (), s32[]{:S(2)}) async-start(), calls=%async_computation.50 | async-start | bytes 3932160 | tf_op jit(solution)/shard_map/all_gather | solution.py:562
  1179.5 333.2 %reduce-scatter.45.cloned.1.call-start = ((), (), s32[]{:S(2)}) async-start(), calls=%async_computation.46 | async-start | bytes 5308416 | tf_op jit(solution)/shard_map/reduce_scatter | solution.py:480
  1212.2 321.6 %reduce-scatter.65.cloned.1.call-start = ((), (), s32[]{:S(2)}) async-start(), calls=%async_computation.59 | async-start | bytes 61440
  1237.7 315.7 %reduce-scatter.55.cloned.1.call-start = ((), (), s32[]{:S(2)}) async-start(), calls=%async_computation.54 | async-start | bytes 61440
  1238.4 339.0 %reduce-scatter.61.cloned.1.call-start = ((), (), s32[]{:S(2)}) async-start(), calls=%async_computation.57 | async-start | bytes 327680
  1240.3 354.7 %reduce-scatter.59.cloned.1.call-start = ((), (), s32[]{:S(2)}) async-start(), calls=%async_computation.56 | async-start | bytes 327680
  1242.2 377.2 %reduce-scatter.63.cloned.1.call-start = ((), (), s32[]{:S(2)}) async-start(), calls=%async_computation.58 | async-start | bytes 983040
  1244.5 403.5 %reduce-scatter.57.cloned.1.call-start = ((), (), s32[]{:S(2)}) async-start(), calls=%async_computation.55 | async-start | bytes 983040
  (138 other events, 2507.1 us)
Sparse Core Ops, SparseCore 0:
  9.9 28.5 all-gather.15
  40.4 25.6 all-gather.17
  68.0 38.9 all-gather.13
  108.7 38.9 all-gather.19
  166.0 47.1 all-gather.25
  278.2 44.9 all-gather.21
  407.3 65.1 reduce-scatter.40
  476.5 61.7 reduce-scatter.36
  540.3 46.6 all-gather.27
  596.3 45.2 all-gather.23
  725.6 65.0 reduce-scatter.42
  795.0 61.7 reduce-scatter.38
  859.0 60.2 reduce-scatter.52
  921.5 72.7 reduce-scatter.70
  997.0 67.4 reduce-scatter.68
  1089.5 37.4 reduce-scatter.48
  1130.1 38.4 reduce-scatter.46
  1172.4 53.8 reduce-scatter.50
  1230.2 33.7 reduce-scatter.66
  1265.6 63.4 all-gather.33
  1330.7 62.0 all-gather.31
  1394.4 61.9 all-gather.29
  1460.2 52.4 reduce-scatter.44
  1621.7 26.3 reduce-scatter.56
  (5 shorter events, 94.6 us)
where the time goes:
time: 1690 us; the launch traced here: 1670 us
  waiting for transfers between devices  474 us (28%)
  matrix products  429 us (25%)
  local copies, waits for them, and re-layouts  291 us (17%)
  other arithmetic  227 us (13%)
  blocking collectives  164 us (10%)
  starting transfers between devices  70.1 us (4%)
  between operations  18.7 us (1%)
    unnamed x286, local copies, waits for them, and re-layouts  157 us
    unnamed x21, other arithmetic  87.6 us
    unnamed x38, waiting for transfers between devices  70.7 us
    all_gather x1, waiting for transfers between devices, on_device(): lax.all_gather(shared_pieces[9].astype(jnp.bfloat16), 'seq', axis=1, tile...  64.1 us
    all_gather x1, waiting for transfers between devices, on_device(): lax.all_gather(shared_pieces[8].astype(jnp.bfloat16), 'seq', axis=1, tile...  58.2 us
    all_gather x1, waiting for transfers between devices, on_device(): lax.all_gather(shared_pieces[7].astype(jnp.bfloat16), 'seq', axis=1, tile...  58.2 us
    reduce_scatter x1, waiting for transfers between devices, on_device(): lax.psum_scatter(acc_query.astype(jnp.bfloat16), 'fsdp', scatter_dimensio...  51 us
    all_to_all x2, waiting for transfers between devices, on_device(): lax.all_to_all(grad_head_rows.reshape(local_sequence, local_token_rows, Q...  41.4 us
  transfers between devices with their start and end apart: 44, of which 24 were waited for; matrix products, arithmetic and copies ran while one was open for 46% of the time, Pallas kernels for 0%

commit v1 on v0

v1 whole, which is shorter than its diff:
```python
import functools

import jax
import jax.numpy as jnp
from jax import lax
from jax.experimental import pallas as pl
from jax.experimental.pallas import tpu as pltpu
from jax.sharding import PartitionSpec as P

HEAD = 64
HALF = HEAD // 2
GROUP = 3
TOPK = 8
EPS = 1e-06
THETA = 10000.0
NEGATIVE = -1e30
LANES = 128
SCALE = HEAD ** (-0.5)
BF = jnp.bfloat16
F32 = jnp.float32
VMEM_BYTES = 60 * 1024 * 1024

NN = (((1,), (0,)), ((), ()))
NT = (((1,), (1,)), ((), ()))
TN = (((0,), (0,)), ((), ()))


def dot(a, b, dims=NN):
    return lax.dot_general(a, b, dims, preferred_element_type=F32)


def params():
    return pltpu.CompilerParams(vmem_limit_bytes=VMEM_BYTES)


def cost(flops, moved, trans=0):
    return pl.CostEstimate(flops=int(flops), bytes_accessed=int(moved), transcendentals=int(trans))


def whole(shape):
    zeros = (0,) * len(shape)
    return pl.BlockSpec(shape, lambda *_: zeros)


def smem():
    return pl.BlockSpec(memory_space=pltpu.SMEM)


def rotate(rows, cosine, sine, sign):
    pieces = []
    for h in range(rows.shape[0] // HEAD):
        a = rows[h * HEAD : h * HEAD + HALF]
        b = rows[h * HEAD + HALF : (h + 1) * HEAD]
        if sign > 0:
            pieces += [a * cosine - b * sine, b * cosine + a * sine]
        else:
            pieces += [a * cosine + b * sine, b * cosine - a * sine]
    return jnp.concatenate(pieces, axis=0)


def kv_kernel(x_ref, gain_ref, w_ref, cos_ref, sin_ref, kv_ref, normed_ref):
    step = pl.program_id(0)

    @pl.when(step == 0)
    def _():
        x = x_ref[...].astype(F32)
        inv = lax.rsqrt(jnp.mean(x * x, axis=-1, keepdims=True) + EPS)
        normed_ref[...] = (x * inv * gain_ref[...]).astype(BF)
        r = dot(normed_ref[...], w_ref[...])
        r = rotate(r.T, cos_ref[...], sin_ref[...], 1)
        kv_ref[...] = r.T.astype(BF)

    @pl.when(step == 1)
    def _():
        kv_ref[...] = dot(normed_ref[...], w_ref[...]).astype(BF)


def kv_project(x, gain, w, cosine, sine):
    rows, dim = x.shape
    width = w.shape[1] // 2
    return pl.pallas_call(
        kv_kernel,
        name="kv_project",
        grid=(2,),
        in_specs=[
            whole((rows, dim)),
            whole((1, dim)),
            pl.BlockSpec((dim, width), lambda i: (0, i)),
            whole((HALF, rows)),
            whole((HALF, rows)),
        ],
        out_specs=[pl.BlockSpec((rows, width), lambda i: (0, i)), whole((rows, dim))],
        out_shape=[
            jax.ShapeDtypeStruct((rows, 2 * width), BF),
            jax.ShapeDtypeStruct((rows, dim), BF),
        ],
        compiler_params=params(),
        cost_estimate=cost(2 * rows * dim * 2 * width, 2 * (2 * rows * dim + dim * 2 * width)),
    )(x, gain, w, cosine, sine)


def q_kernel(normed_ref, w_ref, cos_ref, sin_ref, q_ref):
    r = dot(normed_ref[...], w_ref[...])
    r = rotate(r.T, cos_ref[...], sin_ref[...], 1)
    q_ref[...] = r.astype(BF) * BF(SCALE)


def q_project(normed, w, cosine, sine):
    rows, dim = normed.shape
    width = w.shape[1]
    tile = 512
    return pl.pallas_call(
        q_kernel,
        name="q_project",
        grid=(width // tile,),
        in_specs=[
            whole((rows, dim)),
            pl.BlockSpec((dim, tile), lambda i: (0, i)),
            whole((HALF, rows)),
            whole((HALF, rows)),
        ],
        out_specs=pl.BlockSpec((tile, rows), lambda i: (i, 0)),
        out_shape=jax.ShapeDtypeStruct((width, rows), BF),
        compiler_params=params(),
        cost_estimate=cost(2 * rows * dim * width, 2 * (2 * rows * dim + dim * width)),
    )(normed, w, cosine, sine)


def side_by_side(ref, j):
    base = j * GROUP * HEAD
    return jnp.concatenate(
        [ref[base + h * HEAD : base + (h + 1) * HEAD, :] for h in range(GROUP)], axis=1
    )


def diagonal_mask(tokens, own_len):
    key = lax.broadcasted_iota(jnp.int32, (tokens, tokens), 0)
    query = lax.broadcasted_iota(jnp.int32, (tokens, tokens), 1)
    one = (key <= query) & (key < own_len)
    return jnp.concatenate([one.astype(jnp.int32)] * GROUP, axis=1) > 0


def attend_kernel(n, info_ref, q_ref, *refs):
    k_refs, v_refs = refs[:n], refs[n : 2 * n]
    o_ref, ot_ref, lse_ref, m_ref, l_ref, acc_ref = refs[2 * n :]
    tokens = q_ref.shape[1]
    s = info_ref[0]
    own_len = info_ref[1] - s * tokens
    active = own_len > 0

    @pl.when(jnp.logical_not(active))
    def _():
        o_ref[...] = jnp.zeros_like(o_ref)
        ot_ref[...] = jnp.zeros_like(ot_ref)
        lse_ref[...] = jnp.zeros_like(lse_ref)

    @pl.when(active)
    def _():
        for d in range(n):

            def block(d=d):
                mask = diagonal_mask(tokens, own_len) if d == 0 else None
                for j in range(2):
                    cols = slice(j * HEAD, (j + 1) * HEAD)
                    scores = dot(k_refs[d][:, cols], side_by_side(q_ref, j))
                    value_t = v_refs[d][:, cols].astype(F32).T.astype(BF)
                    if d == 0:
                        scores = jnp.where(mask, scores, NEGATIVE)
                        top = jnp.max(scores, axis=0, keepdims=True)
                        p = jnp.exp(scores - top)
                        l_ref[j : j + 1] = jnp.sum(p, axis=0, keepdims=True)
                        acc_ref[j] = dot(value_t, p.astype(BF))
                    else:
                        old = m_ref[j : j + 1]
                        top = jnp.maximum(old, jnp.max(scores, axis=0, keepdims=True))
                        keep = jnp.exp(old - top)
                        p = jnp.exp(scores - top)
                        l_ref[j : j + 1] = l_ref[j : j + 1] * keep + jnp.sum(
                            p, axis=0, keepdims=True
                        )
                        acc_ref[j] = acc_ref[j] * keep + dot(value_t, p.astype(BF))
                    m_ref[j : j + 1] = top

            if d == 0:
                block()
            else:
                pl.when(d <= s)(block)
        pieces = []
        for j in range(2):
            out = acc_ref[j] / l_ref[j : j + 1]
            lse_ref[j : j + 1] = m_ref[j : j + 1] + jnp.log(l_ref[j : j + 1])
            pieces += [out[:, h * tokens : (h + 1) * tokens] for h in range(GROUP)]
        out = jnp.concatenate(pieces, axis=0)
        ot_ref[...] = out.astype(BF)
        o_ref[...] = out.T.astype(BF)


def attend(info, q_t, kvs, micro, tokens):
    n = len(kvs)
    width = q_t.shape[0]
    kv_width = kvs[0].shape[1] // 2
    steps = kv_width // LANES
    qw = width // steps
    v_first = kv_width // LANES
    return pl.pallas_call(
        functools.partial(attend_kernel, n),
        name="attend",
        grid=(steps,),
        in_specs=[smem(), pl.BlockSpec((qw, tokens), lambda i: (i, micro))]
        + [pl.BlockSpec((tokens, LANES), lambda i: (0, i))] * n
        + [pl.BlockSpec((tokens, LANES), lambda i: (0, v_first + i))] * n,
        out_specs=[
            pl.BlockSpec((tokens, qw), lambda i: (0, i)),
            pl.BlockSpec((qw, tokens), lambda i: (i, 0)),
            pl.BlockSpec((8, GROUP * tokens), lambda i: (i, 0)),
        ],
        out_shape=[
            jax.ShapeDtypeStruct((tokens, width), BF),
            jax.ShapeDtypeStruct((width, tokens), BF),
            jax.ShapeDtypeStruct((8 * steps, GROUP * tokens), F32),
        ],
        scratch_shapes=[
            pltpu.VMEM((8, GROUP * tokens), F32),
            pltpu.VMEM((8, GROUP * tokens), F32),
            pltpu.VMEM((2, HEAD, GROUP * tokens), F32),
        ],
        compiler_params=params(),
        cost_estimate=cost(
            4 * 4 * width * tokens * tokens * n,
            2 * (3 * width * tokens + n * tokens * 2 * kv_width),
            width // HEAD * tokens * tokens * n,
        ),
    )(info, q_t, *kvs, *kvs)


def attend_back_kernel(n, info_ref, q_ref, g_ref, o_ref, lse_ref, cos_ref, sin_ref, *refs):
    k_refs, v_refs = refs[:n], refs[n : 2 * n]
    gq_ref = refs[2 * n]
    dk_refs, dv_refs = refs[2 * n + 1 : 3 * n + 1], refs[3 * n + 1 : 4 * n + 1]
    acc_ref = refs[4 * n + 1]
    tokens = q_ref.shape[1]
    s = info_ref[0]
    own_len = info_ref[1] - s * tokens
    active = own_len > 0

    @pl.when(jnp.logical_not(active))
    def _():
        gq_ref[...] = jnp.zeros_like(gq_ref)
        for d in range(n):
            dk_refs[d][...] = jnp.zeros_like(dk_refs[d])
            dv_refs[d][...] = jnp.zeros_like(dv_refs[d])

    @pl.when(active)
    def _():
        for d in range(n):

            def block(d=d):
                mask = diagonal_mask(tokens, own_len) if d == 0 else None
                dks, dvs = [], []
                for j in range(2):
                    cols = slice(j * HEAD, (j + 1) * HEAD)
                    key, value = k_refs[d][:, cols], v_refs[d][:, cols]
                    query, grad = side_by_side(q_ref, j), side_by_side(g_ref, j)
                    out = side_by_side(o_ref, j)
                    inner = jnp.sum(
                        grad.astype(F32) * out.astype(F32), axis=0, keepdims=True
                    )
                    p = jnp.exp(dot(key, query) - lse_ref[j : j + 1])
                    if d == 0:
                        p = jnp.where(mask, p, 0.0)
                    dp = dot(value, grad)
                    ds = (p * (dp - inner)).astype(BF)
                    dvs.append(dot(p.astype(BF), grad, NT))
                    dks.append(dot(ds, query, NT))
                    part = dot(key.astype(F32).T.astype(BF), ds)
                    if d == 0:
                        acc_ref[j] = part
                    else:
                        acc_ref[j] += part
                dk_refs[d][...] = jnp.concatenate(dks, axis=1).astype(BF)
                dv_refs[d][...] = jnp.concatenate(dvs, axis=1).astype(BF)

            if d == 0:
                block()
            else:
                pl.when(d <= s)(block)
        pieces = []
        for j in range(2):
            for h in range(GROUP):
                piece = acc_ref[j, :, h * tokens : (h + 1) * tokens] * SCALE
                pieces.append(piece.astype(BF).astype(F32))
        grad_q = rotate(jnp.concatenate(pieces, axis=0), cos_ref[...], sin_ref[...], -1)
        gq_ref[...] = grad_q.T.astype(BF)


def attend_back(info, q_t, g_t, o_t, lse, cosine, sine, kvs, micro, tokens):
    n = len(kvs)
    width = q_t.shape[0]
    kv_width = kvs[0].shape[1] // 2
    steps = kv_width // LANES
    qw = width // steps
    v_first = kv_width // LANES
    transposed = pl.BlockSpec((qw, tokens), lambda i: (i, 0))
    kv_block = pl.BlockSpec((tokens, LANES), lambda i: (0, i))
    got = pl.pallas_call(
        functools.partial(attend_back_kernel, n),
        name="attend_back",
        grid=(steps,),
        in_specs=[
            smem(),
            pl.BlockSpec((qw, tokens), lambda i: (i, micro)),
            transposed,
            transposed,
            pl.BlockSpec((8, GROUP * tokens), lambda i: (i, 0)),
            whole((HALF, tokens)),
            whole((HALF, tokens)),
        ]
        + [kv_block] * n
        + [pl.BlockSpec((tokens, LANES), lambda i: (0, v_first + i))] * n,
        out_specs=[pl.BlockSpec((tokens, qw), lambda i: (0, i))] + [kv_block] * (2 * n),
        out_shape=[jax.ShapeDtypeStruct((tokens, width), BF)]
        + [jax.ShapeDtypeStruct((tokens, kv_width), BF)] * (2 * n),
        scratch_shapes=[pltpu.VMEM((2, HEAD, GROUP * tokens), F32)],
        compiler_params=params(),
        cost_estimate=cost(
            10 * 4 * width * tokens * tokens * n,
            2 * (4 * width * tokens + 2 * n * tokens * 2 * kv_width),
            width // HEAD * tokens * tokens * n,
        ),
    )(info, q_t, g_t, o_t, lse, cosine, sine, *kvs, *kvs)
    return got[0], got[1 : n + 1], got[n + 1 :]


def after_kernel(
    steps, a_ref, w_ref, x_ref, gain_ref, router_ref, chosen_ref, res_ref, xg_ref, ge_ref, acc_ref
):
    step = pl.program_id(0)
    part = dot(a_ref[...], w_ref[...])

    @pl.when(step == 0)
    def _():
        acc_ref[...] = part

    @pl.when(step > 0)
    def _():
        acc_ref[...] += part

    @pl.when(step == steps - 1)
    def _():
        dim = x_ref.shape[1]
        residual = x_ref[...].astype(F32) + acc_ref[...]
        res_ref[...] = residual
        inv = lax.rsqrt(jnp.mean(residual * residual, axis=-1, keepdims=True) + EPS)
        normed = (residual * inv * gain_ref[...]).astype(BF)
        logits = dot(normed, router_ref[...])
        chosen = chosen_ref[...] > 0
        logits = jnp.where(chosen, logits, NEGATIVE)
        top = jnp.max(logits, axis=-1, keepdims=True)
        e = jnp.where(chosen, jnp.exp(logits - top), 0.0)
        exact = e / jnp.sum(e, axis=-1, keepdims=True)
        ge_ref[...] = exact
        xg_ref[:, :dim] = normed
        xg_ref[:, dim:] = exact.astype(BF)


def after_attention(attn, w_out, x, micro, gain, router, chosen):
    tokens, width = attn.shape
    dim = w_out.shape[1]
    tile = 512
    steps = width // tile
    return pl.pallas_call(
        functools.partial(after_kernel, steps),
        name="after_attention",
        grid=(steps,),
        in_specs=[
            pl.BlockSpec((tokens, tile), lambda i: (0, i)),
            pl.BlockSpec((tile, dim), lambda i: (i, 0)),
            pl.BlockSpec((tokens, dim), lambda i: (micro, 0)),
            whole((1, dim)),
            whole((dim, LANES)),
            pl.BlockSpec((tokens, LANES), lambda i: (micro, 0)),
        ],
        out_specs=[
            whole((tokens, dim)),
            whole((tokens, dim + LANES)),
            whole((tokens, LANES)),
        ],
        out_shape=[
            jax.ShapeDtypeStruct((tokens, dim), F32),
            jax.ShapeDtypeStruct((tokens, dim + LANES), BF),
            jax.ShapeDtypeStruct((tokens, LANES), F32),
        ],
        scratch_shapes=[pltpu.VMEM((tokens, dim), F32)],
        compiler_params=params(),
        cost_estimate=cost(2 * tokens * width * dim, 2 * width * dim + 10 * tokens * dim),
    )(attn, w_out, x, gain, router, chosen)


def expert_kernel(
    experts, own_ref, xg_ref, g_ref, wg_ref, wu_ref, wd_ref, y_ref, back_ref, hg_ref, gp_ref
):
    dim = g_ref.shape[1]
    hidden = wg_ref.shape[2]
    rows = g_ref.shape[0]
    x = xg_ref[:, :dim]
    g = g_ref[...]
    gates = xg_ref[:, dim:].astype(F32)
    lane = lax.broadcasted_iota(jnp.int32, (rows, LANES), 1)
    gate_cols = jnp.zeros((rows, LANES), F32)
    for e in range(experts):
        mine = lane == own_ref[0] + e
        gate = jnp.sum(jnp.where(mine, gates, 0.0), axis=1, keepdims=True)
        pre_gate = dot(x, wg_ref[e])
        pre_up = dot(x, wu_ref[e])
        grad_hidden = dot(g, wd_ref[e], NT)
        sig = 1.0 / (1.0 + jnp.exp(-pre_gate))
        silu = pre_gate * sig
        h = (silu * pre_up).astype(BF).astype(F32)
        per_gate = jnp.sum(h * grad_hidden, axis=1, keepdims=True)
        gate_cols = jnp.where(mine, per_gate, gate_cols)
        hg_ref[:, e * hidden : (e + 1) * hidden] = (gate * h).astype(BF)
        gh = gate * grad_hidden
        base = 2 * e * hidden
        gp_ref[:, base : base + hidden] = (
            gh * pre_up * (sig * (1.0 + pre_gate * (1.0 - sig)))
        ).astype(BF)
        gp_ref[:, base + hidden : base + 2 * hidden] = (gh * silu).astype(BF)
    y = dot(hg_ref[:, :hidden], wd_ref[0])
    for e in range(1, experts):
        y += dot(hg_ref[:, e * hidden : (e + 1) * hidden], wd_ref[e])
    y_ref[...] = y.astype(BF)
    back = None
    for e in range(experts):
        base = 2 * e * hidden
        part = dot(gp_ref[:, base : base + hidden], wg_ref[e], NT)
        part += dot(gp_ref[:, base + hidden : base + 2 * hidden], wu_ref[e], NT)
        back = part if back is None else back + part
    back_ref[:, :dim] = back.astype(BF)
    back_ref[:, dim:] = gate_cols.astype(BF)


def run_experts(own, xg, g, w_gate, w_up, w_down):
    rows, dim = g.shape
    experts, _, hidden = w_gate.shape
    tile = 256
    row_block = lambda width: pl.BlockSpec((tile, width), lambda i: (i, 0))
    return pl.pallas_call(
        functools.partial(expert_kernel, experts),
        name="run_experts",
        grid=(rows // tile,),
        in_specs=[
            smem(),
            row_block(dim + LANES),
            row_block(dim),
            whole(w_gate.shape),
            whole(w_up.shape),
            whole(w_down.shape),
        ],
        out_specs=[
            row_block(dim),
            row_block(dim + LANES),
            row_block(experts * hidden),
            row_block(2 * experts * hidden),
        ],
        out_shape=[
            jax.ShapeDtypeStruct((rows, dim), BF),
            jax.ShapeDtypeStruct((rows, dim + LANES), BF),
            jax.ShapeDtypeStruct((rows, experts * hidden), BF),
            jax.ShapeDtypeStruct((rows, 2 * experts * hidden), BF),
        ],
        compiler_params=params(),
        cost_estimate=cost(
            12 * rows * dim * hidden * experts,
            2 * (4 * rows * dim + 3 * rows * experts * hidden + 3 * experts * dim * hidden),
            rows * experts * hidden,
        ),
    )(own, xg, g, w_gate, w_up, w_down)


def wide_grad_kernel(steps, micros, *refs):
    a_refs, b_refs = refs[:micros], refs[micros : 2 * micros]
    out_ref, acc_ref = refs[2 * micros :]
    step = pl.program_id(0)
    for m in range(micros):

        @pl.when((step >= m * steps) & (step < (m + 1) * steps))
        def _(m=m):
            part = dot(a_refs[m][...], b_refs[m][...], TN)
            if m == 0:

                @pl.when(step == 0)
                def _():
                    acc_ref[...] = part

                @pl.when(step > 0)
                def _():
                    acc_ref[...] += part
            else:
                acc_ref[...] += part

    @pl.when(step == micros * steps - 1)
    def _():
        out_ref[...] = acc_ref[...].astype(BF)


def wide_grad(lefts, left_block, left_width, rights, right_block, right_width, tile=512):
    micros, rows = len(lefts), lefts[0].shape[0]
    steps = rows // tile

    def spec(m, width, column):
        return pl.BlockSpec(
            (tile, width), lambda i: (jnp.clip(i - m * steps, 0, steps - 1), column)
        )

    return pl.pallas_call(
        functools.partial(wide_grad_kernel, steps, micros),
        name="wide_grad",
        grid=(micros * steps,),
        in_specs=[spec(m, left_width, left_block) for m in range(micros)]
        + [spec(m, right_width, right_block) for m in range(micros)],
        out_specs=whole((left_width, right_width)),
        out_shape=jax.ShapeDtypeStruct((left_width, right_width), BF),
        scratch_shapes=[pltpu.VMEM((left_width, right_width), F32)],
        compiler_params=params(),
        cost_estimate=cost(
            2 * micros * rows * left_width * right_width,
            2 * (micros * rows * (left_width + right_width) + left_width * right_width),
        ),
    )(*lefts, *rights)


def before_kernel(
    ret_ref, res_ref, ge_ref, gout_ref, gain_ref, router_ref, w_ref, gres_ref, ga_ref, gt_ref, small_ref
):
    dim = res_ref.shape[1]

    @pl.when(pl.program_id(0) == 0)
    def _():
        ge = ge_ref[...]
        gg = ret_ref[:, dim:].astype(F32)
        gl = ge * (gg - jnp.sum(ge * gg, axis=-1, keepdims=True))
        high = gl.astype(BF)
        low = (gl - high.astype(F32)).astype(BF)
        router = router_ref[...]
        gn = ret_ref[:, :dim].astype(F32) + (dot(high, router, NT) + dot(low, router, NT))
        residual = res_ref[...]
        gain = gain_ref[...]
        inv = lax.rsqrt(jnp.mean(residual * residual, axis=-1, keepdims=True) + EPS)
        unit = residual * inv
        normed = (unit * gain).astype(BF)
        small_ref[:LANES] = dot(high, normed, TN) + dot(low, normed, TN)
        gain_row = jnp.sum(gn * unit, axis=0, keepdims=True)
        small_ref[LANES:] = jnp.broadcast_to(gain_row, (8, dim))
        u = gn * gain
        gres = gout_ref[...].astype(F32) + inv * (
            u - unit * jnp.mean(u * unit, axis=-1, keepdims=True)
        )
        gres_ref[...] = gres
        ga_ref[...] = gres.astype(BF)

    gt_ref[...] = dot(w_ref[...], ga_ref[...], NT).astype(BF)


def before_attention(returned, residual, exact, gout, gain, router, w_out):
    tokens, dim = residual.shape
    width = w_out.shape[0]
    tile = 512
    return pl.pallas_call(
        before_kernel,
        name="before_attention",
        grid=(width // tile,),
        in_specs=[
            whole((tokens, dim + LANES)),
            whole((tokens, dim)),
            whole((tokens, LANES)),
            whole((tokens, dim)),
            whole((1, dim)),
            whole((dim, LANES)),
            pl.BlockSpec((tile, dim), lambda i: (i, 0)),
        ],
        out_specs=[
            whole((tokens, dim)),
            whole((tokens, dim)),
            pl.BlockSpec((tile, tokens), lambda i: (i, 0)),
            whole((LANES + 8, dim)),
        ],
        out_shape=[
            jax.ShapeDtypeStruct((tokens, dim), F32),
            jax.ShapeDtypeStruct((tokens, dim), BF),
            jax.ShapeDtypeStruct((width, tokens), BF),
            jax.ShapeDtypeStruct((LANES + 8, dim), F32),
        ],
        compiler_params=params(),
        cost_estimate=cost(2 * tokens * width * dim, 2 * width * dim + 14 * tokens * dim),
    )(returned, residual, exact, gout, gain, router, w_out)


def last_kernel(
    q_steps, steps, gq_ref, dkv_ref, wq_ref, wkv_ref, x_ref, gain_ref, gres_ref, din_ref, small_ref, acc_ref
):
    step = pl.program_id(0)

    @pl.when(step == 0)
    def _():
        acc_ref[...] = dot(gq_ref[...], wq_ref[...], NT)

    @pl.when((step > 0) & (step < q_steps))
    def _():
        acc_ref[...] += dot(gq_ref[...], wq_ref[...], NT)

    @pl.when(step >= q_steps)
    def _():
        acc_ref[...] += dot(dkv_ref[...], wkv_ref[...], NT)

    @pl.when(step == steps - 1)
    def _():
        x = x_ref[...].astype(F32)
        gain = gain_ref[...]
        inv = lax.rsqrt(jnp.mean(x * x, axis=-1, keepdims=True) + EPS)
        unit = x * inv
        gn = acc_ref[...]
        small_ref[...] = jnp.broadcast_to(
            jnp.sum(gn * unit, axis=0, keepdims=True), small_ref.shape
        )
        w = gn * gain
        grad = inv * (w - unit * jnp.mean(w * unit, axis=-1, keepdims=True))
        din_ref[...] = (grad + gres_ref[...]).astype(BF)


def last_step(gq, dkv, w_q, w_kv, x, micro, gain, gres):
    tokens, dim = gres.shape
    tile = 512
    q_steps = gq.shape[1] // tile
    steps = q_steps + dkv.shape[1] // tile
    q_at = lambda i: (0, jnp.minimum(i, q_steps - 1))
    kv_at = lambda i: (0, jnp.maximum(i - q_steps, 0))
    return pl.pallas_call(
        functools.partial(last_kernel, q_steps, steps),
        name="last_step",
        grid=(steps,),
        in_specs=[
            pl.BlockSpec((tokens, tile), q_at),
            pl.BlockSpec((tokens, tile), kv_at),
            pl.BlockSpec((dim, tile), q_at),
            pl.BlockSpec((dim, tile), kv_at),
            pl.BlockSpec((tokens, dim), lambda i: (micro, 0)),
            whole((1, dim)),
            whole((tokens, dim)),
        ],
        out_specs=[whole((tokens, dim)), whole((8, dim))],
        out_shape=[
            jax.ShapeDtypeStruct((tokens, dim), BF),
            jax.ShapeDtypeStruct((8, dim), F32),
        ],
        scratch_shapes=[pltpu.VMEM((tokens, dim), F32)],
        compiler_params=params(),
        cost_estimate=cost(
            2 * tokens * steps * tile * dim, 2 * steps * tile * dim + 12 * tokens * dim
        ),
    )(gq, dkv, w_q, w_kv, x, gain, gres)


def add_low(a, b):
    return (a.astype(F32) + b.astype(F32)).astype(BF)


def line_sum(x, n):
    if n == 1:
        return x
    if n % 2:
        return lax.psum(x, "seq")
    half = n // 2
    at = lax.axis_index("seq")
    for k in range(half - 1):
        x = add_low(x, lax.ppermute(x, "seq", [(k, k + 1), (n - 1 - k, n - 2 - k)]))
    x = add_low(x, lax.ppermute(x, "seq", [(half - 1, half), (half, half - 1)]))
    for k in reversed(range(half - 1)):
        got = lax.ppermute(x, "seq", [(k + 1, k), (n - 2 - k, n - 1 - k)])
        x = jnp.where((at == k) | (at == n - 1 - k), got, x)
    return x


def gather_rows(x):
    return lax.all_gather(x, "fsdp", axis=0, tiled=True)


def scatter_rows(x):
    return lax.psum_scatter(x, "fsdp", scatter_dimension=0, tiled=True)


def on_device(
    n_seq,
    inputs,
    lengths,
    expert_ids,
    cotangent,
    gain_attn,
    w_query,
    key_projection,
    value_projection,
    w_out,
    gain_moe,
    router,
    w_gate,
    w_up,
    w_down,
):
    micros, local_seqs, tokens, dim = inputs.shape
    assert local_seqs == 1
    rows = micros * tokens
    experts, _, hidden = w_gate.shape
    n_experts = router.shape[1]
    kv_width = key_projection.shape[1]
    at = lax.axis_index("seq")
    own = (lax.axis_index("fsdp") * experts).astype(jnp.int32).reshape(1)

    small = jnp.concatenate(
        [router, gain_attn[:, None], gain_moe[:, None]], axis=1
    )
    small = jnp.pad(small, ((0, 0), (0, LANES - small.shape[1])))
    kv_all = gather_rows(jnp.concatenate([key_projection, value_projection, small], axis=1))
    q_all = gather_rows(w_query)
    out_all = gather_rows(w_out)
    small_all = kv_all[:, 2 * kv_width :]
    gain_one = small_all[:, n_experts].astype(F32).reshape(1, dim)
    gain_two = small_all[:, n_experts + 1].astype(F32).reshape(1, dim)
    router_all = jnp.where(
        lax.broadcasted_iota(jnp.int32, small_all.shape, 1) < n_experts, small_all, BF(0)
    )
    kv_w = kv_all[:, : 2 * kv_width]

    positions = at * tokens + jnp.arange(tokens, dtype=jnp.int32)
    frequency = THETA ** (-(jnp.arange(HALF, dtype=F32) * 2.0) / HEAD)
    angles = frequency[:, None] * positions.astype(F32)[None, :]
    cosine, sine = jnp.cos(angles), jnp.sin(angles)
    cosine_all, sine_all = jnp.tile(cosine, (1, micros)), jnp.tile(sine, (1, micros))

    x = inputs.reshape(rows, dim)
    chosen = jnp.sum(
        (
            expert_ids.reshape(rows, TOPK)[:, :, None]
            == jnp.arange(LANES, dtype=jnp.int32)[None, None, :]
        ).astype(F32),
        axis=1,
    )
    valid = positions[None, :] < lengths[:, :1]
    gout = jnp.where(valid[:, :, None], cotangent.reshape(micros, tokens, dim), BF(0))
    infos = [
        jnp.stack([at.astype(jnp.int32), lengths[m, 0].astype(jnp.int32)]) for m in range(micros)
    ]

    kv, normed_one = kv_project(x, gain_one, kv_w, cosine_all, sine_all)
    kvs = []
    for m in range(micros):
        mine = kv[m * tokens : (m + 1) * tokens]
        kvs.append(
            [mine]
            + [
                lax.ppermute(mine, "seq", [(i, i + d) for i in range(n_seq - d)])
                for d in range(1, n_seq)
            ]
        )
    q_t = q_project(normed_one, q_all, cosine_all, sine_all)

    state = []
    for m in range(micros):
        attn, attn_t, lse = attend(infos[m], q_t, kvs[m], m, tokens)
        residual, xg, exact = after_attention(
            attn, out_all, x, m, gain_two, router_all, chosen
        )
        state.append((attn_t, lse, residual, exact, gather_rows(xg), gather_rows(gout[m])))

    outs, passed = [], []
    for m in range(micros):
        attn_t, lse, residual, exact, xg_all, g_all = state[m]
        y, back, hg, gp = run_experts(own, xg_all, g_all, w_gate, w_up, w_down)
        passed.append((xg_all, g_all, hg, gp))
        returned = scatter_rows(back)
        moe = scatter_rows(y)
        outs.append(
            jnp.where(valid[m][:, None], residual + moe.astype(F32), 0.0).astype(BF)
        )
        state[m] = (attn_t, lse, residual, exact, returned)

    d_gate, d_up, d_down = [], [], []
    xs, gs = [p[0] for p in passed], [p[1] for p in passed]
    hgs, gps = [p[2] for p in passed], [p[3] for p in passed]
    for e in range(experts):
        d_down.append(line_sum(wide_grad(hgs, e, hidden, gs, 0, dim), n_seq))
        d_gate.append(line_sum(wide_grad(xs, 0, dim, gps, 2 * e, hidden), n_seq))
        d_up.append(line_sum(wide_grad(xs, 0, dim, gps, 2 * e + 1, hidden), n_seq))

    grads, smalls, d_out, d_q, d_kv = [], [], None, None, None
    for m in range(micros):
        attn_t, lse, residual, exact, returned = state[m]
        gres, g_attn, g_t, small_two = before_attention(
            returned, residual, exact, gout[m], gain_two, router_all, out_all
        )
        part = dot(attn_t, g_attn)
        d_out = part if d_out is None else d_out + part
        gq, dks, dvs = attend_back(
            infos[m], q_t, g_t, attn_t, lse, cosine, sine, kvs[m], m, tokens
        )
        dk, dv = dks[0].astype(F32), dvs[0].astype(F32)
        for d in range(1, n_seq):
            pairs = [(i, i - d) for i in range(d, n_seq)]
            dk += lax.ppermute(dks[d], "seq", pairs).astype(F32)
            dv += lax.ppermute(dvs[d], "seq", pairs).astype(F32)
        dk = dk.astype(BF).astype(F32)
        dk = rotate(dk.T, cosine, sine, -1).T
        dkv = jnp.concatenate([dk.astype(BF), dv.astype(BF)], axis=1)
        normed = normed_one[m * tokens : (m + 1) * tokens]
        part_q, part_kv = dot(normed, gq, TN), dot(normed, dkv, TN)
        d_q = part_q if d_q is None else d_q + part_q
        d_kv = part_kv if d_kv is None else d_kv + part_kv
        din, small_one = last_step(gq, dkv, q_all, kv_w, x, m, gain_one, gres)
        grads.append(din)
        smalls.append(
            jnp.concatenate(
                [small_two[:n_experts], small_one[:1], small_two[LANES : LANES + 1]], axis=0
            )
        )
    small_rows = functools.reduce(jnp.add, smalls)
    small_cols = jnp.pad(small_rows, ((0, LANES - small_rows.shape[0]), (0, 0))).T.astype(BF)
    d_out = line_sum(scatter_rows(d_out.astype(BF)), n_seq).astype(F32)
    rest = line_sum(
        scatter_rows(jnp.concatenate([d_q.astype(BF), d_kv.astype(BF), small_cols], axis=1)), n_seq
    ).astype(F32)
    q_width = d_q.shape[1]
    shape = (micros, 1, tokens, dim)
    ends = q_width + 2 * kv_width
    return (
        jnp.stack(outs).reshape(shape),
        jnp.stack(grads).reshape(shape),
        rest[:, ends + n_experts],
        rest[:, :q_width],
        rest[:, q_width : q_width + kv_width],
        rest[:, q_width + kv_width : ends],
        d_out,
        rest[:, ends + n_experts + 1],
        rest[:, ends : ends + n_experts],
        jnp.stack(d_gate).astype(F32),
        jnp.stack(d_up).astype(F32),
        jnp.stack(d_down).astype(F32),
    )


def solution(mesh):
    token_spec = P(None, "fsdp", "seq", None)
    row, matrix, cube = P("fsdp"), P("fsdp", None), P("fsdp", None, None)
    return jax.shard_map(
        functools.partial(on_device, mesh.shape["seq"]),
        mesh=mesh,
        in_specs=(
            token_spec,
            P(None, "fsdp"),
            token_spec,
            token_spec,
            row,
            matrix,
            matrix,
            matrix,
            matrix,
            row,
            matrix,
            cube,
            cube,
            cube,
        ),
        out_specs=(
            token_spec,
            token_spec,
            row,
            matrix,
            matrix,
            matrix,
            matrix,
            row,
            matrix,
            cube,
            cube,
            cube,
        ),
        check_vma=False,
    )
```

time: 1690 us -> 1160 us (0.69)
  matrix products: 429 us -> 14.8 us
  Pallas kernels: 0 us -> 274 us
  local copies, waits for them, and re-layouts: 291 us -> 51.3 us
  waiting for transfers between devices: 474 us -> 649 us
  blocking collectives: 164 us -> 0 us
  other arithmetic: 227 us -> 66.2 us
    ppermute x0 -> x42, waiting for transfers between devices: none -> 425 us  [the longest x8 223 us: line_sum(): got = lax.ppermute(x, 'seq', [(k + 1, k), (n - 2 - k, n - 1 - k)])]
    dot_general x76 -> x6, matrix products: 429 us -> 14.8 us  [dot(): return lax.dot_general(a, b, dims, preferred_element_type=F32)]
    pallas_call x0 -> x20, Pallas kernels: none -> 274 us  [the longest x2 94.2 us: run_experts(): pl.pallas_call(functools.partial(expert_kernel, experts), name='run_exper...]
    unnamed x286 -> x97, local copies, waits for them, and re-layouts: 157 us -> 20.3 us
    all_gather x11 -> x7, waiting for transfers between devices: 260 us -> 154 us  [gather_rows(): return lax.all_gather(x, 'fsdp', axis=0, tiled=True)]
    all_gather x8 -> x0, blocking collectives: 103 us -> none  [the longest x1 20 us: on_device(): lax.all_gather(shared_pieces[3].astype(jnp.bfloat16), 'seq', axis=1, tile...]
    all_to_all x15 -> x0, waiting for transfers between devices: 91.6 us -> none  [the longest x2 41.4 us: on_device(): lax.all_to_all(grad_head_rows.reshape(local_sequence, local_token_rows, Q...]
    unnamed x21 -> x3, other arithmetic: 87.6 us -> 2.56 us
  transfers between devices with their start and end apart: 44 -> 55, of which waited for: 24 -> 30; matrix products, arithmetic and copies ran while one was open for 46% -> 10% of each run, Pallas kernels for 0% -> 24%
where the time goes in v1:
time: 1160 us; the launch traced here: 1150 us
  waiting for transfers between devices  649 us (56%)
  Pallas kernels  274 us (24%)
  starting transfers between devices  75 us (6%)
  other arithmetic  66.2 us (6%)
  local copies, waits for them, and re-layouts  51.3 us (4%)
  between operations  15.5 us (1%)
  matrix products  14.8 us (1%)
    ppermute x8, waiting for transfers between devices, line_sum(): got = lax.ppermute(x, 'seq', [(k + 1, k), (n - 2 - k, n - 1 - k)])  223 us
    all_gather x7, waiting for transfers between devices, gather_rows(): return lax.all_gather(x, 'fsdp', axis=0, tiled=True)  154 us
    ppermute x8, waiting for transfers between devices, line_sum(): x = add_low(x, lax.ppermute(x, 'seq', [(k, k + 1), (n - 1 - k, n - 2 - k)]))  124 us
    pallas_call x2, Pallas kernels, run_experts(): pl.pallas_call(functools.partial(expert_kernel, experts), name='run_exper...  94.2 us
    pallas_call x6, Pallas kernels, wide_grad(): pl.pallas_call(functools.partial(wide_grad_kernel, steps, micros), name='...  88.4 us
    reduce_scatter x6, waiting for transfers between devices, scatter_rows(): return lax.psum_scatter(x, 'fsdp', scatter_dimension=0, tiled=True)  68.1 us
    ppermute x6, waiting for transfers between devices, on_device(): dv += lax.ppermute(dvs[d], 'seq', pairs).astype(F32)  38.9 us
    ppermute x6, waiting for transfers between devices, on_device(): lax.ppermute(mine, 'seq', [(i, i + d) for i in range(n_seq - d)])  27.9 us
  transfers between devices with their start and end apart: 55, of which 30 were waited for; matrix products, arithmetic and copies ran while one was open for 10% of the time, Pallas kernels for 24%

profile of v1, /device:TPU:0, one launch (start us, length us, event | category | flops | bytes accessed | tf_op | source)
XLA Modules:
  0.0 1145.3 jit_solution(14206618752994818165)
XLA Ops:
  23.1 25.1 %all-gather.10.cloned.1.call-done = bf16[1536,1152]{1,0:T(8,128)(2,1)} async-done(((bf16[192,1152]{1,0:T(8,128)(2,1)}), bf16[1536,1152]{1,0:T(8,128)(2,1)}) %all-gather.10.cloned.1.call-update) | async-done | bytes 3538960 | tf_op jit(solution)/shard_map/all_gather | solution.py:684
  73.2 15.8 %all-gather.12.cloned.1.call-done.w_ref.wq_ref = bf16[1536,1536]{1,0:T(8,128)(2,1)} async-done(((bf16[192,1536]{1,0:T(8,128)(2,1)}), bf16[1536,1536]{1,0:T(8,128)(2,1)}) %all-gather.12.cloned.1.call-update) | async-done | bytes 4718608 | tf_op jit(solution)/shard_map/all_gather | solution.py:684
  106.4 23.5 %all-gather.14.cloned.1.call-done.w_ref = bf16[1536,1536]{1,0:T(8,128)(2,1)} async-done(((bf16[192,1536]{1,0:T(8,128)(2,1)}), bf16[1536,1536]{1,0:T(8,128)(2,1)}) %all-gather.14.cloned.1.call-update) | async-done | bytes 4718608 | tf_op jit(solution)/shard_map/all_gather | solution.py:684
  189.2 38.6 %all-gather.16.cloned.1.call-done.xg_ref.refs_0_ = bf16[2048,1664]{1,0:T(8,128)(2,1)} async-done(((bf16[256,1664]{1,0:T(8,128)(2,1)}), bf16[2048,1664]{1,0:T(8,128)(2,1)}) %all-gather.16.cloned.1.call-update) | async-done | bytes 6815760 | tf_op jit(solution)/shard_map/all_gather | solution.py:684
  227.8 47.1 %run_experts.2 = (bf16[2048,1536]{1,0:T(8,128)(2,1)}, bf16[2048,1664]{1,0:T(8,128)(2,1)}, bf16[2048,1024]{1,0:T(8,128)(2,1)}, bf16[2048,2048]{1,0:T(8,128)(2,1)}) custom-call(s32[1]{0:T(128)} %bitcast.5.own_ref, bf16[2048,1664]{1,0:T(8,128)(2,1)} %all-gather.16.cloned.1.call-done.xg_ref.refs_0_, bf16[2048,1536]{1,0:T(8,128)(2,1)} %bitcast.85, ...), custom_call_target="tpu_custom_call" | custom-call | flops 38654705664 | bytes 47185920 | tf_op jit(solution)/shard_map/run_experts/pallas_call | solution.py:447
  275.7 50.2 %all-gather.18.cloned.1.call-done.xg_ref.refs_1_ = bf16[2048,1664]{1,0:T(8,128)(2,1)} async-done(((bf16[256,1664]{1,0:T(8,128)(2,1)}), bf16[2048,1664]{1,0:T(8,128)(2,1)}) %all-gather.18.cloned.1.call-update) | async-done | bytes 6815760 | tf_op jit(solution)/shard_map/all_gather | solution.py:684
  325.9 47.1 %run_experts.3 = (bf16[2048,1536]{1,0:T(8,128)(2,1)}, bf16[2048,1664]{1,0:T(8,128)(2,1)}, bf16[2048,1024]{1,0:T(8,128)(2,1)}, bf16[2048,2048]{1,0:T(8,128)(2,1)}) custom-call(s32[1]{0:T(128)} %bitcast.5.own_ref, bf16[2048,1664]{1,0:T(8,128)(2,1)} %all-gather.18.cloned.1.call-done.xg_ref.refs_1_, bf16[2048,1536]{1,0:T(8,128)(2,1)} %bitcast.88, ...), custom_call_target="tpu_custom_call" | custom-call | flops 38654705664 | bytes 47185920 | tf_op jit(solution)/shard_map/run_experts/pallas_call | solution.py:447
  373.1 20.6 %reduce-scatter.13.cloned.1.call-done.ret_ref = bf16[256,1664]{1,0:T(8,128)(2,1)} async-done(((bf16[2048,1664]{1,0:T(8,128)(2,1)}), bf16[256,1664]{1,0:T(8,128)(2,1)}) %reduce-scatter.13.cloned.1.call-update) | async-done | bytes 851984 | tf_op jit(solution)/shard_map/reduce_scatter | solution.py:688
  414.3 47.5 %reduce-scatter.15.cloned.1.call-done.ret_ref = bf16[256,1664]{1,0:T(8,128)(2,1)} async-done(((bf16[2048,1664]{1,0:T(8,128)(2,1)}), bf16[256,1664]{1,0:T(8,128)(2,1)}) %reduce-scatter.15.cloned.1.call-update) | async-done | bytes 851984 | tf_op jit(solution)/shard_map/reduce_scatter | solution.py:688
  508.0 20.9 %collective-permute-done.11 = bf16[256,512]{1,0:T(8,128)(2,1)S(1)} collective-permute-done((bf16[256,512]{1,0:T(8,128)(2,1)}, bf16[256,512]{1,0:T(8,128)(2,1)S(1)}, u32[]{:S(2)}, u32[]{:S(2)}) %collective-permute-start.11) | collective-permute-done | bytes 262176 | tf_op jit(solution)/shard_map/ppermute | solution.py:808
  530.2 18.1 %collective-permute-done.10 = bf16[256,512]{1,0:T(8,128)(2,1)S(1)} collective-permute-done((bf16[256,512]{1,0:T(8,128)(2,1)}, bf16[256,512]{1,0:T(8,128)(2,1)S(1)}, u32[]{:S(2)}, u32[]{:S(2)}) %collective-permute-start.10) | collective-permute-done | bytes 262176 | tf_op jit(solution)/shard_map/ppermute | solution.py:808
  611.4 15.1 %wide_grad.7 = bf16[1536,512]{1,0:T(8,128)(2,1)} custom-call(bf16[2048,1664]{1,0:T(8,128)(2,1)} %all-gather.16.cloned.1.call-done.xg_ref.refs_0_, bf16[2048,1664]{1,0:T(8,128)(2,1)} %all-gather.18.cloned.1.call-done.xg_ref.refs_1_, bf16[2048,2048]{1,0:T(8,128)(2,1)} %get-tuple-element.112.refs_2_, bf16[2048,2048]{1,0:T(8,128)(2,1)} %get-tuple-element.113.refs_3_), custom_call_target="tpu_custom_call" | custom-call | flops 6442450944 | bytes 18350080 | tf_op jit(solution)/shard_map/wide_grad/pallas_call | solution.py:515
  664.7 14.8 %wide_grad.8 = bf16[1536,512]{1,0:T(8,128)(2,1)} custom-call(bf16[2048,1664]{1,0:T(8,128)(2,1)} %all-gather.16.cloned.1.call-done.xg_ref.refs_0_, bf16[2048,1664]{1,0:T(8,128)(2,1)} %all-gather.18.cloned.1.call-done.xg_ref.refs_1_, bf16[2048,2048]{1,0:T(8,128)(2,1)} %get-tuple-element.112.refs_2_, bf16[2048,2048]{1,0:T(8,128)(2,1)} %get-tuple-element.113.refs_3_), custom_call_target="tpu_custom_call" | custom-call | flops 6442450944 | bytes 18350080 | tf_op jit(solution)/shard_map/wide_grad/pallas_call | solution.py:515
  698.3 15.1 %wide_grad.10 = bf16[512,1536]{1,0:T(8,128)(2,1)} custom-call(bf16[2048,1024]{1,0:T(8,128)(2,1)} %get-tuple-element.114.refs_0_, bf16[2048,1024]{1,0:T(8,128)(2,1)} %get-tuple-element.115.refs_1_, bf16[2048,1536]{1,0:T(8,128)(2,1)} %bitcast.87, bf16[2048,1536]{1,0:T(8,128)(2,1)} %bitcast.90), custom_call_target="tpu_custom_call" | custom-call | flops 6442450944 | bytes 18350080 | tf_op jit(solution)/shard_map/wide_grad/pallas_call | solution.py:515
  735.2 31.0 %collective-permute-done.30 = bf16[1536,512]{1,0:T(8,128)(2,1)} collective-permute-done((bf16[1536,512]{1,0:T(8,128)(2,1)}, bf16[1536,512]{1,0:T(8,128)(2,1)}, u32[]{:S(2)}, u32[]{:S(2)}) %collective-permute-start.30) | collective-permute-done | bytes 1572896 | tf_op jit(solution)/shard_map/ppermute | solution.py:675
  768.9 31.1 %collective-permute-done.39 = bf16[512,1536]{1,0:T(8,128)(2,1)S(1)} collective-permute-done((bf16[512,1536]{1,0:T(8,128)(2,1)}, bf16[512,1536]{1,0:T(8,128)(2,1)S(1)}, u32[]{:S(2)}, u32[]{:S(2)}) %collective-permute-start.39) | collective-permute-done | bytes 1572896 | tf_op jit(solution)/shard_map/ppermute | solution.py:675
  801.1 30.2 %collective-permute-done.36 = bf16[512,1536]{1,0:T(8,128)(2,1)S(1)} collective-permute-done((bf16[512,1536]{1,0:T(8,128)(2,1)}, bf16[512,1536]{1,0:T(8,128)(2,1)S(1)}, u32[]{:S(2)}, u32[]{:S(2)}) %collective-permute-start.36) | collective-permute-done | bytes 1572896 | tf_op jit(solution)/shard_map/ppermute | solution.py:675
  842.4 34.6 %collective-permute-done.29 = bf16[1536,512]{1,0:T(8,128)(2,1)S(1)} collective-permute-done((bf16[1536,512]{1,0:T(8,128)(2,1)S(1)}, bf16[1536,512]{1,0:T(8,128)(2,1)S(1)}, u32[]{:S(2)}, u32[]{:S(2)}) %collective-permute-start.29) | collective-permute-done | bytes 1572896 | tf_op jit(solution)/shard_map/ppermute | solution.py:678
  878.8 32.0 %collective-permute-done.26 = bf16[1536,512]{1,0:T(8,128)(2,1)S(1)} collective-permute-done((bf16[1536,512]{1,0:T(8,128)(2,1)S(1)}, bf16[1536,512]{1,0:T(8,128)(2,1)S(1)}, u32[]{:S(2)}, u32[]{:S(2)}) %collective-permute-start.26) | collective-permute-done | bytes 1572896 | tf_op jit(solution)/shard_map/ppermute | solution.py:678
  914.0 30.4 %collective-permute-done.35 = bf16[1536,512]{1,0:T(8,128)(2,1)S(1)} collective-permute-done((bf16[1536,512]{1,0:T(8,128)(2,1)S(1)}, bf16[1536,512]{1,0:T(8,128)(2,1)S(1)}, u32[]{:S(2)}, u32[]{:S(2)}) %collective-permute-start.35) | collective-permute-done | bytes 1572896 | tf_op jit(solution)/shard_map/ppermute | solution.py:678
  944.6 33.5 %collective-permute-done.32 = bf16[1536,512]{1,0:T(8,128)(2,1)S(1)} collective-permute-done((bf16[1536,512]{1,0:T(8,128)(2,1)S(1)}, bf16[1536,512]{1,0:T(8,128)(2,1)S(1)}, u32[]{:S(2)}, u32[]{:S(2)}) %collective-permute-start.32) | collective-permute-done | bytes 1572896 | tf_op jit(solution)/shard_map/ppermute | solution.py:678
  981.4 30.4 %collective-permute-done.41 = bf16[512,1536]{1,0:T(8,128)(2,1)S(1)} collective-permute-done((bf16[512,1536]{1,0:T(8,128)(2,1)S(1)}, bf16[512,1536]{1,0:T(8,128)(2,1)S(1)}, u32[]{:S(2)}, u32[]{:S(2)}) %collective-permute-start.41) | collective-permute-done | bytes 1572896 | tf_op jit(solution)/shard_map/ppermute | solution.py:678
  1012.0 30.0 %collective-permute-done.38 = bf16[512,1536]{1,0:T(8,128)(2,1)S(1)} collective-permute-done((bf16[512,1536]{1,0:T(8,128)(2,1)S(1)}, bf16[512,1536]{1,0:T(8,128)(2,1)S(1)}, u32[]{:S(2)}, u32[]{:S(2)}) %collective-permute-start.38) | collective-permute-done | bytes 1572896 | tf_op jit(solution)/shard_map/ppermute | solution.py:678
  1104.5 26.8 %collective-permute-done.20 = bf16[192,2688]{1,0:T(8,128)(2,1)} collective-permute-done((bf16[192,2688]{1,0:T(8,128)(2,1)}, bf16[192,2688]{1,0:T(8,128)(2,1)}, u32[]{:S(2)}, u32[]{:S(2)}) %collective-permute-start.20) | collective-permute-done | bytes 1032224 | tf_op jit(solution)/shard_map/ppermute | solution.py:678
  (312 shorter events, 420.1 us)
Async XLA Ops:
  12.1 117.7 %all-gather.14.cloned.1.call-start = ((), (), s32[]{:S(2)}) async-start(), calls=%async_computation.8 | async-start | bytes 5308416 | tf_op jit(solution)/shard_map/all_gather | solution.py:684
  12.8 176.4 %all-gather.20.cloned.1.call-start = ((), (), s32[]{:S(2)}) async-start(), calls=%async_computation.16 | async-start | bytes 7077888 | tf_op jit(solution)/shard_map/all_gather | solution.py:684
  15.4 212.4 %all-gather.16.cloned.1.call-start = ((), (), s32[]{:S(2)}) async-start(), calls=%async_computation.9 | async-start | bytes 7667712 | tf_op jit(solution)/shard_map/all_gather | solution.py:684
  136.9 138.8 %all-gather.22.cloned.1.call-start = ((), (), s32[]{:S(2)}) async-start(), calls=%async_computation.17 | async-start | bytes 7077888 | tf_op jit(solution)/shard_map/all_gather | solution.py:684
  137.5 188.5 %all-gather.18.cloned.1.call-start = ((), (), s32[]{:S(2)}) async-start(), calls=%async_computation.11 | async-start | bytes 7667712 | tf_op jit(solution)/shard_map/all_gather | solution.py:684
  189.2 204.5 %reduce-scatter.13.cloned.1.call-start = ((), (), s32[]{:S(2)}) async-start(), calls=%async_computation.13 | async-start | bytes 7667712 | tf_op jit(solution)/shard_map/reduce_scatter | solution.py:688
  274.9 186.9 %reduce-scatter.15.cloned.1.call-start = ((), (), s32[]{:S(2)}) async-start(), calls=%async_computation.14 | async-start | bytes 7667712 | tf_op jit(solution)/shard_map/reduce_scatter | solution.py:688
  373.1 669.2 %reduce-scatter.17.cloned.1.call-start = ((), (), s32[]{:S(2)}) async-start(), calls=%async_computation.15 | async-start | bytes 5308416 | tf_op jit(solution)/shard_map/reduce_scatter | solution.py:688
  410.2 87.2 %collective-permute-start.8 = (bf16[256,512]{1,0:T(8,128)(2,1)}, bf16[256,512]{1,0:T(8,128)(2,1)S(1)}, u32[]{:S(2)}, u32[]{:S(2)}) collective-permute-start(bf16[256,512]{1,0:T(8,128)(2,1)} %get-tuple-element.83), channel_id=1, source_target_pairs={{24,0},{25,1},{26,2},{27,3},{28,4},{29,5},{30,6},{31,7}} | collective-permute-start | bytes 786440 | tf_op jit(solution)/shard_map/ppermute | solution.py:807
  411.5 87.9 %collective-permute-start.7 = (bf16[256,512]{1,0:T(8,128)(2,1)}, bf16[256,512]{1,0:T(8,128)(2,1)}, u32[]{:S(2)}, u32[]{:S(2)}) collective-permute-start(bf16[256,512]{1,0:T(8,128)(2,1)} %get-tuple-element.82), channel_id=1, source_target_pairs={{16,0},{24,8},{17,1},{25,9},{18,2},{26,10},{19,3},{27,11},{20,4},{... | collective-permute-start | bytes 786440 | tf_op jit(solution)/shard_map/ppermute | solution.py:807
  412.8 87.9 %collective-permute-start.6 = (bf16[256,512]{1,0:T(8,128)(2,1)}, bf16[256,512]{1,0:T(8,128)(2,1)}, u32[]{:S(2)}, u32[]{:S(2)}) collective-permute-start(bf16[256,512]{1,0:T(8,128)(2,1)} %get-tuple-element.81), channel_id=1, source_target_pairs={{8,0},{16,8},{24,16},{9,1},{17,9},{25,17},{10,2},{18,10},{26,18},{... | collective-permute-start | bytes 786440 | tf_op jit(solution)/shard_map/ppermute | solution.py:807
  476.1 571.5 %reduce-scatter.19.cloned.1.call-start = ((), (), s32[]{:S(2)}) async-start(), calls=%async_computation.18 | async-start | bytes 9289728 | tf_op jit(solution)/shard_map/reduce_scatter | solution.py:688
  610.6 439.3 %reduce-scatter.11.cloned.1.call-start = ((), (), s32[]{:S(2)}) async-start(), calls=%async_computation.12 | async-start | bytes 7077888 | tf_op jit(solution)/shard_map/reduce_scatter | solution.py:688
  611.2 471.2 %reduce-scatter.9.cloned.1.call-start = ((), (), s32[]{:S(2)}) async-start(), calls=%async_computation.10 | async-start | bytes 7077888 | tf_op jit(solution)/shard_map/reduce_scatter | solution.py:688
  626.6 86.9 %collective-permute-start.27 = (bf16[1536,512]{1,0:T(8,128)(2,1)}, bf16[1536,512]{1,0:T(8,128)(2,1)}, u32[]{:S(2)}, u32[]{:S(2)}) collective-permute-start(bf16[1536,512]{1,0:T(8,128)(2,1)} %wide_grad.7), channel_id=1, source_target_pairs={{0,8},{24,16},{1,9},{25,17},{2,10},{26,18},{3,11},{27,19},{4,12},{... | collective-permute-start | bytes 4718600 | tf_op jit(solution)/shard_map/ppermute | solution.py:675
  679.5 86.7 %collective-permute-start.30 = (bf16[1536,512]{1,0:T(8,128)(2,1)}, bf16[1536,512]{1,0:T(8,128)(2,1)}, u32[]{:S(2)}, u32[]{:S(2)}) collective-permute-start(bf16[1536,512]{1,0:T(8,128)(2,1)} %wide_grad.8), channel_id=1, source_target_pairs={{0,8},{24,16},{1,9},{25,17},{2,10},{26,18},{3,11},{27,19},{4,12},{... | collective-permute-start | bytes 4718600 | tf_op jit(solution)/shard_map/ppermute | solution.py:675
  696.7 103.3 %collective-permute-start.39 = (bf16[512,1536]{1,0:T(8,128)(2,1)}, bf16[512,1536]{1,0:T(8,128)(2,1)S(1)}, u32[]{:S(2)}, u32[]{:S(2)}) collective-permute-start(bf16[512,1536]{1,0:T(8,128)(2,1)} %wide_grad.11), channel_id=1, source_target_pairs={{0,8},{24,16},{1,9},{25,17},{2,10},{26,18},{3,11},{27,19},{4,12},{... | collective-permute-start | bytes 4718600 | tf_op jit(solution)/shard_map/ppermute | solution.py:675
  713.5 117.9 %collective-permute-start.36 = (bf16[512,1536]{1,0:T(8,128)(2,1)}, bf16[512,1536]{1,0:T(8,128)(2,1)S(1)}, u32[]{:S(2)}, u32[]{:S(2)}) collective-permute-start(bf16[512,1536]{1,0:T(8,128)(2,1)} %wide_grad.10), channel_id=1, source_target_pairs={{0,8},{24,16},{1,9},{25,17},{2,10},{26,18},{3,11},{27,19},{4,12},{... | collective-permute-start | bytes 4718600 | tf_op jit(solution)/shard_map/ppermute | solution.py:675
  717.0 115.6 %collective-permute-start.28 = (bf16[1536,512]{1,0:T(8,128)(2,1)S(1)}, bf16[1536,512]{1,0:T(8,128)(2,1)S(1)}, u32[]{:S(2)}, u32[]{:S(2)}) collective-permute-start(bf16[1536,512]{1,0:T(8,128)(2,1)S(1)} %add_convert_fusion.10), channel_id=1, source_target_pairs={{8,16},{16,8},{9,17},{17,9},{10,18},{18,10},{11,19},{19,11},{12,20... | collective-permute-start | bytes 4718600 | tf_op jit(solution)/shard_map/ppermute | solution.py:676
  732.6 101.2 %collective-permute-start.25 = (bf16[1536,512]{1,0:T(8,128)(2,1)S(1)}, bf16[1536,512]{1,0:T(8,128)(2,1)S(1)}, u32[]{:S(2)}, u32[]{:S(2)}) collective-permute-start(bf16[1536,512]{1,0:T(8,128)(2,1)S(1)} %add_convert_fusion.12), channel_id=1, source_target_pairs={{8,16},{16,8},{9,17},{17,9},{10,18},{18,10},{11,19},{19,11},{12,20... | collective-permute-start | bytes 4718600 | tf_op jit(solution)/shard_map/ppermute | solution.py:676
  837.3 107.2 %collective-permute-start.35 = (bf16[1536,512]{1,0:T(8,128)(2,1)S(1)}, bf16[1536,512]{1,0:T(8,128)(2,1)S(1)}, u32[]{:S(2)}, u32[]{:S(2)}) collective-permute-start(bf16[1536,512]{1,0:T(8,128)(2,1)S(1)} %add_convert_fusion.5), channel_id=1, source_target_pairs={{8,0},{16,24},{9,1},{17,25},{10,2},{18,26},{11,3},{19,27},{12,4},{... | collective-permute-start | bytes 4718600 | tf_op jit(solution)/shard_map/ppermute | solution.py:678
  839.0 139.1 %collective-permute-start.32 = (bf16[1536,512]{1,0:T(8,128)(2,1)S(1)}, bf16[1536,512]{1,0:T(8,128)(2,1)S(1)}, u32[]{:S(2)}, u32[]{:S(2)}) collective-permute-start(bf16[1536,512]{1,0:T(8,128)(2,1)S(1)} %add_convert_fusion.7), channel_id=1, source_target_pairs={{8,0},{16,24},{9,1},{17,25},{10,2},{18,26},{11,3},{19,27},{12,4},{... | collective-permute-start | bytes 4718600 | tf_op jit(solution)/shard_map/ppermute | solution.py:678
  840.7 171.1 %collective-permute-start.41 = (bf16[512,1536]{1,0:T(8,128)(2,1)S(1)}, bf16[512,1536]{1,0:T(8,128)(2,1)S(1)}, u32[]{:S(2)}, u32[]{:S(2)}) collective-permute-start(bf16[512,1536]{1,0:T(8,128)(2,1)S(1)} %add_convert_fusion.1), channel_id=1, source_target_pairs={{8,0},{16,24},{9,1},{17,25},{10,2},{18,26},{11,3},{19,27},{12,4},{... | collective-permute-start | bytes 4718600 | tf_op jit(solution)/shard_map/ppermute | solution.py:678
  877.0 165.0 %collective-permute-start.38 = (bf16[512,1536]{1,0:T(8,128)(2,1)S(1)}, bf16[512,1536]{1,0:T(8,128)(2,1)S(1)}, u32[]{:S(2)}, u32[]{:S(2)}) collective-permute-start(bf16[512,1536]{1,0:T(8,128)(2,1)S(1)} %add_convert_fusion.3), channel_id=1, source_target_pairs={{8,0},{16,24},{9,1},{17,25},{10,2},{18,26},{11,3},{19,27},{12,4},{... | collective-permute-start | bytes 4718600 | tf_op jit(solution)/shard_map/ppermute | solution.py:678
  (76 other events, 1901.2 us)
Sparse Core Ops, SparseCore 0:
  11.5 36.6 all-gather.9
  50.1 38.9 all-gather.11
  90.9 38.9 all-gather.13
  132.2 45.5 all-gather.19
  180.0 47.7 all-gather.15
  230.1 45.5 all-gather.21
  278.2 47.7 all-gather.17
  329.4 64.2 reduce-scatter.12
  397.5 64.2 reduce-scatter.14
  476.3 53.8 reduce-scatter.16
  610.7 69.5 reduce-scatter.18
  683.6 61.7 reduce-scatter.10
  749.1 61.7 reduce-scatter.8

commit v2 on v1

v2 whole, which is shorter than its diff:
```python
import functools

import jax
import jax.numpy as jnp
from jax import lax
from jax.experimental import pallas as pl
from jax.experimental.pallas import tpu as pltpu
from jax.sharding import PartitionSpec as P

HEAD = 64
HALF = HEAD // 2
GROUP = 3
TOPK = 8
EPS = 1e-06
THETA = 10000.0
NEGATIVE = -1e30
LANES = 128
SCALE = HEAD ** (-0.5)
BF = jnp.bfloat16
F32 = jnp.float32
VMEM_BYTES = 60 * 1024 * 1024

NN = (((1,), (0,)), ((), ()))
NT = (((1,), (1,)), ((), ()))
TN = (((0,), (0,)), ((), ()))


def dot(a, b, dims=NN):
    return lax.dot_general(a, b, dims, preferred_element_type=F32)


def params():
    return pltpu.CompilerParams(vmem_limit_bytes=VMEM_BYTES)


def cost(flops, moved, trans=0):
    parts = (int(v) // 10 for v in (flops, moved, trans))
    flops, moved, trans = parts
    return pl.CostEstimate(flops=flops, bytes_accessed=moved, transcendentals=trans)


def whole(shape):
    zeros = (0,) * len(shape)
    return pl.BlockSpec(shape, lambda *_: zeros)


def smem():
    return pl.BlockSpec(memory_space=pltpu.SMEM)


def pick(at, first_ref, second_ref, index=None):
    half = first_ref.shape[0]
    if index is None:
        index = lax.rem(at, half)
    return jnp.where(at < half, first_ref[index], second_ref[index])


def in_order(place_ref, w_refs):
    devices = 2 * w_refs[0].shape[0]
    return jnp.concatenate([pick(place_ref[j], *w_refs) for j in range(devices)], axis=0)


def rotate(rows, cosine, sine, sign):
    pieces = []
    for h in range(rows.shape[0] // HEAD):
        a = rows[h * HEAD : h * HEAD + HALF]
        b = rows[h * HEAD + HALF : (h + 1) * HEAD]
        if sign > 0:
            pieces += [a * cosine - b * sine, b * cosine + a * sine]
        else:
            pieces += [a * cosine + b * sine, b * cosine - a * sine]
    return jnp.concatenate(pieces, axis=0)


def unpack_kernel(n_experts, place_ref, wa_ref, wb_ref, router_ref, rows_ref):
    w = in_order(place_ref, (wa_ref, wb_ref))
    lane = lax.broadcasted_iota(jnp.int32, w.shape, 1)
    router_ref[...] = jnp.where(lane < n_experts, w.astype(F32), 0.0).astype(BF)
    rows_ref[...] = w.astype(F32).T


def unpack(place, w, block, n_experts):
    dim = 2 * w[0].shape[0] * w[0].shape[1]
    return pl.pallas_call(
        functools.partial(unpack_kernel, n_experts),
        name="unpack",
        grid=(1,),
        in_specs=[smem(), *w_columns(w, LANES, lambda i: block)],
        out_specs=[whole((dim, LANES)), whole((LANES, dim))],
        out_shape=[
            jax.ShapeDtypeStruct((dim, LANES), BF),
            jax.ShapeDtypeStruct((LANES, dim), F32),
        ],
        compiler_params=params(),
        cost_estimate=cost(0, 12 * dim * LANES),
    )(place, *w)


def kv_kernel(place_ref, x_ref, gain_ref, wa_ref, wb_ref, cos_ref, sin_ref, kv_ref, normed_ref):
    step = pl.program_id(0)

    @pl.when(step == 0)
    def _():
        x = x_ref[...].astype(F32)
        inv = lax.rsqrt(jnp.mean(x * x, axis=-1, keepdims=True) + EPS)
        normed_ref[...] = (x * inv * gain_ref[...]).astype(BF)
        r = dot(normed_ref[...], in_order(place_ref, (wa_ref, wb_ref)))
        r = rotate(r.T, cos_ref[...], sin_ref[...], 1)
        kv_ref[...] = r.T.astype(BF)

    @pl.when(step == 1)
    def _():
        kv_ref[...] = dot(normed_ref[...], in_order(place_ref, (wa_ref, wb_ref))).astype(BF)


def w_columns(w, tile, at):
    return [pl.BlockSpec((*half.shape[:2], tile), lambda *i: (0, 0, at(*i))) for half in w]


def kv_project(place, x, gain, w, width, cosine, sine):
    rows, dim = x.shape
    return pl.pallas_call(
        kv_kernel,
        name="kv_project",
        grid=(2,),
        in_specs=[
            smem(),
            whole((rows, dim)),
            whole((1, dim)),
            *w_columns(w, width, lambda i: i),
            whole((HALF, rows)),
            whole((HALF, rows)),
        ],
        out_specs=[pl.BlockSpec((rows, width), lambda i: (0, i)), whole((rows, dim))],
        out_shape=[
            jax.ShapeDtypeStruct((rows, 2 * width), BF),
            jax.ShapeDtypeStruct((rows, dim), BF),
        ],
        compiler_params=params(),
        cost_estimate=cost(2 * rows * dim * 2 * width, 2 * (2 * rows * dim + dim * 2 * width)),
    )(place, x, gain, *w, cosine, sine)


def q_kernel(place_ref, normed_ref, wa_ref, wb_ref, cos_ref, sin_ref, q_ref):
    r = dot(normed_ref[...], in_order(place_ref, (wa_ref, wb_ref)))
    r = rotate(r.T, cos_ref[...], sin_ref[...], 1)
    q_ref[...] = r.astype(BF) * BF(SCALE)


def q_project(place, normed, w, cosine, sine):
    rows, dim = normed.shape
    width = w[0].shape[2]
    tile = 512
    return pl.pallas_call(
        q_kernel,
        name="q_project",
        grid=(width // tile,),
        in_specs=[
            smem(),
            whole((rows, dim)),
            *w_columns(w, tile, lambda i: i),
            whole((HALF, rows)),
            whole((HALF, rows)),
        ],
        out_specs=pl.BlockSpec((tile, rows), lambda i: (i, 0)),
        out_shape=jax.ShapeDtypeStruct((width, rows), BF),
        compiler_params=params(),
        cost_estimate=cost(2 * rows * dim * width, 2 * (2 * rows * dim + dim * width)),
    )(place, normed, *w, cosine, sine)


def side_by_side(ref, j):
    base = j * GROUP * HEAD
    return jnp.concatenate(
        [ref[base + h * HEAD : base + (h + 1) * HEAD, :] for h in range(GROUP)], axis=1
    )


def diagonal_mask(tokens, own_len):
    key = lax.broadcasted_iota(jnp.int32, (tokens, tokens), 0)
    query = lax.broadcasted_iota(jnp.int32, (tokens, tokens), 1)
    one = (key <= query) & (key < own_len)
    return jnp.concatenate([one.astype(jnp.int32)] * GROUP, axis=1) > 0


def attend_kernel(n, info_ref, q_ref, k_ref, v_ref, o_ref, ot_ref, lse_ref, m_ref, l_ref, acc_ref):
    tokens = q_ref.shape[1]
    d = pl.program_id(1)
    s = info_ref[0]
    own_len = info_ref[1] - s * tokens
    active = own_len > 0

    def pair(j):
        cols = slice(j * HEAD, (j + 1) * HEAD)
        scores = dot(k_ref[0, :, cols], side_by_side(q_ref, j))
        return scores, v_ref[0, :, cols].astype(F32).T.astype(BF)

    @pl.when(active & (d == 0))
    def _():
        mask = diagonal_mask(tokens, own_len)
        for j in range(2):
            scores, value_t = pair(j)
            scores = jnp.where(mask, scores, NEGATIVE)
            top = jnp.max(scores, axis=0, keepdims=True)
            p = jnp.exp(scores - top)
            l_ref[j : j + 1] = jnp.sum(p, axis=0, keepdims=True)
            acc_ref[j] = dot(value_t, p.astype(BF))
            m_ref[j : j + 1] = top

    @pl.when(active & (d > 0) & (d <= s))
    def _():
        for j in range(2):
            scores, value_t = pair(j)
            old = m_ref[j : j + 1]
            top = jnp.maximum(old, jnp.max(scores, axis=0, keepdims=True))
            keep = jnp.exp(old - top)
            p = jnp.exp(scores - top)
            l_ref[j : j + 1] = l_ref[j : j + 1] * keep + jnp.sum(p, axis=0, keepdims=True)
            acc_ref[j] = acc_ref[j] * keep + dot(value_t, p.astype(BF))
            m_ref[j : j + 1] = top

    @pl.when(active & (d == n - 1))
    def _():
        pieces = []
        for j in range(2):
            out = acc_ref[j] / l_ref[j : j + 1]
            lse_ref[j : j + 1] = m_ref[j : j + 1] + jnp.log(l_ref[j : j + 1])
            pieces += [out[:, h * tokens : (h + 1) * tokens] for h in range(GROUP)]
        out = jnp.concatenate(pieces, axis=0)
        ot_ref[...] = out.astype(BF)
        o_ref[...] = out.T.astype(BF)

    @pl.when(jnp.logical_not(active) & (d == 0))
    def _():
        o_ref[...] = jnp.zeros_like(o_ref)
        ot_ref[...] = jnp.zeros_like(ot_ref)
        lse_ref[...] = jnp.zeros_like(lse_ref)


def owner(info_ref, d, n):
    return lax.rem(info_ref[0] + n - d, n)


def attend(info, q_t, kv, micro, tokens):
    n = kv.shape[0]
    width = q_t.shape[0]
    kv_width = kv.shape[2] // 2
    steps = kv_width // LANES
    qw = width // steps
    return pl.pallas_call(
        functools.partial(attend_kernel, n),
        name="attend",
        grid_spec=pltpu.PrefetchScalarGridSpec(
            num_scalar_prefetch=1,
            grid=(steps, n),
            in_specs=[
                pl.BlockSpec((qw, tokens), lambda i, d, info: (i, micro)),
                pl.BlockSpec((1, tokens, LANES), lambda i, d, info: (owner(info, d, n), 0, i)),
                pl.BlockSpec(
                    (1, tokens, LANES), lambda i, d, info: (owner(info, d, n), 0, steps + i)
                ),
            ],
            out_specs=[
                pl.BlockSpec((tokens, qw), lambda i, d, info: (0, i)),
                pl.BlockSpec((qw, tokens), lambda i, d, info: (i, 0)),
                pl.BlockSpec((8, GROUP * tokens), lambda i, d, info: (i, 0)),
            ],
            scratch_shapes=[
                pltpu.VMEM((8, GROUP * tokens), F32),
                pltpu.VMEM((8, GROUP * tokens), F32),
                pltpu.VMEM((2, HEAD, GROUP * tokens), F32),
            ],
        ),
        out_shape=[
            jax.ShapeDtypeStruct((tokens, width), BF),
            jax.ShapeDtypeStruct((width, tokens), BF),
            jax.ShapeDtypeStruct((8 * steps, GROUP * tokens), F32),
        ],
        compiler_params=params(),
        cost_estimate=cost(
            4 * 4 * width * tokens * tokens * n,
            2 * (3 * width * tokens + n * tokens * 2 * kv_width),
            width // HEAD * tokens * tokens * n,
        ),
    )(info, q_t, kv, kv)


def attend_back_kernel(
    n, info_ref, q_ref, g_ref, o_ref, lse_ref, cos_ref, sin_ref, k_ref, v_ref, gq_ref, dkv_ref, acc_ref
):
    tokens = q_ref.shape[1]
    d = pl.program_id(1)
    s = info_ref[0]
    own_len = info_ref[1] - s * tokens
    active = own_len > 0

    def block(first):
        mask = diagonal_mask(tokens, own_len) if first else None
        dks, dvs = [], []
        for j in range(2):
            cols = slice(j * HEAD, (j + 1) * HEAD)
            key, value = k_ref[0, :, cols], v_ref[0, :, cols]
            query, grad = side_by_side(q_ref, j), side_by_side(g_ref, j)
            out = side_by_side(o_ref, j)
            inner = jnp.sum(grad.astype(F32) * out.astype(F32), axis=0, keepdims=True)
            p = jnp.exp(dot(key, query) - lse_ref[j : j + 1])
            if first:
                p = jnp.where(mask, p, 0.0)
            dp = dot(value, grad)
            ds = (p * (dp - inner)).astype(BF)
            dvs.append(dot(p.astype(BF), grad, NT))
            dks.append(dot(ds, query, NT))
            part = dot(key.astype(F32).T.astype(BF), ds)
            if first:
                acc_ref[j] = part
            else:
                acc_ref[j] += part
        dkv_ref[0, 0] = jnp.concatenate(dks, axis=1).astype(BF)
        dkv_ref[0, 1] = jnp.concatenate(dvs, axis=1).astype(BF)

    pl.when(active & (d == 0))(lambda: block(True))
    pl.when(active & (d > 0) & (d <= s))(lambda: block(False))

    @pl.when(active & (d == n - 1))
    def _():
        pieces = []
        for j in range(2):
            for h in range(GROUP):
                piece = acc_ref[j, :, h * tokens : (h + 1) * tokens] * SCALE
                pieces.append(piece.astype(BF).astype(F32))
        grad_q = rotate(jnp.concatenate(pieces, axis=0), cos_ref[...], sin_ref[...], -1)
        gq_ref[...] = grad_q.T.astype(BF)

    @pl.when(jnp.logical_not(active) | (d > s))
    def _():
        dkv_ref[...] = jnp.zeros_like(dkv_ref)

    @pl.when(jnp.logical_not(active) & (d == 0))
    def _():
        gq_ref[...] = jnp.zeros_like(gq_ref)


def attend_back(info, q_t, g_t, o_t, lse, cosine, sine, kv, micro, tokens):
    n = kv.shape[0]
    width = q_t.shape[0]
    kv_width = kv.shape[2] // 2
    steps = kv_width // LANES
    qw = width // steps
    transposed = pl.BlockSpec((qw, tokens), lambda i, d, info: (i, 0))
    return pl.pallas_call(
        functools.partial(attend_back_kernel, n),
        name="attend_back",
        grid_spec=pltpu.PrefetchScalarGridSpec(
            num_scalar_prefetch=1,
            grid=(steps, n),
            in_specs=[
            pl.BlockSpec((qw, tokens), lambda i, d, info: (i, micro)),
            transposed,
            transposed,
            pl.BlockSpec((8, GROUP * tokens), lambda i, d, info: (i, 0)),
            whole((HALF, tokens)),
            whole((HALF, tokens)),
            pl.BlockSpec((1, tokens, LANES), lambda i, d, info: (owner(info, d, n), 0, i)),
            pl.BlockSpec(
                (1, tokens, LANES), lambda i, d, info: (owner(info, d, n), 0, steps + i)
            ),
        ],
        out_specs=[
            pl.BlockSpec((tokens, qw), lambda i, d, info: (0, i)),
            pl.BlockSpec(
                (1, 2, tokens, LANES), lambda i, d, info: (owner(info, d, n), 0, 0, i)
            ),
        ],
            scratch_shapes=[pltpu.VMEM((2, HEAD, GROUP * tokens), F32)],
        ),
        out_shape=[
            jax.ShapeDtypeStruct((tokens, width), BF),
            jax.ShapeDtypeStruct((n, 2, tokens, kv_width), BF),
        ],
        compiler_params=params(),
        cost_estimate=cost(
            10 * 4 * width * tokens * tokens * n,
            2 * (4 * width * tokens + 2 * n * tokens * 2 * kv_width),
            width // HEAD * tokens * tokens * n,
        ),
    )(info, q_t, g_t, o_t, lse, cosine, sine, kv, kv)


def after_kernel(
    steps, place_ref, a_ref, wa_ref, wb_ref, x_ref, gain_ref, router_ref, chosen_ref, res_ref, xg_ref, ge_ref, acc_ref
):
    step = pl.program_id(0)
    acc_ref[step] = dot(a_ref[...], in_order(place_ref, (wa_ref, wb_ref)))

    @pl.when(step == steps - 1)
    def _():
        dim = x_ref.shape[1]
        product = jnp.concatenate([acc_ref[i] for i in range(steps)], axis=1)
        residual = x_ref[...].astype(F32) + product
        res_ref[...] = residual
        inv = lax.rsqrt(jnp.mean(residual * residual, axis=-1, keepdims=True) + EPS)
        normed = (residual * inv * gain_ref[...]).astype(BF)
        logits = dot(normed, router_ref[...])
        chosen = chosen_ref[...] > 0
        logits = jnp.where(chosen, logits, NEGATIVE)
        top = jnp.max(logits, axis=-1, keepdims=True)
        e = jnp.where(chosen, jnp.exp(logits - top), 0.0)
        exact = e / jnp.sum(e, axis=-1, keepdims=True)
        ge_ref[...] = exact
        xg_ref[:, :dim] = normed
        xg_ref[:, dim:] = exact.astype(BF)


def after_attention(place, attn, w_out, x, micro, gain, router, chosen):
    tokens, width = attn.shape
    dim = w_out[0].shape[2]
    tile = 512
    steps = dim // tile
    return pl.pallas_call(
        functools.partial(after_kernel, steps),
        name="after_attention",
        grid=(steps,),
        in_specs=[
            smem(),
            whole((tokens, width)),
            *w_columns(w_out, tile, lambda i: i),
            pl.BlockSpec((tokens, dim), lambda i: (micro, 0)),
            whole((1, dim)),
            whole((dim, LANES)),
            pl.BlockSpec((tokens, LANES), lambda i: (micro, 0)),
        ],
        out_specs=[
            whole((tokens, dim)),
            whole((tokens, dim + LANES)),
            whole((tokens, LANES)),
        ],
        out_shape=[
            jax.ShapeDtypeStruct((tokens, dim), F32),
            jax.ShapeDtypeStruct((tokens, dim + LANES), BF),
            jax.ShapeDtypeStruct((tokens, LANES), F32),
        ],
        scratch_shapes=[pltpu.VMEM((steps, tokens, tile), F32)],
        compiler_params=params(),
        cost_estimate=cost(2 * tokens * width * dim, 2 * width * dim + 10 * tokens * dim),
    )(place, attn, *w_out, x, gain, router, chosen)


def expert_kernel(
    experts, half, own_ref, place_ref, xg_ref, ga_ref, gb_ref, wg_ref, wu_ref, wd_ref, y_ref, back_ref, hg_ref, gp_ref
):
    rows, dim = ga_ref.shape
    hidden = wg_ref.shape[2]
    x = xg_ref[:, :dim]
    g = jnp.where(place_ref[pl.program_id(0)] < half, ga_ref[...], gb_ref[...])
    gates = xg_ref[:, dim:].astype(F32)
    lane = lax.broadcasted_iota(jnp.int32, (rows, LANES), 1)
    gate_cols = jnp.zeros((rows, LANES), F32)
    for e in range(experts):
        mine = lane == own_ref[0] + e
        gate = jnp.sum(jnp.where(mine, gates, 0.0), axis=1, keepdims=True)
        pre_gate = dot(x, wg_ref[e])
        pre_up = dot(x, wu_ref[e])
        grad_hidden = dot(g, wd_ref[e], NT)
        sig = 1.0 / (1.0 + jnp.exp(-pre_gate))
        silu = pre_gate * sig
        h = (silu * pre_up).astype(BF).astype(F32)
        per_gate = jnp.sum(h * grad_hidden, axis=1, keepdims=True)
        gate_cols = jnp.where(mine, per_gate, gate_cols)
        hg_ref[:, e * hidden : (e + 1) * hidden] = (gate * h).astype(BF)
        gh = gate * grad_hidden
        base = 2 * e * hidden
        gp_ref[:, base : base + hidden] = (
            gh * pre_up * (sig * (1.0 + pre_gate * (1.0 - sig)))
        ).astype(BF)
        gp_ref[:, base + hidden : base + 2 * hidden] = (gh * silu).astype(BF)
    y = dot(hg_ref[:, :hidden], wd_ref[0])
    for e in range(1, experts):
        y += dot(hg_ref[:, e * hidden : (e + 1) * hidden], wd_ref[e])
    y_ref[...] = y.astype(BF)
    back = None
    for e in range(experts):
        base = 2 * e * hidden
        part = dot(gp_ref[:, base : base + hidden], wg_ref[e], NT)
        part += dot(gp_ref[:, base + hidden : base + 2 * hidden], wu_ref[e], NT)
        back = part if back is None else back + part
    back_ref[:, :dim] = back.astype(BF)
    back_ref[:, dim:] = gate_cols.astype(BF)


def run_experts(own, place, xg, g, micro, micros, w_gate, w_up, w_down):
    rows = xg.shape[0]
    dim = g[0].shape[1]
    experts, _, hidden = w_gate.shape
    devices = place.shape[0]
    tile, half = rows // devices, devices // 2
    row_block = lambda width: pl.BlockSpec((tile, width), lambda i, *_: (i, 0))
    arrival = lambda width: pl.BlockSpec((tile, width), lambda i, own, place: (place[i], 0))
    g_block = pl.BlockSpec(
        (tile, dim), lambda i, own, place: (lax.rem(place[i], half) * micros + micro, 0)
    )
    return pl.pallas_call(
        functools.partial(expert_kernel, experts, half),
        name="run_experts",
        grid_spec=pltpu.PrefetchScalarGridSpec(
            num_scalar_prefetch=2,
            grid=(devices,),
            in_specs=[
                row_block(dim + LANES),
                g_block,
                g_block,
                whole(w_gate.shape),
                whole(w_up.shape),
                whole(w_down.shape),
            ],
            out_specs=[
                arrival(dim),
                row_block(dim + LANES),
                arrival(experts * hidden),
                row_block(2 * experts * hidden),
            ],
        ),
        out_shape=[
            jax.ShapeDtypeStruct((rows, dim), BF),
            jax.ShapeDtypeStruct((rows, dim + LANES), BF),
            jax.ShapeDtypeStruct((rows, experts * hidden), BF),
            jax.ShapeDtypeStruct((rows, 2 * experts * hidden), BF),
        ],
        compiler_params=params(),
        cost_estimate=cost(
            12 * rows * dim * hidden * experts,
            2 * (4 * rows * dim + 3 * rows * experts * hidden + 3 * experts * dim * hidden),
            rows * experts * hidden,
        ),
    )(own, place, xg, *g, w_gate, w_up, w_down)


def wide_grad_kernel(steps, micros, *refs):
    a_refs, b_refs = refs[:micros], refs[micros : 2 * micros]
    out_ref, acc_ref = refs[2 * micros :]
    step = pl.program_id(0)
    for m in range(micros):

        @pl.when((step >= m * steps) & (step < (m + 1) * steps))
        def _(m=m):
            part = dot(a_refs[m][...], b_refs[m][...], TN)
            if m == 0:

                @pl.when(step == 0)
                def _():
                    acc_ref[...] = part

                @pl.when(step > 0)
                def _():
                    acc_ref[...] += part
            else:
                acc_ref[...] += part

    @pl.when(step == micros * steps - 1)
    def _():
        out_ref[...] = acc_ref[...].astype(BF)


def wide_grad(lefts, left_block, left_width, rights, right_block, right_width, tile=512):
    micros, rows = len(lefts), lefts[0].shape[0]
    steps = rows // tile

    def spec(m, width, column):
        return pl.BlockSpec(
            (tile, width), lambda i: (jnp.clip(i - m * steps, 0, steps - 1), column)
        )

    return pl.pallas_call(
        functools.partial(wide_grad_kernel, steps, micros),
        name="wide_grad",
        grid=(micros * steps,),
        in_specs=[spec(m, left_width, left_block) for m in range(micros)]
        + [spec(m, right_width, right_block) for m in range(micros)],
        out_specs=whole((left_width, right_width)),
        out_shape=jax.ShapeDtypeStruct((left_width, right_width), BF),
        scratch_shapes=[pltpu.VMEM((left_width, right_width), F32)],
        compiler_params=params(),
        cost_estimate=cost(
            2 * micros * rows * left_width * right_width,
            2 * (micros * rows * (left_width + right_width) + left_width * right_width),
        ),
    )(*lefts, *rights)


def down_grad_kernel(micros, devices, *refs):
    hg_refs, ga_ref, gb_ref, out_ref, acc_ref = refs[:micros], *refs[micros:]
    step = pl.program_id(0)
    g = jnp.where(step < devices // 2, ga_ref[...], gb_ref[...])
    hg = jnp.concatenate([r[...] for r in hg_refs], axis=0)
    part = dot(hg, g, TN)

    @pl.when(step == 0)
    def _():
        acc_ref[...] = part

    @pl.when(step > 0)
    def _():
        acc_ref[...] += part

    @pl.when(step == devices - 1)
    def _():
        out_ref[...] = acc_ref[...].astype(BF)


def down_grad(hgs, expert, hidden, g, devices):
    micros, rows = len(hgs), hgs[0].shape[0]
    tile, half = rows // devices, devices // 2
    dim = g[0].shape[1]
    return pl.pallas_call(
        functools.partial(down_grad_kernel, micros, devices),
        name="down_grad",
        grid=(devices,),
        in_specs=[pl.BlockSpec((tile, hidden), lambda i: (i, expert))] * micros
        + [
            pl.BlockSpec((micros * tile, dim), lambda i: (jnp.minimum(i, half - 1), 0)),
            pl.BlockSpec((micros * tile, dim), lambda i: (jnp.maximum(i - half, 0), 0)),
        ],
        out_specs=whole((hidden, dim)),
        out_shape=jax.ShapeDtypeStruct((hidden, dim), BF),
        scratch_shapes=[pltpu.VMEM((hidden, dim), F32)],
        compiler_params=params(),
        cost_estimate=cost(2 * micros * rows * hidden * dim, 2 * micros * rows * (hidden + dim)),
    )(*hgs, *g)


def before_kernel(
    steps, place_ref, ret_ref, res_ref, ge_ref, gout_ref, gain_ref, router_ref, wa_ref, wb_ref, gres_ref, ga_ref, gt_ref, small_ref, cut_ref, acc_ref
):
    dim = res_ref.shape[1]

    step = pl.program_id(0)
    tile = dim // steps

    @pl.when(step == 0)
    def _():
        ge = ge_ref[...]
        gg = ret_ref[:, dim:].astype(F32)
        gl = ge * (gg - jnp.sum(ge * gg, axis=-1, keepdims=True))
        high = gl.astype(BF)
        low = (gl - high.astype(F32)).astype(BF)
        router = router_ref[...]
        gn = ret_ref[:, :dim].astype(F32) + (dot(high, router, NT) + dot(low, router, NT))
        residual = res_ref[...]
        gain = gain_ref[...]
        inv = lax.rsqrt(jnp.mean(residual * residual, axis=-1, keepdims=True) + EPS)
        unit = residual * inv
        normed = (unit * gain).astype(BF)
        small_ref[:LANES] = dot(high, normed, TN) + dot(low, normed, TN)
        gain_row = jnp.sum(gn * unit, axis=0, keepdims=True)
        small_ref[LANES:] = jnp.broadcast_to(gain_row, (8, dim))
        u = gn * gain
        gres = gout_ref[...].astype(F32) + inv * (
            u - unit * jnp.mean(u * unit, axis=-1, keepdims=True)
        )
        gres_ref[...] = gres
        low_gres = gres.astype(BF)
        ga_ref[...] = low_gres
        for i in range(steps):
            cut_ref[i] = low_gres[:, i * tile : (i + 1) * tile]
        acc_ref[...] = jnp.zeros_like(acc_ref)

    acc_ref[...] += dot(in_order(place_ref, (wa_ref, wb_ref)), cut_ref[step], NT)

    @pl.when(step == steps - 1)
    def _():
        gt_ref[...] = acc_ref[...].astype(BF)


def before_attention(place, returned, residual, exact, gout, gain, router, w_out):
    tokens, dim = residual.shape
    width = 2 * w_out[0].shape[0] * w_out[0].shape[1]
    tile = 512
    steps = dim // tile
    return pl.pallas_call(
        functools.partial(before_kernel, steps),
        name="before_attention",
        grid=(steps,),
        in_specs=[
            smem(),
            whole((tokens, dim + LANES)),
            whole((tokens, dim)),
            whole((tokens, LANES)),
            whole((tokens, dim)),
            whole((1, dim)),
            whole((dim, LANES)),
            *w_columns(w_out, tile, lambda i: i),
        ],
        out_specs=[
            whole((tokens, dim)),
            whole((tokens, dim)),
            whole((width, tokens)),
            whole((LANES + 8, dim)),
        ],
        out_shape=[
            jax.ShapeDtypeStruct((tokens, dim), F32),
            jax.ShapeDtypeStruct((tokens, dim), BF),
            jax.ShapeDtypeStruct((width, tokens), BF),
            jax.ShapeDtypeStruct((LANES + 8, dim), F32),
        ],
        scratch_shapes=[
            pltpu.VMEM((steps, tokens, tile), BF),
            pltpu.VMEM((width, tokens), F32),
        ],
        compiler_params=params(),
        cost_estimate=cost(2 * tokens * width * dim, 2 * width * dim + 14 * tokens * dim),
    )(place, returned, residual, exact, gout, gain, router, *w_out)


def last_kernel(
    q_steps, steps, place_ref, gq_ref, dkv_ref, qa_ref, qb_ref, kva_ref, kvb_ref, x_ref, gain_ref, gres_ref, din_ref, small_ref, acc_ref
):
    step = pl.program_id(0)

    @pl.when(step == 0)
    def _():
        acc_ref[...] = dot(gq_ref[...], in_order(place_ref, (qa_ref, qb_ref)), NT)

    @pl.when((step > 0) & (step < q_steps))
    def _():
        acc_ref[...] += dot(gq_ref[...], in_order(place_ref, (qa_ref, qb_ref)), NT)

    @pl.when(step >= q_steps)
    def _():
        acc_ref[...] += dot(dkv_ref[...], in_order(place_ref, (kva_ref, kvb_ref)), NT)

    @pl.when(step == steps - 1)
    def _():
        x = x_ref[...].astype(F32)
        gain = gain_ref[...]
        inv = lax.rsqrt(jnp.mean(x * x, axis=-1, keepdims=True) + EPS)
        unit = x * inv
        gn = acc_ref[...]
        small_ref[...] = jnp.broadcast_to(
            jnp.sum(gn * unit, axis=0, keepdims=True), small_ref.shape
        )
        w = gn * gain
        grad = inv * (w - unit * jnp.mean(w * unit, axis=-1, keepdims=True))
        din_ref[...] = (grad + gres_ref[...]).astype(BF)


def last_step(place, gq, dkv, w_q, w_kv, x, micro, gain, gres):
    tokens, dim = gres.shape
    tile = 512
    q_steps, kv_steps = gq.shape[1] // tile, dkv.shape[1] // tile
    steps = q_steps + kv_steps
    q_at = lambda i: (0, jnp.minimum(i, q_steps - 1))
    kv_at = lambda i: (0, jnp.maximum(i - q_steps, 0))
    return pl.pallas_call(
        functools.partial(last_kernel, q_steps, steps),
        name="last_step",
        grid=(steps,),
        in_specs=[
            smem(),
            pl.BlockSpec((tokens, tile), q_at),
            pl.BlockSpec((tokens, tile), kv_at),
            *w_columns(w_q, tile, lambda i: q_at(i)[1]),
            *w_columns(w_kv, tile, lambda i: kv_at(i)[1]),
            pl.BlockSpec((tokens, dim), lambda i: (micro, 0)),
            whole((1, dim)),
            whole((tokens, dim)),
        ],
        out_specs=[whole((tokens, dim)), whole((8, dim))],
        out_shape=[
            jax.ShapeDtypeStruct((tokens, dim), BF),
            jax.ShapeDtypeStruct((8, dim), F32),
        ],
        scratch_shapes=[pltpu.VMEM((tokens, dim), F32)],
        compiler_params=params(),
        cost_estimate=cost(
            2 * tokens * steps * tile * dim, 2 * steps * tile * dim + 12 * tokens * dim
        ),
    )(place, gq, dkv, *w_q, *w_kv, x, gain, gres)


def add_low(a, b):
    return (a.astype(F32) + b.astype(F32)).astype(BF)


def line_sum(x, n):
    if n == 1:
        return x
    if n % 2:
        return lax.psum(x, "seq")
    half = n // 2
    at = lax.axis_index("seq")
    for k in range(half - 1):
        x = add_low(x, lax.ppermute(x, "seq", [(k, k + 1), (n - 1 - k, n - 2 - k)]))
    x = add_low(x, lax.ppermute(x, "seq", [(half - 1, half), (half, half - 1)]))
    for k in reversed(range(half - 1)):
        got = lax.ppermute(x, "seq", [(k + 1, k), (n - 2 - k, n - 1 - k)])
        x = jnp.where((at == k) | (at == n - 1 - k), got, x)
    return x


class Line:
    def __init__(self, n):
        self.n = n
        self.held = {}
        self.count = 0
        self.results = []

    def sums(self):
        at = lax.axis_index("seq")
        middle = (at == 1) | (at == 2)
        return [r[0] if len(r) == 1 else jnp.where(middle, *r) for r in self.results]

    def step(self, chunk):
        n = self.n
        if n != 4:
            if chunk is not None:
                self.results.append((line_sum(chunk, n),))
            return
        held, self.held = self.held, {}
        crossing, leaving = held.get("crossing"), held.get("leaving")
        arrived = None
        if chunk is not None:
            arrived = lax.ppermute(chunk, "seq", [(0, 1), (3, 2)])
        if leaving is not None:
            self.results.append((leaving, lax.ppermute(leaving, "seq", [(1, 0), (2, 3)])))
        if crossing is not None:
            other = lax.ppermute(crossing, "seq", [(1, 2), (2, 1)])
            self.held["leaving"] = add_low(crossing, other)
        if chunk is not None:
            self.held["crossing"] = add_low(chunk, arrived)


def gate(x, *others):
    return lax.optimization_barrier((x, others))[0]


CORE, ALONG_X, ALONG_Y = 1, 2, 4


def swap(x, mask):
    return lax.ppermute(x, "fsdp", [(i, i ^ mask) for i in range(8)])


def gather_rows(x):
    return lax.all_gather(x, "fsdp", axis=0, tiled=True)


def assemble_kernel(x_ref, top_x_ref, low_y_ref, top_far_ref, low_far_ref, out_ref):
    rows = x_ref.shape[0]
    half = rows // 2
    out_ref[:rows] = x_ref[...]
    out_ref[rows : rows + half] = top_x_ref[...]
    out_ref[rows + half : 2 * rows] = low_far_ref[:half]
    out_ref[2 * rows : 2 * rows + half] = top_far_ref[:half]
    out_ref[2 * rows + half : 3 * rows] = low_y_ref[...]
    out_ref[3 * rows : 3 * rows + half] = top_far_ref[half:]
    out_ref[3 * rows + half :] = low_far_ref[half:]


def assemble(*pieces):
    rows, width = pieces[0].shape
    block = lambda n: pl.BlockSpec((n, width // 3), lambda i: (0, i))
    return pl.pallas_call(
        assemble_kernel,
        name="assemble",
        grid=(3,),
        in_specs=[block(p.shape[0]) for p in pieces],
        out_specs=block(4 * rows),
        out_shape=jax.ShapeDtypeStruct((4 * rows, width), pieces[0].dtype),
        compiler_params=params(),
        cost_estimate=cost(0, 16 * rows * width),
    )(*pieces)


def gather_near(x, n):
    if n != 8:
        every = gather_rows(x)
        half = every.shape[0] // 2
        return every[:half], every[half:]
    gather = Gather(x, n)
    gather.further()
    return gather.finish()


class Gather:
    def __init__(self, x, n):
        self.n, self.x = n, x
        if n != 8:
            self.halves = gather_near(x, n)
            self.near = self.far = ()
            return
        half = x.shape[0] // 2
        self.near = swap(x[:half], ALONG_X), swap(x[half:], ALONG_Y)

    def further(self, *others):
        if self.n != 8:
            return
        half = self.x.shape[0] // 2
        x, (top_x, low_y) = gate((self.x, self.near), *others)
        self.near = top_x, low_y
        top_far = swap(jnp.concatenate([x[:half], top_x]), ALONG_Y)
        low_far = swap(jnp.concatenate([x[half:], low_y]), ALONG_X)
        self.far = top_far, low_far

    def finish(self, *others):
        if self.n != 8:
            return self.halves
        near, far = gate((self.near, self.far), *others)
        mine = assemble(self.x, *near, *far)
        return mine, swap(mine, CORE)


class Scatter:
    def __init__(self, arrays, n):
        self.arrays, self.n, self.stage = list(arrays), n, 0
        self.rows = arrays[0].shape[0] // n

    def advance(self):
        held, self.stage = self.arrays, self.stage + 1
        rows, half = self.rows, self.rows // 2
        if self.n != 8:
            if self.stage == 1:
                self.arrays = [scatter_rows(a) for a in held]
            return
        if self.stage == 1:
            self.arrays = [add_low(a[: 4 * rows], swap(a[4 * rows :], CORE)) for a in held]
        if self.stage == 2:
            tops = [a[k * rows : k * rows + half] for a in held for k in (2, 3)]
            lows = [a[k * rows + half : (k + 1) * rows] for a in held for k in (1, 3)]
            tops = swap(jnp.concatenate(tops), ALONG_Y)
            lows = swap(jnp.concatenate(lows), ALONG_X)
            self.arrays = []
            for i, a in enumerate(held):
                at = 2 * i * half
                self.arrays.append(
                    (
                        add_low(a[:half], tops[at : at + half]),
                        add_low(a[half:rows], lows[at : at + half]),
                        add_low(a[rows : rows + half], tops[at + half : at + rows]),
                        add_low(a[2 * rows + half : 3 * rows], lows[at + half : at + rows]),
                    )
                )
        if self.stage == 3:
            over_x = swap(jnp.concatenate([a[2] for a in held]), ALONG_X)
            over_y = swap(jnp.concatenate([a[3] for a in held]), ALONG_Y)
            self.arrays = [
                jnp.concatenate(
                    [
                        add_low(a[0], over_x[i * half : (i + 1) * half]),
                        add_low(a[1], over_y[i * half : (i + 1) * half]),
                    ]
                )
                for i, a in enumerate(held)
            ]


def block_places(n):
    if n != 8:
        return jnp.arange(n, dtype=jnp.int32)
    mask = lax.axis_index("fsdp").astype(jnp.int32) ^ jnp.arange(n, dtype=jnp.int32)
    return (mask >> 1) + 4 * (mask & 1)


def scatter_rows(x):
    return lax.psum_scatter(x, "fsdp", scatter_dimension=0, tiled=True)


def on_device(
    n_seq,
    n_fsdp,
    inputs,
    lengths,
    expert_ids,
    cotangent,
    gain_attn,
    w_query,
    key_projection,
    value_projection,
    w_out,
    gain_moe,
    router,
    w_gate,
    w_up,
    w_down,
):
    micros, local_seqs, tokens, dim = inputs.shape
    assert local_seqs == 1
    rows = micros * tokens
    experts, _, hidden = w_gate.shape
    n_experts = router.shape[1]
    kv_width = key_projection.shape[1]
    at = lax.axis_index("seq")
    own = (lax.axis_index("fsdp") * experts).astype(jnp.int32).reshape(1)

    small = jnp.concatenate(
        [router, gain_attn[:, None], gain_moe[:, None]], axis=1
    )
    small = jnp.pad(small, ((0, 0), (0, LANES - small.shape[1])))
    place = block_places(n_fsdp)

    def weights(w):
        return [h.reshape(n_fsdp // 2, -1, h.shape[1]) for h in gather_near(w, n_fsdp)]

    w_kv = weights(jnp.concatenate([key_projection, value_projection, small], axis=1))
    router_all, rows_all = unpack(place, w_kv, 2 * kv_width // LANES, n_experts)
    gain_one = rows_all[n_experts : n_experts + 1]
    gain_two = rows_all[n_experts + 1 : n_experts + 2]

    positions = at * tokens + jnp.arange(tokens, dtype=jnp.int32)
    frequency = THETA ** (-(jnp.arange(HALF, dtype=F32) * 2.0) / HEAD)
    angles = frequency[:, None] * positions.astype(F32)[None, :]
    cosine, sine = jnp.cos(angles), jnp.sin(angles)
    cosine_all, sine_all = jnp.tile(cosine, (1, micros)), jnp.tile(sine, (1, micros))

    x = inputs.reshape(rows, dim)
    chosen = jnp.sum(
        (
            expert_ids.reshape(rows, TOPK)[:, :, None]
            == jnp.arange(LANES, dtype=jnp.int32)[None, None, :]
        ).astype(F32),
        axis=1,
    )
    valid = positions[None, :] < lengths[:, :1]
    gout = jnp.where(valid[:, :, None], cotangent.reshape(micros, tokens, dim), BF(0))
    infos = [
        jnp.stack([at.astype(jnp.int32), lengths[m, 0].astype(jnp.int32)]) for m in range(micros)
    ]

    kv, normed_one = kv_project(place, x, gain_one, w_kv, kv_width, cosine_all, sine_all)
    w_q = weights(gate(w_query, kv))
    q_t = q_project(place, normed_one, w_q, cosine_all, sine_all)
    kvs = []
    for m in range(micros):
        mine = kv[m * tokens : (m + 1) * tokens]
        every = lax.all_gather(mine, "seq", axis=0, tiled=True)
        kvs.append(every.reshape(n_seq, tokens, 2 * kv_width))

    out_all = weights(gate(w_out, w_q[0]))
    g_gather = Gather(gate(gout.reshape(rows, dim), w_q[0]), n_fsdp)

    state, xg_all = [], []
    for m in range(micros):
        if m == 0:
            info = gate(infos[m], g_gather.near)
            g_gather.further()
        else:
            info = gate(infos[m], state[-1][2], g_gather.far)
            g_all = g_gather.finish()
        attn, attn_t, lse = attend(info, q_t, kvs[m], m, tokens)
        residual, xg, exact = after_attention(
            place, attn, out_all, x, m, gain_two, router_all, chosen
        )
        state.append((attn_t, lse, residual, exact))
        xg_all.append(gather_rows(xg))

    xg_all[0] = gate(xg_all[0], state[-1][2])
    passed, backs = [], []
    for m in range(micros):
        y, back, hg, gp = run_experts(
            own, place, xg_all[m], g_all, m, micros, w_gate, w_up, w_down
        )
        passed.append((xg_all[m], hg, gp))
        backs.append((scatter_rows(back), y))

    names = [("down", e) for e in range(experts)]
    names += [(name, e) for e in range(experts) for name in ("gate", "up")]

    def expert_grad(name, e, got):
        xs, hgs, gps = ([p[i] for p in got] for i in range(3))
        if name == "down":
            return down_grad(hgs, e, hidden, g_all, n_fsdp)
        return wide_grad(xs, 0, dim, gps, 2 * e + (name == "up"), hidden)

    line = Line(n_seq)
    found = [{} for _ in range(micros)]

    def to_heads(m):
        attn_t, lse, residual, exact = state[m]
        gres, g_attn, g_t, small_two = before_attention(
            place, backs[m][0], residual, exact, gout[m], gain_two, router_all, out_all
        )
        found[m].update(gres=gres, g_attn=g_attn, g_t=g_t, small_two=small_two)

    def through_heads(m):
        attn_t, lse = state[m][:2]
        gq, by_owner = attend_back(
            infos[m], q_t, found[m]["g_t"], attn_t, lse, cosine, sine, kvs[m], m, tokens
        )
        found[m].update(gq=gq, by_owner=by_owner)

    owned = {}

    def to_owners(m):
        by_owner = found[m].pop("by_owner")
        shape = by_owner.shape
        owned[m] = lax.psum_scatter(
            by_owner.reshape(n_seq * shape[1] * tokens, shape[3]),
            "seq",
            scatter_dimension=0,
            tiled=True,
        ).reshape(shape[1:])

    def own_grads(m):
        dk = rotate(owned[m][0].astype(F32).T, cosine, sine, -1).T
        return jnp.concatenate([dk.astype(BF), owned[m][1]], axis=1)

    def finish(m):
        f = found[m]
        f["dkv"] = own_grads(m)
        din, small_one = last_step(
            place, f["gq"], f["dkv"], w_q, w_kv, x, m, gain_one, f["gres"]
        )
        small_rows = jnp.concatenate(
            [f["small_two"][:n_experts], small_one[:1], f["small_two"][LANES : LANES + 1]], axis=0
        )
        f.update(din=din, small_rows=small_rows)

    def out_grad():
        total = None
        for m in range(micros):
            part = dot(state[m][0], found[m]["g_attn"])
            total = part if total is None else total + part
        return total.astype(BF)

    def projection_grads():
        d_q = d_kv = None
        for m in range(micros):
            normed = normed_one[m * tokens : (m + 1) * tokens]
            part_q = dot(normed, found[m]["gq"], TN)
            part_kv = dot(normed, found[m]["dkv"], TN)
            d_q = part_q if d_q is None else d_q + part_q
            d_kv = part_kv if d_kv is None else d_kv + part_kv
        small_rows = functools.reduce(jnp.add, [f["small_rows"] for f in found])
        pad = ((0, LANES - small_rows.shape[0]), (0, 0))
        small_cols = jnp.pad(small_rows, pad).T
        columns = jnp.concatenate([d_q, d_kv, small_cols], axis=1).astype(BF)
        return scatter_rows(columns)

    n_grads = len(names)
    work = {
        0: [("grad", 1), (to_heads, 0)],
        1: [("grad", 2), (through_heads, 0)],
        2: [("grad", 3), (to_heads, 1)],
        3: [("grad", 4), (through_heads, 1)],
        4: [("grad", 5)],
    }
    chunks = {0: expert_grad(*names[0], passed)}
    chunks.update({i: expert_grad(*names[i], passed) for i in range(6, n_grads)})
    slots = max(n_grads, 6)
    moe = Scatter([b[1] for b in backs], n_fsdp)
    for t in range(slots + 4):
        chunks, line.held, line.results, passed, found, moe.arrays = lax.optimization_barrier(
            (chunks, line.held, line.results, passed, found, moe.arrays)
        )
        sent = chunks.pop(t, None)
        if t == 2:
            to_owners(0)
        if t == 4:
            to_owners(1)
            out_part = scatter_rows(found[0].pop("out"))
        for kind, i in work.get(t, []):
            if kind != "grad":
                kind(i)
            elif i < n_grads:
                chunks[i] = expert_grad(*names[i], passed)
        if t == 3:
            found[0]["out"] = out_grad()
        if t == 5:
            finish(0)
            finish(1)
            rest_part = projection_grads()
        if t == slots - 1:
            chunks[slots] = out_part
        if t == slots:
            chunks[slots + 1] = rest_part
        if t in (4, 5, 6):
            moe.advance()
        line.step(sent)
    totals = line.sums()
    sums = dict(zip(names, totals))
    d_down = [sums["down", e] for e in range(experts)]
    d_gate = [sums["gate", e] for e in range(experts)]
    d_up = [sums["up", e] for e in range(experts)]
    d_out, rest = [part.astype(F32) for part in totals[n_grads:]]

    outs = []
    for m in range(micros):
        outs.append(
            jnp.where(valid[m][:, None], state[m][2] + moe.arrays[m].astype(F32), 0.0).astype(BF)
        )
    grads = [f["din"] for f in found]
    q_width = w_query.shape[1]
    shape = (micros, 1, tokens, dim)
    ends = q_width + 2 * kv_width
    return (
        jnp.stack(outs).reshape(shape),
        jnp.stack(grads).reshape(shape),
        rest[:, ends + n_experts],
        rest[:, :q_width],
        rest[:, q_width : q_width + kv_width],
        rest[:, q_width + kv_width : ends],
        d_out,
        rest[:, ends + n_experts + 1],
        rest[:, ends : ends + n_experts],
        jnp.stack(d_gate).astype(F32),
        jnp.stack(d_up).astype(F32),
        jnp.stack(d_down).astype(F32),
    )


def solution(mesh):
    token_spec = P(None, "fsdp", "seq", None)
    row, matrix, cube = P("fsdp"), P("fsdp", None), P("fsdp", None, None)
    return jax.shard_map(
        functools.partial(on_device, mesh.shape["seq"], mesh.shape["fsdp"]),
        mesh=mesh,
        in_specs=(
            token_spec,
            P(None, "fsdp"),
            token_spec,
            token_spec,
            row,
            matrix,
            matrix,
            matrix,
            matrix,
            row,
            matrix,
            cube,
            cube,
            cube,
        ),
        out_specs=(
            token_spec,
            token_spec,
            row,
            matrix,
            matrix,
            matrix,
            matrix,
            row,
            matrix,
            cube,
            cube,
            cube,
        ),
        check_vma=False,
    )
```

time: 1160 us -> 974 us (0.84)
  waiting for transfers between devices: 649 us -> 315 us
  Pallas kernels: 274 us -> 326 us
  starting transfers between devices: 75 us -> 120 us
  other arithmetic: 66.2 us -> 102 us
  local copies, waits for them, and re-layouts: 51.3 us -> 64.2 us
    all_gather x7 -> x2, waiting for transfers between devices: 154 us -> 0.8 us  [gather_rows(): return lax.all_gather(x, 'fsdp', axis=0, tiled=True)]
    ppermute x42 -> x50, waiting for transfers between devices: 425 us -> 314 us  [the longest x26 157 us: swap(): return lax.ppermute(x, 'fsdp', [(i, i ^ mask) for i in range(8)])]
    pallas_call x7 -> x14, Pallas kernels: 129 us -> 197 us  [the longest x2 97.3 us: run_experts(): pl.pallas_call(functools.partial(expert_kernel, experts, half), name='run...]
    reduce_scatter x6 -> x3, waiting for transfers between devices: 68.1 us -> 0.04 us  [scatter_rows(): return lax.psum_scatter(x, 'fsdp', scatter_dimension=0, tiled=True)]
    ppermute x42 -> x50, starting transfers between devices: 74.1 us -> 119 us  [the longest x8 67.9 us: step(): arrived = lax.ppermute(chunk, 'seq', [(0, 1), (3, 2)])]
    pallas_call x6 -> x4, Pallas kernels: 88.4 us -> 56.7 us  [wide_grad(): pl.pallas_call(functools.partial(wide_grad_kernel, steps, micros), name='...]
    convert_element_type x16 -> x21, other arithmetic: 18.4 us -> 45.7 us  [add_low(): return (a.astype(F32) + b.astype(F32)).astype(BF)]
    pallas_call x2, Pallas kernels: 16.8 us -> 31.1 us  [attend_back(): pl.pallas_call(functools.partial(attend_back_kernel, n), name='attend_bac...]
  transfers between devices with their start and end apart: 55 -> 60, of which waited for: 30 -> 33; matrix products, arithmetic and copies ran while one was open for 10% -> 16% of each run, Pallas kernels for 24% -> 33%
where the time goes in v2:
time: 974 us; the launch traced here: 955 us
  Pallas kernels  326 us (33%)
  waiting for transfers between devices  315 us (32%)
  starting transfers between devices  120 us (12%)
  other arithmetic  102 us (10%)
  local copies, waits for them, and re-layouts  64.2 us (7%)
  between operations  15.8 us (2%)
  matrix products  12.4 us (1%)
    ppermute x26, waiting for transfers between devices, swap(): return lax.ppermute(x, 'fsdp', [(i, i ^ mask) for i in range(8)])  157 us
    ppermute x8, waiting for transfers between devices, step(): arrived = lax.ppermute(chunk, 'seq', [(0, 1), (3, 2)])  113 us
    pallas_call x2, Pallas kernels, run_experts(): pl.pallas_call(functools.partial(expert_kernel, experts, half), name='run...  97.3 us
    ppermute x8, starting transfers between devices, step(): arrived = lax.ppermute(chunk, 'seq', [(0, 1), (3, 2)])  67.9 us
    pallas_call x4, Pallas kernels, wide_grad(): pl.pallas_call(functools.partial(wide_grad_kernel, steps, micros), name='...  56.7 us
    convert_element_type x21, other arithmetic, add_low(): return (a.astype(F32) + b.astype(F32)).astype(BF)  45.7 us
    ppermute x8, waiting for transfers between devices, step(): lax.ppermute(leaving, 'seq', [(1, 0), (2, 3)])  43.8 us
    pallas_call x2, Pallas kernels, attend_back(): pl.pallas_call(functools.partial(attend_back_kernel, n), name='attend_bac...  31.1 us
  transfers between devices with their start and end apart: 60, of which 33 were waited for; matrix products, arithmetic and copies ran while one was open for 16% of the time, Pallas kernels for 33%

profile of v2, /device:TPU:0, one launch (start us, length us, event | category | flops | bytes accessed | tf_op | source)
XLA Modules:
  0.0 955.2 jit_solution(1258264734741949204)
XLA Ops:
  66.4 11.7 %collective-permute-done.7.top_far_ref = bf16[192,1536]{1,0:T(8,128)(2,1)S(1)} collective-permute-done((bf16[192,1536]{1,0:T(8,128)(2,1)S(1)}, bf16[192,1536]{1,0:T(8,128)(2,1)S(1)}, u32[]{:S(2)}, u32[]{:S(2)}) %collective-permute-start.7) | collective-permute-done | bytes 589856 | tf_op jit(solution)/shard_map/ppermute | solution.py:839
  121.5 12.2 %collective-permute-done.10.low_y_ref = bf16[256,1536]{1,0:T(8,128)(2,1)S(1)} collective-permute-done((bf16[256,1536]{1,0:T(8,128)(2,1)}, bf16[256,1536]{1,0:T(8,128)(2,1)S(1)}, u32[]{:S(2)}, u32[]{:S(2)}) %collective-permute-start.10) | collective-permute-done | bytes 786464 | tf_op jit(solution)/shard_map/ppermute | solution.py:839
  141.2 12.6 %attend.2 = (bf16[256,1536]{1,0:T(8,128)(2,1)}, bf16[1536,256]{1,0:T(8,128)(2,1)}, f32[32,768]{1,0:T(8,128)}) custom-call(s32[2]{0:T(128)} %pad_add_fusion.info_ref, bf16[1536,512]{1,0:T(8,128)(2,1)} %q_project.1.q_ref, bf16[4,256,1024]{2,1,0:T(8,128)(2,1)} %bitcast.96, bf16[4,256,1024]{2,1,0:T(8,128)(2,1)} %bitcast.97), custom_call_target="tpu_custom_call" | custom-call | flops 644245120 | bytes 445644 | tf_op jit(solution)/shard_map/attend/pallas_call | solution.py:250
  166.8 43.2 %collective-permute-done.17.top_far_ref = bf16[512,1536]{1,0:T(8,128)(2,1)S(1)} collective-permute-done((bf16[512,1536]{1,0:T(8,128)(2,1)S(1)}, bf16[512,1536]{1,0:T(8,128)(2,1)S(1)}, u32[]{:S(2)}, u32[]{:S(2)}) %collective-permute-start.17) | collective-permute-done | bytes 1572896 | tf_op jit(solution)/shard_map/ppermute | solution.py:839
  212.8 12.7 %attend.3 = (bf16[256,1536]{1,0:T(8,128)(2,1)}, bf16[1536,256]{1,0:T(8,128)(2,1)}, f32[32,768]{1,0:T(8,128)}) custom-call(s32[2]{0:T(128)} %pad_add_fusion.1.info_ref, bf16[1536,512]{1,0:T(8,128)(2,1)} %q_project.1.q_ref, bf16[4,256,1024]{2,1,0:T(8,128)(2,1)} %bitcast.92, bf16[4,256,1024]{2,1,0:T(8,128)(2,1)} %bitcast.93), custom_call_target="tpu_custom_call" | custom-call | flops 644245120 | bytes 445644 | tf_op jit(solution)/shard_map/attend/pallas_call | solution.py:250
  249.3 48.7 %run_experts.2 = (bf16[2048,1536]{1,0:T(8,128)(2,1)}, bf16[2048,1664]{1,0:T(8,128)(2,1)}, bf16[2048,1024]{1,0:T(8,128)(2,1)}, bf16[2048,2048]{1,0:T(8,128)(2,1)}) custom-call(s32[1]{0:T(128)} %bitcast.14.own_ref, s32[8]{0:T(128)} %multiply_add_fusion.place_ref, bf16[2048,1664]{1,0:T(8,128)(2,1)} %all-gather.7.cloned.1.call-done.xg_ref.refs_0_, ...), custom_call_target="tpu_custom_call" | custom-call | flops 3865470464 | bytes 4718592 | tf_op jit(solution)/shard_map/run_experts/pallas_call | solution.py:501
  299.0 48.6 %run_experts.3 = (bf16[2048,1536]{1,0:T(8,128)(2,1)}, bf16[2048,1664]{1,0:T(8,128)(2,1)}, bf16[2048,1024]{1,0:T(8,128)(2,1)}, bf16[2048,2048]{1,0:T(8,128)(2,1)}) custom-call(s32[1]{0:T(128)} %bitcast.14.own_ref, s32[8]{0:T(128)} %multiply_add_fusion.place_ref, bf16[2048,1664]{1,0:T(8,128)(2,1)} %all-gather.11.cloned.1.call-done.xg_ref.refs_1_, ...), custom_call_target="tpu_custom_call" | custom-call | flops 3865470464 | bytes 4718592 | tf_op jit(solution)/shard_map/run_experts/pallas_call | solution.py:501
  347.7 14.9 %down_grad.2 = bf16[512,1536]{1,0:T(8,128)(2,1)} custom-call(bf16[2048,1024]{1,0:T(8,128)(2,1)} %get-tuple-element.303.refs_0_, bf16[2048,1024]{1,0:T(8,128)(2,1)} %get-tuple-element.304.refs_1_, bf16[2048,1536]{1,0:T(8,128)(2,1)} %assemble.7.ga_ref.refs_2_, bf16[2048,1536]{1,0:T(8,128)(2,1)} %collective-permute-done.19.gb_ref.refs_3_), custom_call_target="tpu_custom_call" | custom-call | flops 644245120 | bytes 1677721 | tf_op jit(solution)/shard_map/down_grad/pallas_call | solution.py:613
  362.6 11.6 %collective-permute-start.20 = (bf16[512,1536]{1,0:T(8,128)(2,1)}, bf16[512,1536]{1,0:T(8,128)(2,1)}, u32[]{:S(2)}, u32[]{:S(2)}) collective-permute-start(bf16[512,1536]{1,0:T(8,128)(2,1)} %down_grad.2), channel_id=1, source_target_pairs={{0,8},{24,16},{1,9},{25,17},{2,10},{26,18},{3,11},{27,19},{4,12},{... | collective-permute-start | bytes 4718600 | tf_op jit(solution)/shard_map/ppermute | solution.py:821
  375.7 14.9 %down_grad.3 = bf16[512,1536]{1,0:T(8,128)(2,1)} custom-call(bf16[2048,1024]{1,0:T(8,128)(2,1)} %get-tuple-element.303.refs_0_, bf16[2048,1024]{1,0:T(8,128)(2,1)} %get-tuple-element.304.refs_1_, bf16[2048,1536]{1,0:T(8,128)(2,1)} %assemble.7.ga_ref.refs_2_, bf16[2048,1536]{1,0:T(8,128)(2,1)} %collective-permute-done.19.gb_ref.refs_3_), custom_call_target="tpu_custom_call" | custom-call | flops 644245120 | bytes 1677721 | tf_op jit(solution)/shard_map/down_grad/pallas_call | solution.py:613
  390.6 16.6 %collective-permute-done.20 = bf16[512,1536]{1,0:T(8,128)(2,1)} collective-permute-done((bf16[512,1536]{1,0:T(8,128)(2,1)}, bf16[512,1536]{1,0:T(8,128)(2,1)}, u32[]{:S(2)}, u32[]{:S(2)}) %collective-permute-start.20) | collective-permute-done | bytes 1572896 | tf_op jit(solution)/shard_map/ppermute | solution.py:821
  426.2 14.3 %wide_grad.4 = bf16[1536,512]{1,0:T(8,128)(2,1)} custom-call(bf16[2048,1664]{1,0:T(8,128)(2,1)} %all-gather.7.cloned.1.call-done.xg_ref.refs_0_, bf16[2048,1664]{1,0:T(8,128)(2,1)} %all-gather.11.cloned.1.call-done.xg_ref.refs_1_, bf16[2048,2048]{1,0:T(8,128)(2,1)} %get-tuple-element.378.refs_2_, bf16[2048,2048]{1,0:T(8,128)(2,1)} %get-tuple-element.379.refs_3_), custom_call_target="tpu_custom_call" | custom-call | flops 644245120 | bytes 1835008 | tf_op jit(solution)/shard_map/wide_grad/pallas_call | solution.py:572
  440.5 15.5 %attend_back.2 = (bf16[256,1536]{1,0:T(8,128)(2,1)}, bf16[4,2,256,512]{3,2,1,0:T(8,128)(2,1)}) custom-call(s32[2]{0:T(128)} %pad_add_fusion.info_ref, bf16[1536,512]{1,0:T(8,128)(2,1)} %q_project.1.q_ref, bf16[1536,256]{1,0:T(8,128)(2,1)} %get-tuple-element.324.g_ref, bf16[1536,256]{1,0:T(8,128)(2,1)} %get-tuple-element.325.o_ref, ...), custom_call_target="tpu_custom_call" | custom-call | flops 1610612736 | bytes 734003 | tf_op jit(solution)/shard_map/attend_back/pallas_call | solution.py:350
  483.2 14.2 %wide_grad.5 = bf16[1536,512]{1,0:T(8,128)(2,1)} custom-call(bf16[2048,1664]{1,0:T(8,128)(2,1)} %all-gather.7.cloned.1.call-done.xg_ref.refs_0_, bf16[2048,1664]{1,0:T(8,128)(2,1)} %all-gather.11.cloned.1.call-done.xg_ref.refs_1_, bf16[2048,2048]{1,0:T(8,128)(2,1)} %get-tuple-element.378.refs_2_, bf16[2048,2048]{1,0:T(8,128)(2,1)} %get-tuple-element.379.refs_3_), custom_call_target="tpu_custom_call" | custom-call | flops 644245120 | bytes 1835008 | tf_op jit(solution)/shard_map/wide_grad/pallas_call | solution.py:572
  497.4 20.1 %collective-permute-done.23 = bf16[1536,512]{1,0:T(8,128)(2,1)} collective-permute-done((bf16[1536,512]{1,0:T(8,128)(2,1)S(1)}, bf16[1536,512]{1,0:T(8,128)(2,1)}, u32[]{:S(2)}, u32[]{:S(2)}) %collective-permute-start.23) | collective-permute-done | bytes 1572896 | tf_op jit(solution)/shard_map/ppermute | solution.py:821
  524.1 19.8 %collective-permute-done.25 = bf16[512,1536]{1,0:T(8,128)(2,1)} collective-permute-done((bf16[512,1536]{1,0:T(8,128)(2,1)S(1)}, bf16[512,1536]{1,0:T(8,128)(2,1)}, u32[]{:S(2)}, u32[]{:S(2)}) %collective-permute-start.25) | collective-permute-done | bytes 1572896 | tf_op jit(solution)/shard_map/ppermute | solution.py:823
  555.2 14.1 %wide_grad.6 = bf16[1536,512]{1,0:T(8,128)(2,1)} custom-call(bf16[2048,1664]{1,0:T(8,128)(2,1)} %all-gather.7.cloned.1.call-done.xg_ref.refs_0_, bf16[2048,1664]{1,0:T(8,128)(2,1)} %all-gather.11.cloned.1.call-done.xg_ref.refs_1_, bf16[2048,2048]{1,0:T(8,128)(2,1)} %get-tuple-element.378.refs_2_, bf16[2048,2048]{1,0:T(8,128)(2,1)} %get-tuple-element.379.refs_3_), custom_call_target="tpu_custom_call" | custom-call | flops 644245120 | bytes 1835008 | tf_op jit(solution)/shard_map/wide_grad/pallas_call | solution.py:572
  569.3 15.5 %attend_back.3 = (bf16[256,1536]{1,0:T(8,128)(2,1)}, bf16[4,2,256,512]{3,2,1,0:T(8,128)(2,1)}) custom-call(s32[2]{0:T(128)} %pad_add_fusion.1.info_ref, bf16[1536,512]{1,0:T(8,128)(2,1)} %q_project.1.q_ref, bf16[1536,256]{1,0:T(8,128)(2,1)} %get-tuple-element.368.g_ref, bf16[1536,256]{1,0:T(8,128)(2,1)} %get-tuple-element.365.o_ref, ...), custom_call_target="tpu_custom_call" | custom-call | flops 1610612736 | bytes 734003 | tf_op jit(solution)/shard_map/attend_back/pallas_call | solution.py:350
  611.7 14.1 %wide_grad.7 = bf16[1536,512]{1,0:T(8,128)(2,1)} custom-call(bf16[2048,1664]{1,0:T(8,128)(2,1)} %all-gather.7.cloned.1.call-done.xg_ref.refs_0_, bf16[2048,1664]{1,0:T(8,128)(2,1)} %all-gather.11.cloned.1.call-done.xg_ref.refs_1_, bf16[2048,2048]{1,0:T(8,128)(2,1)} %get-tuple-element.378.refs_2_, bf16[2048,2048]{1,0:T(8,128)(2,1)} %get-tuple-element.379.refs_3_), custom_call_target="tpu_custom_call" | custom-call | flops 644245120 | bytes 1835008 | tf_op jit(solution)/shard_map/wide_grad/pallas_call | solution.py:572
  633.7 33.3 %collective-permute-done.29 = bf16[1536,512]{1,0:T(8,128)(2,1)} collective-permute-done((bf16[1536,512]{1,0:T(8,128)(2,1)S(1)}, bf16[1536,512]{1,0:T(8,128)(2,1)}, u32[]{:S(2)}, u32[]{:S(2)}) %collective-permute-start.29) | collective-permute-done | bytes 1572896 | tf_op jit(solution)/shard_map/ppermute | solution.py:821
  757.0 26.5 %collective-permute-done.34 = bf16[1536,512]{1,0:T(8,128)(2,1)S(1)} collective-permute-done((bf16[1536,512]{1,0:T(8,128)(2,1)}, bf16[1536,512]{1,0:T(8,128)(2,1)S(1)}, u32[]{:S(2)}, u32[]{:S(2)}) %collective-permute-start.34) | collective-permute-done | bytes 1572896 | tf_op jit(solution)/shard_map/ppermute | solution.py:821
  825.7 17.2 %collective-permute-done.43 = bf16[256,1536]{1,0:T(8,128)(2,1)S(1)} collective-permute-done((bf16[256,1536]{1,0:T(8,128)(2,1)S(1)}, bf16[256,1536]{1,0:T(8,128)(2,1)S(1)}, u32[]{:S(2)}, u32[]{:S(2)}) %collective-permute-start.43) | collective-permute-done | bytes 786464 | tf_op jit(solution)/shard_map/ppermute | solution.py:839
  865.0 14.3 %collective-permute-done.44 = bf16[192,2688]{1,0:T(8,128)(2,1)} collective-permute-done((bf16[192,2688]{1,0:T(8,128)(2,1)}, bf16[192,2688]{1,0:T(8,128)(2,1)}, u32[]{:S(2)}, u32[]{:S(2)}) %collective-permute-start.44) | collective-permute-done | bytes 1032224 | tf_op jit(solution)/shard_map/ppermute | solution.py:821
  883.5 12.6 %collective-permute-done.46 = bf16[1536,512]{1,0:T(8,128)(2,1)} collective-permute-done((bf16[1536,512]{1,0:T(8,128)(2,1)}, bf16[1536,512]{1,0:T(8,128)(2,1)}, u32[]{:S(2)}, u32[]{:S(2)}) %collective-permute-start.46) | collective-permute-done | bytes 1572896 | tf_op jit(solution)/shard_map/ppermute | solution.py:823
  (414 shorter events, 460.2 us)
Async XLA Ops:
  7.2 134.1 %all-gather.5.cloned.1.call-start = ((), (), s32[]{:S(2)}) async-start(), calls=%async_computation.6 | async-start | bytes 2621440 | tf_op jit(solution)/shard_map/all_gather | solution.py:1033
  53.6 159.1 %all-gather.9.cloned.1.call-start = ((), (), s32[]{:S(2)}) async-start(), calls=%async_computation.8 | async-start | bytes 2621440 | tf_op jit(solution)/shard_map/all_gather | solution.py:1033
  87.2 151.6 %all-gather.7.cloned.1.call-start = ((), (), s32[]{:S(2)}) async-start(), calls=%async_computation.7 | async-start | bytes 7667712 | tf_op jit(solution)/shard_map/all_gather | solution.py:843
  160.9 138.1 %all-gather.11.cloned.1.call-start = ((), (), s32[]{:S(2)}) async-start(), calls=%async_computation.9 | async-start | bytes 7667712 | tf_op jit(solution)/shard_map/all_gather | solution.py:843
  162.8 47.2 %collective-permute-start.17 = (bf16[512,1536]{1,0:T(8,128)(2,1)S(1)}, bf16[512,1536]{1,0:T(8,128)(2,1)S(1)}, u32[]{:S(2)}, u32[]{:S(2)}) collective-permute-start(bf16[512,1536]{1,0:T(8,128)(2,1)S(1)} %pad_maximum_fusion.1), channel_id=1, source_target_pairs={{0,4},{1,5},{2,6},{3,7},{4,0},{5,1},{6,2},{7,3},{8,12},{9,13},{10,... | collective-permute-start | bytes 4718600 | tf_op jit(solution)/shard_map/ppermute | solution.py:839
  164.1 48.7 %collective-permute-start.18 = (bf16[512,1536]{1,0:T(8,128)(2,1)S(1)}, bf16[512,1536]{1,0:T(8,128)(2,1)S(1)}, u32[]{:S(2)}, u32[]{:S(2)}) collective-permute-start(bf16[512,1536]{1,0:T(8,128)(2,1)S(1)} %pad_maximum_fusion.2), channel_id=1, source_target_pairs={{0,2},{1,3},{2,0},{3,1},{4,6},{5,7},{6,4},{7,5},{8,10},{9,11},{10,... | collective-permute-start | bytes 4718600 | tf_op jit(solution)/shard_map/ppermute | solution.py:839
  232.4 176.6 %reduce-scatter.9.cloned.1.call-start = ((), (), s32[]{:S(2)}) async-start(), calls=%async_computation.10 | async-start | bytes 7667712 | tf_op jit(solution)/shard_map/reduce_scatter | solution.py:963
  298.0 176.5 %reduce-scatter.11.cloned.1.call-start = ((), (), s32[]{:S(2)}) async-start(), calls=%async_computation.11 | async-start | bytes 7667712 | tf_op jit(solution)/shard_map/reduce_scatter | solution.py:963
  347.6 278.2 %reduce-scatter.13.cloned.1.call-start = ((), (), s32[]{:S(2)}) async-start(), calls=%async_computation.12 | async-start | bytes 2621440 | tf_op jit(solution)/shard_map/reduce_scatter | solution.py:1094
  461.0 56.5 %collective-permute-start.23 = (bf16[1536,512]{1,0:T(8,128)(2,1)S(1)}, bf16[1536,512]{1,0:T(8,128)(2,1)}, u32[]{:S(2)}, u32[]{:S(2)}) collective-permute-start(bf16[1536,512]{1,0:T(8,128)(2,1)S(1)} %copy-done.10), channel_id=1, source_target_pairs={{0,8},{24,16},{1,9},{25,17},{2,10},{26,18},{3,11},{27,19},{4,12},{... | collective-permute-start | bytes 4718600 | tf_op jit(solution)/shard_map/ppermute | solution.py:821
  471.3 49.3 %collective-permute-start.24 = (bf16[512,1536]{1,0:T(8,128)(2,1)}, bf16[512,1536]{1,0:T(8,128)(2,1)}, u32[]{:S(2)}, u32[]{:S(2)}) collective-permute-start(bf16[512,1536]{1,0:T(8,128)(2,1)} %add_convert_fusion.13), channel_id=1, source_target_pairs={{8,16},{16,8},{9,17},{17,9},{10,18},{18,10},{11,19},{19,11},{12,20... | collective-permute-start | bytes 4718600 | tf_op jit(solution)/shard_map/ppermute | solution.py:825
  473.1 70.8 %collective-permute-start.25 = (bf16[512,1536]{1,0:T(8,128)(2,1)S(1)}, bf16[512,1536]{1,0:T(8,128)(2,1)}, u32[]{:S(2)}, u32[]{:S(2)}) collective-permute-start(bf16[512,1536]{1,0:T(8,128)(2,1)S(1)} %add_convert_fusion.12), channel_id=1, source_target_pairs={{8,0},{16,24},{9,1},{17,25},{10,2},{18,26},{11,3},{19,27},{12,4},{... | collective-permute-start | bytes 4718600 | tf_op jit(solution)/shard_map/ppermute | solution.py:823
  474.4 230.8 %reduce-scatter.15.cloned.1.call-start = ((), (), s32[]{:S(2)}) async-start(), calls=%async_computation.13 | async-start | bytes 2621440 | tf_op jit(solution)/shard_map/reduce_scatter | solution.py:1094
  588.9 217.7 %reduce-scatter.17.cloned.1.call-start = ((), (), s32[]{:S(2)}) async-start(), calls=%async_computation.14 | async-start | bytes 5308416 | tf_op jit(solution)/shard_map/reduce_scatter | solution.py:963
  593.3 80.5 %collective-permute-start.33 = (bf16[1024,1536]{1,0:T(8,128)(2,1)}, bf16[1024,1536]{1,0:T(8,128)(2,1)}, u32[]{:S(2)}, u32[]{:S(2)}) collective-permute-start(bf16[1024,1536]{1,0:T(8,128)(2,1)} %slice.357), channel_id=1, source_target_pairs={{0,1},{1,0},{2,3},{3,2},{4,5},{5,4},{6,7},{7,6},{8,9},{9,8},{10,11... | collective-permute-start | bytes 9437192 | tf_op jit(solution)/shard_map/ppermute | solution.py:839
  593.3 73.8 %collective-permute-start.29 = (bf16[1536,512]{1,0:T(8,128)(2,1)S(1)}, bf16[1536,512]{1,0:T(8,128)(2,1)}, u32[]{:S(2)}, u32[]{:S(2)}) collective-permute-start(bf16[1536,512]{1,0:T(8,128)(2,1)S(1)} %copy-done.9), channel_id=1, source_target_pairs={{0,8},{24,16},{1,9},{25,17},{2,10},{26,18},{3,11},{27,19},{4,12},{... | collective-permute-start | bytes 4718600 | tf_op jit(solution)/shard_map/ppermute | solution.py:821
  608.1 71.2 %collective-permute-start.32 = (bf16[1024,1536]{1,0:T(8,128)(2,1)}, bf16[1024,1536]{1,0:T(8,128)(2,1)}, u32[]{:S(2)}, u32[]{:S(2)}) collective-permute-start(bf16[1024,1536]{1,0:T(8,128)(2,1)} %slice.355), channel_id=1, source_target_pairs={{0,1},{1,0},{2,3},{3,2},{4,5},{5,4},{6,7},{7,6},{8,9},{9,8},{10,11... | collective-permute-start | bytes 9437192 | tf_op jit(solution)/shard_map/ppermute | solution.py:839
  608.3 61.7 %collective-permute-start.30 = (bf16[1536,512]{1,0:T(8,128)(2,1)}, bf16[1536,512]{1,0:T(8,128)(2,1)}, u32[]{:S(2)}, u32[]{:S(2)}) collective-permute-start(bf16[1536,512]{1,0:T(8,128)(2,1)} %add_convert_fusion.9), channel_id=1, source_target_pairs={{8,16},{16,8},{9,17},{17,9},{10,18},{18,10},{11,19},{19,11},{12,20... | collective-permute-start | bytes 4718600 | tf_op jit(solution)/shard_map/ppermute | solution.py:825
  610.1 73.5 %collective-permute-start.31 = (bf16[1536,512]{1,0:T(8,128)(2,1)S(1)}, bf16[1536,512]{1,0:T(8,128)(2,1)}, u32[]{:S(2)}, u32[]{:S(2)}) collective-permute-start(bf16[1536,512]{1,0:T(8,128)(2,1)S(1)} %add_convert_fusion.8), channel_id=1, source_target_pairs={{8,0},{16,24},{9,1},{17,25},{10,2},{18,26},{11,3},{19,27},{12,4},{... | collective-permute-start | bytes 4718600 | tf_op jit(solution)/shard_map/ppermute | solution.py:823
  611.5 236.3 %reduce-scatter.19.cloned.1.call-start = ((), (), s32[]{:S(2)}) async-start(), calls=%async_computation.15 | async-start | bytes 9289728
  738.8 44.7 %collective-permute-start.34 = (bf16[1536,512]{1,0:T(8,128)(2,1)}, bf16[1536,512]{1,0:T(8,128)(2,1)S(1)}, u32[]{:S(2)}, u32[]{:S(2)}) collective-permute-start(bf16[1536,512]{1,0:T(8,128)(2,1)} %wide_grad.7), channel_id=1, source_target_pairs={{0,8},{24,16},{1,9},{25,17},{2,10},{26,18},{3,11},{27,19},{4,12},{... | collective-permute-start | bytes 4718600 | tf_op jit(solution)/shard_map/ppermute | solution.py:821
  750.5 47.8 %collective-permute-start.37 = (bf16[512,1536]{1,0:T(8,128)(2,1)S(1)}, bf16[512,1536]{1,0:T(8,128)(2,1)S(1)}, u32[]{:S(2)}, u32[]{:S(2)}) collective-permute-start(bf16[512,1536]{1,0:T(8,128)(2,1)S(1)} %pad_maximum_fusion.3), channel_id=1, source_target_pairs={{0,4},{1,5},{2,6},{3,7},{4,0},{5,1},{6,2},{7,3},{8,12},{9,13},{10,... | collective-permute-start | bytes 4718600 | tf_op jit(solution)/shard_map/ppermute | solution.py:839
  752.2 52.5 %collective-permute-start.38 = (bf16[512,1536]{1,0:T(8,128)(2,1)S(1)}, bf16[512,1536]{1,0:T(8,128)(2,1)S(1)}, u32[]{:S(2)}, u32[]{:S(2)}) collective-permute-start(bf16[512,1536]{1,0:T(8,128)(2,1)S(1)} %pad_maximum_fusion.4), channel_id=1, source_target_pairs={{0,2},{1,3},{2,0},{3,1},{4,6},{5,7},{6,4},{7,5},{8,10},{9,11},{10,... | collective-permute-start | bytes 4718600 | tf_op jit(solution)/shard_map/ppermute | solution.py:839
  755.7 50.8 %collective-permute-start.36 = (bf16[1536,512]{1,0:T(8,128)(2,1)S(1)}, bf16[1536,512]{1,0:T(8,128)(2,1)}, u32[]{:S(2)}, u32[]{:S(2)}) collective-permute-start(bf16[1536,512]{1,0:T(8,128)(2,1)S(1)} %copy-done.18), channel_id=1, source_target_pairs={{8,0},{16,24},{9,1},{17,25},{10,2},{18,26},{11,3},{19,27},{12,4},{... | collective-permute-start | bytes 4718600 | tf_op jit(solution)/shard_map/ppermute | solution.py:823
  (110 other events, 2134.0 us)
Sparse Core Ops, SparseCore 0:
  53.8 46.7 all-gather.4
  102.7 44.6 all-gather.8
  161.1 67.4 all-gather.6
  232.5 66.4 all-gather.10
  302.3 78.7 reduce-scatter.8
  384.7 64.2 reduce-scatter.10
  474.5 69.0 reduce-scatter.12
  589.0 86.8 reduce-scatter.14
  679.3 56.5 reduce-scatter.16
  739.8 102.8 reduce-scatter.18

commit v3 on v2

--- a/solution.py
+++ b/solution.py
@@ -147,9 +147,8 @@
     q_ref[...] = r.astype(BF) * BF(SCALE)
 
 
-def q_project(place, normed, w, cosine, sine):
+def q_project(place, normed, w, width, cosine, sine):
     rows, dim = normed.shape
-    width = w[0].shape[2]
     tile = 512
     return pl.pallas_call(
         q_kernel,
@@ -411,9 +410,9 @@
         xg_ref[:, dim:] = exact.astype(BF)
 
 
-def after_attention(place, attn, w_out, x, micro, gain, router, chosen):
+def after_attention(place, attn, w, first, x, micro, gain, router, chosen):
     tokens, width = attn.shape
-    dim = w_out[0].shape[2]
+    dim = x.shape[1]
     tile = 512
     steps = dim // tile
     return pl.pallas_call(
@@ -423,7 +422,7 @@
         in_specs=[
             smem(),
             whole((tokens, width)),
-            *w_columns(w_out, tile, lambda i: i),
+            *w_columns(w, tile, lambda i: first // tile + i),
             pl.BlockSpec((tokens, dim), lambda i: (micro, 0)),
             whole((1, dim)),
             whole((dim, LANES)),
@@ -442,16 +441,17 @@
         scratch_shapes=[pltpu.VMEM((steps, tokens, tile), F32)],
         compiler_params=params(),
         cost_estimate=cost(2 * tokens * width * dim, 2 * width * dim + 10 * tokens * dim),
-    )(place, attn, *w_out, x, gain, router, chosen)
+    )(place, attn, *w, x, gain, router, chosen)
 
 
 def expert_kernel(
-    experts, half, own_ref, place_ref, xg_ref, ga_ref, gb_ref, wg_ref, wu_ref, wd_ref, y_ref, back_ref, hg_ref, gp_ref
+    experts, half, own_ref, order_ref, xg_ref, ga_ref, gb_ref, wg_ref, wu_ref, wd_ref, ya_ref, yb_ref, back_ref, hg_ref, gp_ref
 ):
     rows, dim = ga_ref.shape
     hidden = wg_ref.shape[2]
     x = xg_ref[:, :dim]
-    g = jnp.where(place_ref[pl.program_id(0)] < half, ga_ref[...], gb_ref[...])
+    step = pl.program_id(0)
+    g = jnp.where(step < half, ga_ref[...], gb_ref[...])
     gates = xg_ref[:, dim:].astype(F32)
     lane = lax.broadcasted_iota(jnp.int32, (rows, LANES), 1)
     gate_cols = jnp.zeros((rows, LANES), F32)
@@ -476,7 +476,15 @@
     y = dot(hg_ref[:, :hidden], wd_ref[0])
     for e in range(1, experts):
         y += dot(hg_ref[:, e * hidden : (e + 1) * hidden], wd_ref[e])
-    y_ref[...] = y.astype(BF)
+
+    @pl.when(step < half)
+    def _():
+        ya_ref[...] = y.astype(BF)
+
+    @pl.when(step >= half)
+    def _():
+        yb_ref[...] = y.astype(BF)
+
     back = None
     for e in range(experts):
         base = 2 * e * hidden
@@ -487,17 +495,15 @@
     back_ref[:, dim:] = gate_cols.astype(BF)
 
 
-def run_experts(own, place, xg, g, micro, micros, w_gate, w_up, w_down):
+def run_experts(own, order, xg, g, w_gate, w_up, w_down):
     rows = xg.shape[0]
     dim = g[0].shape[1]
     experts, _, hidden = w_gate.shape
-    devices = place.shape[0]
+    devices = order.shape[0]
     tile, half = rows // devices, devices // 2
-    row_block = lambda width: pl.BlockSpec((tile, width), lambda i, *_: (i, 0))
-    arrival = lambda width: pl.BlockSpec((tile, width), lambda i, own, place: (place[i], 0))
-    g_block = pl.BlockSpec(
-        (tile, dim), lambda i, own, place: (lax.rem(place[i], half) * micros + micro, 0)
-    )
+    named = lambda width: pl.BlockSpec((tile, width), lambda i, own, order: (order[i], 0))
+    first = lambda i: jnp.minimum(i, half - 1)
+    second = lambda i: jnp.maximum(i - half, 0)
     return pl.pallas_call(
         functools.partial(expert_kernel, experts, half),
         name="run_experts",
@@ -505,22 +511,24 @@
             num_scalar_prefetch=2,
             grid=(devices,),
             in_specs=[
-                row_block(dim + LANES),
-                g_block,
-                g_block,
+                named(dim + LANES),
+                pl.BlockSpec((tile, dim), lambda i, *_: (first(i), 0)),
+                pl.BlockSpec((tile, dim), lambda i, *_: (second(i), 0)),
                 whole(w_gate.shape),
                 whole(w_up.shape),
                 whole(w_down.shape),
             ],
             out_specs=[
-                arrival(dim),
-                row_block(dim + LANES),
-                arrival(experts * hidden),
-                row_block(2 * experts * hidden),
+                pl.BlockSpec((tile, dim), lambda i, *_: (first(i), 0)),
+                pl.BlockSpec((tile, dim), lambda i, *_: (second(i), 0)),
+                named(dim + LANES),
+                pl.BlockSpec((tile, experts * hidden), lambda i, *_: (i, 0)),
+                named(2 * experts * hidden),
             ],
         ),
         out_shape=[
-            jax.ShapeDtypeStruct((rows, dim), BF),
+            jax.ShapeDtypeStruct((rows // 2, dim), BF),
+            jax.ShapeDtypeStruct((rows // 2, dim), BF),
             jax.ShapeDtypeStruct((rows, dim + LANES), BF),
             jax.ShapeDtypeStruct((rows, experts * hidden), BF),
             jax.ShapeDtypeStruct((rows, 2 * experts * hidden), BF),
@@ -531,7 +539,7 @@
             2 * (4 * rows * dim + 3 * rows * experts * hidden + 3 * experts * dim * hidden),
             rows * experts * hidden,
         ),
-    )(own, place, xg, *g, w_gate, w_up, w_down)
+    )(own, order, xg, *g, w_gate, w_up, w_down)
 
 
 def wide_grad_kernel(steps, micros, *refs):
@@ -587,11 +595,12 @@
 
 
 def down_grad_kernel(micros, devices, *refs):
-    hg_refs, ga_ref, gb_ref, out_ref, acc_ref = refs[:micros], *refs[micros:]
+    hg_refs, refs = refs[:micros], refs[micros:]
+    ga_refs, gb_refs = refs[:micros], refs[micros : 2 * micros]
+    out_ref, acc_ref = refs[2 * micros :]
     step = pl.program_id(0)
-    g = jnp.where(step < devices // 2, ga_ref[...], gb_ref[...])
-    hg = jnp.concatenate([r[...] for r in hg_refs], axis=0)
-    part = dot(hg, g, TN)
+    g = [jnp.where(step < devices // 2, a[...], b[...]) for a, b in zip(ga_refs, gb_refs)]
+    part = dot(jnp.concatenate(g), jnp.concatenate([r[...] for r in hg_refs]), TN)
 
     @pl.when(step == 0)
     def _():
@@ -606,25 +615,23 @@
         out_ref[...] = acc_ref[...].astype(BF)
 
 
-def down_grad(hgs, expert, hidden, g, devices):
+def down_grad(hgs, expert, hidden, gs, devices):
     micros, rows = len(hgs), hgs[0].shape[0]
     tile, half = rows // devices, devices // 2
-    dim = g[0].shape[1]
+    dim = gs[0][0].shape[1]
     return pl.pallas_call(
         functools.partial(down_grad_kernel, micros, devices),
         name="down_grad",
         grid=(devices,),
         in_specs=[pl.BlockSpec((tile, hidden), lambda i: (i, expert))] * micros
-        + [
-            pl.BlockSpec((micros * tile, dim), lambda i: (jnp.minimum(i, half - 1), 0)),
-            pl.BlockSpec((micros * tile, dim), lambda i: (jnp.maximum(i - half, 0), 0)),
-        ],
-        out_specs=whole((hidden, dim)),
-        out_shape=jax.ShapeDtypeStruct((hidden, dim), BF),
-        scratch_shapes=[pltpu.VMEM((hidden, dim), F32)],
+        + [pl.BlockSpec((tile, dim), lambda i: (jnp.minimum(i, half - 1), 0))] * micros
+        + [pl.BlockSpec((tile, dim), lambda i: (jnp.maximum(i - half, 0), 0))] * micros,
+        out_specs=whole((dim, hidden)),
+        out_shape=jax.ShapeDtypeStruct((dim, hidden), BF),
+        scratch_shapes=[pltpu.VMEM((dim, hidden), F32)],
         compiler_params=params(),
         cost_estimate=cost(2 * micros * rows * hidden * dim, 2 * micros * rows * (hidden + dim)),
-    )(*hgs, *g)
+    )(*hgs, *[g[0] for g in gs], *[g[1] for g in gs])
 
 
 def before_kernel(
@@ -670,9 +677,9 @@
         gt_ref[...] = acc_ref[...].astype(BF)
 
 
-def before_attention(place, returned, residual, exact, gout, gain, router, w_out):
+def before_attention(place, returned, residual, exact, gout, gain, router, w, first):
     tokens, dim = residual.shape
-    width = 2 * w_out[0].shape[0] * w_out[0].shape[1]
+    width = 2 * w[0].shape[0] * w[0].shape[1]
     tile = 512
     steps = dim // tile
     return pl.pallas_call(
@@ -687,7 +694,7 @@
             whole((tokens, dim)),
             whole((1, dim)),
             whole((dim, LANES)),
-            *w_columns(w_out, tile, lambda i: i),
+            *w_columns(w, tile, lambda i: first // tile + i),
         ],
         out_specs=[
             whole((tokens, dim)),
@@ -707,7 +714,7 @@
         ],
         compiler_params=params(),
         cost_estimate=cost(2 * tokens * width * dim, 2 * width * dim + 14 * tokens * dim),
-    )(place, returned, residual, exact, gout, gain, router, *w_out)
+    )(place, returned, residual, exact, gout, gain, router, *w)
 
 
 def last_kernel(
@@ -774,6 +781,112 @@
             2 * tokens * steps * tile * dim, 2 * steps * tile * dim + 12 * tokens * dim
         ),
     )(place, gq, dkv, *w_q, *w_kv, x, gain, gres)
+
+
+def out_grad_kernel(micros, half, order_ref, *refs):
+    t_refs, g_refs, (first_ref, second_ref) = refs[:micros], refs[micros : 2 * micros], refs[2 * micros :]
+    step = pl.program_id(0)
+    total = dot(t_refs[0][...], g_refs[0][...])
+    for t_ref, g_ref in zip(t_refs[1:], g_refs[1:]):
+        total += dot(t_ref[...], g_ref[...])
+
+    @pl.when(step < half)
+    def _():
+        first_ref[...] = total.astype(BF)
+
+    @pl.when(step >= half)
+    def _():
+        second_ref[...] = total.astype(BF)
+
+
+def out_grad(order, heads_t, grads):
+    micros, devices = len(heads_t), order.shape[0]
+    width, tokens = heads_t[0].shape
+    dim = grads[0].shape[1]
+    tile, half = width // devices, devices // 2
+    return pl.pallas_call(
+        functools.partial(out_grad_kernel, micros, half),
+        name="out_grad",
+        grid_spec=pltpu.PrefetchScalarGridSpec(
+            num_scalar_prefetch=1,
+            grid=(devices,),
+            in_specs=[pl.BlockSpec((tile, tokens), lambda i, order: (order[i], 0))] * micros
+            + [whole((tokens, dim))] * micros,
+            out_specs=[
+                pl.BlockSpec((tile, dim), lambda i, order: (jnp.minimum(i, half - 1), 0)),
+                pl.BlockSpec((tile, dim), lambda i, order: (jnp.maximum(i - half, 0), 0)),
+            ],
+        ),
+        out_shape=[jax.ShapeDtypeStruct((width // 2, dim), BF)] * 2,
+        compiler_params=params(),
+        cost_estimate=cost(2 * micros * tokens * width * dim, 4 * width * dim),
+    )(order, *heads_t, *grads)
+
+
+def turn_kernel(kv_ref, cos_ref, sin_ref, out_ref):
+    width = kv_ref.shape[2]
+    key = rotate(kv_ref[0].astype(F32).T, cos_ref[...], sin_ref[...], -1)
+    out_ref[:, :width] = key.T.astype(BF)
+    out_ref[:, width:] = kv_ref[1]
+
+
+def turn_back(kv, cosine, sine):
+    _, tokens, width = kv.shape
+    return pl.pallas_call(
+        turn_kernel,
+        name="turn_back",
+        out_shape=jax.ShapeDtypeStruct((tokens, 2 * width), BF),
+        compiler_params=params(),
+        cost_estimate=cost(0, 8 * tokens * width),
+    )(kv, cosine, sine)
+
+
+def projection_kernel(micros, q_steps, steps, n_experts, normed_ref, *refs):
+    gq_refs, refs = refs[:micros], refs[micros:]
+    dkv_refs, refs = refs[:micros], refs[micros:]
+    two_refs, refs = refs[:micros], refs[micros:]
+    one_refs, (out_ref, turned_ref) = refs[:micros], refs[micros:]
+    step = pl.program_id(0)
+    tile = gq_refs[0].shape[1]
+
+    @pl.when(step == 0)
+    def _():
+        turned_ref[...] = normed_ref[...].astype(F32).T.astype(BF)
+        rows = functools.reduce(jnp.add, [r[:LANES] for r in two_refs])
+        gain_two = functools.reduce(jnp.add, [r[LANES : LANES + 1] for r in two_refs])
+        gain_one = functools.reduce(jnp.add, [r[:1] for r in one_refs])
+        at = lax.broadcasted_iota(jnp.int32, rows.shape, 0)
+        rows = jnp.where(at == n_experts, gain_one, rows)
+        rows = jnp.where(at == n_experts + 1, gain_two, rows)
+        out_ref[:, steps * tile :] = rows.T.astype(BF)
+
+    q = jnp.concatenate([r[...] for r in gq_refs], axis=0)
+    kv = jnp.concatenate([r[...] for r in dkv_refs], axis=0)
+    g = jnp.where(step < q_steps, q, kv)
+    out_ref[:, pl.ds(pl.multiple_of(step * tile, tile), tile)] = dot(turned_ref[...], g).astype(BF)
+
+
+def projection_grads(normed, gqs, dkvs, twos, ones, n_experts):
+    rows, dim = normed.shape
+    micros, tokens, tile = len(gqs), gqs[0].shape[0], 512
+    q_steps, kv_steps = gqs[0].shape[1] // tile, dkvs[0].shape[1] // tile
+    steps = q_steps + kv_steps
+    width = steps * tile + LANES
+    return pl.pallas_call(
+        functools.partial(projection_kernel, micros, q_steps, steps, n_experts),
+        name="projection_grads",
+        grid=(steps,),
+        in_specs=[whole((rows, dim))]
+        + [pl.BlockSpec((tokens, tile), lambda i: (0, jnp.minimum(i, q_steps - 1)))] * micros
+        + [pl.BlockSpec((tokens, tile), lambda i: (0, jnp.maximum(i - q_steps, 0)))] * micros
+        + [whole(twos[0].shape)] * micros
+        + [whole(ones[0].shape)] * micros,
+        out_specs=whole((dim, width)),
+        out_shape=jax.ShapeDtypeStruct((dim, width), BF),
+        scratch_shapes=[pltpu.VMEM((dim, rows), BF)],
+        compiler_params=params(),
+        cost_estimate=cost(2 * rows * dim * width, 2 * rows * (dim + width) + 2 * dim * width),
+    )(normed, *gqs, *dkvs, *twos, *ones)
 
 
 def add_low(a, b):
@@ -800,7 +913,6 @@
     def __init__(self, n):
         self.n = n
         self.held = {}
-        self.count = 0
         self.results = []
 
     def sums(self):
@@ -808,24 +920,34 @@
         middle = (at == 1) | (at == 2)
         return [r[0] if len(r) == 1 else jnp.where(middle, *r) for r in self.results]
 
-    def step(self, chunk):
+    def step(self, chunk, beside):
         n = self.n
         if n != 4:
             if chunk is not None:
                 self.results.append((line_sum(chunk, n),))
             return
+        at = lax.axis_index("seq")
+        middle = (at == 1) | (at == 2)
+        come, go = [(0, 1), (3, 2)], [(1, 0), (2, 3)]
         held, self.held = self.held, {}
-        crossing, leaving = held.get("crossing"), held.get("leaving")
-        arrived = None
-        if chunk is not None:
-            arrived = lax.ppermute(chunk, "seq", [(0, 1), (3, 2)])
-        if leaving is not None:
-            self.results.append((leaving, lax.ppermute(leaving, "seq", [(1, 0), (2, 3)])))
+        summed = held.get("summed")
+        if summed is not None:
+            summed = add_low(*summed)
+        crossing = held.get("crossing")
         if crossing is not None:
-            other = lax.ppermute(crossing, "seq", [(1, 2), (2, 1)])
-            self.held["leaving"] = add_low(crossing, other)
-        if chunk is not None:
-            self.held["crossing"] = add_low(chunk, arrived)
+            crossing = add_low(*crossing)
+            self.held["summed"] = (crossing, lax.ppermute(crossing, "seq", [(1, 2), (2, 1)]))
+        if chunk is not None and summed is not None and chunk.shape == summed.shape:
+            sent = jnp.where(middle, summed, chunk)
+            got = lax.ppermute(sent, "seq", come + go)
+            self.results.append((sent, got))
+            self.held["crossing"] = (chunk, got)
+        else:
+            if summed is not None:
+                self.results.append((summed, lax.ppermute(summed, "seq", go)))
+            if chunk is not None:
+                self.held["crossing"] = (chunk, lax.ppermute(chunk, "seq", come))
+        self.held, self.results = gate((self.held, self.results), beside)
 
 
 def gate(x, *others):
@@ -911,17 +1033,17 @@
 class Scatter:
     def __init__(self, arrays, n):
         self.arrays, self.n, self.stage = list(arrays), n, 0
-        self.rows = arrays[0].shape[0] // n
+        self.rows = 2 * arrays[0][0].shape[0] // n
 
     def advance(self):
         held, self.stage = self.arrays, self.stage + 1
         rows, half = self.rows, self.rows // 2
         if self.n != 8:
             if self.stage == 1:
-                self.arrays = [scatter_rows(a) for a in held]
+                self.arrays = [scatter_rows(jnp.concatenate(a)) for a in held]
             return
         if self.stage == 1:
-            self.arrays = [add_low(a[: 4 * rows], swap(a[4 * rows :], CORE)) for a in held]
+            self.arrays = [add_low(mine, swap(other, CORE)) for mine, other in held]
         if self.stage == 2:
             tops = [a[k * rows : k * rows + half] for a in held for k in (2, 3)]
             lows = [a[k * rows + half : (k + 1) * rows] for a in held for k in (1, 3)]
@@ -952,6 +1074,13 @@
             ]
 
 
+def block_order(n):
+    at = jnp.arange(n, dtype=jnp.int32)
+    if n != 8:
+        return at
+    return lax.axis_index("fsdp").astype(jnp.int32) ^ (2 * lax.rem(at, 4) + at // 4)
+
+
 def block_places(n):
     if n != 8:
         return jnp.arange(n, dtype=jnp.int32)
@@ -994,7 +1123,7 @@
         [router, gain_attn[:, None], gain_moe[:, None]], axis=1
     )
     small = jnp.pad(small, ((0, 0), (0, LANES - small.shape[1])))
-    place = block_places(n_fsdp)
+    place, order = block_places(n_fsdp), block_order(n_fsdp)
 
     def weights(w):
         return [h.reshape(n_fsdp // 2, -1, h.shape[1]) for h in gather_near(w, n_fsdp)]
@@ -1025,43 +1154,51 @@
     ]
 
     kv, normed_one = kv_project(place, x, gain_one, w_kv, kv_width, cosine_all, sine_all)
-    w_q = weights(gate(w_query, kv))
-    q_t = q_project(place, normed_one, w_q, cosine_all, sine_all)
+    q_width = w_query.shape[1]
+    w_gather = Gather(gate(jnp.concatenate([w_query, w_out], axis=1), kv), n_fsdp)
+    w_gather.further()
     kvs = []
     for m in range(micros):
         mine = kv[m * tokens : (m + 1) * tokens]
         every = lax.all_gather(mine, "seq", axis=0, tiled=True)
         kvs.append(every.reshape(n_seq, tokens, 2 * kv_width))
-
-    out_all = weights(gate(w_out, w_q[0]))
-    g_gather = Gather(gate(gout.reshape(rows, dim), w_q[0]), n_fsdp)
+    w_qo = [h.reshape(n_fsdp // 2, -1, h.shape[1]) for h in w_gather.finish(kvs[0])]
+    g_gathers = [Gather(gate(gout[0], w_gather.far), n_fsdp)]
+    for m in range(1, micros):
+        g_gathers.append(Gather(gate(gout[m], g_gathers[-1].near), n_fsdp))
+    q_t = q_project(
+        place, gate(normed_one, kvs[0]), w_qo, q_width, cosine_all, sine_all
+    )
 
     state, xg_all = [], []
     for m in range(micros):
         if m == 0:
-            info = gate(infos[m], g_gather.near)
-            g_gather.further()
+            info = gate(infos[m], g_gathers[0].near)
+            g_gathers[0].further(q_t)
         else:
-            info = gate(infos[m], state[-1][2], g_gather.far)
-            g_all = g_gather.finish()
+            info = gate(infos[m], state[-1][2], g_gathers[m].far)
+            g_all = [g.finish() for g in g_gathers]
         attn, attn_t, lse = attend(info, q_t, kvs[m], m, tokens)
+        if m == 0:
+            attn = gate(attn, g_gathers[0].far)
+            for g in g_gathers[1:]:
+                g.further(g_gathers[0].far)
         residual, xg, exact = after_attention(
-            place, attn, out_all, x, m, gain_two, router_all, chosen
+            place, attn, w_qo, q_width, x, m, gain_two, router_all, chosen
         )
         state.append((attn_t, lse, residual, exact))
         xg_all.append(gather_rows(xg))
 
-    xg_all[0] = gate(xg_all[0], state[-1][2])
+    xg_all[0] = gate(xg_all[0], state[-1][2], g_all)
     passed, backs = [], []
     for m in range(micros):
-        y, back, hg, gp = run_experts(
-            own, place, xg_all[m], g_all, m, micros, w_gate, w_up, w_down
+        *y, back, hg, gp = run_experts(
+            own, order, xg_all[m], g_all[m], w_gate, w_up, w_down
         )
         passed.append((xg_all[m], hg, gp))
         backs.append((scatter_rows(back), y))
 
-    names = [("down", e) for e in range(experts)]
-    names += [(name, e) for e in range(experts) for name in ("gate", "up")]
+    names = [(name, e) for name in ("down", "gate", "up") for e in range(experts)]
 
     def expert_grad(name, e, got):
         xs, hgs, gps = ([p[i] for p in got] for i in range(3))
@@ -1075,7 +1212,7 @@
     def to_heads(m):
         attn_t, lse, residual, exact = state[m]
         gres, g_attn, g_t, small_two = before_attention(
-            place, backs[m][0], residual, exact, gout[m], gain_two, router_all, out_all
+            place, backs[m][0], residual, exact, gout[m], gain_two, router_all, w_qo, q_width
         )
         found[m].update(gres=gres, g_attn=g_attn, g_t=g_t, small_two=small_two)
 
@@ -1098,88 +1235,80 @@
             tiled=True,
         ).reshape(shape[1:])
 
-    def own_grads(m):
-        dk = rotate(owned[m][0].astype(F32).T, cosine, sine, -1).T
-        return jnp.concatenate([dk.astype(BF), owned[m][1]], axis=1)
-
     def finish(m):
         f = found[m]
-        f["dkv"] = own_grads(m)
-        din, small_one = last_step(
-            place, f["gq"], f["dkv"], w_q, w_kv, x, m, gain_one, f["gres"]
+        f["dkv"] = turn_back(f["mine"], cosine, sine)
+        f["din"], f["small_one"] = last_step(
+            place, f["gq"], f["dkv"], w_qo, w_kv, x, m, gain_one, f["gres"]
         )
-        small_rows = jnp.concatenate(
-            [f["small_two"][:n_experts], small_one[:1], f["small_two"][LANES : LANES + 1]], axis=0
+
+    def rest_grads():
+        every = lambda name: [f[name] for f in found]
+        return projection_grads(
+            normed_one, every("gq"), every("dkv"), every("small_two"), every("small_one"), n_experts
         )
-        f.update(din=din, small_rows=small_rows)
-
-    def out_grad():
-        total = None
-        for m in range(micros):
-            part = dot(state[m][0], found[m]["g_attn"])
-            total = part if total is None else total + part
-        return total.astype(BF)
-
-    def projection_grads():
-        d_q = d_kv = None
-        for m in range(micros):
-            normed = normed_one[m * tokens : (m + 1) * tokens]
-            part_q = dot(normed, found[m]["gq"], TN)
-            part_kv = dot(normed, found[m]["dkv"], TN)
-            d_q = part_q if d_q is None else d_q + part_q
-            d_kv = part_kv if d_kv is None else d_kv + part_kv
-        small_rows = functools.reduce(jnp.add, [f["small_rows"] for f in found])
-        pad = ((0, LANES - small_rows.shape[0]), (0, 0))
-        small_cols = jnp.pad(small_rows, pad).T
-        columns = jnp.concatenate([d_q, d_kv, small_cols], axis=1).astype(BF)
-        return scatter_rows(columns)
 
     n_grads = len(names)
     work = {
         0: [("grad", 1), (to_heads, 0)],
         1: [("grad", 2), (through_heads, 0)],
-        2: [("grad", 3), (to_heads, 1)],
-        3: [("grad", 4), (through_heads, 1)],
-        4: [("grad", 5)],
+        2: [("grad", 3), (to_heads, 1), (through_heads, 1)],
+        3: [("grad", 4), (finish, 0), ("grad", 5)],
+        4: [(finish, 1)],
     }
+    def widen(parts, turned):
+        return jnp.stack([(p.T if turned else p).astype(F32) for p in parts])
+
+    experts_out = []
     chunks = {0: expert_grad(*names[0], passed)}
     chunks.update({i: expert_grad(*names[i], passed) for i in range(6, n_grads)})
     slots = max(n_grads, 6)
     moe = Scatter([b[1] for b in backs], n_fsdp)
-    for t in range(slots + 4):
-        chunks, line.held, line.results, passed, found, moe.arrays = lax.optimization_barrier(
-            (chunks, line.held, line.results, passed, found, moe.arrays)
-        )
+    for t in range(slots + 3):
+        if t in (3, 4):
+            found[t - 3]["mine"] = owned[t - 3]
+        if t == 3:
+            heads = Scatter([found[0].pop("out")], n_fsdp)
+        if t in (6, 8):
+            found[0]["rest"] = rest
+        held = (chunks, line.held, line.results, passed, found, moe.arrays)
+        if t >= 3:
+            *held, heads.arrays = lax.optimization_barrier((*held, heads.arrays))
+        else:
+            held = lax.optimization_barrier(held)
+        chunks, line.held, line.results, passed, found, moe.arrays = held
+        if t == 6:
+            rest = lax.psum(found[0].pop("rest"), "seq")
+        if len(line.results) in (experts, 2 * experts) and t < slots + 2:
+            pair = line.sums()[-experts:]
+            experts_out.append(widen(pair, len(experts_out) == 0))
+            found[1]["wide"] = experts_out[-1]
+        if t == slots:
+            chunks[slots] = heads.arrays[0]
         sent = chunks.pop(t, None)
-        if t == 2:
-            to_owners(0)
-        if t == 4:
-            to_owners(1)
-            out_part = scatter_rows(found[0].pop("out"))
+        if t in (2, 3):
+            to_owners(t - 2)
         for kind, i in work.get(t, []):
             if kind != "grad":
                 kind(i)
             elif i < n_grads:
                 chunks[i] = expert_grad(*names[i], passed)
-        if t == 3:
-            found[0]["out"] = out_grad()
-        if t == 5:
-            finish(0)
-            finish(1)
-            rest_part = projection_grads()
-        if t == slots - 1:
-            chunks[slots] = out_part
-        if t == slots:
-            chunks[slots + 1] = rest_part
-        if t in (4, 5, 6):
+        if t == 2:
+            found[0]["out"] = out_grad(
+                order, [st[0] for st in state], [f["g_attn"] for f in found]
+            )
+        if t == 4:
+            rest = scatter_rows(rest_grads())
+        if t in (2, 3, 4):
             moe.advance()
-        line.step(sent)
+        if t in (3, 4, 5):
+            heads.advance()
+        line.step(sent, (chunks, found))
+    rest = found[0]["rest"].astype(F32)
     totals = line.sums()
-    sums = dict(zip(names, totals))
-    d_down = [sums["down", e] for e in range(experts)]
-    d_gate = [sums["gate", e] for e in range(experts)]
-    d_up = [sums["up", e] for e in range(experts)]
-    d_out, rest = [part.astype(F32) for part in totals[n_grads:]]
+    for i in range(len(experts_out), 3):
+        experts_out.append(widen(totals[i * experts : (i + 1) * experts], i == 0))
+    d_out = totals[n_grads].astype(F32)
 
     outs = []
     for m in range(micros):
@@ -1187,7 +1316,7 @@
             jnp.where(valid[m][:, None], state[m][2] + moe.arrays[m].astype(F32), 0.0).astype(BF)
         )
     grads = [f["din"] for f in found]
-    q_width = w_query.shape[1]
+    assert len(totals) == n_grads + 1
     shape = (micros, 1, tokens, dim)
     ends = q_width + 2 * kv_width
     return (
@@ -1200,9 +1329,8 @@
         d_out,
         rest[:, ends + n_experts + 1],
         rest[:, ends : ends + n_experts],
-        jnp.stack(d_gate).astype(F32),
-        jnp.stack(d_up).astype(F32),
-        jnp.stack(d_down).astype(F32),
+        *experts_out[1:],
+        experts_out[0],
     )
 
 

time: 974 us -> 899 us (0.923)
  starting transfers between devices: 120 us -> 81.6 us
  local copies, waits for them, and re-layouts: 64.2 us -> 30.6 us
  Pallas kernels: 326 us -> 357 us
  other arithmetic: 102 us -> 87.3 us
  matrix products: 12.4 us -> 0 us
    ppermute x24 -> x17, starting transfers between devices: 88.9 us -> 48.8 us  [the longest x3 26.1 us: step(): self.held['crossing'] = (chunk, lax.ppermute(chunk, 'seq', come))]
    ppermute x26 -> x31, waiting for transfers between devices: 157 us -> 126 us  [swap(): return lax.ppermute(x, 'fsdp', [(i, i ^ mask) for i in range(8)])]
    pallas_call x0 -> x4, Pallas kernels: none -> 25.5 us  [the longest x1 11.6 us: projection_grads(): pl.pallas_call(functools.partial(projection_kernel, micros, q_steps, step...]
    ppermute x24 -> x17, waiting for transfers between devices: 157 us -> 175 us  [the longest x3 83.2 us: step(): self.results.append((summed, lax.ppermute(summed, 'seq', go)))]
    slice x8 -> x0, local copies, waits for them, and re-layouts: 14.3 us -> none  [the longest x2 8.11 us: advance(): a[4 * rows:]]
    dot_general x6 -> x0, matrix products: 12.4 us -> none  [dot(): return lax.dot_general(a, b, dims, preferred_element_type=F32)]
    convert_element_type x21 -> x19, other arithmetic: 45.7 us -> 37.3 us  [add_low(): return (a.astype(F32) + b.astype(F32)).astype(BF)]
    ppermute x26 -> x31, starting transfers between devices: 29.8 us -> 31.8 us  [swap(): return lax.ppermute(x, 'fsdp', [(i, i ^ mask) for i in range(8)])]
  transfers between devices with their start and end apart: 60 -> 58, of which waited for: 33 -> 31; matrix products, arithmetic and copies ran while one was open for 16% -> 10% of each run, Pallas kernels for 33% -> 36%
where the time goes in v3:
time: 899 us; the launch traced here: 886 us
  Pallas kernels  357 us (40%)
  waiting for transfers between devices  314 us (35%)
  other arithmetic  87.3 us (10%)
  starting transfers between devices  81.6 us (9%)
  local copies, waits for them, and re-layouts  30.6 us (3%)
  between operations  15.3 us (2%)
    ppermute x31, waiting for transfers between devices, swap(): return lax.ppermute(x, 'fsdp', [(i, i ^ mask) for i in range(8)])  126 us
    pallas_call x2, Pallas kernels, run_experts(): pl.pallas_call(functools.partial(expert_kernel, experts, half), name='run...  102 us
    ppermute x3, waiting for transfers between devices, step(): self.results.append((summed, lax.ppermute(summed, 'seq', go)))  83.2 us
    ppermute x4, waiting for transfers between devices, step(): got = lax.ppermute(sent, 'seq', come + go)  81.3 us
    pallas_call x4, Pallas kernels, wide_grad(): pl.pallas_call(functools.partial(wide_grad_kernel, steps, micros), name='...  57.2 us
    convert_element_type x19, other arithmetic, add_low(): return (a.astype(F32) + b.astype(F32)).astype(BF)  37.3 us
    ppermute x31, starting transfers between devices, swap(): return lax.ppermute(x, 'fsdp', [(i, i ^ mask) for i in range(8)])  31.8 us
    pallas_call x2, Pallas kernels, attend_back(): pl.pallas_call(functools.partial(attend_back_kernel, n), name='attend_bac...  31.1 us
  transfers between devices with their start and end apart: 58, of which 31 were waited for; matrix products, arithmetic and copies ran while one was open for 10% of the time, Pallas kernels for 36%

profile of v3, /device:TPU:0, one launch (start us, length us, event | category | flops | bytes accessed | tf_op | source)
XLA Modules:
  0.0 885.6 jit_solution(10093013848505517247)
XLA Ops:
  55.1 11.8 %collective-permute-done.6.low_y_ref = bf16[96,3072]{1,0:T(8,128)(2,1)S(1)} collective-permute-done((bf16[96,3072]{1,0:T(8,128)(2,1)S(1)}, bf16[96,3072]{1,0:T(8,128)(2,1)S(1)}, u32[]{:S(2)}, u32[]{:S(2)}) %collective-permute-start.6) | collective-permute-done | bytes 589856 | tf_op jit(solution)/shard_map/ppermute | solution.py:961
  71.1 24.6 %collective-permute-done.7.top_far_ref = bf16[192,3072]{1,0:T(8,128)(2,1)S(1)} collective-permute-done((bf16[192,3072]{1,0:T(8,128)(2,1)S(1)}, bf16[192,3072]{1,0:T(8,128)(2,1)S(1)}, u32[]{:S(2)}, u32[]{:S(2)}) %collective-permute-start.7) | collective-permute-done | bytes 1179680 | tf_op jit(solution)/shard_map/ppermute | solution.py:961
  132.0 12.7 %attend.2 = (bf16[256,1536]{1,0:T(8,128)(2,1)}, bf16[1536,256]{1,0:T(8,128)(2,1)}, f32[32,768]{1,0:T(8,128)}) custom-call(s32[2]{0:T(128)} %pad_add_fusion.info_ref, bf16[1536,512]{1,0:T(8,128)(2,1)} %q_project.1.q_ref, bf16[4,256,1024]{2,1,0:T(8,128)(2,1)} %bitcast.77, bf16[4,256,1024]{2,1,0:T(8,128)(2,1)} %bitcast.78), custom_call_target="tpu_custom_call" | custom-call | flops 644245120 | bytes 445644 | tf_op jit(solution)/shard_map/attend/pallas_call | solution.py:249
  167.5 23.7 %collective-permute-done.16.top_far_ref = bf16[256,1536]{1,0:T(8,128)(2,1)S(1)} collective-permute-done((bf16[256,1536]{1,0:T(8,128)(2,1)S(1)}, bf16[256,1536]{1,0:T(8,128)(2,1)S(1)}, u32[]{:S(2)}, u32[]{:S(2)}) %collective-permute-start.16) | collective-permute-done | bytes 786464 | tf_op jit(solution)/shard_map/ppermute | solution.py:961
  193.2 12.7 %attend.3 = (bf16[256,1536]{1,0:T(8,128)(2,1)}, bf16[1536,256]{1,0:T(8,128)(2,1)}, f32[32,768]{1,0:T(8,128)}) custom-call(s32[2]{0:T(128)} %pad_add_fusion.1.info_ref, bf16[1536,512]{1,0:T(8,128)(2,1)} %q_project.1.q_ref, bf16[4,256,1024]{2,1,0:T(8,128)(2,1)} %bitcast.73, bf16[4,256,1024]{2,1,0:T(8,128)(2,1)} %bitcast.74), custom_call_target="tpu_custom_call" | custom-call | flops 644245120 | bytes 445644 | tf_op jit(solution)/shard_map/attend/pallas_call | solution.py:249
  228.0 51.6 %run_experts.2 = (bf16[1024,1536]{1,0:T(8,128)(2,1)}, bf16[1024,1536]{1,0:T(8,128)(2,1)}, bf16[2048,1664]{1,0:T(8,128)(2,1)}, bf16[2048,1024]{1,0:T(8,128)(2,1)}, bf16[2048,2048]{1,0:T(8,128)(2,1)}) custom-call(s32[1]{0:T(128)} %bitcast.12.own_ref, s32[8]{0:T(128)} %fusion.10.order_ref, bf16[2048,1664]{1,0:T(8,128)(2,1)} %all-gather.7.cloned.1.call-done.xg_ref.refs_0_, ...), custom_call_target="tpu_custom_call" | custom-call | flops 3865470464 | bytes 4718592 | tf_op jit(solution)/shard_map/run_experts/pallas_call | solution.py:507
  280.1 50.8 %run_experts.3 = (bf16[1024,1536]{1,0:T(8,128)(2,1)}, bf16[1024,1536]{1,0:T(8,128)(2,1)}, bf16[2048,1664]{1,0:T(8,128)(2,1)}, bf16[2048,1024]{1,0:T(8,128)(2,1)}, bf16[2048,2048]{1,0:T(8,128)(2,1)}) custom-call(s32[1]{0:T(128)} %bitcast.12.own_ref, s32[8]{0:T(128)} %fusion.10.order_ref, bf16[2048,1664]{1,0:T(8,128)(2,1)} %all-gather.11.cloned.1.call-done.xg_ref.refs_1_, ...), custom_call_target="tpu_custom_call" | custom-call | flops 3865470464 | bytes 4718592 | tf_op jit(solution)/shard_map/run_experts/pallas_call | solution.py:507
  331.0 15.0 %down_grad.2 = bf16[1536,512]{1,0:T(8,128)(2,1)} custom-call(bf16[2048,1024]{1,0:T(8,128)(2,1)} %get-tuple-element.404.refs_0_, bf16[2048,1024]{1,0:T(8,128)(2,1)} %get-tuple-element.405.refs_1_, bf16[1024,1536]{1,0:T(8,128)(2,1)} %assemble.6.ga_ref.refs_2_, bf16[1024,1536]{1,0:T(8,128)(2,1)} %assemble.7.ga_ref.refs_3_, bf16[1024,1536]{1,0:T(8,128)(2,1)} %copy-done.1, ...), custom_call_target="tpu_custom_call" | custom-call | flops 644245120 | bytes 1677721 | tf_op jit(solution)/shard_map/down_grad/pallas_call | solution.py:622
  353.8 15.3 %down_grad.3 = bf16[1536,512]{1,0:T(8,128)(2,1)} custom-call(bf16[2048,1024]{1,0:T(8,128)(2,1)} %get-tuple-element.404.refs_0_, bf16[2048,1024]{1,0:T(8,128)(2,1)} %get-tuple-element.405.refs_1_, bf16[1024,1536]{1,0:T(8,128)(2,1)} %assemble.6.ga_ref.refs_2_, bf16[1024,1536]{1,0:T(8,128)(2,1)} %assemble.7.ga_ref.refs_3_, bf16[1024,1536]{1,0:T(8,128)(2,1)} %copy-done.1, ...), custom_call_target="tpu_custom_call" | custom-call | flops 644245120 | bytes 1677721 | tf_op jit(solution)/shard_map/down_grad/pallas_call | solution.py:622
  389.7 14.7 %collective-permute-start.21 = (bf16[1536,512]{1,0:T(8,128)(2,1)}, bf16[1536,512]{1,0:T(8,128)(2,1)}, u32[]{:S(2)}, u32[]{:S(2)}) collective-permute-start(bf16[1536,512]{1,0:T(8,128)(2,1)} %down_grad.3), channel_id=1, source_target_pairs={{0,8},{24,16},{1,9},{25,17},{2,10},{26,18},{3,11},{27,19},{4,12},{... | collective-permute-start | bytes 4718600 | tf_op jit(solution)/shard_map/ppermute | solution.py:949
  404.5 14.6 %wide_grad.4 = bf16[1536,512]{1,0:T(8,128)(2,1)} custom-call(bf16[2048,1664]{1,0:T(8,128)(2,1)} %all-gather.7.cloned.1.call-done.xg_ref.refs_0_, bf16[2048,1664]{1,0:T(8,128)(2,1)} %all-gather.11.cloned.1.call-done.xg_ref.refs_1_, bf16[2048,2048]{1,0:T(8,128)(2,1)} %get-tuple-element.485.refs_2_, bf16[2048,2048]{1,0:T(8,128)(2,1)} %get-tuple-element.486.refs_3_), custom_call_target="tpu_custom_call" | custom-call | flops 644245120 | bytes 1835008 | tf_op jit(solution)/shard_map/wide_grad/pallas_call | solution.py:580
  419.1 15.6 %attend_back.2 = (bf16[256,1536]{1,0:T(8,128)(2,1)}, bf16[4,2,256,512]{3,2,1,0:T(8,128)(2,1)}) custom-call(s32[2]{0:T(128)} %pad_add_fusion.info_ref, bf16[1536,512]{1,0:T(8,128)(2,1)} %q_project.1.q_ref, bf16[1536,256]{1,0:T(8,128)(2,1)} %get-tuple-element.646.g_ref, bf16[1536,256]{1,0:T(8,128)(2,1)} %get-tuple-element.431.o_ref.refs_0_, ...), custom_call_target="tpu_custom_call" | custom-call | flops 1610612736 | bytes 734003 | tf_op jit(solution)/shard_map/attend_back/pallas_call | solution.py:349
  455.2 15.6 %attend_back.3 = (bf16[256,1536]{1,0:T(8,128)(2,1)}, bf16[4,2,256,512]{3,2,1,0:T(8,128)(2,1)}) custom-call(s32[2]{0:T(128)} %pad_add_fusion.1.info_ref, bf16[1536,512]{1,0:T(8,128)(2,1)} %q_project.1.q_ref, bf16[1536,256]{1,0:T(8,128)(2,1)} %get-tuple-element.655.g_ref, bf16[1536,256]{1,0:T(8,128)(2,1)} %get-tuple-element.459.refs_1_.o_ref, ...), custom_call_target="tpu_custom_call" | custom-call | flops 1610612736 | bytes 734003 | tf_op jit(solution)/shard_map/attend_back/pallas_call | solution.py:349
  480.4 14.2 %wide_grad.5 = bf16[1536,512]{1,0:T(8,128)(2,1)} custom-call(bf16[2048,1664]{1,0:T(8,128)(2,1)} %all-gather.7.cloned.1.call-done.xg_ref.refs_0_, bf16[2048,1664]{1,0:T(8,128)(2,1)} %all-gather.11.cloned.1.call-done.xg_ref.refs_1_, bf16[2048,2048]{1,0:T(8,128)(2,1)} %get-tuple-element.485.refs_2_, bf16[2048,2048]{1,0:T(8,128)(2,1)} %get-tuple-element.486.refs_3_), custom_call_target="tpu_custom_call" | custom-call | flops 644245120 | bytes 1835008 | tf_op jit(solution)/shard_map/wide_grad/pallas_call | solution.py:580
  494.5 18.4 %collective-permute-done.23 = bf16[1536,512]{1,0:T(8,128)(2,1)} collective-permute-done((bf16[1536,512]{1,0:T(8,128)(2,1)S(1)}, bf16[1536,512]{1,0:T(8,128)(2,1)}, u32[]{:S(2)}, u32[]{:S(2)}) %collective-permute-start.23) | collective-permute-done | bytes 1572896 | tf_op jit(solution)/shard_map/ppermute | solution.py:942
  552.2 14.2 %wide_grad.7 = bf16[1536,512]{1,0:T(8,128)(2,1)} custom-call(bf16[2048,1664]{1,0:T(8,128)(2,1)} %all-gather.7.cloned.1.call-done.xg_ref.refs_0_, bf16[2048,1664]{1,0:T(8,128)(2,1)} %all-gather.11.cloned.1.call-done.xg_ref.refs_1_, bf16[2048,2048]{1,0:T(8,128)(2,1)} %get-tuple-element.485.refs_2_, bf16[2048,2048]{1,0:T(8,128)(2,1)} %get-tuple-element.486.refs_3_), custom_call_target="tpu_custom_call" | custom-call | flops 644245120 | bytes 1835008 | tf_op jit(solution)/shard_map/wide_grad/pallas_call | solution.py:580
  566.4 14.1 %wide_grad.6 = bf16[1536,512]{1,0:T(8,128)(2,1)} custom-call(bf16[2048,1664]{1,0:T(8,128)(2,1)} %all-gather.7.cloned.1.call-done.xg_ref.refs_0_, bf16[2048,1664]{1,0:T(8,128)(2,1)} %all-gather.11.cloned.1.call-done.xg_ref.refs_1_, bf16[2048,2048]{1,0:T(8,128)(2,1)} %get-tuple-element.485.refs_2_, bf16[2048,2048]{1,0:T(8,128)(2,1)} %get-tuple-element.486.refs_3_), custom_call_target="tpu_custom_call" | custom-call | flops 644245120 | bytes 1835008 | tf_op jit(solution)/shard_map/wide_grad/pallas_call | solution.py:580
  580.6 17.1 %collective-permute-done.27 = bf16[1536,512]{1,0:T(8,128)(2,1)} collective-permute-done((bf16[1536,512]{1,0:T(8,128)(2,1)S(1)}, bf16[1536,512]{1,0:T(8,128)(2,1)}, u32[]{:S(2)}, u32[]{:S(2)}) %collective-permute-start.27) | collective-permute-done | bytes 1572896 | tf_op jit(solution)/shard_map/ppermute | solution.py:942
  617.9 11.6 %projection_grads.1 = bf16[1536,2688]{1,0:T(8,128)(2,1)} custom-call(bf16[512,1536]{1,0:T(8,128)(2,1)} %get-tuple-element.366.normed_ref, bf16[256,1536]{1,0:T(8,128)(2,1)} %get-tuple-element.647.gq_ref.refs_0_, bf16[256,1536]{1,0:T(8,128)(2,1)} %get-tuple-element.656.gq_ref.refs_1_, bf16[256,1024]{1,0:T(8,128)(2,1)} %turn_back.2.dkv_ref.refs_2_, ...), custom_call_target="tpu_custom_call" | custom-call | flops 422785856 | bytes 1258291 | tf_op jit(solution)/shard_map/projection_grads/pallas_call | solution.py:875
  650.0 20.2 %collective-permute-done.36 = bf16[192,1536]{1,0:T(8,128)(2,1)S(1)} collective-permute-done((bf16[192,1536]{1,0:T(8,128)(2,1)S(1)}, bf16[192,1536]{1,0:T(8,128)(2,1)S(1)}, u32[]{:S(2)}, u32[]{:S(2)}) %collective-permute-start.36) | collective-permute-done | bytes 589856 | tf_op jit(solution)/shard_map/ppermute | solution.py:961
  678.8 25.1 %collective-permute-done.32 = bf16[1536,512]{1,0:T(8,128)(2,1)S(1)} collective-permute-done((bf16[1536,512]{1,0:T(8,128)(2,1)S(1)}, bf16[1536,512]{1,0:T(8,128)(2,1)S(1)}, u32[]{:S(2)}, u32[]{:S(2)}) %collective-permute-start.32) | collective-permute-done | bytes 1572896 | tf_op jit(solution)/shard_map/ppermute | solution.py:942
  720.6 20.7 %collective-permute-done.38 = bf16[1536,512]{1,0:T(8,128)(2,1)} collective-permute-done((bf16[1536,512]{1,0:T(8,128)(2,1)S(1)}, bf16[1536,512]{1,0:T(8,128)(2,1)}, u32[]{:S(2)}, u32[]{:S(2)}) %collective-permute-start.38) | collective-permute-done | bytes 1572896 | tf_op jit(solution)/shard_map/ppermute | solution.py:942
  756.8 24.1 %collective-permute-done.44 = bf16[1536,512]{1,0:T(8,128)(2,1)S(1)} collective-permute-done((bf16[1536,512]{1,0:T(8,128)(2,1)S(1)}, bf16[1536,512]{1,0:T(8,128)(2,1)S(1)}, u32[]{:S(2)}, u32[]{:S(2)}) %collective-permute-start.44) | collective-permute-done | bytes 1572896 | tf_op jit(solution)/shard_map/ppermute | solution.py:947
  792.1 50.6 %collective-permute-done.46 = bf16[1536,512]{1,0:T(8,128)(2,1)} collective-permute-done((bf16[1536,512]{1,0:T(8,128)(2,1)S(1)}, bf16[1536,512]{1,0:T(8,128)(2,1)}, u32[]{:S(2)}, u32[]{:S(2)}) %collective-permute-start.46) | collective-permute-done | bytes 1572896 | tf_op jit(solution)/shard_map/ppermute | solution.py:947
  (361 shorter events, 361.2 us)
Async XLA Ops:
  7.2 93.7 %all-gather.5.cloned.1.call-start = ((), (), s32[]{:S(2)}) async-start(), calls=%async_computation.5 | async-start | bytes 2621440 | tf_op jit(solution)/shard_map/all_gather | solution.py:1163
  55.1 138.1 %all-gather.9.cloned.1.call-start = ((), (), s32[]{:S(2)}) async-start(), calls=%async_computation.7 | async-start | bytes 2621440 | tf_op jit(solution)/shard_map/all_gather | solution.py:1163
  107.0 121.0 %all-gather.7.cloned.1.call-start = ((), (), s32[]{:S(2)}) async-start(), calls=%async_computation.6 | async-start | bytes 7667712 | tf_op jit(solution)/shard_map/all_gather | solution.py:965
  152.1 128.0 %all-gather.11.cloned.1.call-start = ((), (), s32[]{:S(2)}) async-start(), calls=%async_computation.8 | async-start | bytes 7667712 | tf_op jit(solution)/shard_map/all_gather | solution.py:965
  212.9 156.2 %reduce-scatter.6.cloned.1.call-start = ((), (), s32[]{:S(2)}) async-start(), calls=%async_computation.9 | async-start | bytes 7667712 | tf_op jit(solution)/shard_map/reduce_scatter | solution.py:1092
  279.7 166.9 %reduce-scatter.8.cloned.1.call-start = ((), (), s32[]{:S(2)}) async-start(), calls=%async_computation.10 | async-start | bytes 7667712 | tf_op jit(solution)/shard_map/reduce_scatter | solution.py:1092
  331.0 191.9 %reduce-scatter.10.cloned.1.call-start = ((), (), s32[]{:S(2)}) async-start(), calls=%async_computation.11 | async-start | bytes 2621440 | tf_op jit(solution)/shard_map/reduce_scatter | solution.py:1231
  389.0 45.7 %collective-permute-start.22 = (bf16[1536,512]{1,0:T(8,128)(2,1)S(1)}, bf16[1536,512]{1,0:T(8,128)(2,1)S(1)}, u32[]{:S(2)}, u32[]{:S(2)}) collective-permute-start(bf16[1536,512]{1,0:T(8,128)(2,1)S(1)} %add_convert_fusion.14), channel_id=1, source_target_pairs={{8,16},{16,8},{9,17},{17,9},{10,18},{18,10},{11,19},{19,11},{12,20... | collective-permute-start | bytes 4718600 | tf_op jit(solution)/shard_map/ppermute | solution.py:939
  389.7 47.1 %collective-permute-start.21 = (bf16[1536,512]{1,0:T(8,128)(2,1)}, bf16[1536,512]{1,0:T(8,128)(2,1)}, u32[]{:S(2)}, u32[]{:S(2)}) collective-permute-start(bf16[1536,512]{1,0:T(8,128)(2,1)} %down_grad.3), channel_id=1, source_target_pairs={{0,8},{24,16},{1,9},{25,17},{2,10},{26,18},{3,11},{27,19},{4,12},{... | collective-permute-start | bytes 4718600 | tf_op jit(solution)/shard_map/ppermute | solution.py:949
  436.8 76.2 %collective-permute-start.25 = (bf16[1024,1536]{1,0:T(8,128)(2,1)}, bf16[1024,1536]{1,0:T(8,128)(2,1)}, u32[]{:S(2)}, u32[]{:S(2)}) collective-permute-start(bf16[1024,1536]{1,0:T(8,128)(2,1)} %get-tuple-element.480), channel_id=1, source_target_pairs={{0,1},{1,0},{2,3},{3,2},{4,5},{5,4},{6,7},{7,6},{8,9},{9,8},{10,11... | collective-permute-start | bytes 9437192 | tf_op jit(solution)/shard_map/ppermute | solution.py:961
  436.8 81.7 %collective-permute-start.26 = (bf16[1024,1536]{1,0:T(8,128)(2,1)}, bf16[1024,1536]{1,0:T(8,128)(2,1)}, u32[]{:S(2)}, u32[]{:S(2)}) collective-permute-start(bf16[1024,1536]{1,0:T(8,128)(2,1)} %get-tuple-element.482), channel_id=1, source_target_pairs={{0,1},{1,0},{2,3},{3,2},{4,5},{5,4},{6,7},{7,6},{8,9},{9,8},{10,11... | collective-permute-start | bytes 9437192 | tf_op jit(solution)/shard_map/ppermute | solution.py:961
  437.4 168.9 %reduce-scatter.12.cloned.1.call-start = ((), (), s32[]{:S(2)}) async-start(), calls=%async_computation.12 | async-start | bytes 2621440 | tf_op jit(solution)/shard_map/reduce_scatter | solution.py:1231
  441.1 53.5 %collective-permute-start.24 = (bf16[1536,512]{1,0:T(8,128)(2,1)}, bf16[1536,512]{1,0:T(8,128)(2,1)}, u32[]{:S(2)}, u32[]{:S(2)}) collective-permute-start(bf16[1536,512]{1,0:T(8,128)(2,1)} %add_convert_fusion.12), channel_id=1, source_target_pairs={{8,16},{16,8},{9,17},{17,9},{10,18},{18,10},{11,19},{19,11},{12,20... | collective-permute-start | bytes 4718600 | tf_op jit(solution)/shard_map/ppermute | solution.py:939
  443.6 69.4 %collective-permute-start.23 = (bf16[1536,512]{1,0:T(8,128)(2,1)S(1)}, bf16[1536,512]{1,0:T(8,128)(2,1)}, u32[]{:S(2)}, u32[]{:S(2)}) collective-permute-start(bf16[1536,512]{1,0:T(8,128)(2,1)S(1)} %fusion), channel_id=1, source_target_pairs={{0,8},{24,16},{8,0},{16,24},{1,9},{25,17},{9,1},{17,25},{2,10},{26... | collective-permute-start | bytes 4718600 | tf_op jit(solution)/shard_map/ppermute | solution.py:942
  522.9 218.3 %reduce-scatter.14.cloned.1.call-start = ((), (), s32[]{:S(2)}) async-start(), calls=%async_computation.13 | async-start | bytes 9289728 | tf_op jit(solution)/shard_map/reduce_scatter | solution.py:1092
  526.7 70.9 %collective-permute-start.29 = (bf16[512,1536]{1,0:T(8,128)(2,1)}, bf16[512,1536]{1,0:T(8,128)(2,1)}, u32[]{:S(2)}, u32[]{:S(2)}) collective-permute-start(bf16[512,1536]{1,0:T(8,128)(2,1)} %pad_maximum_fusion), channel_id=1, source_target_pairs={{0,4},{1,5},{2,6},{3,7},{4,0},{5,1},{6,2},{7,3},{8,12},{9,13},{10,... | collective-permute-start | bytes 4718600 | tf_op jit(solution)/shard_map/ppermute | solution.py:961
  529.9 50.6 %collective-permute-start.28 = (bf16[1536,512]{1,0:T(8,128)(2,1)}, bf16[1536,512]{1,0:T(8,128)(2,1)}, u32[]{:S(2)}, u32[]{:S(2)}) collective-permute-start(bf16[1536,512]{1,0:T(8,128)(2,1)} %add_convert_fusion.10), channel_id=1, source_target_pairs={{8,16},{16,8},{9,17},{17,9},{10,18},{18,10},{11,19},{19,11},{12,20... | collective-permute-start | bytes 4718600 | tf_op jit(solution)/shard_map/ppermute | solution.py:939
  534.2 63.4 %collective-permute-start.27 = (bf16[1536,512]{1,0:T(8,128)(2,1)S(1)}, bf16[1536,512]{1,0:T(8,128)(2,1)}, u32[]{:S(2)}, u32[]{:S(2)}) collective-permute-start(bf16[1536,512]{1,0:T(8,128)(2,1)S(1)} %fusion.1), channel_id=1, source_target_pairs={{0,8},{24,16},{8,0},{16,24},{1,9},{25,17},{9,1},{17,25},{2,10},{26... | collective-permute-start | bytes 4718600 | tf_op jit(solution)/shard_map/ppermute | solution.py:942
  537.4 65.1 %collective-permute-start.31 = (bf16[768,1536]{1,0:T(8,128)(2,1)}, bf16[768,1536]{1,0:T(8,128)(2,1)}, u32[]{:S(2)}, u32[]{:S(2)}) collective-permute-start(bf16[768,1536]{1,0:T(8,128)(2,1)} %get-tuple-element.519), channel_id=1, source_target_pairs={{0,1},{1,0},{2,3},{3,2},{4,5},{5,4},{6,7},{7,6},{8,9},{9,8},{10,11... | collective-permute-start | bytes 7077896 | tf_op jit(solution)/shard_map/ppermute | solution.py:961
  538.6 59.0 %collective-permute-start.30 = (bf16[512,1536]{1,0:T(8,128)(2,1)}, bf16[512,1536]{1,0:T(8,128)(2,1)}, u32[]{:S(2)}, u32[]{:S(2)}) collective-permute-start(bf16[512,1536]{1,0:T(8,128)(2,1)} %pad_maximum_fusion.1), channel_id=1, source_target_pairs={{0,2},{1,3},{2,0},{3,1},{4,6},{5,7},{6,4},{7,5},{8,10},{9,11},{10,... | collective-permute-start | bytes 4718600 | tf_op jit(solution)/shard_map/ppermute | solution.py:961
  629.5 221.3 %all-reduce.3.cloned.1.call-start = ((), (), s32[]{:S(2)}) async-start(), calls=%async_computation.14 | async-start | bytes 2064384 | tf_op jit(solution)/shard_map/psum | solution.py:1281
  630.9 44.9 %collective-permute-start.35 = (bf16[256,1536]{1,0:T(8,128)(2,1)S(1)}, bf16[256,1536]{1,0:T(8,128)(2,1)S(1)}, u32[]{:S(2)}, u32[]{:S(2)}) collective-permute-start(bf16[256,1536]{1,0:T(8,128)(2,1)S(1)} %pad_maximum_fusion.10), channel_id=1, source_target_pairs={{0,4},{1,5},{2,6},{3,7},{4,0},{5,1},{6,2},{7,3},{8,12},{9,13},{10,... | collective-permute-start | bytes 2359304 | tf_op jit(solution)/shard_map/ppermute | solution.py:961
  633.6 42.4 %collective-permute-start.34 = (bf16[256,1536]{1,0:T(8,128)(2,1)S(1)}, bf16[256,1536]{1,0:T(8,128)(2,1)S(1)}, u32[]{:S(2)}, u32[]{:S(2)}) collective-permute-start(bf16[256,1536]{1,0:T(8,128)(2,1)S(1)} %pad_maximum_fusion.9), channel_id=1, source_target_pairs={{0,2},{1,3},{2,0},{3,1},{4,6},{5,7},{6,4},{7,5},{8,10},{9,11},{10,... | collective-permute-start | bytes 2359304 | tf_op jit(solution)/shard_map/ppermute | solution.py:961
  782.1 60.6 %collective-permute-start.46 = (bf16[1536,512]{1,0:T(8,128)(2,1)S(1)}, bf16[1536,512]{1,0:T(8,128)(2,1)}, u32[]{:S(2)}, u32[]{:S(2)}) collective-permute-start(bf16[1536,512]{1,0:T(8,128)(2,1)S(1)} %add_convert_fusion.3), channel_id=1, source_target_pairs={{8,0},{16,24},{9,1},{17,25},{10,2},{18,26},{11,3},{19,27},{12,4},{... | collective-permute-start | bytes 4718600 | tf_op jit(solution)/shard_map/ppermute | solution.py:947
  (100 other events, 1164.9 us)
Sparse Core Ops, SparseCore 0:
  55.2 45.6 all-gather.4
  107.1 44.8 all-gather.8
  154.5 57.8 all-gather.6
  214.6 56.1 all-gather.10
  279.8 73.5 reduce-scatter.5
  357.1 64.2 reduce-scatter.7
  437.5 73.4 reduce-scatter.9
  523.0 67.7 reduce-scatter.11
  629.6 78.3 reduce-scatter.13
  783.7 67.1 all-reduce.2

commit v4 on v3

--- a/solution.py
+++ b/solution.py
@@ -1299,9 +1299,9 @@
             )
         if t == 4:
             rest = scatter_rows(rest_grads())
-        if t in (2, 3, 4):
+        if t in (5, 6, 7):
             moe.advance()
-        if t in (3, 4, 5):
+        for _ in range(3 if t == 3 else 0):
             heads.advance()
         line.step(sent, (chunks, found))
     rest = found[0]["rest"].astype(F32)

time: 899 us -> 880 us (0.979)
  waiting for transfers between devices: 314 us -> 297 us
    ppermute x3, waiting for transfers between devices: 83.2 us -> 69.2 us  [step(): self.results.append((summed, lax.ppermute(summed, 'seq', go)))]
    unnamed x136 -> x132, local copies, waits for them, and re-layouts: 19.5 us -> 19 us
where the time goes in v4:
time: 880 us; the launch traced here: 869 us
  Pallas kernels  355 us (40%)
  waiting for transfers between devices  297 us (34%)
  starting transfers between devices  87.4 us (10%)
  other arithmetic  83.5 us (9%)
  local copies, waits for them, and re-layouts  30 us (3%)
  between operations  15.3 us (2%)
    ppermute x31, waiting for transfers between devices, swap(): return lax.ppermute(x, 'fsdp', [(i, i ^ mask) for i in range(8)])  129 us
    pallas_call x2, Pallas kernels, run_experts(): pl.pallas_call(functools.partial(expert_kernel, experts, half), name='run...  102 us
    ppermute x4, waiting for transfers between devices, step(): got = lax.ppermute(sent, 'seq', come + go)  75 us
    ppermute x3, waiting for transfers between devices, step(): self.results.append((summed, lax.ppermute(summed, 'seq', go)))  69.2 us
    pallas_call x4, Pallas kernels, wide_grad(): pl.pallas_call(functools.partial(wide_grad_kernel, steps, micros), name='...  56.8 us
    ppermute x31, starting transfers between devices, swap(): return lax.ppermute(x, 'fsdp', [(i, i ^ mask) for i in range(8)])  34.3 us
    convert_element_type x19, other arithmetic, add_low(): return (a.astype(F32) + b.astype(F32)).astype(BF)  34.2 us
    pallas_call x2, Pallas kernels, attend_back(): pl.pallas_call(functools.partial(attend_back_kernel, n), name='attend_bac...  31.1 us
  transfers between devices with their start and end apart: 58, of which 31 were waited for; matrix products, arithmetic and copies ran while one was open for 10% of the time, Pallas kernels for 36%

profile of v4, /device:TPU:0, one launch (start us, length us, event | category | flops | bytes accessed | tf_op | source)
XLA Modules:
  0.0 868.6 jit_solution(6613724763905177806)
XLA Ops:
  55.2 11.8 %collective-permute-done.6.low_y_ref = bf16[96,3072]{1,0:T(8,128)(2,1)S(1)} collective-permute-done((bf16[96,3072]{1,0:T(8,128)(2,1)S(1)}, bf16[96,3072]{1,0:T(8,128)(2,1)S(1)}, u32[]{:S(2)}, u32[]{:S(2)}) %collective-permute-start.6) | collective-permute-done | bytes 589856 | tf_op jit(solution)/shard_map/ppermute | solution.py:961
  71.2 24.6 %collective-permute-done.7.top_far_ref = bf16[192,3072]{1,0:T(8,128)(2,1)S(1)} collective-permute-done((bf16[192,3072]{1,0:T(8,128)(2,1)S(1)}, bf16[192,3072]{1,0:T(8,128)(2,1)S(1)}, u32[]{:S(2)}, u32[]{:S(2)}) %collective-permute-start.7) | collective-permute-done | bytes 1179680 | tf_op jit(solution)/shard_map/ppermute | solution.py:961
  132.0 12.7 %attend.2 = (bf16[256,1536]{1,0:T(8,128)(2,1)}, bf16[1536,256]{1,0:T(8,128)(2,1)}, f32[32,768]{1,0:T(8,128)}) custom-call(s32[2]{0:T(128)} %pad_add_fusion.info_ref, bf16[1536,512]{1,0:T(8,128)(2,1)} %q_project.1.q_ref, bf16[4,256,1024]{2,1,0:T(8,128)(2,1)} %bitcast.77, bf16[4,256,1024]{2,1,0:T(8,128)(2,1)} %bitcast.78), custom_call_target="tpu_custom_call" | custom-call | flops 644245120 | bytes 445644 | tf_op jit(solution)/shard_map/attend/pallas_call | solution.py:249
  167.4 23.7 %collective-permute-done.16.top_far_ref = bf16[256,1536]{1,0:T(8,128)(2,1)S(1)} collective-permute-done((bf16[256,1536]{1,0:T(8,128)(2,1)S(1)}, bf16[256,1536]{1,0:T(8,128)(2,1)S(1)}, u32[]{:S(2)}, u32[]{:S(2)}) %collective-permute-start.16) | collective-permute-done | bytes 786464 | tf_op jit(solution)/shard_map/ppermute | solution.py:961
  193.2 12.7 %attend.3 = (bf16[256,1536]{1,0:T(8,128)(2,1)}, bf16[1536,256]{1,0:T(8,128)(2,1)}, f32[32,768]{1,0:T(8,128)}) custom-call(s32[2]{0:T(128)} %pad_add_fusion.1.info_ref, bf16[1536,512]{1,0:T(8,128)(2,1)} %q_project.1.q_ref, bf16[4,256,1024]{2,1,0:T(8,128)(2,1)} %bitcast.73, bf16[4,256,1024]{2,1,0:T(8,128)(2,1)} %bitcast.74), custom_call_target="tpu_custom_call" | custom-call | flops 644245120 | bytes 445644 | tf_op jit(solution)/shard_map/attend/pallas_call | solution.py:249
  227.9 51.3 %run_experts.2 = (bf16[1024,1536]{1,0:T(8,128)(2,1)}, bf16[1024,1536]{1,0:T(8,128)(2,1)}, bf16[2048,1664]{1,0:T(8,128)(2,1)}, bf16[2048,1024]{1,0:T(8,128)(2,1)}, bf16[2048,2048]{1,0:T(8,128)(2,1)}) custom-call(s32[1]{0:T(128)} %bitcast.12.own_ref, s32[8]{0:T(128)} %fusion.10.order_ref, bf16[2048,1664]{1,0:T(8,128)(2,1)} %all-gather.7.cloned.1.call-done.xg_ref.refs_0_, ...), custom_call_target="tpu_custom_call" | custom-call | flops 3865470464 | bytes 4718592 | tf_op jit(solution)/shard_map/run_experts/pallas_call | solution.py:507
  279.7 50.8 %run_experts.3 = (bf16[1024,1536]{1,0:T(8,128)(2,1)}, bf16[1024,1536]{1,0:T(8,128)(2,1)}, bf16[2048,1664]{1,0:T(8,128)(2,1)}, bf16[2048,1024]{1,0:T(8,128)(2,1)}, bf16[2048,2048]{1,0:T(8,128)(2,1)}) custom-call(s32[1]{0:T(128)} %bitcast.12.own_ref, s32[8]{0:T(128)} %fusion.10.order_ref, bf16[2048,1664]{1,0:T(8,128)(2,1)} %all-gather.11.cloned.1.call-done.xg_ref.refs_1_, ...), custom_call_target="tpu_custom_call" | custom-call | flops 3865470464 | bytes 4718592 | tf_op jit(solution)/shard_map/run_experts/pallas_call | solution.py:507
  330.5 14.6 %down_grad.2 = bf16[1536,512]{1,0:T(8,128)(2,1)} custom-call(bf16[2048,1024]{1,0:T(8,128)(2,1)} %get-tuple-element.407.refs_0_, bf16[2048,1024]{1,0:T(8,128)(2,1)} %get-tuple-element.408.refs_1_, bf16[1024,1536]{1,0:T(8,128)(2,1)} %assemble.6.ga_ref.refs_2_, bf16[1024,1536]{1,0:T(8,128)(2,1)} %assemble.7.ga_ref.refs_3_, bf16[1024,1536]{1,0:T(8,128)(2,1)} %copy-done.1, ...), custom_call_target="tpu_custom_call" | custom-call | flops 644245120 | bytes 1677721 | tf_op jit(solution)/shard_map/down_grad/pallas_call | solution.py:622
  353.5 15.0 %down_grad.3 = bf16[1536,512]{1,0:T(8,128)(2,1)} custom-call(bf16[2048,1024]{1,0:T(8,128)(2,1)} %get-tuple-element.407.refs_0_, bf16[2048,1024]{1,0:T(8,128)(2,1)} %get-tuple-element.408.refs_1_, bf16[1024,1536]{1,0:T(8,128)(2,1)} %assemble.6.ga_ref.refs_2_, bf16[1024,1536]{1,0:T(8,128)(2,1)} %assemble.7.ga_ref.refs_3_, bf16[1024,1536]{1,0:T(8,128)(2,1)} %copy-done.1, ...), custom_call_target="tpu_custom_call" | custom-call | flops 644245120 | bytes 1677721 | tf_op jit(solution)/shard_map/down_grad/pallas_call | solution.py:622
  393.2 13.8 %collective-permute-start.21 = (bf16[1536,512]{1,0:T(8,128)(2,1)S(1)}, bf16[1536,512]{1,0:T(8,128)(2,1)}, u32[]{:S(2)}, u32[]{:S(2)}) collective-permute-start(bf16[1536,512]{1,0:T(8,128)(2,1)S(1)} %copy-done.28), channel_id=1, source_target_pairs={{0,8},{24,16},{1,9},{25,17},{2,10},{26,18},{3,11},{27,19},{4,12},{... | collective-permute-start | bytes 4718600 | tf_op jit(solution)/shard_map/ppermute | solution.py:949
  407.0 14.4 %wide_grad.4 = bf16[1536,512]{1,0:T(8,128)(2,1)} custom-call(bf16[2048,1664]{1,0:T(8,128)(2,1)} %all-gather.7.cloned.1.call-done.xg_ref.refs_0_, bf16[2048,1664]{1,0:T(8,128)(2,1)} %all-gather.11.cloned.1.call-done.xg_ref.refs_1_, bf16[2048,2048]{1,0:T(8,128)(2,1)} %get-tuple-element.488.refs_2_, bf16[2048,2048]{1,0:T(8,128)(2,1)} %get-tuple-element.489.refs_3_), custom_call_target="tpu_custom_call" | custom-call | flops 644245120 | bytes 1835008 | tf_op jit(solution)/shard_map/wide_grad/pallas_call | solution.py:580
  421.5 15.5 %attend_back.2 = (bf16[256,1536]{1,0:T(8,128)(2,1)}, bf16[4,2,256,512]{3,2,1,0:T(8,128)(2,1)}) custom-call(s32[2]{0:T(128)} %pad_add_fusion.info_ref, bf16[1536,512]{1,0:T(8,128)(2,1)} %q_project.1.q_ref, bf16[1536,256]{1,0:T(8,128)(2,1)} %get-tuple-element.646.g_ref, bf16[1536,256]{1,0:T(8,128)(2,1)} %get-tuple-element.434.o_ref.refs_0_, ...), custom_call_target="tpu_custom_call" | custom-call | flops 1610612736 | bytes 734003 | tf_op jit(solution)/shard_map/attend_back/pallas_call | solution.py:349
  458.4 15.6 %attend_back.3 = (bf16[256,1536]{1,0:T(8,128)(2,1)}, bf16[4,2,256,512]{3,2,1,0:T(8,128)(2,1)}) custom-call(s32[2]{0:T(128)} %pad_add_fusion.1.info_ref, bf16[1536,512]{1,0:T(8,128)(2,1)} %q_project.1.q_ref, bf16[1536,256]{1,0:T(8,128)(2,1)} %get-tuple-element.655.g_ref, bf16[1536,256]{1,0:T(8,128)(2,1)} %get-tuple-element.462.refs_1_.o_ref, ...), custom_call_target="tpu_custom_call" | custom-call | flops 1610612736 | bytes 734003 | tf_op jit(solution)/shard_map/attend_back/pallas_call | solution.py:349
  483.5 14.1 %wide_grad.5 = bf16[1536,512]{1,0:T(8,128)(2,1)} custom-call(bf16[2048,1664]{1,0:T(8,128)(2,1)} %all-gather.7.cloned.1.call-done.xg_ref.refs_0_, bf16[2048,1664]{1,0:T(8,128)(2,1)} %all-gather.11.cloned.1.call-done.xg_ref.refs_1_, bf16[2048,2048]{1,0:T(8,128)(2,1)} %get-tuple-element.488.refs_2_, bf16[2048,2048]{1,0:T(8,128)(2,1)} %get-tuple-element.489.refs_3_), custom_call_target="tpu_custom_call" | custom-call | flops 644245120 | bytes 1835008 | tf_op jit(solution)/shard_map/wide_grad/pallas_call | solution.py:580
  497.6 19.1 %collective-permute-done.23 = bf16[1536,512]{1,0:T(8,128)(2,1)} collective-permute-done((bf16[1536,512]{1,0:T(8,128)(2,1)S(1)}, bf16[1536,512]{1,0:T(8,128)(2,1)}, u32[]{:S(2)}, u32[]{:S(2)}) %collective-permute-start.23) | collective-permute-done | bytes 1572896 | tf_op jit(solution)/shard_map/ppermute | solution.py:942
  558.3 10.0 %last_step.2 = (bf16[256,1536]{1,0:T(8,128)(2,1)}, f32[8,1536]{1,0:T(8,128)}) custom-call(s32[8]{0:T(128)} %multiply_add_fusion.place_ref, bf16[256,1536]{1,0:T(8,128)(2,1)} %get-tuple-element.647.gq_ref.refs_0_, bf16[256,1024]{1,0:T(8,128)(2,1)} %turn_back.2.dkv_ref.refs_2_, bf16[4,192,3072]{2,1,0:T(8,128)(2,1)} %bitcast.62, ...), custom_call_target="tpu_custom_call" | custom-call | flops 201326592 | bytes 1258291 | tf_op jit(solution)/shard_map/last_step/pallas_call | solution.py:759
  568.3 14.1 %wide_grad.7 = bf16[1536,512]{1,0:T(8,128)(2,1)} custom-call(bf16[2048,1664]{1,0:T(8,128)(2,1)} %all-gather.7.cloned.1.call-done.xg_ref.refs_0_, bf16[2048,1664]{1,0:T(8,128)(2,1)} %all-gather.11.cloned.1.call-done.xg_ref.refs_1_, bf16[2048,2048]{1,0:T(8,128)(2,1)} %get-tuple-element.488.refs_2_, bf16[2048,2048]{1,0:T(8,128)(2,1)} %get-tuple-element.489.refs_3_), custom_call_target="tpu_custom_call" | custom-call | flops 644245120 | bytes 1835008 | tf_op jit(solution)/shard_map/wide_grad/pallas_call | solution.py:580
  582.4 14.1 %wide_grad.6 = bf16[1536,512]{1,0:T(8,128)(2,1)} custom-call(bf16[2048,1664]{1,0:T(8,128)(2,1)} %all-gather.7.cloned.1.call-done.xg_ref.refs_0_, bf16[2048,1664]{1,0:T(8,128)(2,1)} %all-gather.11.cloned.1.call-done.xg_ref.refs_1_, bf16[2048,2048]{1,0:T(8,128)(2,1)} %get-tuple-element.488.refs_2_, bf16[2048,2048]{1,0:T(8,128)(2,1)} %get-tuple-element.489.refs_3_), custom_call_target="tpu_custom_call" | custom-call | flops 644245120 | bytes 1835008 | tf_op jit(solution)/shard_map/wide_grad/pallas_call | solution.py:580
  610.4 11.4 %projection_grads.1 = bf16[1536,2688]{1,0:T(8,128)(2,1)} custom-call(bf16[512,1536]{1,0:T(8,128)(2,1)} %get-tuple-element.369.normed_ref, bf16[256,1536]{1,0:T(8,128)(2,1)} %get-tuple-element.647.gq_ref.refs_0_, bf16[256,1536]{1,0:T(8,128)(2,1)} %get-tuple-element.656.gq_ref.refs_1_, bf16[256,1024]{1,0:T(8,128)(2,1)} %turn_back.2.dkv_ref.refs_2_, ...), custom_call_target="tpu_custom_call" | custom-call | flops 422785856 | bytes 1258291 | tf_op jit(solution)/shard_map/projection_grads/pallas_call | solution.py:875
  637.8 27.7 %collective-permute-done.32 = bf16[1536,512]{1,0:T(8,128)(2,1)S(1)} collective-permute-done((bf16[1536,512]{1,0:T(8,128)(2,1)S(1)}, bf16[1536,512]{1,0:T(8,128)(2,1)S(1)}, u32[]{:S(2)}, u32[]{:S(2)}) %collective-permute-start.32) | collective-permute-done | bytes 1572896 | tf_op jit(solution)/shard_map/ppermute | solution.py:942
  678.7 28.1 %collective-permute-done.34 = bf16[1536,512]{1,0:T(8,128)(2,1)} collective-permute-done((bf16[1536,512]{1,0:T(8,128)(2,1)S(1)}, bf16[1536,512]{1,0:T(8,128)(2,1)}, u32[]{:S(2)}, u32[]{:S(2)}) %collective-permute-start.34) | collective-permute-done | bytes 1572896 | tf_op jit(solution)/shard_map/ppermute | solution.py:942
  744.9 46.9 %collective-permute-done.40 = bf16[1536,512]{1,0:T(8,128)(2,1)S(1)} collective-permute-done((bf16[1536,512]{1,0:T(8,128)(2,1)S(1)}, bf16[1536,512]{1,0:T(8,128)(2,1)S(1)}, u32[]{:S(2)}, u32[]{:S(2)}) %collective-permute-start.40) | collective-permute-done | bytes 1572896 | tf_op jit(solution)/shard_map/ppermute | solution.py:947
  800.9 11.6 %collective-permute-done.46 = bf16[256,1536]{1,0:T(8,128)(2,1)S(1)} collective-permute-done((bf16[256,1536]{1,0:T(8,128)(2,1)S(1)}, bf16[256,1536]{1,0:T(8,128)(2,1)S(1)}, u32[]{:S(2)}, u32[]{:S(2)}) %collective-permute-start.46) | collective-permute-done | bytes 786464 | tf_op jit(solution)/shard_map/ppermute | solution.py:961
  816.9 18.3 %collective-permute-done.44 = bf16[1536,512]{1,0:T(8,128)(2,1)} collective-permute-done((bf16[1536,512]{1,0:T(8,128)(2,1)S(1)}, bf16[1536,512]{1,0:T(8,128)(2,1)}, u32[]{:S(2)}, u32[]{:S(2)}) %collective-permute-start.44) | collective-permute-done | bytes 1572896 | tf_op jit(solution)/shard_map/ppermute | solution.py:947
  (357 shorter events, 361.3 us)
Async XLA Ops:
  7.2 93.7 %all-gather.5.cloned.1.call-start = ((), (), s32[]{:S(2)}) async-start(), calls=%async_computation.5 | async-start | bytes 2621440 | tf_op jit(solution)/shard_map/all_gather | solution.py:1163
  55.1 138.1 %all-gather.9.cloned.1.call-start = ((), (), s32[]{:S(2)}) async-start(), calls=%async_computation.7 | async-start | bytes 2621440 | tf_op jit(solution)/shard_map/all_gather | solution.py:1163
  106.7 121.2 %all-gather.7.cloned.1.call-start = ((), (), s32[]{:S(2)}) async-start(), calls=%async_computation.6 | async-start | bytes 7667712 | tf_op jit(solution)/shard_map/all_gather | solution.py:965
  152.1 127.6 %all-gather.11.cloned.1.call-start = ((), (), s32[]{:S(2)}) async-start(), calls=%async_computation.8 | async-start | bytes 7667712 | tf_op jit(solution)/shard_map/all_gather | solution.py:965
  212.9 155.6 %reduce-scatter.6.cloned.1.call-start = ((), (), s32[]{:S(2)}) async-start(), calls=%async_computation.9 | async-start | bytes 7667712 | tf_op jit(solution)/shard_map/reduce_scatter | solution.py:1092
  279.2 170.5 %reduce-scatter.8.cloned.1.call-start = ((), (), s32[]{:S(2)}) async-start(), calls=%async_computation.10 | async-start | bytes 7667712 | tf_op jit(solution)/shard_map/reduce_scatter | solution.py:1092
  330.5 186.2 %reduce-scatter.10.cloned.1.call-start = ((), (), s32[]{:S(2)}) async-start(), calls=%async_computation.11 | async-start | bytes 2621440 | tf_op jit(solution)/shard_map/reduce_scatter | solution.py:1231
  345.1 42.7 %collective-permute-start.20 = (bf16[1536,512]{1,0:T(8,128)(2,1)}, bf16[1536,512]{1,0:T(8,128)(2,1)S(1)}, u32[]{:S(2)}, u32[]{:S(2)}) collective-permute-start(bf16[1536,512]{1,0:T(8,128)(2,1)} %down_grad.2), channel_id=1, source_target_pairs={{0,8},{24,16},{1,9},{25,17},{2,10},{26,18},{3,11},{27,19},{4,12},{... | collective-permute-start | bytes 4718600 | tf_op jit(solution)/shard_map/ppermute | solution.py:949
  391.4 45.6 %collective-permute-start.22 = (bf16[1536,512]{1,0:T(8,128)(2,1)S(1)}, bf16[1536,512]{1,0:T(8,128)(2,1)}, u32[]{:S(2)}, u32[]{:S(2)}) collective-permute-start(bf16[1536,512]{1,0:T(8,128)(2,1)S(1)} %add_convert_fusion.14), channel_id=1, source_target_pairs={{8,16},{16,8},{9,17},{17,9},{10,18},{18,10},{11,19},{19,11},{12,20... | collective-permute-start | bytes 4718600 | tf_op jit(solution)/shard_map/ppermute | solution.py:939
  393.2 46.0 %collective-permute-start.21 = (bf16[1536,512]{1,0:T(8,128)(2,1)S(1)}, bf16[1536,512]{1,0:T(8,128)(2,1)}, u32[]{:S(2)}, u32[]{:S(2)}) collective-permute-start(bf16[1536,512]{1,0:T(8,128)(2,1)S(1)} %copy-done.28), channel_id=1, source_target_pairs={{0,8},{24,16},{1,9},{25,17},{2,10},{26,18},{3,11},{27,19},{4,12},{... | collective-permute-start | bytes 4718600 | tf_op jit(solution)/shard_map/ppermute | solution.py:949
  439.3 159.4 %reduce-scatter.12.cloned.1.call-start = ((), (), s32[]{:S(2)}) async-start(), calls=%async_computation.12 | async-start | bytes 2621440 | tf_op jit(solution)/shard_map/reduce_scatter | solution.py:1231
  442.5 55.1 %collective-permute-start.24 = (bf16[1536,512]{1,0:T(8,128)(2,1)}, bf16[1536,512]{1,0:T(8,128)(2,1)}, u32[]{:S(2)}, u32[]{:S(2)}) collective-permute-start(bf16[1536,512]{1,0:T(8,128)(2,1)} %add_convert_fusion.12), channel_id=1, source_target_pairs={{8,16},{16,8},{9,17},{17,9},{10,18},{18,10},{11,19},{19,11},{12,20... | collective-permute-start | bytes 4718600 | tf_op jit(solution)/shard_map/ppermute | solution.py:939
  446.6 70.1 %collective-permute-start.23 = (bf16[1536,512]{1,0:T(8,128)(2,1)S(1)}, bf16[1536,512]{1,0:T(8,128)(2,1)}, u32[]{:S(2)}, u32[]{:S(2)}) collective-permute-start(bf16[1536,512]{1,0:T(8,128)(2,1)S(1)} %fusion), channel_id=1, source_target_pairs={{0,8},{24,16},{8,0},{16,24},{1,9},{25,17},{9,1},{17,25},{2,10},{26... | collective-permute-start | bytes 4718600 | tf_op jit(solution)/shard_map/ppermute | solution.py:942
  516.8 199.9 %reduce-scatter.14.cloned.1.call-start = ((), (), s32[]{:S(2)}) async-start(), calls=%async_computation.13 | async-start | bytes 9289728 | tf_op jit(solution)/shard_map/reduce_scatter | solution.py:1092
  520.0 76.6 %collective-permute-start.26 = (bf16[1536,512]{1,0:T(8,128)(2,1)}, bf16[1536,512]{1,0:T(8,128)(2,1)}, u32[]{:S(2)}, u32[]{:S(2)}) collective-permute-start(bf16[1536,512]{1,0:T(8,128)(2,1)} %add_convert_fusion.10), channel_id=1, source_target_pairs={{8,16},{16,8},{9,17},{17,9},{10,18},{18,10},{11,19},{19,11},{12,20... | collective-permute-start | bytes 4718600 | tf_op jit(solution)/shard_map/ppermute | solution.py:939
  528.9 67.6 %collective-permute-start.25 = (bf16[1536,512]{1,0:T(8,128)(2,1)S(1)}, bf16[1536,512]{1,0:T(8,128)(2,1)}, u32[]{:S(2)}, u32[]{:S(2)}) collective-permute-start(bf16[1536,512]{1,0:T(8,128)(2,1)S(1)} %fusion.1), channel_id=1, source_target_pairs={{0,8},{24,16},{8,0},{16,24},{1,9},{25,17},{9,1},{17,25},{2,10},{26... | collective-permute-start | bytes 4718600 | tf_op jit(solution)/shard_map/ppermute | solution.py:942
  554.3 42.3 %collective-permute-start.31 = (bf16[96,1536]{1,0:T(8,128)(2,1)S(1)}, bf16[96,1536]{1,0:T(8,128)(2,1)}, u32[]{:S(2)}, u32[]{:S(2)}) collective-permute-start(bf16[96,1536]{1,0:T(8,128)(2,1)S(1)} %get-tuple-element.771), channel_id=1, source_target_pairs={{0,4},{1,5},{2,6},{3,7},{4,0},{5,1},{6,2},{7,3},{8,12},{9,13},{10,... | collective-permute-start | bytes 884744 | tf_op jit(solution)/shard_map/ppermute | solution.py:961
  621.8 213.4 %all-reduce.3.cloned.1.call-start = ((), (), s32[]{:S(2)}) async-start(), calls=%async_computation.14 | async-start | bytes 2064384 | tf_op jit(solution)/shard_map/psum | solution.py:1281
  665.6 41.2 %collective-permute-start.36 = (bf16[1024,1536]{1,0:T(8,128)(2,1)}, bf16[1024,1536]{1,0:T(8,128)(2,1)}, u32[]{:S(2)}, u32[]{:S(2)}) collective-permute-start(bf16[1024,1536]{1,0:T(8,128)(2,1)} %get-tuple-element.598), channel_id=1, source_target_pairs={{0,1},{1,0},{2,3},{3,2},{4,5},{5,4},{6,7},{7,6},{8,9},{9,8},{10,11... | collective-permute-start | bytes 9437192 | tf_op jit(solution)/shard_map/ppermute | solution.py:961
  665.6 46.7 %collective-permute-start.37 = (bf16[1024,1536]{1,0:T(8,128)(2,1)}, bf16[1024,1536]{1,0:T(8,128)(2,1)}, u32[]{:S(2)}, u32[]{:S(2)}) collective-permute-start(bf16[1024,1536]{1,0:T(8,128)(2,1)} %get-tuple-element.600), channel_id=1, source_target_pairs={{0,1},{1,0},{2,3},{3,2},{4,5},{5,4},{6,7},{7,6},{8,9},{9,8},{10,11... | collective-permute-start | bytes 9437192 | tf_op jit(solution)/shard_map/ppermute | solution.py:961
  722.4 69.4 %collective-permute-start.41 = (bf16[512,1536]{1,0:T(8,128)(2,1)S(1)}, bf16[512,1536]{1,0:T(8,128)(2,1)S(1)}, u32[]{:S(2)}, u32[]{:S(2)}) collective-permute-start(bf16[512,1536]{1,0:T(8,128)(2,1)S(1)} %pad_maximum_fusion), channel_id=1, source_target_pairs={{0,4},{1,5},{2,6},{3,7},{4,0},{5,1},{6,2},{7,3},{8,12},{9,13},{10,... | collective-permute-start | bytes 4718600 | tf_op jit(solution)/shard_map/ppermute | solution.py:961
  724.0 68.9 %collective-permute-start.42 = (bf16[512,1536]{1,0:T(8,128)(2,1)S(1)}, bf16[512,1536]{1,0:T(8,128)(2,1)S(1)}, u32[]{:S(2)}, u32[]{:S(2)}) collective-permute-start(bf16[512,1536]{1,0:T(8,128)(2,1)S(1)} %pad_maximum_fusion.1), channel_id=1, source_target_pairs={{0,2},{1,3},{2,0},{3,1},{4,6},{5,7},{6,4},{7,5},{8,10},{9,11},{10,... | collective-permute-start | bytes 4718600 | tf_op jit(solution)/shard_map/ppermute | solution.py:961
  727.9 63.9 %collective-permute-start.40 = (bf16[1536,512]{1,0:T(8,128)(2,1)S(1)}, bf16[1536,512]{1,0:T(8,128)(2,1)S(1)}, u32[]{:S(2)}, u32[]{:S(2)}) collective-permute-start(bf16[1536,512]{1,0:T(8,128)(2,1)S(1)} %add_convert_fusion.4), channel_id=1, source_target_pairs={{8,0},{16,24},{9,1},{17,25},{10,2},{18,26},{11,3},{19,27},{12,4},{... | collective-permute-start | bytes 4718600 | tf_op jit(solution)/shard_map/ppermute | solution.py:947
  731.4 60.5 %collective-permute-start.39 = (bf16[1536,512]{1,0:T(8,128)(2,1)S(1)}, bf16[1536,512]{1,0:T(8,128)(2,1)S(1)}, u32[]{:S(2)}, u32[]{:S(2)}) collective-permute-start(bf16[1536,512]{1,0:T(8,128)(2,1)S(1)} %add_convert_fusion.5), channel_id=1, source_target_pairs={{8,16},{16,8},{9,17},{17,9},{10,18},{18,10},{11,19},{19,11},{12,20... | collective-permute-start | bytes 4718600 | tf_op jit(solution)/shard_map/ppermute | solution.py:939
  (98 other events, 1082.4 us)
Sparse Core Ops, SparseCore 0:
  55.2 45.6 all-gather.4
  106.8 44.7 all-gather.8
  154.1 58.1 all-gather.6
  214.6 58.4 all-gather.10
  279.3 76.1 reduce-scatter.5
  359.2 64.2 reduce-scatter.7
  439.4 77.1 reduce-scatter.9
  519.0 72.6 reduce-scatter.11
  621.9 69.8 reduce-scatter.13
  716.8 70.3 all-reduce.2

commit v5 on v4

--- a/solution.py
+++ b/solution.py
@@ -1162,7 +1162,7 @@
         mine = kv[m * tokens : (m + 1) * tokens]
         every = lax.all_gather(mine, "seq", axis=0, tiled=True)
         kvs.append(every.reshape(n_seq, tokens, 2 * kv_width))
-    w_qo = [h.reshape(n_fsdp // 2, -1, h.shape[1]) for h in w_gather.finish(kvs[0])]
+    w_qo = [h.reshape(n_fsdp // 2, -1, h.shape[1]) for h in w_gather.finish(kvs[0], chosen, infos)]
     g_gathers = [Gather(gate(gout[0], w_gather.far), n_fsdp)]
     for m in range(1, micros):
         g_gathers.append(Gather(gate(gout[m], g_gathers[-1].near), n_fsdp))
@@ -1176,19 +1176,21 @@
             info = gate(infos[m], g_gathers[0].near)
             g_gathers[0].further(q_t)
         else:
-            info = gate(infos[m], state[-1][2], g_gathers[m].far)
-            g_all = [g.finish() for g in g_gathers]
+            info = gate(infos[m], state[-1][2])
         attn, attn_t, lse = attend(info, q_t, kvs[m], m, tokens)
         if m == 0:
-            attn = gate(attn, g_gathers[0].far)
+            attn = gate(attn, g_gathers[0].far, [g.near for g in g_gathers[1:]])
             for g in g_gathers[1:]:
                 g.further(g_gathers[0].far)
+        else:
+            attn = gate(attn, g_gathers[m].far)
         residual, xg, exact = after_attention(
             place, attn, w_qo, q_width, x, m, gain_two, router_all, chosen
         )
         state.append((attn_t, lse, residual, exact))
         xg_all.append(gather_rows(xg))
 
+    g_all = [g.finish(state[-1][2]) for g in g_gathers]
     xg_all[0] = gate(xg_all[0], state[-1][2], g_all)
     passed, backs = [], []
     for m in range(micros):

time: 880 us -> 859 us (0.976)
  waiting for transfers between devices: 297 us -> 285 us
  starting transfers between devices: 87.4 us -> 77.6 us
    ppermute x31, waiting for transfers between devices: 129 us -> 117 us  [swap(): return lax.ppermute(x, 'fsdp', [(i, i ^ mask) for i in range(8)])]
    ppermute x3, starting transfers between devices: 26.1 us -> 14.6 us  [step(): self.held['crossing'] = (chunk, lax.ppermute(chunk, 'seq', come))]
    unnamed x132 -> x136, local copies, waits for them, and re-layouts: 19 us -> 16.9 us
  transfers between devices with their start and end apart: 58 -> 58, of which waited for: 31 -> 35; matrix products, arithmetic and copies ran while one was open for 10% -> 11% of each run, Pallas kernels for 36% -> 37%
where the time goes in v5:
time: 859 us; the launch traced here: 847 us
  Pallas kernels  356 us (41%)
  waiting for transfers between devices  285 us (33%)
  other arithmetic  85 us (10%)
  starting transfers between devices  77.6 us (9%)
  local copies, waits for them, and re-layouts  27.9 us (3%)
  between operations  15.3 us (2%)
    ppermute x31, waiting for transfers between devices, swap(): return lax.ppermute(x, 'fsdp', [(i, i ^ mask) for i in range(8)])  117 us
    pallas_call x2, Pallas kernels, run_experts(): pl.pallas_call(functools.partial(expert_kernel, experts, half), name='run...  102 us
    ppermute x4, waiting for transfers between devices, step(): got = lax.ppermute(sent, 'seq', come + go)  74.3 us
    ppermute x3, waiting for transfers between devices, step(): self.results.append((summed, lax.ppermute(summed, 'seq', go)))  69.2 us
    pallas_call x4, Pallas kernels, wide_grad(): pl.pallas_call(functools.partial(wide_grad_kernel, steps, micros), name='...  57.2 us
    ppermute x31, starting transfers between devices, swap(): return lax.ppermute(x, 'fsdp', [(i, i ^ mask) for i in range(8)])  35 us
    convert_element_type x19, other arithmetic, add_low(): return (a.astype(F32) + b.astype(F32)).astype(BF)  34.1 us
    pallas_call x2, Pallas kernels, attend_back(): pl.pallas_call(functools.partial(attend_back_kernel, n), name='attend_bac...  31.2 us
  transfers between devices with their start and end apart: 58, of which 35 were waited for; matrix products, arithmetic and copies ran while one was open for 11% of the time, Pallas kernels for 37%

profile of v5, /device:TPU:0, one launch (start us, length us, event | category | flops | bytes accessed | tf_op | source)
XLA Modules:
  0.0 846.5 jit_solution(10610596177473060520)
XLA Ops:
  55.1 11.8 %collective-permute-done.6.low_y_ref = bf16[96,3072]{1,0:T(8,128)(2,1)S(1)} collective-permute-done((bf16[96,3072]{1,0:T(8,128)(2,1)S(1)}, bf16[96,3072]{1,0:T(8,128)(2,1)S(1)}, u32[]{:S(2)}, u32[]{:S(2)}) %collective-permute-start.6) | collective-permute-done | bytes 589856 | tf_op jit(solution)/shard_map/ppermute | solution.py:961
  79.2 17.1 %collective-permute-done.7.top_far_ref = bf16[192,3072]{1,0:T(8,128)(2,1)S(1)} collective-permute-done((bf16[192,3072]{1,0:T(8,128)(2,1)}, bf16[192,3072]{1,0:T(8,128)(2,1)S(1)}, u32[]{:S(2)}, u32[]{:S(2)}) %collective-permute-start.7) | collective-permute-done | bytes 1179680 | tf_op jit(solution)/shard_map/ppermute | solution.py:961
  132.6 12.7 %attend.2 = (bf16[256,1536]{1,0:T(8,128)(2,1)}, bf16[1536,256]{1,0:T(8,128)(2,1)}, f32[32,768]{1,0:T(8,128)}) custom-call(s32[2]{0:T(128)} %pad_add_fusion.info_ref, bf16[1536,512]{1,0:T(8,128)(2,1)} %q_project.1.q_ref, bf16[4,256,1024]{2,1,0:T(8,128)(2,1)} %bitcast.73, bf16[4,256,1024]{2,1,0:T(8,128)(2,1)} %bitcast.74), custom_call_target="tpu_custom_call" | custom-call | flops 644245120 | bytes 445644 | tf_op jit(solution)/shard_map/attend/pallas_call | solution.py:249
  167.4 12.7 %attend.3 = (bf16[256,1536]{1,0:T(8,128)(2,1)}, bf16[1536,256]{1,0:T(8,128)(2,1)}, f32[32,768]{1,0:T(8,128)}) custom-call(s32[2]{0:T(128)} %pad_add_fusion.1.info_ref, bf16[1536,512]{1,0:T(8,128)(2,1)} %q_project.1.q_ref, bf16[4,256,1024]{2,1,0:T(8,128)(2,1)} %bitcast.77, bf16[4,256,1024]{2,1,0:T(8,128)(2,1)} %bitcast.78), custom_call_target="tpu_custom_call" | custom-call | flops 644245120 | bytes 445644 | tf_op jit(solution)/shard_map/attend/pallas_call | solution.py:249
  180.1 11.4 %collective-permute-done.16.top_far_ref = bf16[256,1536]{1,0:T(8,128)(2,1)S(1)} collective-permute-done((bf16[256,1536]{1,0:T(8,128)(2,1)S(1)}, bf16[256,1536]{1,0:T(8,128)(2,1)S(1)}, u32[]{:S(2)}, u32[]{:S(2)}) %collective-permute-start.16) | collective-permute-done | bytes 786464 | tf_op jit(solution)/shard_map/ppermute | solution.py:961
  217.8 50.8 %run_experts.2 = (bf16[1024,1536]{1,0:T(8,128)(2,1)}, bf16[1024,1536]{1,0:T(8,128)(2,1)}, bf16[2048,1664]{1,0:T(8,128)(2,1)}, bf16[2048,1024]{1,0:T(8,128)(2,1)}, bf16[2048,2048]{1,0:T(8,128)(2,1)}) custom-call(s32[1]{0:T(128)} %bitcast.14.own_ref, s32[8]{0:T(128)} %fusion.10.order_ref, bf16[2048,1664]{1,0:T(8,128)(2,1)} %all-gather.7.cloned.1.call-done.xg_ref.refs_0_, ...), custom_call_target="tpu_custom_call" | custom-call | flops 3865470464 | bytes 4718592 | tf_op jit(solution)/shard_map/run_experts/pallas_call | solution.py:507
  269.2 50.8 %run_experts.3 = (bf16[1024,1536]{1,0:T(8,128)(2,1)}, bf16[1024,1536]{1,0:T(8,128)(2,1)}, bf16[2048,1664]{1,0:T(8,128)(2,1)}, bf16[2048,1024]{1,0:T(8,128)(2,1)}, bf16[2048,2048]{1,0:T(8,128)(2,1)}) custom-call(s32[1]{0:T(128)} %bitcast.14.own_ref, s32[8]{0:T(128)} %fusion.10.order_ref, bf16[2048,1664]{1,0:T(8,128)(2,1)} %all-gather.11.cloned.1.call-done.xg_ref.refs_1_, ...), custom_call_target="tpu_custom_call" | custom-call | flops 3865470464 | bytes 4718592 | tf_op jit(solution)/shard_map/run_experts/pallas_call | solution.py:507
  320.0 14.7 %down_grad.2 = bf16[1536,512]{1,0:T(8,128)(2,1)} custom-call(bf16[2048,1024]{1,0:T(8,128)(2,1)} %get-tuple-element.409.refs_0_, bf16[2048,1024]{1,0:T(8,128)(2,1)} %get-tuple-element.410.refs_1_, bf16[1024,1536]{1,0:T(8,128)(2,1)} %assemble.6.ga_ref.refs_2_, bf16[1024,1536]{1,0:T(8,128)(2,1)} %assemble.7.ga_ref.refs_3_, ...), custom_call_target="tpu_custom_call" | custom-call | flops 644245120 | bytes 1677721 | tf_op jit(solution)/shard_map/down_grad/pallas_call | solution.py:622
  338.2 15.1 %down_grad.3 = bf16[1536,512]{1,0:T(8,128)(2,1)} custom-call(bf16[2048,1024]{1,0:T(8,128)(2,1)} %get-tuple-element.409.refs_0_, bf16[2048,1024]{1,0:T(8,128)(2,1)} %get-tuple-element.410.refs_1_, bf16[1024,1536]{1,0:T(8,128)(2,1)} %assemble.6.ga_ref.refs_2_, bf16[1024,1536]{1,0:T(8,128)(2,1)} %assemble.7.ga_ref.refs_3_, ...), custom_call_target="tpu_custom_call" | custom-call | flops 644245120 | bytes 1677721 | tf_op jit(solution)/shard_map/down_grad/pallas_call | solution.py:622
  362.3 10.1 %collective-permute-done.20 = bf16[1536,512]{1,0:T(8,128)(2,1)S(1)} collective-permute-done((bf16[1536,512]{1,0:T(8,128)(2,1)}, bf16[1536,512]{1,0:T(8,128)(2,1)S(1)}, u32[]{:S(2)}, u32[]{:S(2)}) %collective-permute-start.20) | collective-permute-done | bytes 1572896 | tf_op jit(solution)/shard_map/ppermute | solution.py:949
  385.0 14.7 %wide_grad.4 = bf16[1536,512]{1,0:T(8,128)(2,1)} custom-call(bf16[2048,1664]{1,0:T(8,128)(2,1)} %all-gather.7.cloned.1.call-done.xg_ref.refs_0_, bf16[2048,1664]{1,0:T(8,128)(2,1)} %all-gather.11.cloned.1.call-done.xg_ref.refs_1_, bf16[2048,2048]{1,0:T(8,128)(2,1)} %get-tuple-element.490.refs_2_, bf16[2048,2048]{1,0:T(8,128)(2,1)} %get-tuple-element.491.refs_3_), custom_call_target="tpu_custom_call" | custom-call | flops 644245120 | bytes 1835008 | tf_op jit(solution)/shard_map/wide_grad/pallas_call | solution.py:580
  399.8 15.6 %attend_back.2 = (bf16[256,1536]{1,0:T(8,128)(2,1)}, bf16[4,2,256,512]{3,2,1,0:T(8,128)(2,1)}) custom-call(s32[2]{0:T(128)} %pad_add_fusion.info_ref, bf16[1536,512]{1,0:T(8,128)(2,1)} %q_project.1.q_ref, bf16[1536,256]{1,0:T(8,128)(2,1)} %get-tuple-element.648.g_ref, bf16[1536,256]{1,0:T(8,128)(2,1)} %get-tuple-element.436.o_ref.refs_0_, ...), custom_call_target="tpu_custom_call" | custom-call | flops 1610612736 | bytes 734003 | tf_op jit(solution)/shard_map/attend_back/pallas_call | solution.py:349
  435.9 15.6 %attend_back.3 = (bf16[256,1536]{1,0:T(8,128)(2,1)}, bf16[4,2,256,512]{3,2,1,0:T(8,128)(2,1)}) custom-call(s32[2]{0:T(128)} %pad_add_fusion.1.info_ref, bf16[1536,512]{1,0:T(8,128)(2,1)} %q_project.1.q_ref, bf16[1536,256]{1,0:T(8,128)(2,1)} %get-tuple-element.657.g_ref, bf16[1536,256]{1,0:T(8,128)(2,1)} %get-tuple-element.464.refs_1_.o_ref, ...), custom_call_target="tpu_custom_call" | custom-call | flops 1610612736 | bytes 734003 | tf_op jit(solution)/shard_map/attend_back/pallas_call | solution.py:349
  461.0 14.2 %wide_grad.5 = bf16[1536,512]{1,0:T(8,128)(2,1)} custom-call(bf16[2048,1664]{1,0:T(8,128)(2,1)} %all-gather.7.cloned.1.call-done.xg_ref.refs_0_, bf16[2048,1664]{1,0:T(8,128)(2,1)} %all-gather.11.cloned.1.call-done.xg_ref.refs_1_, bf16[2048,2048]{1,0:T(8,128)(2,1)} %get-tuple-element.490.refs_2_, bf16[2048,2048]{1,0:T(8,128)(2,1)} %get-tuple-element.491.refs_3_), custom_call_target="tpu_custom_call" | custom-call | flops 644245120 | bytes 1835008 | tf_op jit(solution)/shard_map/wide_grad/pallas_call | solution.py:580
  475.2 18.3 %collective-permute-done.23 = bf16[1536,512]{1,0:T(8,128)(2,1)} collective-permute-done((bf16[1536,512]{1,0:T(8,128)(2,1)S(1)}, bf16[1536,512]{1,0:T(8,128)(2,1)}, u32[]{:S(2)}, u32[]{:S(2)}) %collective-permute-start.23) | collective-permute-done | bytes 1572896 | tf_op jit(solution)/shard_map/ppermute | solution.py:942
  535.3 10.0 %last_step.2 = (bf16[256,1536]{1,0:T(8,128)(2,1)}, f32[8,1536]{1,0:T(8,128)}) custom-call(s32[8]{0:T(128)} %multiply_add_fusion.place_ref, bf16[256,1536]{1,0:T(8,128)(2,1)} %get-tuple-element.649.gq_ref.refs_0_, bf16[256,1024]{1,0:T(8,128)(2,1)} %turn_back.2.dkv_ref.refs_2_, bf16[4,192,3072]{2,1,0:T(8,128)(2,1)} %bitcast.62, ...), custom_call_target="tpu_custom_call" | custom-call | flops 201326592 | bytes 1258291 | tf_op jit(solution)/shard_map/last_step/pallas_call | solution.py:759
  545.2 14.1 %wide_grad.7 = bf16[1536,512]{1,0:T(8,128)(2,1)} custom-call(bf16[2048,1664]{1,0:T(8,128)(2,1)} %all-gather.7.cloned.1.call-done.xg_ref.refs_0_, bf16[2048,1664]{1,0:T(8,128)(2,1)} %all-gather.11.cloned.1.call-done.xg_ref.refs_1_, bf16[2048,2048]{1,0:T(8,128)(2,1)} %get-tuple-element.490.refs_2_, bf16[2048,2048]{1,0:T(8,128)(2,1)} %get-tuple-element.491.refs_3_), custom_call_target="tpu_custom_call" | custom-call | flops 644245120 | bytes 1835008 | tf_op jit(solution)/shard_map/wide_grad/pallas_call | solution.py:580
  559.4 14.1 %wide_grad.6 = bf16[1536,512]{1,0:T(8,128)(2,1)} custom-call(bf16[2048,1664]{1,0:T(8,128)(2,1)} %all-gather.7.cloned.1.call-done.xg_ref.refs_0_, bf16[2048,1664]{1,0:T(8,128)(2,1)} %all-gather.11.cloned.1.call-done.xg_ref.refs_1_, bf16[2048,2048]{1,0:T(8,128)(2,1)} %get-tuple-element.490.refs_2_, bf16[2048,2048]{1,0:T(8,128)(2,1)} %get-tuple-element.491.refs_3_), custom_call_target="tpu_custom_call" | custom-call | flops 644245120 | bytes 1835008 | tf_op jit(solution)/shard_map/wide_grad/pallas_call | solution.py:580
  587.5 11.4 %projection_grads.1 = bf16[1536,2688]{1,0:T(8,128)(2,1)} custom-call(bf16[512,1536]{1,0:T(8,128)(2,1)} %get-tuple-element.370.normed_ref, bf16[256,1536]{1,0:T(8,128)(2,1)} %get-tuple-element.649.gq_ref.refs_0_, bf16[256,1536]{1,0:T(8,128)(2,1)} %get-tuple-element.658.gq_ref.refs_1_, bf16[256,1024]{1,0:T(8,128)(2,1)} %turn_back.2.dkv_ref.refs_2_, ...), custom_call_target="tpu_custom_call" | custom-call | flops 422785856 | bytes 1258291 | tf_op jit(solution)/shard_map/projection_grads/pallas_call | solution.py:875
  615.8 27.7 %collective-permute-done.32 = bf16[1536,512]{1,0:T(8,128)(2,1)S(1)} collective-permute-done((bf16[1536,512]{1,0:T(8,128)(2,1)S(1)}, bf16[1536,512]{1,0:T(8,128)(2,1)S(1)}, u32[]{:S(2)}, u32[]{:S(2)}) %collective-permute-start.32) | collective-permute-done | bytes 1572896 | tf_op jit(solution)/shard_map/ppermute | solution.py:942
  656.7 28.1 %collective-permute-done.34 = bf16[1536,512]{1,0:T(8,128)(2,1)} collective-permute-done((bf16[1536,512]{1,0:T(8,128)(2,1)S(1)}, bf16[1536,512]{1,0:T(8,128)(2,1)}, u32[]{:S(2)}, u32[]{:S(2)}) %collective-permute-start.34) | collective-permute-done | bytes 1572896 | tf_op jit(solution)/shard_map/ppermute | solution.py:942
  722.9 46.9 %collective-permute-done.40 = bf16[1536,512]{1,0:T(8,128)(2,1)S(1)} collective-permute-done((bf16[1536,512]{1,0:T(8,128)(2,1)S(1)}, bf16[1536,512]{1,0:T(8,128)(2,1)S(1)}, u32[]{:S(2)}, u32[]{:S(2)}) %collective-permute-start.40) | collective-permute-done | bytes 1572896 | tf_op jit(solution)/shard_map/ppermute | solution.py:947
  778.8 11.6 %collective-permute-done.46 = bf16[256,1536]{1,0:T(8,128)(2,1)S(1)} collective-permute-done((bf16[256,1536]{1,0:T(8,128)(2,1)S(1)}, bf16[256,1536]{1,0:T(8,128)(2,1)S(1)}, u32[]{:S(2)}, u32[]{:S(2)}) %collective-permute-start.46) | collective-permute-done | bytes 786464 | tf_op jit(solution)/shard_map/ppermute | solution.py:961
  794.9 18.3 %collective-permute-done.44 = bf16[1536,512]{1,0:T(8,128)(2,1)} collective-permute-done((bf16[1536,512]{1,0:T(8,128)(2,1)S(1)}, bf16[1536,512]{1,0:T(8,128)(2,1)}, u32[]{:S(2)}, u32[]{:S(2)}) %collective-permute-start.44) | collective-permute-done | bytes 1572896 | tf_op jit(solution)/shard_map/ppermute | solution.py:947
  (361 shorter events, 363.3 us)
Async XLA Ops:
  7.2 93.7 %all-gather.5.cloned.1.call-start = ((), (), s32[]{:S(2)}) async-start(), calls=%async_computation.5 | async-start | bytes 2621440 | tf_op jit(solution)/shard_map/all_gather | solution.py:1163
  55.1 112.3 %all-gather.9.cloned.1.call-start = ((), (), s32[]{:S(2)}) async-start(), calls=%async_computation.7 | async-start | bytes 2621440 | tf_op jit(solution)/shard_map/all_gather | solution.py:1163
  106.6 111.2 %all-gather.7.cloned.1.call-start = ((), (), s32[]{:S(2)}) async-start(), calls=%async_computation.6 | async-start | bytes 7667712 | tf_op jit(solution)/shard_map/all_gather | solution.py:965
  164.1 105.1 %all-gather.11.cloned.1.call-start = ((), (), s32[]{:S(2)}) async-start(), calls=%async_computation.8 | async-start | bytes 7667712 | tf_op jit(solution)/shard_map/all_gather | solution.py:965
  200.2 153.2 %reduce-scatter.6.cloned.1.call-start = ((), (), s32[]{:S(2)}) async-start(), calls=%async_computation.9 | async-start | bytes 7667712 | tf_op jit(solution)/shard_map/reduce_scatter | solution.py:1092
  268.7 158.5 %reduce-scatter.8.cloned.1.call-start = ((), (), s32[]{:S(2)}) async-start(), calls=%async_computation.10 | async-start | bytes 7667712 | tf_op jit(solution)/shard_map/reduce_scatter | solution.py:1092
  320.0 174.6 %reduce-scatter.10.cloned.1.call-start = ((), (), s32[]{:S(2)}) async-start(), calls=%async_computation.11 | async-start | bytes 2621440 | tf_op jit(solution)/shard_map/reduce_scatter | solution.py:1233
  376.0 39.3 %collective-permute-start.22 = (bf16[1536,512]{1,0:T(8,128)(2,1)S(1)}, bf16[1536,512]{1,0:T(8,128)(2,1)}, u32[]{:S(2)}, u32[]{:S(2)}) collective-permute-start(bf16[1536,512]{1,0:T(8,128)(2,1)S(1)} %add_convert_fusion.14), channel_id=1, source_target_pairs={{8,16},{16,8},{9,17},{17,9},{10,18},{18,10},{11,19},{19,11},{12,20... | collective-permute-start | bytes 4718600 | tf_op jit(solution)/shard_map/ppermute | solution.py:939
  377.9 38.9 %collective-permute-start.21 = (bf16[1536,512]{1,0:T(8,128)(2,1)S(1)}, bf16[1536,512]{1,0:T(8,128)(2,1)}, u32[]{:S(2)}, u32[]{:S(2)}) collective-permute-start(bf16[1536,512]{1,0:T(8,128)(2,1)S(1)} %copy-done.28), channel_id=1, source_target_pairs={{0,8},{24,16},{1,9},{25,17},{2,10},{26,18},{3,11},{27,19},{4,12},{... | collective-permute-start | bytes 4718600 | tf_op jit(solution)/shard_map/ppermute | solution.py:949
  416.8 159.1 %reduce-scatter.12.cloned.1.call-start = ((), (), s32[]{:S(2)}) async-start(), calls=%async_computation.12 | async-start | bytes 2621440 | tf_op jit(solution)/shard_map/reduce_scatter | solution.py:1233
  420.0 55.2 %collective-permute-start.24 = (bf16[1536,512]{1,0:T(8,128)(2,1)}, bf16[1536,512]{1,0:T(8,128)(2,1)}, u32[]{:S(2)}, u32[]{:S(2)}) collective-permute-start(bf16[1536,512]{1,0:T(8,128)(2,1)} %add_convert_fusion.12), channel_id=1, source_target_pairs={{8,16},{16,8},{9,17},{17,9},{10,18},{18,10},{11,19},{19,11},{12,20... | collective-permute-start | bytes 4718600 | tf_op jit(solution)/shard_map/ppermute | solution.py:939
  423.9 69.6 %collective-permute-start.23 = (bf16[1536,512]{1,0:T(8,128)(2,1)S(1)}, bf16[1536,512]{1,0:T(8,128)(2,1)}, u32[]{:S(2)}, u32[]{:S(2)}) collective-permute-start(bf16[1536,512]{1,0:T(8,128)(2,1)S(1)} %fusion), channel_id=1, source_target_pairs={{0,8},{24,16},{8,0},{16,24},{1,9},{25,17},{9,1},{17,25},{2,10},{26... | collective-permute-start | bytes 4718600 | tf_op jit(solution)/shard_map/ppermute | solution.py:942
  494.7 199.9 %reduce-scatter.14.cloned.1.call-start = ((), (), s32[]{:S(2)}) async-start(), calls=%async_computation.13 | async-start | bytes 9289728 | tf_op jit(solution)/shard_map/reduce_scatter | solution.py:1092
  497.9 75.6 %collective-permute-start.26 = (bf16[1536,512]{1,0:T(8,128)(2,1)}, bf16[1536,512]{1,0:T(8,128)(2,1)}, u32[]{:S(2)}, u32[]{:S(2)}) collective-permute-start(bf16[1536,512]{1,0:T(8,128)(2,1)} %add_convert_fusion.10), channel_id=1, source_target_pairs={{8,16},{16,8},{9,17},{17,9},{10,18},{18,10},{11,19},{19,11},{12,20... | collective-permute-start | bytes 4718600 | tf_op jit(solution)/shard_map/ppermute | solution.py:939
  506.9 66.9 %collective-permute-start.25 = (bf16[1536,512]{1,0:T(8,128)(2,1)S(1)}, bf16[1536,512]{1,0:T(8,128)(2,1)}, u32[]{:S(2)}, u32[]{:S(2)}) collective-permute-start(bf16[1536,512]{1,0:T(8,128)(2,1)S(1)} %fusion.1), channel_id=1, source_target_pairs={{0,8},{24,16},{8,0},{16,24},{1,9},{25,17},{9,1},{17,25},{2,10},{26... | collective-permute-start | bytes 4718600 | tf_op jit(solution)/shard_map/ppermute | solution.py:942
  532.0 41.7 %collective-permute-start.31 = (bf16[96,1536]{1,0:T(8,128)(2,1)S(1)}, bf16[96,1536]{1,0:T(8,128)(2,1)}, u32[]{:S(2)}, u32[]{:S(2)}) collective-permute-start(bf16[96,1536]{1,0:T(8,128)(2,1)S(1)} %get-tuple-element.773), channel_id=1, source_target_pairs={{0,4},{1,5},{2,6},{3,7},{4,0},{5,1},{6,2},{7,3},{8,12},{9,13},{10,... | collective-permute-start | bytes 884744 | tf_op jit(solution)/shard_map/ppermute | solution.py:961
  599.0 214.2 %all-reduce.3.cloned.1.call-start = ((), (), s32[]{:S(2)}) async-start(), calls=%async_computation.14 | async-start | bytes 2064384 | tf_op jit(solution)/shard_map/psum | solution.py:1283
  604.6 38.9 %collective-permute-start.32 = (bf16[1536,512]{1,0:T(8,128)(2,1)S(1)}, bf16[1536,512]{1,0:T(8,128)(2,1)S(1)}, u32[]{:S(2)}, u32[]{:S(2)}) collective-permute-start(bf16[1536,512]{1,0:T(8,128)(2,1)S(1)} %fusion.2), channel_id=1, source_target_pairs={{0,8},{24,16},{8,0},{16,24},{1,9},{25,17},{9,1},{17,25},{2,10},{26... | collective-permute-start | bytes 4718600 | tf_op jit(solution)/shard_map/ppermute | solution.py:942
  643.5 41.2 %collective-permute-start.36 = (bf16[1024,1536]{1,0:T(8,128)(2,1)}, bf16[1024,1536]{1,0:T(8,128)(2,1)}, u32[]{:S(2)}, u32[]{:S(2)}) collective-permute-start(bf16[1024,1536]{1,0:T(8,128)(2,1)} %get-tuple-element.600), channel_id=1, source_target_pairs={{0,1},{1,0},{2,3},{3,2},{4,5},{5,4},{6,7},{7,6},{8,9},{9,8},{10,11... | collective-permute-start | bytes 9437192 | tf_op jit(solution)/shard_map/ppermute | solution.py:961
  643.5 46.7 %collective-permute-start.37 = (bf16[1024,1536]{1,0:T(8,128)(2,1)}, bf16[1024,1536]{1,0:T(8,128)(2,1)}, u32[]{:S(2)}, u32[]{:S(2)}) collective-permute-start(bf16[1024,1536]{1,0:T(8,128)(2,1)} %get-tuple-element.602), channel_id=1, source_target_pairs={{0,1},{1,0},{2,3},{3,2},{4,5},{5,4},{6,7},{7,6},{8,9},{9,8},{10,11... | collective-permute-start | bytes 9437192 | tf_op jit(solution)/shard_map/ppermute | solution.py:961
  700.4 69.4 %collective-permute-start.41 = (bf16[512,1536]{1,0:T(8,128)(2,1)S(1)}, bf16[512,1536]{1,0:T(8,128)(2,1)S(1)}, u32[]{:S(2)}, u32[]{:S(2)}) collective-permute-start(bf16[512,1536]{1,0:T(8,128)(2,1)S(1)} %pad_maximum_fusion), channel_id=1, source_target_pairs={{0,4},{1,5},{2,6},{3,7},{4,0},{5,1},{6,2},{7,3},{8,12},{9,13},{10,... | collective-permute-start | bytes 4718600 | tf_op jit(solution)/shard_map/ppermute | solution.py:961
  702.0 68.9 %collective-permute-start.42 = (bf16[512,1536]{1,0:T(8,128)(2,1)S(1)}, bf16[512,1536]{1,0:T(8,128)(2,1)S(1)}, u32[]{:S(2)}, u32[]{:S(2)}) collective-permute-start(bf16[512,1536]{1,0:T(8,128)(2,1)S(1)} %pad_maximum_fusion.1), channel_id=1, source_target_pairs={{0,2},{1,3},{2,0},{3,1},{4,6},{5,7},{6,4},{7,5},{8,10},{9,11},{10,... | collective-permute-start | bytes 4718600 | tf_op jit(solution)/shard_map/ppermute | solution.py:961
  705.9 63.9 %collective-permute-start.40 = (bf16[1536,512]{1,0:T(8,128)(2,1)S(1)}, bf16[1536,512]{1,0:T(8,128)(2,1)S(1)}, u32[]{:S(2)}, u32[]{:S(2)}) collective-permute-start(bf16[1536,512]{1,0:T(8,128)(2,1)S(1)} %add_convert_fusion.4), channel_id=1, source_target_pairs={{8,0},{16,24},{9,1},{17,25},{10,2},{18,26},{11,3},{19,27},{12,4},{... | collective-permute-start | bytes 4718600 | tf_op jit(solution)/shard_map/ppermute | solution.py:947
  709.3 60.5 %collective-permute-start.39 = (bf16[1536,512]{1,0:T(8,128)(2,1)S(1)}, bf16[1536,512]{1,0:T(8,128)(2,1)S(1)}, u32[]{:S(2)}, u32[]{:S(2)}) collective-permute-start(bf16[1536,512]{1,0:T(8,128)(2,1)S(1)} %add_convert_fusion.5), channel_id=1, source_target_pairs={{8,16},{16,8},{9,17},{17,9},{10,18},{18,10},{11,19},{19,11},{12,20... | collective-permute-start | bytes 4718600 | tf_op jit(solution)/shard_map/ppermute | solution.py:939
  (100 other events, 1211.2 us)
Sparse Core Ops, SparseCore 0:
  55.2 45.6 all-gather.4
  106.8 45.1 all-gather.8
  164.2 53.5 all-gather.6
  220.2 47.7 all-gather.10
  271.2 64.2 reduce-scatter.5
  339.2 64.2 reduce-scatter.7
  416.9 77.6 reduce-scatter.9
  497.0 73.0 reduce-scatter.11
  599.1 70.6 reduce-scatter.13
  694.8 70.3 all-reduce.2

commit v6 on v5

--- a/solution.py
+++ b/solution.py
@@ -1271,7 +1271,7 @@
             found[t - 3]["mine"] = owned[t - 3]
         if t == 3:
             heads = Scatter([found[0].pop("out")], n_fsdp)
-        if t in (6, 8):
+        if t == 7:
             found[0]["rest"] = rest
         held = (chunks, line.held, line.results, passed, found, moe.arrays)
         if t >= 3:
@@ -1279,9 +1279,9 @@
         else:
             held = lax.optimization_barrier(held)
         chunks, line.held, line.results, passed, found, moe.arrays = held
-        if t == 6:
+        if t == 7:
             rest = lax.psum(found[0].pop("rest"), "seq")
-        if len(line.results) in (experts, 2 * experts) and t < slots + 2:
+        if len(line.results) in (experts, 2 * experts, 3 * experts) and len(experts_out) < 3:
             pair = line.sums()[-experts:]
             experts_out.append(widen(pair, len(experts_out) == 0))
             found[1]["wide"] = experts_out[-1]
@@ -1299,14 +1299,15 @@
             found[0]["out"] = out_grad(
                 order, [st[0] for st in state], [f["g_attn"] for f in found]
             )
-        if t == 4:
-            rest = scatter_rows(rest_grads())
         if t in (5, 6, 7):
             moe.advance()
         for _ in range(3 if t == 3 else 0):
             heads.advance()
         line.step(sent, (chunks, found))
-    rest = found[0]["rest"].astype(F32)
+        if t == 4:
+            normed_one, line.held = lax.optimization_barrier((normed_one, line.held))
+            rest = scatter_rows(rest_grads())
+    rest = rest.astype(F32)
     totals = line.sums()
     for i in range(len(experts_out), 3):
         experts_out.append(widen(totals[i * experts : (i + 1) * experts], i == 0))

time: 859 us -> 853 us (level)
    psum x1, waiting for transfers between devices: 0.01 us -> 41.7 us  [on_device(): rest = lax.psum(found[0].pop('rest'), 'seq')]
    ppermute x3, waiting for transfers between devices: 69.2 us -> 32.9 us  [step(): self.results.append((summed, lax.ppermute(summed, 'seq', go)))]
    ppermute x4, waiting for transfers between devices: 74.3 us -> 64.2 us  [step(): got = lax.ppermute(sent, 'seq', come + go)]
  transfers between devices with their start and end apart: 58 -> 58, of which waited for: 35 -> 36; matrix products, arithmetic and copies ran while one was open for 11% -> 11% of each run, Pallas kernels for 37% -> 39%
where the time goes in v6:
time: 853 us; the launch traced here: 842 us
  Pallas kernels  355 us (42%)
  waiting for transfers between devices  278 us (33%)
  other arithmetic  87.6 us (10%)
  starting transfers between devices  80.4 us (9%)
  local copies, waits for them, and re-layouts  25.3 us (3%)
  between operations  15.6 us (2%)
    ppermute x31, waiting for transfers between devices, swap(): return lax.ppermute(x, 'fsdp', [(i, i ^ mask) for i in range(8)])  121 us
    pallas_call x2, Pallas kernels, run_experts(): pl.pallas_call(functools.partial(expert_kernel, experts, half), name='run...  102 us
    ppermute x4, waiting for transfers between devices, step(): got = lax.ppermute(sent, 'seq', come + go)  64.2 us
    pallas_call x4, Pallas kernels, wide_grad(): pl.pallas_call(functools.partial(wide_grad_kernel, steps, micros), name='...  57.3 us
    psum x1, waiting for transfers between devices, on_device(): rest = lax.psum(found[0].pop('rest'), 'seq')  41.7 us
    ppermute x31, starting transfers between devices, swap(): return lax.ppermute(x, 'fsdp', [(i, i ^ mask) for i in range(8)])  38 us
    convert_element_type x19, other arithmetic, add_low(): return (a.astype(F32) + b.astype(F32)).astype(BF)  36.9 us
    ppermute x3, waiting for transfers between devices, step(): self.results.append((summed, lax.ppermute(summed, 'seq', go)))  32.9 us
  transfers between devices with their start and end apart: 58, of which 36 were waited for; matrix products, arithmetic and copies ran while one was open for 11% of the time, Pallas kernels for 39%

profile of v6, /device:TPU:0, one launch (start us, length us, event | category | flops | bytes accessed | tf_op | source)
XLA Modules:
  0.0 841.7 jit_solution(10724257929470771404)
XLA Ops:
  55.2 11.8 %collective-permute-done.6.low_y_ref = bf16[96,3072]{1,0:T(8,128)(2,1)S(1)} collective-permute-done((bf16[96,3072]{1,0:T(8,128)(2,1)S(1)}, bf16[96,3072]{1,0:T(8,128)(2,1)S(1)}, u32[]{:S(2)}, u32[]{:S(2)}) %collective-permute-start.6) | collective-permute-done | bytes 589856 | tf_op jit(solution)/shard_map/ppermute | solution.py:961
  79.4 17.0 %collective-permute-done.7.top_far_ref = bf16[192,3072]{1,0:T(8,128)(2,1)S(1)} collective-permute-done((bf16[192,3072]{1,0:T(8,128)(2,1)}, bf16[192,3072]{1,0:T(8,128)(2,1)S(1)}, u32[]{:S(2)}, u32[]{:S(2)}) %collective-permute-start.7) | collective-permute-done | bytes 1179680 | tf_op jit(solution)/shard_map/ppermute | solution.py:961
  132.7 12.7 %attend.2 = (bf16[256,1536]{1,0:T(8,128)(2,1)}, bf16[1536,256]{1,0:T(8,128)(2,1)}, f32[32,768]{1,0:T(8,128)}) custom-call(s32[2]{0:T(128)} %pad_add_fusion.info_ref, bf16[1536,512]{1,0:T(8,128)(2,1)} %q_project.1.q_ref, bf16[4,256,1024]{2,1,0:T(8,128)(2,1)} %bitcast.73, bf16[4,256,1024]{2,1,0:T(8,128)(2,1)} %bitcast.74), custom_call_target="tpu_custom_call" | custom-call | flops 644245120 | bytes 445644 | tf_op jit(solution)/shard_map/attend/pallas_call | solution.py:249
  145.4 9.8 %collective-permute-done.15.low_y_ref = bf16[128,1536]{1,0:T(8,128)(2,1)S(1)} collective-permute-done((bf16[128,1536]{1,0:T(8,128)(2,1)S(1)}, bf16[128,1536]{1,0:T(8,128)(2,1)S(1)}, u32[]{:S(2)}, u32[]{:S(2)}) %collective-permute-start.15) | collective-permute-done | bytes 393248 | tf_op jit(solution)/shard_map/ppermute | solution.py:961
  167.5 12.7 %attend.3 = (bf16[256,1536]{1,0:T(8,128)(2,1)}, bf16[1536,256]{1,0:T(8,128)(2,1)}, f32[32,768]{1,0:T(8,128)}) custom-call(s32[2]{0:T(128)} %pad_add_fusion.1.info_ref, bf16[1536,512]{1,0:T(8,128)(2,1)} %q_project.1.q_ref, bf16[4,256,1024]{2,1,0:T(8,128)(2,1)} %bitcast.77, bf16[4,256,1024]{2,1,0:T(8,128)(2,1)} %bitcast.78), custom_call_target="tpu_custom_call" | custom-call | flops 644245120 | bytes 445644 | tf_op jit(solution)/shard_map/attend/pallas_call | solution.py:249
  180.2 11.4 %collective-permute-done.16.top_far_ref = bf16[256,1536]{1,0:T(8,128)(2,1)S(1)} collective-permute-done((bf16[256,1536]{1,0:T(8,128)(2,1)S(1)}, bf16[256,1536]{1,0:T(8,128)(2,1)S(1)}, u32[]{:S(2)}, u32[]{:S(2)}) %collective-permute-start.16) | collective-permute-done | bytes 786464 | tf_op jit(solution)/shard_map/ppermute | solution.py:961
  217.9 50.8 %run_experts.2 = (bf16[1024,1536]{1,0:T(8,128)(2,1)}, bf16[1024,1536]{1,0:T(8,128)(2,1)}, bf16[2048,1664]{1,0:T(8,128)(2,1)}, bf16[2048,1024]{1,0:T(8,128)(2,1)}, bf16[2048,2048]{1,0:T(8,128)(2,1)}) custom-call(s32[1]{0:T(128)} %bitcast.14.own_ref, s32[8]{0:T(128)} %fusion.10.order_ref, bf16[2048,1664]{1,0:T(8,128)(2,1)} %all-gather.7.cloned.1.call-done.xg_ref.refs_0_, ...), custom_call_target="tpu_custom_call" | custom-call | flops 3865470464 | bytes 4718592 | tf_op jit(solution)/shard_map/run_experts/pallas_call | solution.py:507
  269.0 50.8 %run_experts.3 = (bf16[1024,1536]{1,0:T(8,128)(2,1)}, bf16[1024,1536]{1,0:T(8,128)(2,1)}, bf16[2048,1664]{1,0:T(8,128)(2,1)}, bf16[2048,1024]{1,0:T(8,128)(2,1)}, bf16[2048,2048]{1,0:T(8,128)(2,1)}) custom-call(s32[1]{0:T(128)} %bitcast.14.own_ref, s32[8]{0:T(128)} %fusion.10.order_ref, bf16[2048,1664]{1,0:T(8,128)(2,1)} %all-gather.11.cloned.1.call-done.xg_ref.refs_1_, ...), custom_call_target="tpu_custom_call" | custom-call | flops 3865470464 | bytes 4718592 | tf_op jit(solution)/shard_map/run_experts/pallas_call | solution.py:507
  319.9 14.7 %down_grad.2 = bf16[1536,512]{1,0:T(8,128)(2,1)} custom-call(bf16[2048,1024]{1,0:T(8,128)(2,1)} %get-tuple-element.409.refs_0_, bf16[2048,1024]{1,0:T(8,128)(2,1)} %get-tuple-element.410.refs_1_, bf16[1024,1536]{1,0:T(8,128)(2,1)} %assemble.6.ga_ref.refs_2_, bf16[1024,1536]{1,0:T(8,128)(2,1)} %assemble.7.ga_ref.refs_3_, ...), custom_call_target="tpu_custom_call" | custom-call | flops 644245120 | bytes 1677721 | tf_op jit(solution)/shard_map/down_grad/pallas_call | solution.py:622
  338.1 15.1 %down_grad.3 = bf16[1536,512]{1,0:T(8,128)(2,1)} custom-call(bf16[2048,1024]{1,0:T(8,128)(2,1)} %get-tuple-element.409.refs_0_, bf16[2048,1024]{1,0:T(8,128)(2,1)} %get-tuple-element.410.refs_1_, bf16[1024,1536]{1,0:T(8,128)(2,1)} %assemble.6.ga_ref.refs_2_, bf16[1024,1536]{1,0:T(8,128)(2,1)} %assemble.7.ga_ref.refs_3_, ...), custom_call_target="tpu_custom_call" | custom-call | flops 644245120 | bytes 1677721 | tf_op jit(solution)/shard_map/down_grad/pallas_call | solution.py:622
  362.2 10.2 %collective-permute-done.20 = bf16[1536,512]{1,0:T(8,128)(2,1)S(1)} collective-permute-done((bf16[1536,512]{1,0:T(8,128)(2,1)}, bf16[1536,512]{1,0:T(8,128)(2,1)S(1)}, u32[]{:S(2)}, u32[]{:S(2)}) %collective-permute-start.20) | collective-permute-done | bytes 1572896 | tf_op jit(solution)/shard_map/ppermute | solution.py:949
  385.2 14.8 %wide_grad.4 = bf16[1536,512]{1,0:T(8,128)(2,1)} custom-call(bf16[2048,1664]{1,0:T(8,128)(2,1)} %all-gather.7.cloned.1.call-done.xg_ref.refs_0_, bf16[2048,1664]{1,0:T(8,128)(2,1)} %all-gather.11.cloned.1.call-done.xg_ref.refs_1_, bf16[2048,2048]{1,0:T(8,128)(2,1)} %get-tuple-element.490.refs_2_, bf16[2048,2048]{1,0:T(8,128)(2,1)} %get-tuple-element.491.refs_3_), custom_call_target="tpu_custom_call" | custom-call | flops 644245120 | bytes 1835008 | tf_op jit(solution)/shard_map/wide_grad/pallas_call | solution.py:580
  399.9 15.6 %attend_back.2 = (bf16[256,1536]{1,0:T(8,128)(2,1)}, bf16[4,2,256,512]{3,2,1,0:T(8,128)(2,1)}) custom-call(s32[2]{0:T(128)} %pad_add_fusion.info_ref, bf16[1536,512]{1,0:T(8,128)(2,1)} %q_project.1.q_ref, bf16[1536,256]{1,0:T(8,128)(2,1)} %get-tuple-element.653.g_ref, bf16[1536,256]{1,0:T(8,128)(2,1)} %get-tuple-element.436.o_ref.refs_0_, ...), custom_call_target="tpu_custom_call" | custom-call | flops 1610612736 | bytes 734003 | tf_op jit(solution)/shard_map/attend_back/pallas_call | solution.py:349
  435.9 15.5 %attend_back.3 = (bf16[256,1536]{1,0:T(8,128)(2,1)}, bf16[4,2,256,512]{3,2,1,0:T(8,128)(2,1)}) custom-call(s32[2]{0:T(128)} %pad_add_fusion.1.info_ref, bf16[1536,512]{1,0:T(8,128)(2,1)} %q_project.1.q_ref, bf16[1536,256]{1,0:T(8,128)(2,1)} %get-tuple-element.662.g_ref, bf16[1536,256]{1,0:T(8,128)(2,1)} %get-tuple-element.464.refs_1_.o_ref, ...), custom_call_target="tpu_custom_call" | custom-call | flops 1610612736 | bytes 734003 | tf_op jit(solution)/shard_map/attend_back/pallas_call | solution.py:349
  460.9 14.2 %wide_grad.5 = bf16[1536,512]{1,0:T(8,128)(2,1)} custom-call(bf16[2048,1664]{1,0:T(8,128)(2,1)} %all-gather.7.cloned.1.call-done.xg_ref.refs_0_, bf16[2048,1664]{1,0:T(8,128)(2,1)} %all-gather.11.cloned.1.call-done.xg_ref.refs_1_, bf16[2048,2048]{1,0:T(8,128)(2,1)} %get-tuple-element.490.refs_2_, bf16[2048,2048]{1,0:T(8,128)(2,1)} %get-tuple-element.491.refs_3_), custom_call_target="tpu_custom_call" | custom-call | flops 644245120 | bytes 1835008 | tf_op jit(solution)/shard_map/wide_grad/pallas_call | solution.py:580
  475.1 18.4 %collective-permute-done.23 = bf16[1536,512]{1,0:T(8,128)(2,1)} collective-permute-done((bf16[1536,512]{1,0:T(8,128)(2,1)S(1)}, bf16[1536,512]{1,0:T(8,128)(2,1)}, u32[]{:S(2)}, u32[]{:S(2)}) %collective-permute-start.23) | collective-permute-done | bytes 1572896 | tf_op jit(solution)/shard_map/ppermute | solution.py:942
  547.7 14.2 %wide_grad.7 = bf16[1536,512]{1,0:T(8,128)(2,1)} custom-call(bf16[2048,1664]{1,0:T(8,128)(2,1)} %all-gather.7.cloned.1.call-done.xg_ref.refs_0_, bf16[2048,1664]{1,0:T(8,128)(2,1)} %all-gather.11.cloned.1.call-done.xg_ref.refs_1_, bf16[2048,2048]{1,0:T(8,128)(2,1)} %get-tuple-element.490.refs_2_, bf16[2048,2048]{1,0:T(8,128)(2,1)} %get-tuple-element.491.refs_3_), custom_call_target="tpu_custom_call" | custom-call | flops 644245120 | bytes 1835008 | tf_op jit(solution)/shard_map/wide_grad/pallas_call | solution.py:580
  561.9 14.2 %wide_grad.6 = bf16[1536,512]{1,0:T(8,128)(2,1)} custom-call(bf16[2048,1664]{1,0:T(8,128)(2,1)} %all-gather.7.cloned.1.call-done.xg_ref.refs_0_, bf16[2048,1664]{1,0:T(8,128)(2,1)} %all-gather.11.cloned.1.call-done.xg_ref.refs_1_, bf16[2048,2048]{1,0:T(8,128)(2,1)} %get-tuple-element.490.refs_2_, bf16[2048,2048]{1,0:T(8,128)(2,1)} %get-tuple-element.491.refs_3_), custom_call_target="tpu_custom_call" | custom-call | flops 644245120 | bytes 1835008 | tf_op jit(solution)/shard_map/wide_grad/pallas_call | solution.py:580
  607.2 18.3 %collective-permute-done.32 = bf16[1536,512]{1,0:T(8,128)(2,1)} collective-permute-done((bf16[1536,512]{1,0:T(8,128)(2,1)}, bf16[1536,512]{1,0:T(8,128)(2,1)}, u32[]{:S(2)}, u32[]{:S(2)}) %collective-permute-start.32) | collective-permute-done | bytes 1572896 | tf_op jit(solution)/shard_map/ppermute | solution.py:942
  625.5 11.4 %projection_grads.1 = bf16[1536,2688]{1,0:T(8,128)(2,1)} custom-call(bf16[512,1536]{1,0:T(8,128)(2,1)} %get-tuple-element.641.normed_ref, bf16[256,1536]{1,0:T(8,128)(2,1)} %get-tuple-element.654.gq_ref.refs_0_, bf16[256,1536]{1,0:T(8,128)(2,1)} %get-tuple-element.663.gq_ref.refs_1_, bf16[256,1024]{1,0:T(8,128)(2,1)} %turn_back.2.dkv_ref.refs_2_, ...), custom_call_target="tpu_custom_call" | custom-call | flops 422785856 | bytes 1258291 | tf_op jit(solution)/shard_map/projection_grads/pallas_call | solution.py:875
  654.1 27.5 %collective-permute-done.34 = bf16[1536,512]{1,0:T(8,128)(2,1)} collective-permute-done((bf16[1536,512]{1,0:T(8,128)(2,1)S(1)}, bf16[1536,512]{1,0:T(8,128)(2,1)}, u32[]{:S(2)}, u32[]{:S(2)}) %collective-permute-start.34) | collective-permute-done | bytes 1572896 | tf_op jit(solution)/shard_map/ppermute | solution.py:942
  708.8 25.5 %collective-permute-done.40 = bf16[1536,512]{1,0:T(8,128)(2,1)S(1)} collective-permute-done((bf16[1536,512]{1,0:T(8,128)(2,1)S(1)}, bf16[1536,512]{1,0:T(8,128)(2,1)S(1)}, u32[]{:S(2)}, u32[]{:S(2)}) %collective-permute-start.40) | collective-permute-done | bytes 1572896 | tf_op jit(solution)/shard_map/ppermute | solution.py:947
  750.7 11.9 %collective-permute-done.46 = bf16[256,1536]{1,0:T(8,128)(2,1)S(1)} collective-permute-done((bf16[256,1536]{1,0:T(8,128)(2,1)S(1)}, bf16[256,1536]{1,0:T(8,128)(2,1)S(1)}, u32[]{:S(2)}, u32[]{:S(2)}) %collective-permute-start.46) | collective-permute-done | bytes 786464 | tf_op jit(solution)/shard_map/ppermute | solution.py:961
  765.6 41.7 %all-reduce.3.cloned.1.call-done = bf16[192,2688]{1,0:T(8,128)(2,1)} async-done(((bf16[192,2688]{1,0:T(8,128)(2,1)}), bf16[192,2688]{1,0:T(8,128)(2,1)}) %all-reduce.3.cloned.1.call-update) | async-done | bytes 1032208 | tf_op jit(solution)/shard_map/psum | solution.py:1283
  (365 shorter events, 366.1 us)
Async XLA Ops:
  7.2 93.8 %all-gather.5.cloned.1.call-start = ((), (), s32[]{:S(2)}) async-start(), calls=%async_computation.5 | async-start | bytes 2621440 | tf_op jit(solution)/shard_map/all_gather | solution.py:1163
  55.2 112.3 %all-gather.9.cloned.1.call-start = ((), (), s32[]{:S(2)}) async-start(), calls=%async_computation.7 | async-start | bytes 2621440 | tf_op jit(solution)/shard_map/all_gather | solution.py:1163
  106.7 111.2 %all-gather.7.cloned.1.call-start = ((), (), s32[]{:S(2)}) async-start(), calls=%async_computation.6 | async-start | bytes 7667712 | tf_op jit(solution)/shard_map/all_gather | solution.py:965
  164.2 104.9 %all-gather.11.cloned.1.call-start = ((), (), s32[]{:S(2)}) async-start(), calls=%async_computation.8 | async-start | bytes 7667712 | tf_op jit(solution)/shard_map/all_gather | solution.py:965
  200.2 153.0 %reduce-scatter.6.cloned.1.call-start = ((), (), s32[]{:S(2)}) async-start(), calls=%async_computation.9 | async-start | bytes 7667712 | tf_op jit(solution)/shard_map/reduce_scatter | solution.py:1092
  268.8 158.3 %reduce-scatter.8.cloned.1.call-start = ((), (), s32[]{:S(2)}) async-start(), calls=%async_computation.10 | async-start | bytes 7667712 | tf_op jit(solution)/shard_map/reduce_scatter | solution.py:1092
  319.9 174.6 %reduce-scatter.10.cloned.1.call-start = ((), (), s32[]{:S(2)}) async-start(), calls=%async_computation.11 | async-start | bytes 2621440 | tf_op jit(solution)/shard_map/reduce_scatter | solution.py:1233
  334.6 37.7 %collective-permute-start.20 = (bf16[1536,512]{1,0:T(8,128)(2,1)}, bf16[1536,512]{1,0:T(8,128)(2,1)S(1)}, u32[]{:S(2)}, u32[]{:S(2)}) collective-permute-start(bf16[1536,512]{1,0:T(8,128)(2,1)} %down_grad.2), channel_id=1, source_target_pairs={{0,8},{24,16},{1,9},{25,17},{2,10},{26,18},{3,11},{27,19},{4,12},{... | collective-permute-start | bytes 4718600 | tf_op jit(solution)/shard_map/ppermute | solution.py:949
  375.9 39.6 %collective-permute-start.22 = (bf16[1536,512]{1,0:T(8,128)(2,1)S(1)}, bf16[1536,512]{1,0:T(8,128)(2,1)}, u32[]{:S(2)}, u32[]{:S(2)}) collective-permute-start(bf16[1536,512]{1,0:T(8,128)(2,1)S(1)} %add_convert_fusion.14), channel_id=1, source_target_pairs={{8,16},{16,8},{9,17},{17,9},{10,18},{18,10},{11,19},{19,11},{12,20... | collective-permute-start | bytes 4718600 | tf_op jit(solution)/shard_map/ppermute | solution.py:939
  377.8 38.9 %collective-permute-start.21 = (bf16[1536,512]{1,0:T(8,128)(2,1)S(1)}, bf16[1536,512]{1,0:T(8,128)(2,1)}, u32[]{:S(2)}, u32[]{:S(2)}) collective-permute-start(bf16[1536,512]{1,0:T(8,128)(2,1)S(1)} %copy-done.24), channel_id=1, source_target_pairs={{0,8},{24,16},{1,9},{25,17},{2,10},{26,18},{3,11},{27,19},{4,12},{... | collective-permute-start | bytes 4718600 | tf_op jit(solution)/shard_map/ppermute | solution.py:949
  416.6 161.6 %reduce-scatter.12.cloned.1.call-start = ((), (), s32[]{:S(2)}) async-start(), calls=%async_computation.12 | async-start | bytes 2621440 | tf_op jit(solution)/shard_map/reduce_scatter | solution.py:1233
  419.9 55.2 %collective-permute-start.24 = (bf16[1536,512]{1,0:T(8,128)(2,1)}, bf16[1536,512]{1,0:T(8,128)(2,1)}, u32[]{:S(2)}, u32[]{:S(2)}) collective-permute-start(bf16[1536,512]{1,0:T(8,128)(2,1)} %add_convert_fusion.12), channel_id=1, source_target_pairs={{8,16},{16,8},{9,17},{17,9},{10,18},{18,10},{11,19},{19,11},{12,20... | collective-permute-start | bytes 4718600 | tf_op jit(solution)/shard_map/ppermute | solution.py:939
  423.8 69.7 %collective-permute-start.23 = (bf16[1536,512]{1,0:T(8,128)(2,1)S(1)}, bf16[1536,512]{1,0:T(8,128)(2,1)}, u32[]{:S(2)}, u32[]{:S(2)}) collective-permute-start(bf16[1536,512]{1,0:T(8,128)(2,1)S(1)} %fusion), channel_id=1, source_target_pairs={{0,8},{24,16},{8,0},{16,24},{1,9},{25,17},{9,1},{17,25},{2,10},{26... | collective-permute-start | bytes 4718600 | tf_op jit(solution)/shard_map/ppermute | solution.py:942
  494.6 247.1 %reduce-scatter.14.cloned.1.call-start = ((), (), s32[]{:S(2)}) async-start(), calls=%async_computation.13 | async-start | bytes 9289728 | tf_op jit(solution)/shard_map/reduce_scatter | solution.py:1092
  497.8 78.3 %collective-permute-start.26 = (bf16[1536,512]{1,0:T(8,128)(2,1)}, bf16[1536,512]{1,0:T(8,128)(2,1)}, u32[]{:S(2)}, u32[]{:S(2)}) collective-permute-start(bf16[1536,512]{1,0:T(8,128)(2,1)} %add_convert_fusion.10), channel_id=1, source_target_pairs={{8,16},{16,8},{9,17},{17,9},{10,18},{18,10},{11,19},{19,11},{12,20... | collective-permute-start | bytes 4718600 | tf_op jit(solution)/shard_map/ppermute | solution.py:939
  508.5 67.5 %collective-permute-start.25 = (bf16[1536,512]{1,0:T(8,128)(2,1)S(1)}, bf16[1536,512]{1,0:T(8,128)(2,1)}, u32[]{:S(2)}, u32[]{:S(2)}) collective-permute-start(bf16[1536,512]{1,0:T(8,128)(2,1)S(1)} %fusion.1), channel_id=1, source_target_pairs={{0,8},{24,16},{8,0},{16,24},{1,9},{25,17},{9,1},{17,25},{2,10},{26... | collective-permute-start | bytes 4718600 | tf_op jit(solution)/shard_map/ppermute | solution.py:942
  534.4 41.7 %collective-permute-start.31 = (bf16[96,1536]{1,0:T(8,128)(2,1)S(1)}, bf16[96,1536]{1,0:T(8,128)(2,1)}, u32[]{:S(2)}, u32[]{:S(2)}) collective-permute-start(bf16[96,1536]{1,0:T(8,128)(2,1)S(1)} %get-tuple-element.773), channel_id=1, source_target_pairs={{0,4},{1,5},{2,6},{3,7},{4,0},{5,1},{6,2},{7,3},{8,12},{9,13},{10,... | collective-permute-start | bytes 884744 | tf_op jit(solution)/shard_map/ppermute | solution.py:961
  636.9 170.3 %all-reduce.3.cloned.1.call-start = ((), (), s32[]{:S(2)}) async-start(), calls=%async_computation.14 | async-start | bytes 2064384 | tf_op jit(solution)/shard_map/psum | solution.py:1283
  636.9 44.6 %collective-permute-start.36 = (bf16[1024,1536]{1,0:T(8,128)(2,1)}, bf16[1024,1536]{1,0:T(8,128)(2,1)}, u32[]{:S(2)}, u32[]{:S(2)}) collective-permute-start(bf16[1024,1536]{1,0:T(8,128)(2,1)} %get-tuple-element.604), channel_id=1, source_target_pairs={{0,1},{1,0},{2,3},{3,2},{4,5},{5,4},{6,7},{7,6},{8,9},{9,8},{10,11... | collective-permute-start | bytes 9437192 | tf_op jit(solution)/shard_map/ppermute | solution.py:961
  637.0 48.4 %collective-permute-start.37 = (bf16[1024,1536]{1,0:T(8,128)(2,1)}, bf16[1024,1536]{1,0:T(8,128)(2,1)}, u32[]{:S(2)}, u32[]{:S(2)}) collective-permute-start(bf16[1024,1536]{1,0:T(8,128)(2,1)} %get-tuple-element.606), channel_id=1, source_target_pairs={{0,1},{1,0},{2,3},{3,2},{4,5},{5,4},{6,7},{7,6},{8,9},{9,8},{10,11... | collective-permute-start | bytes 9437192 | tf_op jit(solution)/shard_map/ppermute | solution.py:961
  692.3 46.2 %collective-permute-start.41 = (bf16[512,1536]{1,0:T(8,128)(2,1)S(1)}, bf16[512,1536]{1,0:T(8,128)(2,1)S(1)}, u32[]{:S(2)}, u32[]{:S(2)}) collective-permute-start(bf16[512,1536]{1,0:T(8,128)(2,1)S(1)} %pad_maximum_fusion), channel_id=1, source_target_pairs={{0,4},{1,5},{2,6},{3,7},{4,0},{5,1},{6,2},{7,3},{8,12},{9,13},{10,... | collective-permute-start | bytes 4718600 | tf_op jit(solution)/shard_map/ppermute | solution.py:961
  694.0 45.8 %collective-permute-start.42 = (bf16[512,1536]{1,0:T(8,128)(2,1)S(1)}, bf16[512,1536]{1,0:T(8,128)(2,1)S(1)}, u32[]{:S(2)}, u32[]{:S(2)}) collective-permute-start(bf16[512,1536]{1,0:T(8,128)(2,1)S(1)} %pad_maximum_fusion.1), channel_id=1, source_target_pairs={{0,2},{1,3},{2,0},{3,1},{4,6},{5,7},{6,4},{7,5},{8,10},{9,11},{10,... | collective-permute-start | bytes 4718600 | tf_op jit(solution)/shard_map/ppermute | solution.py:961
  743.9 69.1 %collective-permute-start.43 = (bf16[192,1536]{1,0:T(8,128)(2,1)}, bf16[192,1536]{1,0:T(8,128)(2,1)}, u32[]{:S(2)}, u32[]{:S(2)}) collective-permute-start(bf16[192,1536]{1,0:T(8,128)(2,1)} %add_convert_fusion.16), channel_id=1, source_target_pairs={{8,16},{16,8},{9,17},{17,9},{10,18},{18,10},{11,19},{19,11},{12,20... | collective-permute-start | bytes 1769480 | tf_op jit(solution)/shard_map/ppermute | solution.py:939
  749.4 66.4 %collective-permute-start.44 = (bf16[1536,512]{1,0:T(8,128)(2,1)}, bf16[1536,512]{1,0:T(8,128)(2,1)}, u32[]{:S(2)}, u32[]{:S(2)}) collective-permute-start(bf16[1536,512]{1,0:T(8,128)(2,1)} %add_convert_fusion.3), channel_id=1, source_target_pairs={{8,0},{16,24},{9,1},{17,25},{10,2},{18,26},{11,3},{19,27},{12,4},{... | collective-permute-start | bytes 4718600 | tf_op jit(solution)/shard_map/ppermute | solution.py:947
  (102 other events, 1261.8 us)
Sparse Core Ops, SparseCore 0:
  55.3 45.6 all-gather.4
  106.8 45.1 all-gather.8
  164.3 53.5 all-gather.6
  220.2 47.7 all-gather.10
  271.3 64.2 reduce-scatter.5
  339.3 64.2 reduce-scatter.7
  416.8 77.6 reduce-scatter.9
  496.8 73.5 reduce-scatter.11
  637.0 84.2 reduce-scatter.13
  741.8 65.3 all-reduce.2

commit v7 on v6

--- a/solution.py
+++ b/solution.py
@@ -1307,7 +1307,7 @@
         if t == 4:
             normed_one, line.held = lax.optimization_barrier((normed_one, line.held))
             rest = scatter_rows(rest_grads())
-    rest = rest.astype(F32)
+    rest = gate(rest, line.results).astype(F32)
     totals = line.sums()
     for i in range(len(experts_out), 3):
         experts_out.append(widen(totals[i * experts : (i + 1) * experts], i == 0))

time: 853 us -> 858 us (level)
  waiting for transfers between devices: 278 us -> 289 us
    ppermute x3, waiting for transfers between devices: 32.9 us -> 84.6 us  [step(): self.results.append((summed, lax.ppermute(summed, 'seq', go)))]
    psum x1, waiting for transfers between devices: 41.7 us -> 0.01 us  [on_device(): rest = lax.psum(found[0].pop('rest'), 'seq')]
  transfers between devices with their start and end apart: 58 -> 58, of which waited for: 36 -> 36; matrix products, arithmetic and copies ran while one was open for 11% -> 10% of each run, Pallas kernels for 39% -> 38%
where the time goes in v7:
time: 858 us; the launch traced here: 846 us
  Pallas kernels  355 us (41%)
  waiting for transfers between devices  289 us (34%)
  other arithmetic  82.3 us (10%)
  starting transfers between devices  76.6 us (9%)
  local copies, waits for them, and re-layouts  27.5 us (3%)
  between operations  15.6 us (2%)
    ppermute x31, waiting for transfers between devices, swap(): return lax.ppermute(x, 'fsdp', [(i, i ^ mask) for i in range(8)])  122 us
    pallas_call x2, Pallas kernels, run_experts(): pl.pallas_call(functools.partial(expert_kernel, experts, half), name='run...  102 us
    ppermute x3, waiting for transfers between devices, step(): self.results.append((summed, lax.ppermute(summed, 'seq', go)))  84.6 us
    ppermute x4, waiting for transfers between devices, step(): got = lax.ppermute(sent, 'seq', come + go)  65.1 us
    pallas_call x4, Pallas kernels, wide_grad(): pl.pallas_call(functools.partial(wide_grad_kernel, steps, micros), name='...  57.2 us
    ppermute x31, starting transfers between devices, swap(): return lax.ppermute(x, 'fsdp', [(i, i ^ mask) for i in range(8)])  34.1 us
    convert_element_type x19, other arithmetic, add_low(): return (a.astype(F32) + b.astype(F32)).astype(BF)  32.4 us
    pallas_call x2, Pallas kernels, attend_back(): pl.pallas_call(functools.partial(attend_back_kernel, n), name='attend_bac...  31.1 us
  transfers between devices with their start and end apart: 58, of which 36 were waited for; matrix products, arithmetic and copies ran while one was open for 10% of the time, Pallas kernels for 38%

profile of v7, /device:TPU:0, one launch (start us, length us, event | category | flops | bytes accessed | tf_op | source)
XLA Modules:
  0.0 846.3 jit_solution(9034952974208845216)
XLA Ops:
  55.2 11.8 %collective-permute-done.6.low_y_ref = bf16[96,3072]{1,0:T(8,128)(2,1)S(1)} collective-permute-done((bf16[96,3072]{1,0:T(8,128)(2,1)S(1)}, bf16[96,3072]{1,0:T(8,128)(2,1)S(1)}, u32[]{:S(2)}, u32[]{:S(2)}) %collective-permute-start.6) | collective-permute-done | bytes 589856 | tf_op jit(solution)/shard_map/ppermute | solution.py:961
  79.2 17.2 %collective-permute-done.7.top_far_ref = bf16[192,3072]{1,0:T(8,128)(2,1)S(1)} collective-permute-done((bf16[192,3072]{1,0:T(8,128)(2,1)}, bf16[192,3072]{1,0:T(8,128)(2,1)S(1)}, u32[]{:S(2)}, u32[]{:S(2)}) %collective-permute-start.7) | collective-permute-done | bytes 1179680 | tf_op jit(solution)/shard_map/ppermute | solution.py:961
  132.7 12.7 %attend.2 = (bf16[256,1536]{1,0:T(8,128)(2,1)}, bf16[1536,256]{1,0:T(8,128)(2,1)}, f32[32,768]{1,0:T(8,128)}) custom-call(s32[2]{0:T(128)} %pad_add_fusion.info_ref, bf16[1536,512]{1,0:T(8,128)(2,1)} %q_project.1.q_ref, bf16[4,256,1024]{2,1,0:T(8,128)(2,1)} %bitcast.73, bf16[4,256,1024]{2,1,0:T(8,128)(2,1)} %bitcast.74), custom_call_target="tpu_custom_call" | custom-call | flops 644245120 | bytes 445644 | tf_op jit(solution)/shard_map/attend/pallas_call | solution.py:249
  145.3 9.8 %collective-permute-done.15.low_y_ref = bf16[128,1536]{1,0:T(8,128)(2,1)S(1)} collective-permute-done((bf16[128,1536]{1,0:T(8,128)(2,1)S(1)}, bf16[128,1536]{1,0:T(8,128)(2,1)S(1)}, u32[]{:S(2)}, u32[]{:S(2)}) %collective-permute-start.15) | collective-permute-done | bytes 393248 | tf_op jit(solution)/shard_map/ppermute | solution.py:961
  167.4 12.7 %attend.3 = (bf16[256,1536]{1,0:T(8,128)(2,1)}, bf16[1536,256]{1,0:T(8,128)(2,1)}, f32[32,768]{1,0:T(8,128)}) custom-call(s32[2]{0:T(128)} %pad_add_fusion.1.info_ref, bf16[1536,512]{1,0:T(8,128)(2,1)} %q_project.1.q_ref, bf16[4,256,1024]{2,1,0:T(8,128)(2,1)} %bitcast.77, bf16[4,256,1024]{2,1,0:T(8,128)(2,1)} %bitcast.78), custom_call_target="tpu_custom_call" | custom-call | flops 644245120 | bytes 445644 | tf_op jit(solution)/shard_map/attend/pallas_call | solution.py:249
  180.1 11.5 %collective-permute-done.16.top_far_ref = bf16[256,1536]{1,0:T(8,128)(2,1)S(1)} collective-permute-done((bf16[256,1536]{1,0:T(8,128)(2,1)S(1)}, bf16[256,1536]{1,0:T(8,128)(2,1)S(1)}, u32[]{:S(2)}, u32[]{:S(2)}) %collective-permute-start.16) | collective-permute-done | bytes 786464 | tf_op jit(solution)/shard_map/ppermute | solution.py:961
  217.9 50.8 %run_experts.2 = (bf16[1024,1536]{1,0:T(8,128)(2,1)}, bf16[1024,1536]{1,0:T(8,128)(2,1)}, bf16[2048,1664]{1,0:T(8,128)(2,1)}, bf16[2048,1024]{1,0:T(8,128)(2,1)}, bf16[2048,2048]{1,0:T(8,128)(2,1)}) custom-call(s32[1]{0:T(128)} %bitcast.14.own_ref, s32[8]{0:T(128)} %fusion.10.order_ref, bf16[2048,1664]{1,0:T(8,128)(2,1)} %all-gather.7.cloned.1.call-done.xg_ref.refs_0_, ...), custom_call_target="tpu_custom_call" | custom-call | flops 3865470464 | bytes 4718592 | tf_op jit(solution)/shard_map/run_experts/pallas_call | solution.py:507
  269.0 50.8 %run_experts.3 = (bf16[1024,1536]{1,0:T(8,128)(2,1)}, bf16[1024,1536]{1,0:T(8,128)(2,1)}, bf16[2048,1664]{1,0:T(8,128)(2,1)}, bf16[2048,1024]{1,0:T(8,128)(2,1)}, bf16[2048,2048]{1,0:T(8,128)(2,1)}) custom-call(s32[1]{0:T(128)} %bitcast.14.own_ref, s32[8]{0:T(128)} %fusion.10.order_ref, bf16[2048,1664]{1,0:T(8,128)(2,1)} %all-gather.11.cloned.1.call-done.xg_ref.refs_1_, ...), custom_call_target="tpu_custom_call" | custom-call | flops 3865470464 | bytes 4718592 | tf_op jit(solution)/shard_map/run_experts/pallas_call | solution.py:507
  319.9 14.7 %down_grad.2 = bf16[1536,512]{1,0:T(8,128)(2,1)} custom-call(bf16[2048,1024]{1,0:T(8,128)(2,1)} %get-tuple-element.410.refs_0_, bf16[2048,1024]{1,0:T(8,128)(2,1)} %get-tuple-element.411.refs_1_, bf16[1024,1536]{1,0:T(8,128)(2,1)} %assemble.6.ga_ref.refs_2_, bf16[1024,1536]{1,0:T(8,128)(2,1)} %assemble.7.ga_ref.refs_3_, ...), custom_call_target="tpu_custom_call" | custom-call | flops 644245120 | bytes 1677721 | tf_op jit(solution)/shard_map/down_grad/pallas_call | solution.py:622
  338.1 15.1 %down_grad.3 = bf16[1536,512]{1,0:T(8,128)(2,1)} custom-call(bf16[2048,1024]{1,0:T(8,128)(2,1)} %get-tuple-element.410.refs_0_, bf16[2048,1024]{1,0:T(8,128)(2,1)} %get-tuple-element.411.refs_1_, bf16[1024,1536]{1,0:T(8,128)(2,1)} %assemble.6.ga_ref.refs_2_, bf16[1024,1536]{1,0:T(8,128)(2,1)} %assemble.7.ga_ref.refs_3_, ...), custom_call_target="tpu_custom_call" | custom-call | flops 644245120 | bytes 1677721 | tf_op jit(solution)/shard_map/down_grad/pallas_call | solution.py:622
  362.1 10.2 %collective-permute-done.20 = bf16[1536,512]{1,0:T(8,128)(2,1)S(1)} collective-permute-done((bf16[1536,512]{1,0:T(8,128)(2,1)}, bf16[1536,512]{1,0:T(8,128)(2,1)S(1)}, u32[]{:S(2)}, u32[]{:S(2)}) %collective-permute-start.20) | collective-permute-done | bytes 1572896 | tf_op jit(solution)/shard_map/ppermute | solution.py:949
  385.2 14.8 %wide_grad.4 = bf16[1536,512]{1,0:T(8,128)(2,1)} custom-call(bf16[2048,1664]{1,0:T(8,128)(2,1)} %all-gather.7.cloned.1.call-done.xg_ref.refs_0_, bf16[2048,1664]{1,0:T(8,128)(2,1)} %all-gather.11.cloned.1.call-done.xg_ref.refs_1_, bf16[2048,2048]{1,0:T(8,128)(2,1)} %get-tuple-element.491.refs_2_, bf16[2048,2048]{1,0:T(8,128)(2,1)} %get-tuple-element.492.refs_3_), custom_call_target="tpu_custom_call" | custom-call | flops 644245120 | bytes 1835008 | tf_op jit(solution)/shard_map/wide_grad/pallas_call | solution.py:580
  399.9 15.6 %attend_back.2 = (bf16[256,1536]{1,0:T(8,128)(2,1)}, bf16[4,2,256,512]{3,2,1,0:T(8,128)(2,1)}) custom-call(s32[2]{0:T(128)} %pad_add_fusion.info_ref, bf16[1536,512]{1,0:T(8,128)(2,1)} %q_project.1.q_ref, bf16[1536,256]{1,0:T(8,128)(2,1)} %get-tuple-element.654.g_ref, bf16[1536,256]{1,0:T(8,128)(2,1)} %get-tuple-element.437.o_ref.refs_0_, ...), custom_call_target="tpu_custom_call" | custom-call | flops 1610612736 | bytes 734003 | tf_op jit(solution)/shard_map/attend_back/pallas_call | solution.py:349
  435.8 15.6 %attend_back.3 = (bf16[256,1536]{1,0:T(8,128)(2,1)}, bf16[4,2,256,512]{3,2,1,0:T(8,128)(2,1)}) custom-call(s32[2]{0:T(128)} %pad_add_fusion.1.info_ref, bf16[1536,512]{1,0:T(8,128)(2,1)} %q_project.1.q_ref, bf16[1536,256]{1,0:T(8,128)(2,1)} %get-tuple-element.663.g_ref, bf16[1536,256]{1,0:T(8,128)(2,1)} %get-tuple-element.465.refs_1_.o_ref, ...), custom_call_target="tpu_custom_call" | custom-call | flops 1610612736 | bytes 734003 | tf_op jit(solution)/shard_map/attend_back/pallas_call | solution.py:349
  460.9 14.2 %wide_grad.5 = bf16[1536,512]{1,0:T(8,128)(2,1)} custom-call(bf16[2048,1664]{1,0:T(8,128)(2,1)} %all-gather.7.cloned.1.call-done.xg_ref.refs_0_, bf16[2048,1664]{1,0:T(8,128)(2,1)} %all-gather.11.cloned.1.call-done.xg_ref.refs_1_, bf16[2048,2048]{1,0:T(8,128)(2,1)} %get-tuple-element.491.refs_2_, bf16[2048,2048]{1,0:T(8,128)(2,1)} %get-tuple-element.492.refs_3_), custom_call_target="tpu_custom_call" | custom-call | flops 644245120 | bytes 1835008 | tf_op jit(solution)/shard_map/wide_grad/pallas_call | solution.py:580
  475.0 18.3 %collective-permute-done.23 = bf16[1536,512]{1,0:T(8,128)(2,1)} collective-permute-done((bf16[1536,512]{1,0:T(8,128)(2,1)S(1)}, bf16[1536,512]{1,0:T(8,128)(2,1)}, u32[]{:S(2)}, u32[]{:S(2)}) %collective-permute-start.23) | collective-permute-done | bytes 1572896 | tf_op jit(solution)/shard_map/ppermute | solution.py:942
  544.9 14.1 %wide_grad.7 = bf16[1536,512]{1,0:T(8,128)(2,1)} custom-call(bf16[2048,1664]{1,0:T(8,128)(2,1)} %all-gather.7.cloned.1.call-done.xg_ref.refs_0_, bf16[2048,1664]{1,0:T(8,128)(2,1)} %all-gather.11.cloned.1.call-done.xg_ref.refs_1_, bf16[2048,2048]{1,0:T(8,128)(2,1)} %get-tuple-element.491.refs_2_, bf16[2048,2048]{1,0:T(8,128)(2,1)} %get-tuple-element.492.refs_3_), custom_call_target="tpu_custom_call" | custom-call | flops 644245120 | bytes 1835008 | tf_op jit(solution)/shard_map/wide_grad/pallas_call | solution.py:580
  559.1 14.2 %wide_grad.6 = bf16[1536,512]{1,0:T(8,128)(2,1)} custom-call(bf16[2048,1664]{1,0:T(8,128)(2,1)} %all-gather.7.cloned.1.call-done.xg_ref.refs_0_, bf16[2048,1664]{1,0:T(8,128)(2,1)} %all-gather.11.cloned.1.call-done.xg_ref.refs_1_, bf16[2048,2048]{1,0:T(8,128)(2,1)} %get-tuple-element.491.refs_2_, bf16[2048,2048]{1,0:T(8,128)(2,1)} %get-tuple-element.492.refs_3_), custom_call_target="tpu_custom_call" | custom-call | flops 644245120 | bytes 1835008 | tf_op jit(solution)/shard_map/wide_grad/pallas_call | solution.py:580
  606.6 18.3 %collective-permute-done.32 = bf16[1536,512]{1,0:T(8,128)(2,1)} collective-permute-done((bf16[1536,512]{1,0:T(8,128)(2,1)}, bf16[1536,512]{1,0:T(8,128)(2,1)}, u32[]{:S(2)}, u32[]{:S(2)}) %collective-permute-start.32) | collective-permute-done | bytes 1572896 | tf_op jit(solution)/shard_map/ppermute | solution.py:942
  624.9 11.4 %projection_grads.1 = bf16[1536,2688]{1,0:T(8,128)(2,1)} custom-call(bf16[512,1536]{1,0:T(8,128)(2,1)} %get-tuple-element.642.normed_ref, bf16[256,1536]{1,0:T(8,128)(2,1)} %get-tuple-element.655.gq_ref.refs_0_, bf16[256,1536]{1,0:T(8,128)(2,1)} %get-tuple-element.664.gq_ref.refs_1_, bf16[256,1024]{1,0:T(8,128)(2,1)} %turn_back.2.dkv_ref.refs_2_, ...), custom_call_target="tpu_custom_call" | custom-call | flops 422785856 | bytes 1258291 | tf_op jit(solution)/shard_map/projection_grads/pallas_call | solution.py:875
  653.5 27.5 %collective-permute-done.34 = bf16[1536,512]{1,0:T(8,128)(2,1)} collective-permute-done((bf16[1536,512]{1,0:T(8,128)(2,1)S(1)}, bf16[1536,512]{1,0:T(8,128)(2,1)}, u32[]{:S(2)}, u32[]{:S(2)}) %collective-permute-start.34) | collective-permute-done | bytes 1572896 | tf_op jit(solution)/shard_map/ppermute | solution.py:942
  708.2 25.5 %collective-permute-done.40 = bf16[1536,512]{1,0:T(8,128)(2,1)S(1)} collective-permute-done((bf16[1536,512]{1,0:T(8,128)(2,1)S(1)}, bf16[1536,512]{1,0:T(8,128)(2,1)S(1)}, u32[]{:S(2)}, u32[]{:S(2)}) %collective-permute-start.40) | collective-permute-done | bytes 1572896 | tf_op jit(solution)/shard_map/ppermute | solution.py:947
  748.2 11.1 %collective-permute-done.46 = bf16[256,1536]{1,0:T(8,128)(2,1)S(1)} collective-permute-done((bf16[256,1536]{1,0:T(8,128)(2,1)S(1)}, bf16[256,1536]{1,0:T(8,128)(2,1)S(1)}, u32[]{:S(2)}, u32[]{:S(2)}) %collective-permute-start.46) | collective-permute-done | bytes 786464 | tf_op jit(solution)/shard_map/ppermute | solution.py:961
  761.6 53.4 %collective-permute-done.44 = bf16[1536,512]{1,0:T(8,128)(2,1)S(1)} collective-permute-done((bf16[1536,512]{1,0:T(8,128)(2,1)S(1)}, bf16[1536,512]{1,0:T(8,128)(2,1)S(1)}, u32[]{:S(2)}, u32[]{:S(2)}) %collective-permute-start.44) | collective-permute-done | bytes 1572896 | tf_op jit(solution)/shard_map/ppermute | solution.py:947
  (353 shorter events, 359.7 us)
Async XLA Ops:
  7.2 93.7 %all-gather.5.cloned.1.call-start = ((), (), s32[]{:S(2)}) async-start(), calls=%async_computation.5 | async-start | bytes 2621440 | tf_op jit(solution)/shard_map/all_gather | solution.py:1163
  55.1 112.3 %all-gather.9.cloned.1.call-start = ((), (), s32[]{:S(2)}) async-start(), calls=%async_computation.7 | async-start | bytes 2621440 | tf_op jit(solution)/shard_map/all_gather | solution.py:1163
  106.7 111.2 %all-gather.7.cloned.1.call-start = ((), (), s32[]{:S(2)}) async-start(), calls=%async_computation.6 | async-start | bytes 7667712 | tf_op jit(solution)/shard_map/all_gather | solution.py:965
  164.1 104.9 %all-gather.11.cloned.1.call-start = ((), (), s32[]{:S(2)}) async-start(), calls=%async_computation.8 | async-start | bytes 7667712 | tf_op jit(solution)/shard_map/all_gather | solution.py:965
  200.2 153.0 %reduce-scatter.6.cloned.1.call-start = ((), (), s32[]{:S(2)}) async-start(), calls=%async_computation.9 | async-start | bytes 7667712 | tf_op jit(solution)/shard_map/reduce_scatter | solution.py:1092
  268.7 158.3 %reduce-scatter.8.cloned.1.call-start = ((), (), s32[]{:S(2)}) async-start(), calls=%async_computation.10 | async-start | bytes 7667712 | tf_op jit(solution)/shard_map/reduce_scatter | solution.py:1092
  319.8 174.6 %reduce-scatter.10.cloned.1.call-start = ((), (), s32[]{:S(2)}) async-start(), calls=%async_computation.11 | async-start | bytes 2621440 | tf_op jit(solution)/shard_map/reduce_scatter | solution.py:1233
  334.5 37.8 %collective-permute-start.20 = (bf16[1536,512]{1,0:T(8,128)(2,1)}, bf16[1536,512]{1,0:T(8,128)(2,1)S(1)}, u32[]{:S(2)}, u32[]{:S(2)}) collective-permute-start(bf16[1536,512]{1,0:T(8,128)(2,1)} %down_grad.2), channel_id=1, source_target_pairs={{0,8},{24,16},{1,9},{25,17},{2,10},{26,18},{3,11},{27,19},{4,12},{... | collective-permute-start | bytes 4718600 | tf_op jit(solution)/shard_map/ppermute | solution.py:949
  375.9 39.6 %collective-permute-start.22 = (bf16[1536,512]{1,0:T(8,128)(2,1)S(1)}, bf16[1536,512]{1,0:T(8,128)(2,1)}, u32[]{:S(2)}, u32[]{:S(2)}) collective-permute-start(bf16[1536,512]{1,0:T(8,128)(2,1)S(1)} %add_convert_fusion.14), channel_id=1, source_target_pairs={{8,16},{16,8},{9,17},{17,9},{10,18},{18,10},{11,19},{19,11},{12,20... | collective-permute-start | bytes 4718600 | tf_op jit(solution)/shard_map/ppermute | solution.py:939
  377.7 38.9 %collective-permute-start.21 = (bf16[1536,512]{1,0:T(8,128)(2,1)S(1)}, bf16[1536,512]{1,0:T(8,128)(2,1)}, u32[]{:S(2)}, u32[]{:S(2)}) collective-permute-start(bf16[1536,512]{1,0:T(8,128)(2,1)S(1)} %copy-done.24), channel_id=1, source_target_pairs={{0,8},{24,16},{1,9},{25,17},{2,10},{26,18},{3,11},{27,19},{4,12},{... | collective-permute-start | bytes 4718600 | tf_op jit(solution)/shard_map/ppermute | solution.py:949
  416.6 159.7 %reduce-scatter.12.cloned.1.call-start = ((), (), s32[]{:S(2)}) async-start(), calls=%async_computation.12 | async-start | bytes 2621440 | tf_op jit(solution)/shard_map/reduce_scatter | solution.py:1233
  419.8 55.2 %collective-permute-start.24 = (bf16[1536,512]{1,0:T(8,128)(2,1)}, bf16[1536,512]{1,0:T(8,128)(2,1)}, u32[]{:S(2)}, u32[]{:S(2)}) collective-permute-start(bf16[1536,512]{1,0:T(8,128)(2,1)} %add_convert_fusion.12), channel_id=1, source_target_pairs={{8,16},{16,8},{9,17},{17,9},{10,18},{18,10},{11,19},{19,11},{12,20... | collective-permute-start | bytes 4718600 | tf_op jit(solution)/shard_map/ppermute | solution.py:939
  423.8 69.5 %collective-permute-start.23 = (bf16[1536,512]{1,0:T(8,128)(2,1)S(1)}, bf16[1536,512]{1,0:T(8,128)(2,1)}, u32[]{:S(2)}, u32[]{:S(2)}) collective-permute-start(bf16[1536,512]{1,0:T(8,128)(2,1)S(1)} %fusion), channel_id=1, source_target_pairs={{0,8},{24,16},{8,0},{16,24},{1,9},{25,17},{9,1},{17,25},{2,10},{26... | collective-permute-start | bytes 4718600 | tf_op jit(solution)/shard_map/ppermute | solution.py:942
  494.6 246.4 %reduce-scatter.14.cloned.1.call-start = ((), (), s32[]{:S(2)}) async-start(), calls=%async_computation.13 | async-start | bytes 9289728 | tf_op jit(solution)/shard_map/reduce_scatter | solution.py:1092
  497.8 75.4 %collective-permute-start.26 = (bf16[1536,512]{1,0:T(8,128)(2,1)}, bf16[1536,512]{1,0:T(8,128)(2,1)}, u32[]{:S(2)}, u32[]{:S(2)}) collective-permute-start(bf16[1536,512]{1,0:T(8,128)(2,1)} %add_convert_fusion.10), channel_id=1, source_target_pairs={{8,16},{16,8},{9,17},{17,9},{10,18},{18,10},{11,19},{19,11},{12,20... | collective-permute-start | bytes 4718600 | tf_op jit(solution)/shard_map/ppermute | solution.py:939
  507.0 67.2 %collective-permute-start.25 = (bf16[1536,512]{1,0:T(8,128)(2,1)S(1)}, bf16[1536,512]{1,0:T(8,128)(2,1)}, u32[]{:S(2)}, u32[]{:S(2)}) collective-permute-start(bf16[1536,512]{1,0:T(8,128)(2,1)S(1)} %fusion.1), channel_id=1, source_target_pairs={{0,8},{24,16},{8,0},{16,24},{1,9},{25,17},{9,1},{17,25},{2,10},{26... | collective-permute-start | bytes 4718600 | tf_op jit(solution)/shard_map/ppermute | solution.py:942
  532.0 42.2 %collective-permute-start.31 = (bf16[96,1536]{1,0:T(8,128)(2,1)S(1)}, bf16[96,1536]{1,0:T(8,128)(2,1)}, u32[]{:S(2)}, u32[]{:S(2)}) collective-permute-start(bf16[96,1536]{1,0:T(8,128)(2,1)S(1)} %get-tuple-element.775), channel_id=1, source_target_pairs={{0,4},{1,5},{2,6},{3,7},{4,0},{5,1},{6,2},{7,3},{8,12},{9,13},{10,... | collective-permute-start | bytes 884744 | tf_op jit(solution)/shard_map/ppermute | solution.py:961
  587.3 37.6 %collective-permute-start.32 = (bf16[1536,512]{1,0:T(8,128)(2,1)}, bf16[1536,512]{1,0:T(8,128)(2,1)}, u32[]{:S(2)}, u32[]{:S(2)}) collective-permute-start(bf16[1536,512]{1,0:T(8,128)(2,1)} %fusion.2), channel_id=1, source_target_pairs={{0,8},{24,16},{8,0},{16,24},{1,9},{25,17},{9,1},{17,25},{2,10},{26... | collective-permute-start | bytes 4718600 | tf_op jit(solution)/shard_map/ppermute | solution.py:942
  636.3 195.5 %all-reduce.3.cloned.1.call-start = ((), (), s32[]{:S(2)}) async-start(), calls=%async_computation.14 | async-start | bytes 2064384 | tf_op jit(solution)/shard_map/psum | solution.py:1283
  636.4 44.6 %collective-permute-start.36 = (bf16[1024,1536]{1,0:T(8,128)(2,1)}, bf16[1024,1536]{1,0:T(8,128)(2,1)}, u32[]{:S(2)}, u32[]{:S(2)}) collective-permute-start(bf16[1024,1536]{1,0:T(8,128)(2,1)} %get-tuple-element.605), channel_id=1, source_target_pairs={{0,1},{1,0},{2,3},{3,2},{4,5},{5,4},{6,7},{7,6},{8,9},{9,8},{10,11... | collective-permute-start | bytes 9437192 | tf_op jit(solution)/shard_map/ppermute | solution.py:961
  636.5 48.4 %collective-permute-start.37 = (bf16[1024,1536]{1,0:T(8,128)(2,1)}, bf16[1024,1536]{1,0:T(8,128)(2,1)}, u32[]{:S(2)}, u32[]{:S(2)}) collective-permute-start(bf16[1024,1536]{1,0:T(8,128)(2,1)} %get-tuple-element.607), channel_id=1, source_target_pairs={{0,1},{1,0},{2,3},{3,2},{4,5},{5,4},{6,7},{7,6},{8,9},{9,8},{10,11... | collective-permute-start | bytes 9437192 | tf_op jit(solution)/shard_map/ppermute | solution.py:961
  691.7 46.2 %collective-permute-start.41 = (bf16[512,1536]{1,0:T(8,128)(2,1)S(1)}, bf16[512,1536]{1,0:T(8,128)(2,1)S(1)}, u32[]{:S(2)}, u32[]{:S(2)}) collective-permute-start(bf16[512,1536]{1,0:T(8,128)(2,1)S(1)} %pad_maximum_fusion), channel_id=1, source_target_pairs={{0,4},{1,5},{2,6},{3,7},{4,0},{5,1},{6,2},{7,3},{8,12},{9,13},{10,... | collective-permute-start | bytes 4718600 | tf_op jit(solution)/shard_map/ppermute | solution.py:961
  693.3 45.9 %collective-permute-start.42 = (bf16[512,1536]{1,0:T(8,128)(2,1)S(1)}, bf16[512,1536]{1,0:T(8,128)(2,1)S(1)}, u32[]{:S(2)}, u32[]{:S(2)}) collective-permute-start(bf16[512,1536]{1,0:T(8,128)(2,1)S(1)} %pad_maximum_fusion.1), channel_id=1, source_target_pairs={{0,2},{1,3},{2,0},{3,1},{4,6},{5,7},{6,4},{7,5},{8,10},{9,11},{10,... | collective-permute-start | bytes 4718600 | tf_op jit(solution)/shard_map/ppermute | solution.py:961
  746.1 69.0 %collective-permute-start.44 = (bf16[1536,512]{1,0:T(8,128)(2,1)S(1)}, bf16[1536,512]{1,0:T(8,128)(2,1)S(1)}, u32[]{:S(2)}, u32[]{:S(2)}) collective-permute-start(bf16[1536,512]{1,0:T(8,128)(2,1)S(1)} %add_convert_fusion.3), channel_id=1, source_target_pairs={{8,0},{16,24},{9,1},{17,25},{10,2},{18,26},{11,3},{19,27},{12,4},{... | collective-permute-start | bytes 4718600 | tf_op jit(solution)/shard_map/ppermute | solution.py:947
  (96 other events, 1214.4 us)
Sparse Core Ops, SparseCore 0:
  55.2 45.6 all-gather.4
  106.8 45.1 all-gather.8
  164.2 53.6 all-gather.6
  220.2 47.7 all-gather.10
  271.3 64.2 reduce-scatter.5
  339.3 64.2 reduce-scatter.7
  416.7 77.6 reduce-scatter.9
  496.8 73.9 reduce-scatter.11
  636.4 84.2 reduce-scatter.13
  741.1 66.5 all-reduce.2

commit v8 on v6

--- a/solution.py
+++ b/solution.py
@@ -890,7 +890,7 @@
 
 
 def add_low(a, b):
-    return (a.astype(F32) + b.astype(F32)).astype(BF)
+    return a + b
 
 
 def line_sum(x, n):

time: 853 us -> 865 us (1.014)
  waiting for transfers between devices: 278 us -> 296 us
    convert_element_type x19 -> x0, other arithmetic: 36.9 us -> none  [add_low(): return (a.astype(F32) + b.astype(F32)).astype(BF)]
    add x0 -> x19, other arithmetic: none -> 30.4 us  [add_low(): return a + b]
    psum x1, waiting for transfers between devices: 41.7 us -> 54.1 us  [on_device(): rest = lax.psum(found[0].pop('rest'), 'seq')]
  transfers between devices with their start and end apart: 58 -> 58, of which waited for: 36 -> 34; matrix products, arithmetic and copies ran while one was open for 11% -> 10% of each run, Pallas kernels for 39% -> 38%
where the time goes in v8:
time: 865 us; the launch traced here: 852 us
  Pallas kernels  355 us (41%)
  waiting for transfers between devices  296 us (34%)
  other arithmetic  80.3 us (9%)
  starting transfers between devices  77.6 us (9%)
  local copies, waits for them, and re-layouts  27.3 us (3%)
  between operations  15.3 us (2%)
    ppermute x31, waiting for transfers between devices, swap(): return lax.ppermute(x, 'fsdp', [(i, i ^ mask) for i in range(8)])  120 us
    pallas_call x2, Pallas kernels, run_experts(): pl.pallas_call(functools.partial(expert_kernel, experts, half), name='run...  102 us
    ppermute x4, waiting for transfers between devices, step(): got = lax.ppermute(sent, 'seq', come + go)  69.5 us
    pallas_call x4, Pallas kernels, wide_grad(): pl.pallas_call(functools.partial(wide_grad_kernel, steps, micros), name='...  57.2 us
    psum x1, waiting for transfers between devices, on_device(): rest = lax.psum(found[0].pop('rest'), 'seq')  54.1 us
    ppermute x3, waiting for transfers between devices, step(): self.results.append((summed, lax.ppermute(summed, 'seq', go)))  34 us
    ppermute x31, starting transfers between devices, swap(): return lax.ppermute(x, 'fsdp', [(i, i ^ mask) for i in range(8)])  32.8 us
    pallas_call x2, Pallas kernels, attend_back(): pl.pallas_call(functools.partial(attend_back_kernel, n), name='attend_bac...  31.1 us
  transfers between devices with their start and end apart: 58, of which 34 were waited for; matrix products, arithmetic and copies ran while one was open for 10% of the time, Pallas kernels for 38%

profile of v8, /device:TPU:0, one launch (start us, length us, event | category | flops | bytes accessed | tf_op | source)
XLA Modules:
  0.0 852.1 jit_solution(15104556160375291366)
XLA Ops:
  55.1 11.8 %collective-permute-done.6.low_y_ref = bf16[96,3072]{1,0:T(8,128)(2,1)S(1)} collective-permute-done((bf16[96,3072]{1,0:T(8,128)(2,1)S(1)}, bf16[96,3072]{1,0:T(8,128)(2,1)S(1)}, u32[]{:S(2)}, u32[]{:S(2)}) %collective-permute-start.6) | collective-permute-done | bytes 589856 | tf_op jit(solution)/shard_map/ppermute | solution.py:961
  79.3 17.1 %collective-permute-done.7.top_far_ref = bf16[192,3072]{1,0:T(8,128)(2,1)S(1)} collective-permute-done((bf16[192,3072]{1,0:T(8,128)(2,1)}, bf16[192,3072]{1,0:T(8,128)(2,1)S(1)}, u32[]{:S(2)}, u32[]{:S(2)}) %collective-permute-start.7) | collective-permute-done | bytes 1179680 | tf_op jit(solution)/shard_map/ppermute | solution.py:961
  133.0 12.7 %attend.2 = (bf16[256,1536]{1,0:T(8,128)(2,1)}, bf16[1536,256]{1,0:T(8,128)(2,1)}, f32[32,768]{1,0:T(8,128)}) custom-call(s32[2]{0:T(128)} %pad_add_fusion.info_ref, bf16[1536,512]{1,0:T(8,128)(2,1)} %q_project.1.q_ref, bf16[4,256,1024]{2,1,0:T(8,128)(2,1)} %bitcast.73, bf16[4,256,1024]{2,1,0:T(8,128)(2,1)} %bitcast.74), custom_call_target="tpu_custom_call" | custom-call | flops 644245120 | bytes 445644 | tf_op jit(solution)/shard_map/attend/pallas_call | solution.py:249
  145.7 9.8 %collective-permute-done.15.low_y_ref = bf16[128,1536]{1,0:T(8,128)(2,1)S(1)} collective-permute-done((bf16[128,1536]{1,0:T(8,128)(2,1)S(1)}, bf16[128,1536]{1,0:T(8,128)(2,1)S(1)}, u32[]{:S(2)}, u32[]{:S(2)}) %collective-permute-start.15) | collective-permute-done | bytes 393248 | tf_op jit(solution)/shard_map/ppermute | solution.py:961
  167.9 12.7 %attend.3 = (bf16[256,1536]{1,0:T(8,128)(2,1)}, bf16[1536,256]{1,0:T(8,128)(2,1)}, f32[32,768]{1,0:T(8,128)}) custom-call(s32[2]{0:T(128)} %pad_add_fusion.1.info_ref, bf16[1536,512]{1,0:T(8,128)(2,1)} %q_project.1.q_ref, bf16[4,256,1024]{2,1,0:T(8,128)(2,1)} %bitcast.77, bf16[4,256,1024]{2,1,0:T(8,128)(2,1)} %bitcast.78), custom_call_target="tpu_custom_call" | custom-call | flops 644245120 | bytes 445644 | tf_op jit(solution)/shard_map/attend/pallas_call | solution.py:249
  180.6 11.5 %collective-permute-done.16.top_far_ref = bf16[256,1536]{1,0:T(8,128)(2,1)S(1)} collective-permute-done((bf16[256,1536]{1,0:T(8,128)(2,1)S(1)}, bf16[256,1536]{1,0:T(8,128)(2,1)S(1)}, u32[]{:S(2)}, u32[]{:S(2)}) %collective-permute-start.16) | collective-permute-done | bytes 786464 | tf_op jit(solution)/shard_map/ppermute | solution.py:961
  218.3 50.8 %run_experts.2 = (bf16[1024,1536]{1,0:T(8,128)(2,1)}, bf16[1024,1536]{1,0:T(8,128)(2,1)}, bf16[2048,1664]{1,0:T(8,128)(2,1)}, bf16[2048,1024]{1,0:T(8,128)(2,1)}, bf16[2048,2048]{1,0:T(8,128)(2,1)}) custom-call(s32[1]{0:T(128)} %bitcast.14.own_ref, s32[8]{0:T(128)} %fusion.8.order_ref, bf16[2048,1664]{1,0:T(8,128)(2,1)} %all-gather.7.cloned.1.call-done.xg_ref.refs_0_, ...), custom_call_target="tpu_custom_call" | custom-call | flops 3865470464 | bytes 4718592 | tf_op jit(solution)/shard_map/run_experts/pallas_call | solution.py:507
  269.7 50.8 %run_experts.3 = (bf16[1024,1536]{1,0:T(8,128)(2,1)}, bf16[1024,1536]{1,0:T(8,128)(2,1)}, bf16[2048,1664]{1,0:T(8,128)(2,1)}, bf16[2048,1024]{1,0:T(8,128)(2,1)}, bf16[2048,2048]{1,0:T(8,128)(2,1)}) custom-call(s32[1]{0:T(128)} %bitcast.14.own_ref, s32[8]{0:T(128)} %fusion.8.order_ref, bf16[2048,1664]{1,0:T(8,128)(2,1)} %all-gather.11.cloned.1.call-done.xg_ref.refs_1_, ...), custom_call_target="tpu_custom_call" | custom-call | flops 3865470464 | bytes 4718592 | tf_op jit(solution)/shard_map/run_experts/pallas_call | solution.py:507
  320.6 14.7 %down_grad.2 = bf16[1536,512]{1,0:T(8,128)(2,1)} custom-call(bf16[2048,1024]{1,0:T(8,128)(2,1)} %get-tuple-element.409.refs_0_, bf16[2048,1024]{1,0:T(8,128)(2,1)} %get-tuple-element.410.refs_1_, bf16[1024,1536]{1,0:T(8,128)(2,1)} %assemble.6.ga_ref.refs_2_, bf16[1024,1536]{1,0:T(8,128)(2,1)} %assemble.7.ga_ref.refs_3_, ...), custom_call_target="tpu_custom_call" | custom-call | flops 644245120 | bytes 1677721 | tf_op jit(solution)/shard_map/down_grad/pallas_call | solution.py:622
  338.7 15.2 %down_grad.3 = bf16[1536,512]{1,0:T(8,128)(2,1)} custom-call(bf16[2048,1024]{1,0:T(8,128)(2,1)} %get-tuple-element.409.refs_0_, bf16[2048,1024]{1,0:T(8,128)(2,1)} %get-tuple-element.410.refs_1_, bf16[1024,1536]{1,0:T(8,128)(2,1)} %assemble.6.ga_ref.refs_2_, bf16[1024,1536]{1,0:T(8,128)(2,1)} %assemble.7.ga_ref.refs_3_, ...), custom_call_target="tpu_custom_call" | custom-call | flops 644245120 | bytes 1677721 | tf_op jit(solution)/shard_map/down_grad/pallas_call | solution.py:622
  362.9 10.0 %collective-permute-done.20 = bf16[1536,512]{1,0:T(8,128)(2,1)S(1)} collective-permute-done((bf16[1536,512]{1,0:T(8,128)(2,1)}, bf16[1536,512]{1,0:T(8,128)(2,1)S(1)}, u32[]{:S(2)}, u32[]{:S(2)}) %collective-permute-start.20) | collective-permute-done | bytes 1572896 | tf_op jit(solution)/shard_map/ppermute | solution.py:949
  385.6 14.8 %wide_grad.4 = bf16[1536,512]{1,0:T(8,128)(2,1)} custom-call(bf16[2048,1664]{1,0:T(8,128)(2,1)} %all-gather.7.cloned.1.call-done.xg_ref.refs_0_, bf16[2048,1664]{1,0:T(8,128)(2,1)} %all-gather.11.cloned.1.call-done.xg_ref.refs_1_, bf16[2048,2048]{1,0:T(8,128)(2,1)} %get-tuple-element.490.refs_2_, bf16[2048,2048]{1,0:T(8,128)(2,1)} %get-tuple-element.491.refs_3_), custom_call_target="tpu_custom_call" | custom-call | flops 644245120 | bytes 1835008 | tf_op jit(solution)/shard_map/wide_grad/pallas_call | solution.py:580
  400.3 15.6 %attend_back.2 = (bf16[256,1536]{1,0:T(8,128)(2,1)}, bf16[4,2,256,512]{3,2,1,0:T(8,128)(2,1)}) custom-call(s32[2]{0:T(128)} %pad_add_fusion.info_ref, bf16[1536,512]{1,0:T(8,128)(2,1)} %q_project.1.q_ref, bf16[1536,256]{1,0:T(8,128)(2,1)} %get-tuple-element.653.g_ref, bf16[1536,256]{1,0:T(8,128)(2,1)} %get-tuple-element.436.o_ref.refs_0_, ...), custom_call_target="tpu_custom_call" | custom-call | flops 1610612736 | bytes 734003 | tf_op jit(solution)/shard_map/attend_back/pallas_call | solution.py:349
  436.1 15.6 %attend_back.3 = (bf16[256,1536]{1,0:T(8,128)(2,1)}, bf16[4,2,256,512]{3,2,1,0:T(8,128)(2,1)}) custom-call(s32[2]{0:T(128)} %pad_add_fusion.1.info_ref, bf16[1536,512]{1,0:T(8,128)(2,1)} %q_project.1.q_ref, bf16[1536,256]{1,0:T(8,128)(2,1)} %get-tuple-element.662.g_ref, bf16[1536,256]{1,0:T(8,128)(2,1)} %get-tuple-element.464.refs_1_.o_ref, ...), custom_call_target="tpu_custom_call" | custom-call | flops 1610612736 | bytes 734003 | tf_op jit(solution)/shard_map/attend_back/pallas_call | solution.py:349
  461.2 14.2 %wide_grad.5 = bf16[1536,512]{1,0:T(8,128)(2,1)} custom-call(bf16[2048,1664]{1,0:T(8,128)(2,1)} %all-gather.7.cloned.1.call-done.xg_ref.refs_0_, bf16[2048,1664]{1,0:T(8,128)(2,1)} %all-gather.11.cloned.1.call-done.xg_ref.refs_1_, bf16[2048,2048]{1,0:T(8,128)(2,1)} %get-tuple-element.490.refs_2_, bf16[2048,2048]{1,0:T(8,128)(2,1)} %get-tuple-element.491.refs_3_), custom_call_target="tpu_custom_call" | custom-call | flops 644245120 | bytes 1835008 | tf_op jit(solution)/shard_map/wide_grad/pallas_call | solution.py:580
  475.3 18.3 %collective-permute-done.23 = bf16[1536,512]{1,0:T(8,128)(2,1)} collective-permute-done((bf16[1536,512]{1,0:T(8,128)(2,1)S(1)}, bf16[1536,512]{1,0:T(8,128)(2,1)}, u32[]{:S(2)}, u32[]{:S(2)}) %collective-permute-start.23) | collective-permute-done | bytes 1572896 | tf_op jit(solution)/shard_map/ppermute | solution.py:942
  520.2 19.3 %collective-permute-done.29 = bf16[96,1536]{1,0:T(8,128)(2,1)S(1)} collective-permute-done((bf16[96,1536]{1,0:T(8,128)(2,1)S(1)}, bf16[96,1536]{1,0:T(8,128)(2,1)S(1)}, u32[]{:S(2)}, u32[]{:S(2)}) %collective-permute-start.29) | collective-permute-done | bytes 294944 | tf_op jit(solution)/shard_map/ppermute | solution.py:961
  553.5 14.2 %wide_grad.7 = bf16[1536,512]{1,0:T(8,128)(2,1)} custom-call(bf16[2048,1664]{1,0:T(8,128)(2,1)} %all-gather.7.cloned.1.call-done.xg_ref.refs_0_, bf16[2048,1664]{1,0:T(8,128)(2,1)} %all-gather.11.cloned.1.call-done.xg_ref.refs_1_, bf16[2048,2048]{1,0:T(8,128)(2,1)} %get-tuple-element.490.refs_2_, bf16[2048,2048]{1,0:T(8,128)(2,1)} %get-tuple-element.491.refs_3_), custom_call_target="tpu_custom_call" | custom-call | flops 644245120 | bytes 1835008 | tf_op jit(solution)/shard_map/wide_grad/pallas_call | solution.py:580
  567.7 14.1 %wide_grad.6 = bf16[1536,512]{1,0:T(8,128)(2,1)} custom-call(bf16[2048,1664]{1,0:T(8,128)(2,1)} %all-gather.7.cloned.1.call-done.xg_ref.refs_0_, bf16[2048,1664]{1,0:T(8,128)(2,1)} %all-gather.11.cloned.1.call-done.xg_ref.refs_1_, bf16[2048,2048]{1,0:T(8,128)(2,1)} %get-tuple-element.490.refs_2_, bf16[2048,2048]{1,0:T(8,128)(2,1)} %get-tuple-element.491.refs_3_), custom_call_target="tpu_custom_call" | custom-call | flops 644245120 | bytes 1835008 | tf_op jit(solution)/shard_map/wide_grad/pallas_call | solution.py:580
  614.1 16.9 %collective-permute-done.32 = bf16[1536,512]{1,0:T(8,128)(2,1)} collective-permute-done((bf16[1536,512]{1,0:T(8,128)(2,1)}, bf16[1536,512]{1,0:T(8,128)(2,1)}, u32[]{:S(2)}, u32[]{:S(2)}) %collective-permute-start.32) | collective-permute-done | bytes 1572896 | tf_op jit(solution)/shard_map/ppermute | solution.py:942
  631.0 11.4 %projection_grads.1 = bf16[1536,2688]{1,0:T(8,128)(2,1)} custom-call(bf16[512,1536]{1,0:T(8,128)(2,1)} %get-tuple-element.641.normed_ref, bf16[256,1536]{1,0:T(8,128)(2,1)} %get-tuple-element.654.gq_ref.refs_0_, bf16[256,1536]{1,0:T(8,128)(2,1)} %get-tuple-element.663.gq_ref.refs_1_, bf16[256,1024]{1,0:T(8,128)(2,1)} %turn_back.2.dkv_ref.refs_2_, ...), custom_call_target="tpu_custom_call" | custom-call | flops 422785856 | bytes 1258291 | tf_op jit(solution)/shard_map/projection_grads/pallas_call | solution.py:875
  652.5 34.4 %collective-permute-done.34 = bf16[1536,512]{1,0:T(8,128)(2,1)S(1)} collective-permute-done((bf16[1536,512]{1,0:T(8,128)(2,1)S(1)}, bf16[1536,512]{1,0:T(8,128)(2,1)S(1)}, u32[]{:S(2)}, u32[]{:S(2)}) %collective-permute-start.34) | collective-permute-done | bytes 1572896 | tf_op jit(solution)/shard_map/ppermute | solution.py:942
  705.1 28.0 %collective-permute-done.40 = bf16[1536,512]{1,0:T(8,128)(2,1)S(1)} collective-permute-done((bf16[1536,512]{1,0:T(8,128)(2,1)S(1)}, bf16[1536,512]{1,0:T(8,128)(2,1)S(1)}, u32[]{:S(2)}, u32[]{:S(2)}) %collective-permute-start.40) | collective-permute-done | bytes 1572896 | tf_op jit(solution)/shard_map/ppermute | solution.py:947
  765.2 54.1 %all-reduce.3.cloned.1.call-done = bf16[192,2688]{1,0:T(8,128)(2,1)} async-done(((bf16[192,2688]{1,0:T(8,128)(2,1)}), bf16[192,2688]{1,0:T(8,128)(2,1)}) %all-reduce.3.cloned.1.call-update) | async-done | bytes 1032208 | tf_op jit(solution)/shard_map/psum | solution.py:1283
  (359 shorter events, 349.0 us)
Async XLA Ops:
  7.2 93.7 %all-gather.5.cloned.1.call-start = ((), (), s32[]{:S(2)}) async-start(), calls=%async_computation.5 | async-start | bytes 2621440 | tf_op jit(solution)/shard_map/all_gather | solution.py:1163
  55.1 112.8 %all-gather.9.cloned.1.call-start = ((), (), s32[]{:S(2)}) async-start(), calls=%async_computation.7 | async-start | bytes 2621440 | tf_op jit(solution)/shard_map/all_gather | solution.py:1163
  107.0 111.3 %all-gather.7.cloned.1.call-start = ((), (), s32[]{:S(2)}) async-start(), calls=%async_computation.6 | async-start | bytes 7667712 | tf_op jit(solution)/shard_map/all_gather | solution.py:965
  164.5 105.2 %all-gather.11.cloned.1.call-start = ((), (), s32[]{:S(2)}) async-start(), calls=%async_computation.8 | async-start | bytes 7667712 | tf_op jit(solution)/shard_map/all_gather | solution.py:965
  200.6 153.4 %reduce-scatter.6.cloned.1.call-start = ((), (), s32[]{:S(2)}) async-start(), calls=%async_computation.9 | async-start | bytes 7667712 | tf_op jit(solution)/shard_map/reduce_scatter | solution.py:1092
  269.1 158.2 %reduce-scatter.8.cloned.1.call-start = ((), (), s32[]{:S(2)}) async-start(), calls=%async_computation.10 | async-start | bytes 7667712 | tf_op jit(solution)/shard_map/reduce_scatter | solution.py:1092
  320.5 174.0 %reduce-scatter.10.cloned.1.call-start = ((), (), s32[]{:S(2)}) async-start(), calls=%async_computation.11 | async-start | bytes 2621440 | tf_op jit(solution)/shard_map/reduce_scatter | solution.py:1233
  376.5 39.4 %collective-permute-start.22 = (bf16[1536,512]{1,0:T(8,128)(2,1)S(1)}, bf16[1536,512]{1,0:T(8,128)(2,1)}, u32[]{:S(2)}, u32[]{:S(2)}) collective-permute-start(bf16[1536,512]{1,0:T(8,128)(2,1)S(1)} %add.149), channel_id=1, source_target_pairs={{8,16},{16,8},{9,17},{17,9},{10,18},{18,10},{11,19},{19,11},{12,20... | collective-permute-start | bytes 4718600 | tf_op jit(solution)/shard_map/ppermute | solution.py:939
  378.4 38.9 %collective-permute-start.21 = (bf16[1536,512]{1,0:T(8,128)(2,1)S(1)}, bf16[1536,512]{1,0:T(8,128)(2,1)}, u32[]{:S(2)}, u32[]{:S(2)}) collective-permute-start(bf16[1536,512]{1,0:T(8,128)(2,1)S(1)} %copy-done.22), channel_id=1, source_target_pairs={{0,8},{24,16},{1,9},{25,17},{2,10},{26,18},{3,11},{27,19},{4,12},{... | collective-permute-start | bytes 4718600 | tf_op jit(solution)/shard_map/ppermute | solution.py:949
  417.3 166.7 %reduce-scatter.12.cloned.1.call-start = ((), (), s32[]{:S(2)}) async-start(), calls=%async_computation.12 | async-start | bytes 2621440 | tf_op jit(solution)/shard_map/reduce_scatter | solution.py:1233
  420.5 54.8 %collective-permute-start.24 = (bf16[1536,512]{1,0:T(8,128)(2,1)}, bf16[1536,512]{1,0:T(8,128)(2,1)}, u32[]{:S(2)}, u32[]{:S(2)}) collective-permute-start(bf16[1536,512]{1,0:T(8,128)(2,1)} %add.151), channel_id=1, source_target_pairs={{8,16},{16,8},{9,17},{17,9},{10,18},{18,10},{11,19},{19,11},{12,20... | collective-permute-start | bytes 4718600 | tf_op jit(solution)/shard_map/ppermute | solution.py:939
  424.0 69.7 %collective-permute-start.23 = (bf16[1536,512]{1,0:T(8,128)(2,1)S(1)}, bf16[1536,512]{1,0:T(8,128)(2,1)}, u32[]{:S(2)}, u32[]{:S(2)}) collective-permute-start(bf16[1536,512]{1,0:T(8,128)(2,1)S(1)} %add_select_fusion.3), channel_id=1, source_target_pairs={{0,8},{24,16},{8,0},{16,24},{1,9},{25,17},{9,1},{17,25},{2,10},{26... | collective-permute-start | bytes 4718600 | tf_op jit(solution)/shard_map/ppermute | solution.py:942
  494.6 247.3 %reduce-scatter.14.cloned.1.call-start = ((), (), s32[]{:S(2)}) async-start(), calls=%async_computation.13 | async-start | bytes 9289728 | tf_op jit(solution)/shard_map/reduce_scatter | solution.py:1092
  497.8 84.0 %collective-permute-start.26 = (bf16[1536,512]{1,0:T(8,128)(2,1)}, bf16[1536,512]{1,0:T(8,128)(2,1)}, u32[]{:S(2)}, u32[]{:S(2)}) collective-permute-start(bf16[1536,512]{1,0:T(8,128)(2,1)} %add.153), channel_id=1, source_target_pairs={{8,16},{16,8},{9,17},{17,9},{10,18},{18,10},{11,19},{19,11},{12,20... | collective-permute-start | bytes 4718600 | tf_op jit(solution)/shard_map/ppermute | solution.py:939
  506.6 75.2 %collective-permute-start.25 = (bf16[1536,512]{1,0:T(8,128)(2,1)S(1)}, bf16[1536,512]{1,0:T(8,128)(2,1)}, u32[]{:S(2)}, u32[]{:S(2)}) collective-permute-start(bf16[1536,512]{1,0:T(8,128)(2,1)S(1)} %add_select_fusion.2), channel_id=1, source_target_pairs={{0,8},{24,16},{8,0},{16,24},{1,9},{25,17},{9,1},{17,25},{2,10},{26... | collective-permute-start | bytes 4718600 | tf_op jit(solution)/shard_map/ppermute | solution.py:942
  540.3 41.5 %collective-permute-start.31 = (bf16[96,1536]{1,0:T(8,128)(2,1)S(1)}, bf16[96,1536]{1,0:T(8,128)(2,1)}, u32[]{:S(2)}, u32[]{:S(2)}) collective-permute-start(bf16[96,1536]{1,0:T(8,128)(2,1)S(1)} %get-tuple-element.773), channel_id=1, source_target_pairs={{0,4},{1,5},{2,6},{3,7},{4,0},{5,1},{6,2},{7,3},{8,12},{9,13},{10,... | collective-permute-start | bytes 884744 | tf_op jit(solution)/shard_map/ppermute | solution.py:961
  642.5 176.8 %all-reduce.3.cloned.1.call-start = ((), (), s32[]{:S(2)}) async-start(), calls=%async_computation.14 | async-start | bytes 2064384 | tf_op jit(solution)/shard_map/psum | solution.py:1283
  642.5 44.3 %collective-permute-start.36 = (bf16[1024,1536]{1,0:T(8,128)(2,1)}, bf16[1024,1536]{1,0:T(8,128)(2,1)S(1)}, u32[]{:S(2)}, u32[]{:S(2)}) collective-permute-start(bf16[1024,1536]{1,0:T(8,128)(2,1)} %get-tuple-element.604), channel_id=1, source_target_pairs={{0,1},{1,0},{2,3},{3,2},{4,5},{5,4},{6,7},{7,6},{8,9},{9,8},{10,11... | collective-permute-start | bytes 9437192 | tf_op jit(solution)/shard_map/ppermute | solution.py:961
  642.6 45.1 %collective-permute-start.37 = (bf16[1024,1536]{1,0:T(8,128)(2,1)}, bf16[1024,1536]{1,0:T(8,128)(2,1)S(1)}, u32[]{:S(2)}, u32[]{:S(2)}) collective-permute-start(bf16[1024,1536]{1,0:T(8,128)(2,1)} %get-tuple-element.606), channel_id=1, source_target_pairs={{0,1},{1,0},{2,3},{3,2},{4,5},{5,4},{6,7},{7,6},{8,9},{9,8},{10,11... | collective-permute-start | bytes 9437192 | tf_op jit(solution)/shard_map/ppermute | solution.py:961
  648.4 38.4 %collective-permute-start.34 = (bf16[1536,512]{1,0:T(8,128)(2,1)S(1)}, bf16[1536,512]{1,0:T(8,128)(2,1)S(1)}, u32[]{:S(2)}, u32[]{:S(2)}) collective-permute-start(bf16[1536,512]{1,0:T(8,128)(2,1)S(1)} %add_select_fusion), channel_id=1, source_target_pairs={{0,8},{24,16},{8,0},{16,24},{1,9},{25,17},{9,1},{17,25},{2,10},{26... | collective-permute-start | bytes 4718600 | tf_op jit(solution)/shard_map/ppermute | solution.py:942
  693.7 46.2 %collective-permute-start.41 = (bf16[512,1536]{1,0:T(8,128)(2,1)S(1)}, bf16[512,1536]{1,0:T(8,128)(2,1)S(1)}, u32[]{:S(2)}, u32[]{:S(2)}) collective-permute-start(bf16[512,1536]{1,0:T(8,128)(2,1)S(1)} %pad_maximum_fusion), channel_id=1, source_target_pairs={{0,4},{1,5},{2,6},{3,7},{4,0},{5,1},{6,2},{7,3},{8,12},{9,13},{10,... | collective-permute-start | bytes 4718600 | tf_op jit(solution)/shard_map/ppermute | solution.py:961
  694.5 46.1 %collective-permute-start.42 = (bf16[512,1536]{1,0:T(8,128)(2,1)S(1)}, bf16[512,1536]{1,0:T(8,128)(2,1)S(1)}, u32[]{:S(2)}, u32[]{:S(2)}) collective-permute-start(bf16[512,1536]{1,0:T(8,128)(2,1)S(1)} %pad_maximum_fusion.1), channel_id=1, source_target_pairs={{0,2},{1,3},{2,0},{3,1},{4,6},{5,7},{6,4},{7,5},{8,10},{9,11},{10,... | collective-permute-start | bytes 4718600 | tf_op jit(solution)/shard_map/ppermute | solution.py:961
  754.7 70.3 %collective-permute-start.43 = (bf16[192,1536]{1,0:T(8,128)(2,1)}, bf16[192,1536]{1,0:T(8,128)(2,1)}, u32[]{:S(2)}, u32[]{:S(2)}) collective-permute-start(bf16[192,1536]{1,0:T(8,128)(2,1)} %add.177), channel_id=1, source_target_pairs={{8,16},{16,8},{9,17},{17,9},{10,18},{18,10},{11,19},{19,11},{12,20... | collective-permute-start | bytes 1769480 | tf_op jit(solution)/shard_map/ppermute | solution.py:939
  759.4 66.9 %collective-permute-start.44 = (bf16[1536,512]{1,0:T(8,128)(2,1)}, bf16[1536,512]{1,0:T(8,128)(2,1)}, u32[]{:S(2)}, u32[]{:S(2)}) collective-permute-start(bf16[1536,512]{1,0:T(8,128)(2,1)} %add.178), channel_id=1, source_target_pairs={{8,0},{16,24},{9,1},{17,25},{10,2},{18,26},{11,3},{19,27},{12,4},{... | collective-permute-start | bytes 4718600 | tf_op jit(solution)/shard_map/ppermute | solution.py:947
  (99 other events, 1231.0 us)
Sparse Core Ops, SparseCore 0:
  55.2 45.6 all-gather.4
  107.1 45.1 all-gather.8
  164.6 53.6 all-gather.6
  220.6 47.7 all-gather.10
  271.6 64.2 reduce-scatter.5
  339.6 64.2 reduce-scatter.7
  417.4 77.0 reduce-scatter.9
  496.9 73.6 reduce-scatter.11
  642.6 84.9 reduce-scatter.13
  752.5 66.7 all-reduce.2

commit v9 on v6

--- a/solution.py
+++ b/solution.py
@@ -1252,9 +1252,9 @@
 
     n_grads = len(names)
     work = {
-        0: [("grad", 1), (to_heads, 0)],
-        1: [("grad", 2), (through_heads, 0)],
-        2: [("grad", 3), (to_heads, 1), (through_heads, 1)],
+        0: [("grad", 1), (to_heads, 0), (through_heads, 0)],
+        1: [("grad", 2), ("grad", 3)],
+        2: [(to_heads, 1), (through_heads, 1)],
         3: [("grad", 4), (finish, 0), ("grad", 5)],
         4: [(finish, 1)],
     }
@@ -1288,8 +1288,8 @@
         if t == slots:
             chunks[slots] = heads.arrays[0]
         sent = chunks.pop(t, None)
-        if t in (2, 3):
-            to_owners(t - 2)
+        if t in (1, 3):
+            to_owners(t // 2)
         for kind, i in work.get(t, []):
             if kind != "grad":
                 kind(i)

time: 853 us -> 855 us (level)
  starting transfers between devices: 80.4 us -> 91.9 us
    ppermute x4, waiting for transfers between devices: 64.2 us -> 46.4 us  [step(): got = lax.ppermute(sent, 'seq', come + go)]
    ppermute x3, waiting for transfers between devices: 11.3 us -> 23.7 us  [step(): self.held['crossing'] = (chunk, lax.ppermute(chunk, 'seq', come))]
    ppermute x3, starting transfers between devices: 14.6 us -> 24.6 us  [step(): self.held['crossing'] = (chunk, lax.ppermute(chunk, 'seq', come))]
    ppermute x4, starting transfers between devices: 11 us -> 20.6 us  [step(): got = lax.ppermute(sent, 'seq', come + go)]
  transfers between devices with their start and end apart: 58 -> 58, of which waited for: 36 -> 32; matrix products, arithmetic and copies ran while one was open for 11% -> 11% of each run, Pallas kernels for 39% -> 38%
where the time goes in v9:
time: 855 us; the launch traced here: 850 us
  Pallas kernels  356 us (42%)
  waiting for transfers between devices  272 us (32%)
  starting transfers between devices  91.9 us (11%)
  other arithmetic  87.4 us (10%)
  local copies, waits for them, and re-layouts  27.4 us (3%)
  between operations  15.4 us (2%)
    ppermute x31, waiting for transfers between devices, swap(): return lax.ppermute(x, 'fsdp', [(i, i ^ mask) for i in range(8)])  124 us
    pallas_call x2, Pallas kernels, run_experts(): pl.pallas_call(functools.partial(expert_kernel, experts, half), name='run...  102 us
    pallas_call x4, Pallas kernels, wide_grad(): pl.pallas_call(functools.partial(wide_grad_kernel, steps, micros), name='...  56.7 us
    ppermute x4, waiting for transfers between devices, step(): got = lax.ppermute(sent, 'seq', come + go)  46.4 us
    psum x1, waiting for transfers between devices, on_device(): rest = lax.psum(found[0].pop('rest'), 'seq')  39.8 us
    convert_element_type x19, other arithmetic, add_low(): return (a.astype(F32) + b.astype(F32)).astype(BF)  36.8 us
    ppermute x3, waiting for transfers between devices, step(): self.results.append((summed, lax.ppermute(summed, 'seq', go)))  32.6 us
    pallas_call x2, Pallas kernels, attend_back(): pl.pallas_call(functools.partial(attend_back_kernel, n), name='attend_bac...  31.2 us
  transfers between devices with their start and end apart: 58, of which 32 were waited for; matrix products, arithmetic and copies ran while one was open for 11% of the time, Pallas kernels for 38%

profile of v9, /device:TPU:0, one launch (start us, length us, event | category | flops | bytes accessed | tf_op | source)
XLA Modules:
  0.0 849.9 jit_solution(9494956230167382272)
XLA Ops:
  55.2 11.8 %collective-permute-done.6.low_y_ref = bf16[96,3072]{1,0:T(8,128)(2,1)S(1)} collective-permute-done((bf16[96,3072]{1,0:T(8,128)(2,1)S(1)}, bf16[96,3072]{1,0:T(8,128)(2,1)S(1)}, u32[]{:S(2)}, u32[]{:S(2)}) %collective-permute-start.6) | collective-permute-done | bytes 589856 | tf_op jit(solution)/shard_map/ppermute | solution.py:961
  79.4 17.0 %collective-permute-done.7.top_far_ref = bf16[192,3072]{1,0:T(8,128)(2,1)S(1)} collective-permute-done((bf16[192,3072]{1,0:T(8,128)(2,1)}, bf16[192,3072]{1,0:T(8,128)(2,1)S(1)}, u32[]{:S(2)}, u32[]{:S(2)}) %collective-permute-start.7) | collective-permute-done | bytes 1179680 | tf_op jit(solution)/shard_map/ppermute | solution.py:961
  132.7 12.7 %attend.2 = (bf16[256,1536]{1,0:T(8,128)(2,1)}, bf16[1536,256]{1,0:T(8,128)(2,1)}, f32[32,768]{1,0:T(8,128)}) custom-call(s32[2]{0:T(128)} %pad_add_fusion.info_ref, bf16[1536,512]{1,0:T(8,128)(2,1)} %q_project.1.q_ref, bf16[4,256,1024]{2,1,0:T(8,128)(2,1)} %bitcast.77, bf16[4,256,1024]{2,1,0:T(8,128)(2,1)} %bitcast.78), custom_call_target="tpu_custom_call" | custom-call | flops 644245120 | bytes 445644 | tf_op jit(solution)/shard_map/attend/pallas_call | solution.py:249
  167.6 12.7 %attend.3 = (bf16[256,1536]{1,0:T(8,128)(2,1)}, bf16[1536,256]{1,0:T(8,128)(2,1)}, f32[32,768]{1,0:T(8,128)}) custom-call(s32[2]{0:T(128)} %pad_add_fusion.1.info_ref, bf16[1536,512]{1,0:T(8,128)(2,1)} %q_project.1.q_ref, bf16[4,256,1024]{2,1,0:T(8,128)(2,1)} %bitcast.73, bf16[4,256,1024]{2,1,0:T(8,128)(2,1)} %bitcast.74), custom_call_target="tpu_custom_call" | custom-call | flops 644245120 | bytes 445644 | tf_op jit(solution)/shard_map/attend/pallas_call | solution.py:249
  180.3 11.4 %collective-permute-done.16.top_far_ref = bf16[256,1536]{1,0:T(8,128)(2,1)S(1)} collective-permute-done((bf16[256,1536]{1,0:T(8,128)(2,1)S(1)}, bf16[256,1536]{1,0:T(8,128)(2,1)S(1)}, u32[]{:S(2)}, u32[]{:S(2)}) %collective-permute-start.16) | collective-permute-done | bytes 786464 | tf_op jit(solution)/shard_map/ppermute | solution.py:961
  218.0 50.8 %run_experts.2 = (bf16[1024,1536]{1,0:T(8,128)(2,1)}, bf16[1024,1536]{1,0:T(8,128)(2,1)}, bf16[2048,1664]{1,0:T(8,128)(2,1)}, bf16[2048,1024]{1,0:T(8,128)(2,1)}, bf16[2048,2048]{1,0:T(8,128)(2,1)}) custom-call(s32[1]{0:T(128)} %bitcast.14.own_ref, s32[8]{0:T(128)} %fusion.10.order_ref, bf16[2048,1664]{1,0:T(8,128)(2,1)} %all-gather.7.cloned.1.call-done.xg_ref.refs_0_, ...), custom_call_target="tpu_custom_call" | custom-call | flops 3865470464 | bytes 4718592 | tf_op jit(solution)/shard_map/run_experts/pallas_call | solution.py:507
  268.9 50.8 %run_experts.3 = (bf16[1024,1536]{1,0:T(8,128)(2,1)}, bf16[1024,1536]{1,0:T(8,128)(2,1)}, bf16[2048,1664]{1,0:T(8,128)(2,1)}, bf16[2048,1024]{1,0:T(8,128)(2,1)}, bf16[2048,2048]{1,0:T(8,128)(2,1)}) custom-call(s32[1]{0:T(128)} %bitcast.14.own_ref, s32[8]{0:T(128)} %fusion.10.order_ref, bf16[2048,1664]{1,0:T(8,128)(2,1)} %all-gather.11.cloned.1.call-done.xg_ref.refs_1_, ...), custom_call_target="tpu_custom_call" | custom-call | flops 3865470464 | bytes 4718592 | tf_op jit(solution)/shard_map/run_experts/pallas_call | solution.py:507
  319.8 14.6 %down_grad.2 = bf16[1536,512]{1,0:T(8,128)(2,1)} custom-call(bf16[2048,1024]{1,0:T(8,128)(2,1)} %get-tuple-element.411.refs_0_, bf16[2048,1024]{1,0:T(8,128)(2,1)} %get-tuple-element.412.refs_1_, bf16[1024,1536]{1,0:T(8,128)(2,1)} %assemble.6.ga_ref.refs_2_, bf16[1024,1536]{1,0:T(8,128)(2,1)} %assemble.7.ga_ref.refs_3_, ...), custom_call_target="tpu_custom_call" | custom-call | flops 644245120 | bytes 1677721 | tf_op jit(solution)/shard_map/down_grad/pallas_call | solution.py:622
  334.4 12.3 %collective-permute-start.20 = (bf16[1536,512]{1,0:T(8,128)(2,1)}, bf16[1536,512]{1,0:T(8,128)(2,1)S(1)}, u32[]{:S(2)}, u32[]{:S(2)}) collective-permute-start(bf16[1536,512]{1,0:T(8,128)(2,1)} %down_grad.2), channel_id=1, source_target_pairs={{0,8},{24,16},{1,9},{25,17},{2,10},{26,18},{3,11},{27,19},{4,12},{... | collective-permute-start | bytes 4718600 | tf_op jit(solution)/shard_map/ppermute | solution.py:949
  346.7 15.6 %down_grad.3 = bf16[1536,512]{1,0:T(8,128)(2,1)} custom-call(bf16[2048,1024]{1,0:T(8,128)(2,1)} %get-tuple-element.411.refs_0_, bf16[2048,1024]{1,0:T(8,128)(2,1)} %get-tuple-element.412.refs_1_, bf16[1024,1536]{1,0:T(8,128)(2,1)} %assemble.6.ga_ref.refs_2_, bf16[1024,1536]{1,0:T(8,128)(2,1)} %assemble.7.ga_ref.refs_3_, ...), custom_call_target="tpu_custom_call" | custom-call | flops 644245120 | bytes 1677721 | tf_op jit(solution)/shard_map/down_grad/pallas_call | solution.py:622
  362.3 9.8 %before_attention.2 = (f32[256,1536]{1,0:T(8,128)}, bf16[256,1536]{1,0:T(8,128)(2,1)}, bf16[1536,256]{1,0:T(8,128)(2,1)}, f32[136,1536]{1,0:T(8,128)}) custom-call(s32[8]{0:T(128)} %multiply_add_fusion.place_ref, bf16[256,1664]{1,0:T(8,128)(2,1)} %reduce-scatter.6.cloned.1.call-done.ret_ref, f32[256,1536]{1,0:T(8,128)} %get-tuple-element.384.res_ref, ...), custom_call_target="tpu_custom_call" | custom-call | flops 120795952 | bytes 1022361 | tf_op jit(solution)/shard_map/before_attention/pallas_call | solution.py:685
  372.2 15.7 %attend_back.2 = (bf16[256,1536]{1,0:T(8,128)(2,1)}, bf16[4,2,256,512]{3,2,1,0:T(8,128)(2,1)}) custom-call(s32[2]{0:T(128)} %pad_add_fusion.info_ref, bf16[1536,512]{1,0:T(8,128)(2,1)} %q_project.1.q_ref, bf16[1536,256]{1,0:T(8,128)(2,1)} %get-tuple-element.657.g_ref, bf16[1536,256]{1,0:T(8,128)(2,1)} %get-tuple-element.417.o_ref.refs_0_, ...), custom_call_target="tpu_custom_call" | custom-call | flops 1610612736 | bytes 734003 | tf_op jit(solution)/shard_map/attend_back/pallas_call | solution.py:349
  401.4 14.3 %wide_grad.5 = bf16[1536,512]{1,0:T(8,128)(2,1)} custom-call(bf16[2048,1664]{1,0:T(8,128)(2,1)} %all-gather.7.cloned.1.call-done.xg_ref.refs_0_, bf16[2048,1664]{1,0:T(8,128)(2,1)} %all-gather.11.cloned.1.call-done.xg_ref.refs_1_, bf16[2048,2048]{1,0:T(8,128)(2,1)} %get-tuple-element.494.refs_2_, bf16[2048,2048]{1,0:T(8,128)(2,1)} %get-tuple-element.495.refs_3_), custom_call_target="tpu_custom_call" | custom-call | flops 644245120 | bytes 1835008 | tf_op jit(solution)/shard_map/wide_grad/pallas_call | solution.py:580
  415.6 14.1 %wide_grad.4 = bf16[1536,512]{1,0:T(8,128)(2,1)} custom-call(bf16[2048,1664]{1,0:T(8,128)(2,1)} %all-gather.7.cloned.1.call-done.xg_ref.refs_0_, bf16[2048,1664]{1,0:T(8,128)(2,1)} %all-gather.11.cloned.1.call-done.xg_ref.refs_1_, bf16[2048,2048]{1,0:T(8,128)(2,1)} %get-tuple-element.494.refs_2_, bf16[2048,2048]{1,0:T(8,128)(2,1)} %get-tuple-element.495.refs_3_), custom_call_target="tpu_custom_call" | custom-call | flops 644245120 | bytes 1835008 | tf_op jit(solution)/shard_map/wide_grad/pallas_call | solution.py:580
  429.8 23.6 %collective-permute-done.21 = bf16[1536,512]{1,0:T(8,128)(2,1)} collective-permute-done((bf16[1536,512]{1,0:T(8,128)(2,1)}, bf16[1536,512]{1,0:T(8,128)(2,1)}, u32[]{:S(2)}, u32[]{:S(2)}) %collective-permute-start.21) | collective-permute-done | bytes 1572896 | tf_op jit(solution)/shard_map/ppermute | solution.py:949
  479.1 15.5 %attend_back.3 = (bf16[256,1536]{1,0:T(8,128)(2,1)}, bf16[4,2,256,512]{3,2,1,0:T(8,128)(2,1)}) custom-call(s32[2]{0:T(128)} %pad_add_fusion.1.info_ref, bf16[1536,512]{1,0:T(8,128)(2,1)} %q_project.1.q_ref, bf16[1536,256]{1,0:T(8,128)(2,1)} %get-tuple-element.666.g_ref, bf16[1536,256]{1,0:T(8,128)(2,1)} %get-tuple-element.464.refs_1_.o_ref, ...), custom_call_target="tpu_custom_call" | custom-call | flops 1610612736 | bytes 734003 | tf_op jit(solution)/shard_map/attend_back/pallas_call | solution.py:349
  557.7 14.2 %wide_grad.7 = bf16[1536,512]{1,0:T(8,128)(2,1)} custom-call(bf16[2048,1664]{1,0:T(8,128)(2,1)} %all-gather.7.cloned.1.call-done.xg_ref.refs_0_, bf16[2048,1664]{1,0:T(8,128)(2,1)} %all-gather.11.cloned.1.call-done.xg_ref.refs_1_, bf16[2048,2048]{1,0:T(8,128)(2,1)} %get-tuple-element.494.refs_2_, bf16[2048,2048]{1,0:T(8,128)(2,1)} %get-tuple-element.495.refs_3_), custom_call_target="tpu_custom_call" | custom-call | flops 644245120 | bytes 1835008 | tf_op jit(solution)/shard_map/wide_grad/pallas_call | solution.py:580
  571.9 14.1 %wide_grad.6 = bf16[1536,512]{1,0:T(8,128)(2,1)} custom-call(bf16[2048,1664]{1,0:T(8,128)(2,1)} %all-gather.7.cloned.1.call-done.xg_ref.refs_0_, bf16[2048,1664]{1,0:T(8,128)(2,1)} %all-gather.11.cloned.1.call-done.xg_ref.refs_1_, bf16[2048,2048]{1,0:T(8,128)(2,1)} %get-tuple-element.494.refs_2_, bf16[2048,2048]{1,0:T(8,128)(2,1)} %get-tuple-element.495.refs_3_), custom_call_target="tpu_custom_call" | custom-call | flops 644245120 | bytes 1835008 | tf_op jit(solution)/shard_map/wide_grad/pallas_call | solution.py:580
  616.0 18.9 %collective-permute-done.32 = bf16[1536,512]{1,0:T(8,128)(2,1)} collective-permute-done((bf16[1536,512]{1,0:T(8,128)(2,1)}, bf16[1536,512]{1,0:T(8,128)(2,1)}, u32[]{:S(2)}, u32[]{:S(2)}) %collective-permute-start.32) | collective-permute-done | bytes 1572896 | tf_op jit(solution)/shard_map/ppermute | solution.py:942
  634.9 11.4 %projection_grads.1 = bf16[1536,2688]{1,0:T(8,128)(2,1)} custom-call(bf16[512,1536]{1,0:T(8,128)(2,1)} %get-tuple-element.645.normed_ref, bf16[256,1536]{1,0:T(8,128)(2,1)} %get-tuple-element.658.gq_ref.refs_0_, bf16[256,1536]{1,0:T(8,128)(2,1)} %get-tuple-element.667.gq_ref.refs_1_, bf16[256,1024]{1,0:T(8,128)(2,1)} %turn_back.2.dkv_ref.refs_2_, ...), custom_call_target="tpu_custom_call" | custom-call | flops 422785856 | bytes 1258291 | tf_op jit(solution)/shard_map/projection_grads/pallas_call | solution.py:875
  664.2 27.5 %collective-permute-done.34 = bf16[1536,512]{1,0:T(8,128)(2,1)} collective-permute-done((bf16[1536,512]{1,0:T(8,128)(2,1)S(1)}, bf16[1536,512]{1,0:T(8,128)(2,1)}, u32[]{:S(2)}, u32[]{:S(2)}) %collective-permute-start.34) | collective-permute-done | bytes 1572896 | tf_op jit(solution)/shard_map/ppermute | solution.py:942
  717.9 25.4 %collective-permute-done.40 = bf16[1536,512]{1,0:T(8,128)(2,1)S(1)} collective-permute-done((bf16[1536,512]{1,0:T(8,128)(2,1)S(1)}, bf16[1536,512]{1,0:T(8,128)(2,1)S(1)}, u32[]{:S(2)}, u32[]{:S(2)}) %collective-permute-start.40) | collective-permute-done | bytes 1572896 | tf_op jit(solution)/shard_map/ppermute | solution.py:947
  759.9 13.8 %collective-permute-done.46 = bf16[256,1536]{1,0:T(8,128)(2,1)S(1)} collective-permute-done((bf16[256,1536]{1,0:T(8,128)(2,1)S(1)}, bf16[256,1536]{1,0:T(8,128)(2,1)S(1)}, u32[]{:S(2)}, u32[]{:S(2)}) %collective-permute-start.46) | collective-permute-done | bytes 786464 | tf_op jit(solution)/shard_map/ppermute | solution.py:961
  776.1 39.8 %all-reduce.3.cloned.1.call-done = bf16[192,2688]{1,0:T(8,128)(2,1)} async-done(((bf16[192,2688]{1,0:T(8,128)(2,1)}), bf16[192,2688]{1,0:T(8,128)(2,1)}) %all-reduce.3.cloned.1.call-update) | async-done | bytes 1032208 | tf_op jit(solution)/shard_map/psum | solution.py:1283
  (365 shorter events, 366.4 us)
Async XLA Ops:
  7.2 93.8 %all-gather.5.cloned.1.call-start = ((), (), s32[]{:S(2)}) async-start(), calls=%async_computation.5 | async-start | bytes 2621440 | tf_op jit(solution)/shard_map/all_gather | solution.py:1163
  55.2 112.4 %all-gather.9.cloned.1.call-start = ((), (), s32[]{:S(2)}) async-start(), calls=%async_computation.7 | async-start | bytes 2621440 | tf_op jit(solution)/shard_map/all_gather | solution.py:1163
  106.7 111.3 %all-gather.7.cloned.1.call-start = ((), (), s32[]{:S(2)}) async-start(), calls=%async_computation.6 | async-start | bytes 7667712 | tf_op jit(solution)/shard_map/all_gather | solution.py:965
  164.1 104.7 %all-gather.11.cloned.1.call-start = ((), (), s32[]{:S(2)}) async-start(), calls=%async_computation.8 | async-start | bytes 7667712 | tf_op jit(solution)/shard_map/all_gather | solution.py:965
  200.3 162.0 %reduce-scatter.6.cloned.1.call-start = ((), (), s32[]{:S(2)}) async-start(), calls=%async_computation.9 | async-start | bytes 7667712 | tf_op jit(solution)/shard_map/reduce_scatter | solution.py:1092
  268.8 201.6 %reduce-scatter.8.cloned.1.call-start = ((), (), s32[]{:S(2)}) async-start(), calls=%async_computation.10 | async-start | bytes 7667712 | tf_op jit(solution)/shard_map/reduce_scatter | solution.py:1092
  319.7 184.4 %reduce-scatter.10.cloned.1.call-start = ((), (), s32[]{:S(2)}) async-start(), calls=%async_computation.11 | async-start | bytes 2621440 | tf_op jit(solution)/shard_map/reduce_scatter | solution.py:1233
  334.4 53.4 %collective-permute-start.20 = (bf16[1536,512]{1,0:T(8,128)(2,1)}, bf16[1536,512]{1,0:T(8,128)(2,1)S(1)}, u32[]{:S(2)}, u32[]{:S(2)}) collective-permute-start(bf16[1536,512]{1,0:T(8,128)(2,1)} %down_grad.2), channel_id=1, source_target_pairs={{0,8},{24,16},{1,9},{25,17},{2,10},{26,18},{3,11},{27,19},{4,12},{... | collective-permute-start | bytes 4718600 | tf_op jit(solution)/shard_map/ppermute | solution.py:949
  390.9 38.9 %collective-permute-start.22 = (bf16[1536,512]{1,0:T(8,128)(2,1)S(1)}, bf16[1536,512]{1,0:T(8,128)(2,1)}, u32[]{:S(2)}, u32[]{:S(2)}) collective-permute-start(bf16[1536,512]{1,0:T(8,128)(2,1)S(1)} %add_convert_fusion.14), channel_id=1, source_target_pairs={{8,16},{16,8},{9,17},{17,9},{10,18},{18,10},{11,19},{19,11},{12,20... | collective-permute-start | bytes 4718600 | tf_op jit(solution)/shard_map/ppermute | solution.py:939
  392.7 60.7 %collective-permute-start.21 = (bf16[1536,512]{1,0:T(8,128)(2,1)}, bf16[1536,512]{1,0:T(8,128)(2,1)}, u32[]{:S(2)}, u32[]{:S(2)}) collective-permute-start(bf16[1536,512]{1,0:T(8,128)(2,1)} %down_grad.3), channel_id=1, source_target_pairs={{0,8},{24,16},{1,9},{25,17},{2,10},{26,18},{3,11},{27,19},{4,12},{... | collective-permute-start | bytes 4718600 | tf_op jit(solution)/shard_map/ppermute | solution.py:949
  401.3 186.9 %reduce-scatter.12.cloned.1.call-start = ((), (), s32[]{:S(2)}) async-start(), calls=%async_computation.12 | async-start | bytes 2621440 | tf_op jit(solution)/shard_map/reduce_scatter | solution.py:1233
  456.9 47.1 %collective-permute-start.24 = (bf16[1536,512]{1,0:T(8,128)(2,1)}, bf16[1536,512]{1,0:T(8,128)(2,1)}, u32[]{:S(2)}, u32[]{:S(2)}) collective-permute-start(bf16[1536,512]{1,0:T(8,128)(2,1)} %add_convert_fusion.12), channel_id=1, source_target_pairs={{8,16},{16,8},{9,17},{17,9},{10,18},{18,10},{11,19},{19,11},{12,20... | collective-permute-start | bytes 4718600 | tf_op jit(solution)/shard_map/ppermute | solution.py:939
  461.2 42.8 %collective-permute-start.23 = (bf16[1536,512]{1,0:T(8,128)(2,1)S(1)}, bf16[1536,512]{1,0:T(8,128)(2,1)}, u32[]{:S(2)}, u32[]{:S(2)}) collective-permute-start(bf16[1536,512]{1,0:T(8,128)(2,1)S(1)} %fusion), channel_id=1, source_target_pairs={{0,8},{24,16},{8,0},{16,24},{1,9},{25,17},{9,1},{17,25},{2,10},{26... | collective-permute-start | bytes 4718600 | tf_op jit(solution)/shard_map/ppermute | solution.py:942
  504.2 247.8 %reduce-scatter.14.cloned.1.call-start = ((), (), s32[]{:S(2)}) async-start(), calls=%async_computation.13 | async-start | bytes 9289728 | tf_op jit(solution)/shard_map/reduce_scatter | solution.py:1092
  507.4 78.7 %collective-permute-start.26 = (bf16[1536,512]{1,0:T(8,128)(2,1)}, bf16[1536,512]{1,0:T(8,128)(2,1)}, u32[]{:S(2)}, u32[]{:S(2)}) collective-permute-start(bf16[1536,512]{1,0:T(8,128)(2,1)} %add_convert_fusion.10), channel_id=1, source_target_pairs={{8,16},{16,8},{9,17},{17,9},{10,18},{18,10},{11,19},{19,11},{12,20... | collective-permute-start | bytes 4718600 | tf_op jit(solution)/shard_map/ppermute | solution.py:939
  516.4 69.6 %collective-permute-start.25 = (bf16[1536,512]{1,0:T(8,128)(2,1)S(1)}, bf16[1536,512]{1,0:T(8,128)(2,1)}, u32[]{:S(2)}, u32[]{:S(2)}) collective-permute-start(bf16[1536,512]{1,0:T(8,128)(2,1)S(1)} %fusion.1), channel_id=1, source_target_pairs={{0,8},{24,16},{8,0},{16,24},{1,9},{25,17},{9,1},{17,25},{2,10},{26... | collective-permute-start | bytes 4718600 | tf_op jit(solution)/shard_map/ppermute | solution.py:942
  546.0 40.1 %collective-permute-start.31 = (bf16[96,1536]{1,0:T(8,128)(2,1)S(1)}, bf16[96,1536]{1,0:T(8,128)(2,1)}, u32[]{:S(2)}, u32[]{:S(2)}) collective-permute-start(bf16[96,1536]{1,0:T(8,128)(2,1)S(1)} %get-tuple-element.777), channel_id=1, source_target_pairs={{0,4},{1,5},{2,6},{3,7},{4,0},{5,1},{6,2},{7,3},{8,12},{9,13},{10,... | collective-permute-start | bytes 884744 | tf_op jit(solution)/shard_map/ppermute | solution.py:961
  646.4 169.5 %all-reduce.3.cloned.1.call-start = ((), (), s32[]{:S(2)}) async-start(), calls=%async_computation.14 | async-start | bytes 2064384 | tf_op jit(solution)/shard_map/psum | solution.py:1283
  646.4 45.3 %collective-permute-start.36 = (bf16[1024,1536]{1,0:T(8,128)(2,1)}, bf16[1024,1536]{1,0:T(8,128)(2,1)}, u32[]{:S(2)}, u32[]{:S(2)}) collective-permute-start(bf16[1024,1536]{1,0:T(8,128)(2,1)} %get-tuple-element.608), channel_id=1, source_target_pairs={{0,1},{1,0},{2,3},{3,2},{4,5},{5,4},{6,7},{7,6},{8,9},{9,8},{10,11... | collective-permute-start | bytes 9437192 | tf_op jit(solution)/shard_map/ppermute | solution.py:961
  646.5 49.1 %collective-permute-start.37 = (bf16[1024,1536]{1,0:T(8,128)(2,1)}, bf16[1024,1536]{1,0:T(8,128)(2,1)}, u32[]{:S(2)}, u32[]{:S(2)}) collective-permute-start(bf16[1024,1536]{1,0:T(8,128)(2,1)} %get-tuple-element.610), channel_id=1, source_target_pairs={{0,1},{1,0},{2,3},{3,2},{4,5},{5,4},{6,7},{7,6},{8,9},{9,8},{10,11... | collective-permute-start | bytes 9437192 | tf_op jit(solution)/shard_map/ppermute | solution.py:961
  702.5 45.9 %collective-permute-start.41 = (bf16[512,1536]{1,0:T(8,128)(2,1)S(1)}, bf16[512,1536]{1,0:T(8,128)(2,1)S(1)}, u32[]{:S(2)}, u32[]{:S(2)}) collective-permute-start(bf16[512,1536]{1,0:T(8,128)(2,1)S(1)} %pad_maximum_fusion), channel_id=1, source_target_pairs={{0,4},{1,5},{2,6},{3,7},{4,0},{5,1},{6,2},{7,3},{8,12},{9,13},{10,... | collective-permute-start | bytes 4718600 | tf_op jit(solution)/shard_map/ppermute | solution.py:961
  704.4 45.7 %collective-permute-start.42 = (bf16[512,1536]{1,0:T(8,128)(2,1)S(1)}, bf16[512,1536]{1,0:T(8,128)(2,1)S(1)}, u32[]{:S(2)}, u32[]{:S(2)}) collective-permute-start(bf16[512,1536]{1,0:T(8,128)(2,1)S(1)} %pad_maximum_fusion.1), channel_id=1, source_target_pairs={{0,2},{1,3},{2,0},{3,1},{4,6},{5,7},{6,4},{7,5},{8,10},{9,11},{10,... | collective-permute-start | bytes 4718600 | tf_op jit(solution)/shard_map/ppermute | solution.py:961
  754.2 67.4 %collective-permute-start.43 = (bf16[192,1536]{1,0:T(8,128)(2,1)}, bf16[192,1536]{1,0:T(8,128)(2,1)}, u32[]{:S(2)}, u32[]{:S(2)}) collective-permute-start(bf16[192,1536]{1,0:T(8,128)(2,1)} %add_convert_fusion.16), channel_id=1, source_target_pairs={{8,16},{16,8},{9,17},{17,9},{10,18},{18,10},{11,19},{19,11},{12,20... | collective-permute-start | bytes 1769480 | tf_op jit(solution)/shard_map/ppermute | solution.py:939
  758.6 65.6 %collective-permute-start.44 = (bf16[1536,512]{1,0:T(8,128)(2,1)}, bf16[1536,512]{1,0:T(8,128)(2,1)}, u32[]{:S(2)}, u32[]{:S(2)}) collective-permute-start(bf16[1536,512]{1,0:T(8,128)(2,1)} %add_convert_fusion.3), channel_id=1, source_target_pairs={{8,0},{16,24},{9,1},{17,25},{10,2},{18,26},{11,3},{19,27},{12,4},{... | collective-permute-start | bytes 4718600 | tf_op jit(solution)/shard_map/ppermute | solution.py:947
  (102 other events, 1337.1 us)
Sparse Core Ops, SparseCore 0:
  55.3 45.6 all-gather.4
  106.8 45.1 all-gather.8
  164.3 53.6 all-gather.6
  220.3 47.7 all-gather.10
  271.3 64.2 reduce-scatter.5
  339.3 64.2 reduce-scatter.7
  406.0 63.7 reduce-scatter.9
  504.3 70.2 reduce-scatter.11
  646.5 83.7 reduce-scatter.13
  752.1 63.7 all-reduce.2
